TPU v7x, 32 devices: a whole 2x2x4 slice. The times are simulated.
32 devices in a mesh: seq: 8 (over z, x), shard: 4 (over y, core).
Axes of the slice: x: 2, y: 2, z: 4, core: 2. Of those that a mesh axis runs over, the one named last changes fastest.
Arguments:
- tokens: bfloat16 [2, 4, 512, 2048], P(None, 'shard', 'seq'), may hold values from -6 to 6
- first_gain: float32 [2048], replicated, may hold values from 0.5 to 1.5
- branch_weight: bfloat16 [2048, 2736], P('shard'), may hold values from -0.125 to 0.125
- input_weight: bfloat16 [2048, 2736], P('shard'), may hold values from -0.125 to 0.125
- conv_weight: bfloat16 [4, 2736], P(None, 'seq'), may hold values from -3 to 3
- conv_bias: float32 [2736], P('seq'), may hold values from -3 to 3
- rate_weight: bfloat16 [16, 171, 171], P('seq'), may hold values from -0.4375 to 0.4375
- rate_bias: float32 [2736], P('seq'), may hold values from -4 to 4
- entry_weight: bfloat16 [16, 171, 171], P('seq'), may hold values from -0.4375 to 0.4375
- entry_bias: float32 [2736], P('seq'), may hold values from -4 to 4
- decay_param: float32 [2736], P('seq'), may hold values from 4.3 to 9
- output_weight: bfloat16 [2736, 2048], P(None, 'shard'), may hold values from -0.109375 to 0.109375
- second_gain: float32 [2048], replicated, may hold values from 0.5 to 1.5
- hidden_gate: bfloat16 [2048, 6144], P(None, 'shard'), may hold values from -0.125 to 0.125
- hidden_up: bfloat16 [2048, 6144], P(None, 'shard'), may hold values from -0.125 to 0.125
- hidden_down: bfloat16 [6144, 2048], P('shard'), may hold values from -0.078125 to 0.078125
- cotangent: bfloat16 [2, 4, 512, 2048], P(None, 'shard', 'seq'), may hold values from -6 to 6
Outputs:
- result: bfloat16 [2, 4, 512, 2048], P(None, 'shard', 'seq')
- tokens_grad: float32 [2, 4, 512, 2048], P(None, 'shard', 'seq')
- first_gain_grad: float32 [2048], P(('seq', 'shard'))
- branch_weight_grad: float32 [2048, 2736], P(('seq', 'shard'))
- input_weight_grad: float32 [2048, 2736], P(('seq', 'shard'))
- conv_weight_grad: float32 [4, 2736], P(None, 'seq')
- conv_bias_grad: float32 [2736], P('seq')
- rate_weight_grad: float32 [16, 171, 171], P('seq')
- rate_bias_grad: float32 [2736], P('seq')
- entry_weight_grad: float32 [16, 171, 171], P('seq')
- entry_bias_grad: float32 [2736], P('seq')
- decay_grad: float32 [2736], P('seq')
- output_weight_grad: float32 [2736, 2048], P(None, ('seq', 'shard'))
- second_gain_grad: float32 [2048], P(('seq', 'shard'))
- hidden_gate_grad: float32 [2048, 6144], P(('seq', 'shard'))
- hidden_up_grad: float32 [2048, 6144], P(('seq', 'shard'))
- hidden_down_grad: float32 [6144, 2048], P(None, ('seq', 'shard'))
All inputs are finite; a program needn't handle non-finite values.
Results may differ from a plain program's by a relative error of at most 0.012.
Values may be sent and summed in bfloat16 or wider, within the bound.
A program may use at most 576 MiB of HBM per device.

v0:
```python
import jax
import jax.numpy as jnp
from jax import lax
from jax.sharding import PartitionSpec as P

EPSILON = 1e-06
DECAY_SCALE = 8.0
MULT_FLOOR = 0.01


def norm_scale(values, gain_vec):
    inv_root = lax.rsqrt(jnp.mean(values * values, axis=-1, keepdims=True) + EPSILON)
    return values * inv_root * gain_vec


def gelu_tanh(values):
    return jax.nn.gelu(values, approximate=True)


def gate_product(gate_pre, up_pre):
    return gelu_tanh(gate_pre) * up_pre


def causal_conv(series, weight, shift_bias):
    tap_count = weight.shape[0]
    length = series.shape[0]
    padded = jnp.pad(series, ((tap_count - 1, 0), (0, 0)))
    running = jnp.zeros_like(series) + shift_bias
    for offset in range(tap_count):
        running = (
            running
            + weight[offset] * padded[tap_count - 1 - offset : tap_count - 1 - offset + length]
        )
    return running


def combine_pairs(earlier, later_pair):
    return (earlier[0] * later_pair[0], later_pair[0] * earlier[1] + later_pair[1])


def recurrence(rate_pre, entry_pre, mixed_vals, decay_raw):
    log_decay = -DECAY_SCALE * jax.nn.sigmoid(rate_pre) * jax.nn.softplus(-decay_raw)
    decay_step = jnp.exp(log_decay)
    multiplier = jnp.sqrt(jnp.maximum(1.0 - decay_step * decay_step, MULT_FLOOR))
    pushed = multiplier * jax.nn.sigmoid(entry_pre) * mixed_vals
    decay_total, states = lax.associative_scan(combine_pairs, (decay_step, pushed), axis=0)
    return states


def matmul(left_op, right_op):
    return jnp.dot(left_op, right_op, preferred_element_type=jnp.float32)


def against(left_op, right_op):
    return lax.dot_general(
        left_op, right_op, (((1,), (1,)), ((), ())), preferred_element_type=jnp.float32
    )


def contract_rows(left_op, right_op):
    return lax.dot_general(
        left_op, right_op, (((0,), (0,)), ((), ())), preferred_element_type=jnp.float32
    )


def body(
    tokens,
    first_gain,
    branch_weight,
    input_weight,
    conv_weight,
    conv_bias,
    rate_weight,
    rate_bias,
    entry_weight,
    entry_bias,
    decay_param,
    output_weight,
    second_gain,
    hidden_gate,
    hidden_up,
    hidden_down,
    cotangent,
):
    quarters = tokens.shape[0]
    quarter_len = tokens.shape[2]
    model_width = tokens.shape[3]
    row_count = quarters * quarter_len
    seq_parts = lax.axis_size("seq")
    lru_width = branch_weight.shape[1]
    channels = lru_width // seq_parts
    length = row_count * seq_parts
    blocks = rate_weight.shape[0]
    block_width = rate_weight.shape[1]
    inputs = tokens.reshape(row_count, model_width).astype(jnp.float32)
    first_normed, first_pullback = jax.vjp(norm_scale, inputs, first_gain)
    first_low = first_normed.astype(jnp.bfloat16)
    full_branch, full_input, full_output = (
        lax.all_gather(branch_weight, "shard", axis=0, tiled=True),
        lax.all_gather(input_weight, "shard", axis=0, tiled=True),
        lax.all_gather(output_weight, "shard", axis=1, tiled=True),
    )
    branch_pre = matmul(first_low, full_branch)
    input_low = matmul(first_low, full_input).astype(jnp.bfloat16)
    arriving = lax.all_to_all(
        input_low.reshape(quarters, quarter_len, lru_width),
        "seq",
        split_axis=2,
        concat_axis=1,
        tiled=True,
    )
    series = arriving.reshape(length, channels).astype(jnp.float32)
    mixed_vals, conv_pullback = jax.vjp(
        causal_conv, series, conv_weight.astype(jnp.float32), conv_bias
    )
    mixed_low = mixed_vals.astype(jnp.bfloat16)
    grouped = mixed_low.reshape(length, blocks, block_width)
    rate_pre = (
        jnp.einsum(
            "lkb,kbc->lkc", grouped, rate_weight, preferred_element_type=jnp.float32
        ).reshape(length, channels)
        + rate_bias
    )
    entry_pre = (
        jnp.einsum(
            "lkb,kbc->lkc", grouped, entry_weight, preferred_element_type=jnp.float32
        ).reshape(length, channels)
        + entry_bias
    )
    states, scan_pullback = jax.vjp(
        recurrence, rate_pre, entry_pre, mixed_low.astype(jnp.float32), decay_param
    )
    state_low = states.astype(jnp.bfloat16).reshape(quarters, quarter_len * seq_parts, channels)
    returned = lax.all_to_all(state_low, "seq", split_axis=1, concat_axis=2, tiled=True)
    state_rows = returned.reshape(row_count, lru_width).astype(jnp.float32)
    branch_act, branch_pullback = jax.vjp(gelu_tanh, branch_pre)
    gated_low = (state_rows * branch_act).astype(jnp.bfloat16)
    middle = inputs + matmul(gated_low, full_output)
    second_normed, second_pullback = jax.vjp(norm_scale, middle, second_gain)
    second_low = second_normed.astype(jnp.bfloat16)
    pieces = (
        lax.all_gather(hidden_gate, "shard", axis=1, tiled=True),
        lax.all_gather(hidden_up, "shard", axis=1, tiled=True),
    )
    gate_part = matmul(second_low, pieces[0])
    up_part = matmul(second_low, pieces[1])
    gate_pre = gate_part
    up_pre = up_part
    hidden_act, hidden_pullback = jax.vjp(gate_product, gate_pre, up_pre)
    hidden_low = hidden_act.astype(jnp.bfloat16)
    ffn_out = matmul(hidden_low, lax.all_gather(hidden_down, "shard", axis=0, tiled=True))
    result = (middle + ffn_out).astype(jnp.bfloat16).reshape(tokens.shape)
    upstream = cotangent.reshape(row_count, model_width)
    hidden_grad = against(upstream, lax.all_gather(hidden_down, "shard", axis=0, tiled=True))
    gate_grad, up_grad = hidden_pullback(hidden_grad)
    gate_low = gate_grad.astype(jnp.bfloat16)
    up_low = up_grad.astype(jnp.bfloat16)
    pieces = (
        lax.all_gather(hidden_gate, "shard", axis=1, tiled=True),
        lax.all_gather(hidden_up, "shard", axis=1, tiled=True),
    )
    gate_part = gate_low
    up_part = up_low
    second_grad = against(gate_part, pieces[0]) + against(up_part, pieces[1])
    ffn_terms = (
        contract_rows(second_low, gate_low),
        contract_rows(second_low, up_low),
        contract_rows(upstream, hidden_low),
    )
    gate_sum, up_sum, down_sum = (
        lax.psum_scatter(ffn_terms[0], ("seq", "shard"), scatter_dimension=0, tiled=True),
        lax.psum_scatter(ffn_terms[1], ("seq", "shard"), scatter_dimension=0, tiled=True),
        lax.psum_scatter(ffn_terms[2], ("seq", "shard"), scatter_dimension=0, tiled=True),
    )
    middle_norm_grad, second_gain_grad = second_pullback(second_grad)
    middle_grad = middle_norm_grad + upstream.astype(jnp.float32)
    middle_low = middle_grad.astype(jnp.bfloat16)
    back_branch, back_input, back_output = (
        lax.all_gather(branch_weight, "shard", axis=0, tiled=True),
        lax.all_gather(input_weight, "shard", axis=0, tiled=True),
        lax.all_gather(output_weight, "shard", axis=1, tiled=True),
    )
    gated_grad = against(middle_low, back_output)
    state_grad = (gated_grad * branch_act).astype(jnp.bfloat16)
    branch_low = branch_pullback(gated_grad * state_rows)[0].astype(jnp.bfloat16)
    back_arriving = lax.all_to_all(
        state_grad.reshape(quarters, quarter_len, lru_width),
        "seq",
        split_axis=2,
        concat_axis=1,
        tiled=True,
    )
    state_series = back_arriving.reshape(length, channels).astype(jnp.float32)
    rate_grad, entry_grad, mixed_scan, decay_grad = scan_pullback(state_series)
    rate_low = rate_grad.astype(jnp.bfloat16).reshape(length, blocks, block_width)
    entry_low = entry_grad.astype(jnp.bfloat16).reshape(length, blocks, block_width)
    through_gates = jnp.einsum(
        "lkc,kbc->lkb", rate_low, rate_weight, preferred_element_type=jnp.float32
    ) + jnp.einsum("lkc,kbc->lkb", entry_low, entry_weight, preferred_element_type=jnp.float32)
    mixed_grad = mixed_scan + through_gates.reshape(length, channels)
    rate_weight_grad = jnp.einsum(
        "lkb,lkc->kbc", grouped, rate_low, preferred_element_type=jnp.float32
    )
    entry_weight_grad = jnp.einsum(
        "lkb,lkc->kbc", grouped, entry_low, preferred_element_type=jnp.float32
    )
    rate_bias_grad = jnp.sum(rate_low.astype(jnp.float32), axis=0).reshape(channels)
    entry_bias_grad = jnp.sum(entry_low.astype(jnp.float32), axis=0).reshape(channels)
    series_grad, conv_weight_grad, conv_bias_grad = conv_pullback(mixed_grad)
    series_low = series_grad.astype(jnp.bfloat16).reshape(
        quarters, quarter_len * seq_parts, channels
    )
    input_back = lax.all_to_all(series_low, "seq", split_axis=1, concat_axis=2, tiled=True).reshape(
        row_count, lru_width
    )
    first_grad = against(branch_low, back_branch) + against(input_back, back_input)
    inputs_grad, first_gain_grad = first_pullback(first_grad)
    tokens_grad = (middle_grad + inputs_grad).reshape(tokens.shape)
    block_terms = (
        contract_rows(first_low, branch_low),
        contract_rows(first_low, input_back),
        contract_rows(middle_low, gated_low),
        first_gain_grad,
        second_gain_grad,
    )
    branch_sum, input_sum, output_sum, first_gain_sum, second_gain_sum = (
        lax.psum_scatter(block_terms[0], ("seq", "shard"), scatter_dimension=0, tiled=True),
        lax.psum_scatter(block_terms[1], ("seq", "shard"), scatter_dimension=0, tiled=True),
        lax.psum_scatter(block_terms[2], ("seq", "shard"), scatter_dimension=0, tiled=True),
        lax.psum_scatter(block_terms[3], ("seq", "shard"), scatter_dimension=0, tiled=True),
        lax.psum_scatter(block_terms[4], ("seq", "shard"), scatter_dimension=0, tiled=True),
    )
    channel_sums = lax.psum(
        (
            conv_weight_grad,
            conv_bias_grad,
            rate_weight_grad,
            rate_bias_grad,
            entry_weight_grad,
            entry_bias_grad,
            decay_grad,
        ),
        "shard",
    )
    return (
        result,
        tokens_grad,
        first_gain_sum,
        branch_sum,
        input_sum,
        channel_sums[0],
        channel_sums[1],
        channel_sums[2],
        channel_sums[3],
        channel_sums[4],
        channel_sums[5],
        channel_sums[6],
        output_sum.T,
        second_gain_sum,
        gate_sum,
        up_sum,
        down_sum.T,
    )


def solution(mesh):
    placed = (
        P(None, "shard", "seq", None),
        P(),
        P("shard", None),
        P("shard", None),
        P(None, "seq"),
        P("seq"),
        P("seq", None, None),
        P("seq"),
        P("seq", None, None),
        P("seq"),
        P("seq"),
        P(None, "shard"),
        P(),
        P(None, "shard"),
        P(None, "shard"),
        P("shard", None),
        P(None, "shard", "seq", None),
    )
    return jax.shard_map(
        body,
        mesh=mesh,
        in_specs=placed,
        out_specs=(
            P(None, "shard", "seq", None),
            P(None, "shard", "seq", None),
            P(("seq", "shard")),
            P(("seq", "shard"), None),
            P(("seq", "shard"), None),
            P(None, "seq"),
            P("seq"),
            P("seq", None, None),
            P("seq"),
            P("seq", None, None),
            P("seq"),
            P("seq"),
            P(None, ("seq", "shard")),
            P(("seq", "shard")),
            P(("seq", "shard"), None),
            P(("seq", "shard"), None),
            P(None, ("seq", "shard")),
        ),
        check_vma=False,
    )
```

profile of v0, /device:TPU:9, one launch (start us, length us, event | category | flops | bytes accessed | tf_op | source)
XLA Modules:
  0.0 3183.4 jit_solution(8229641516323657590)
XLA Ops:
  13.9 71.6 %all-gather.7.cloned.1.call-done = bf16[2048,2736]{0,1:T(8,128)(2,1)} async-done(((bf16[512,2736]{0,1:T(8,128)(2,1)}), bf16[2048,2736]{0,1:T(8,128)(2,1)}) %all-gather.7.cloned.1.call-update) | async-done | bytes 11206672 | tf_op jit(solution)/shard_map/all_gather | solution.py:100
  102.7 15.2 all-to-all-done
  344.8 24.8 all_to_all.42
  398.2 17.5 fusion.114
  415.8 134.1 %all-gather.15.cloned.1.call-done = bf16[2048,6144]{1,0:T(8,128)(2,1)} async-done(((bf16[2048,1536]{1,0:T(8,128)(2,1)}), bf16[2048,6144]{1,0:T(8,128)(2,1)}) %all-gather.15.cloned.1.call-update) | async-done | bytes 25165840 | tf_op jit(solution)/shard_map/all_gather | solution.py:143
  549.8 14.3 fusion.115
  564.1 142.0 %all-gather.17.cloned.1.call-done = bf16[6144,2048]{1,0:T(8,128)(2,1)} async-done(((bf16[1536,2048]{1,0:T(8,128)(2,1)}), bf16[6144,2048]{1,0:T(8,128)(2,1)}) %all-gather.17.cloned.1.call-update) | async-done | bytes 25165840 | tf_op jit(solution)/shard_map/all_gather | solution.py:151
  706.1 17.3 multiply_convert_fusion
  723.4 14.3 fusion.116
  737.7 15.6 multiply_reduce_fusion.5
  775.0 22.9 all_to_all.43
  1080.3 12.5 fusion.33
  1114.0 26.6 all-to-all-done.3
  1153.1 19.9 fusion.122
  1174.4 20.0 fusion.123
  1195.9 19.9 convolution_bitcast_fusion
  1215.9 49.2 %copy.97 = f32[2048,6144]{1,0:T(8,128)} copy(f32[2048,6144]{0,1:T(8,128)} %convolution_bitcast_fusion) | data formatting | bytes 100663296
  1283.8 19.5 all-reduce.107
  1315.0 47.3 %all-reduce.106 = (f32[2048]{0:T(1024)S(1)}, f32[2048]{0:T(1024)S(1)}) all-reduce(f32[2048]{0:T(1024)S(1)} %get-tuple-element.78, f32[2048]{0:T(1024)S(1)} %copy-done.43), channel_id=2, replica_groups=mesh['seq'=8,'shard'=4] {'seq','shard'}, use_global_device_ids=true, to_apply=%region_5.6.clone | all-reduce | flops 4096 | bytes 32768
  1366.1 246.4 %reduce-scatter.13.cloned.1.call-done = f32[64,2736]{1,0:T(8,128)} async-done(((f32[2048,2736]{1,0:T(8,128)}), f32[64,2736]{1,0:T(8,128)}) %reduce-scatter.13.cloned.1.call-update) | async-done | bytes 700432 | tf_op jit(solution)/shard_map/reduce_scatter | solution.py:229
  1612.4 252.4 %reduce-scatter.11.cloned.1.call-done = f32[64,2736]{1,0:T(8,128)} async-done(((f32[2048,2736]{1,0:T(8,128)}), f32[64,2736]{1,0:T(8,128)}) %reduce-scatter.11.cloned.1.call-update) | async-done | bytes 700432 | tf_op jit(solution)/shard_map/reduce_scatter | solution.py:228
  1864.8 436.6 %reduce-scatter.15.cloned.1.call-done = f32[64,6144]{1,0:T(8,128)} async-done(((f32[2048,6144]{1,0:T(8,128)}), f32[64,6144]{1,0:T(8,128)}) %reduce-scatter.15.cloned.1.call-update) | async-done | bytes 1572880 | tf_op jit(solution)/shard_map/reduce_scatter | solution.py:171
  2301.4 437.5 %reduce-scatter.17.cloned.1.call-done = f32[64,6144]{1,0:T(8,128)} async-done(((f32[2048,6144]{1,0:T(8,128)}), f32[64,6144]{1,0:T(8,128)}) %reduce-scatter.17.cloned.1.call-update) | async-done | bytes 1572880 | tf_op jit(solution)/shard_map/reduce_scatter | solution.py:172
  2738.9 437.6 %reduce-scatter.19.cloned.1.call-done = f32[64,6144]{1,0:T(8,128)} async-done(((f32[2048,6144]{1,0:T(8,128)}), f32[64,6144]{1,0:T(8,128)}) %reduce-scatter.19.cloned.1.call-update) | async-done | bytes 1572880
  (506 shorter events, 653.3 us)
Async XLA Ops:
  7.2 121.7 %copy-start = (bf16[2,171,171]{2,0,1:T(2,128)(2,1)S(1)}, bf16[2,171,171]{2,0,1:T(2,128)(2,1)}, u32[]{:S(2)}) copy-start(bf16[2,171,171]{2,0,1:T(2,128)(2,1)} %param.23) | copy-start | bytes 350896
  7.2 78.3 %all-gather.7.cloned.1.call-start = ((), (), s32[]{:S(2)}) async-start(), calls=%async_computation.10 | async-start | bytes 14008320 | tf_op jit(solution)/shard_map/all_gather | solution.py:100
  7.9 372.6 %all-gather.9.cloned.1.call-start = ((), (), s32[]{:S(2)}) async-start(), calls=%async_computation.11 | async-start | bytes 14008320 | tf_op jit(solution)/shard_map/all_gather | solution.py:99
  8.7 381.1 %all-gather.11.cloned.1.call-start = ((), (), s32[]{:S(2)}) async-start(), calls=%async_computation.12 | async-start | bytes 14008320 | tf_op jit(solution)/shard_map/all_gather | solution.py:101
  9.4 388.8 %all-gather.13.cloned.1.call-start = ((), (), s32[]{:S(2)}) async-start(), calls=%async_computation.13 | async-start | bytes 31457280 | tf_op jit(solution)/shard_map/all_gather | solution.py:142
  10.0 539.8 %all-gather.15.cloned.1.call-start = ((), (), s32[]{:S(2)}) async-start(), calls=%async_computation.14 | async-start | bytes 31457280 | tf_op jit(solution)/shard_map/all_gather | solution.py:143
  10.6 695.5 %all-gather.17.cloned.1.call-start = ((), (), s32[]{:S(2)}) async-start(), calls=%async_computation.15 | async-start | bytes 31457280 | tf_op jit(solution)/shard_map/all_gather | solution.py:151
  13.9 78.9 %copy-start.15 = (bf16[128,2048]{1,0:T(8,128)(2,1)}, bf16[128,2048]{1,0:T(8,128)(2,1)S(1)}, u32[]{:S(2)}) copy-start(bf16[128,2048]{1,0:T(8,128)(2,1)S(1)} %fusion.27) | copy-start | bytes 1572868
  96.9 21.0 all-to-all-start
  102.4 1201.0 %all-reduce.111.cloned.1.call-start = ((), (), s32[]{:S(2)}) async-start(), calls=%async_computation.22 | async-start | bytes 1441792 | tf_op jit(solution)/shard_map/psum | solution.py:233
  227.5 66.8 %copy-start.34 = (f32[4,342]{1,0:T(4,128)}, f32[4,342]{1,0:T(4,128)S(1)}, u32[]{:S(2)}) copy-start(f32[4,342]{1,0:T(4,128)S(1)} %slice.381) | copy-start | bytes 16420
  850.0 64.0 %slice-start.4 = ((f32[32,342]{1,0:T(8,128)}), f32[1,342]{1,0:T(1,128)S(1)}, s32[]{:S(2)}) async-start(f32[32,342]{1,0:T(8,128)} %slice.420), calls=%async_computation.27 | async-start | bytes 3072 | tf_op jit(solution)/shard_map/transpose(jvp())/split | solution.py:46
  865.2 57.4 %slice-start.3 = ((f32[64,342]{1,0:T(8,128)}), f32[1,342]{1,0:T(1,128)S(1)}, s32[]{:S(2)}) async-start(f32[64,342]{1,0:T(8,128)} %slice.418), calls=%async_computation.26 | async-start | bytes 3072 | tf_op jit(solution)/shard_map/transpose(jvp())/split | solution.py:46
  1067.8 298.2 %reduce-scatter.9.cloned.1.call-start = ((), (), s32[]{:S(2)}) async-start(), calls=%async_computation.16 | async-start | bytes 23789568 | tf_op jit(solution)/shard_map/reduce_scatter | solution.py:227
  1080.3 532.1 %reduce-scatter.13.cloned.1.call-start = ((), (), s32[]{:S(2)}) async-start(), calls=%async_computation.18 | async-start | bytes 23789568 | tf_op jit(solution)/shard_map/reduce_scatter | solution.py:229
  1109.1 31.5 all-to-all-start.3
  1113.8 751.1 %reduce-scatter.11.cloned.1.call-start = ((), (), s32[]{:S(2)}) async-start(), calls=%async_computation.17 | async-start | bytes 23789568 | tf_op jit(solution)/shard_map/reduce_scatter | solution.py:228
  1151.5 1150.0 %reduce-scatter.15.cloned.1.call-start = ((), (), s32[]{:S(2)}) async-start(), calls=%async_computation.19 | async-start | bytes 51904512 | tf_op jit(solution)/shard_map/reduce_scatter | solution.py:171
  1173.0 1565.9 %reduce-scatter.17.cloned.1.call-start = ((), (), s32[]{:S(2)}) async-start(), calls=%async_computation.20 | async-start | bytes 51904512 | tf_op jit(solution)/shard_map/reduce_scatter | solution.py:172
  1194.4 1982.1 %reduce-scatter.19.cloned.1.call-start = ((), (), s32[]{:S(2)}) async-start(), calls=%async_computation.21 | async-start | bytes 51904512
  1272.5 34.8 %copy-start.33 = (f32[2048]{0:T(1024)S(1)}, f32[2048]{0:T(1024)}, u32[]{:S(2)}) copy-start(f32[2048]{0:T(1024)} %param.18) | copy-start | bytes 24580
  1307.3 56.1 %copy-start.74 = (f32[128]{0:T(128)S(1)}, f32[128]{0:T(128)}, u32[]{:S(2)}) copy-start(f32[128]{0:T(128)} %copy-done.73) | copy-start | bytes 1540
  1307.3 56.1 %copy-start.20 = (f32[128,2048]{1,0:T(8,128)S(1)}, f32[128,2048]{1,0:T(8,128)}, u32[]{:S(2)}) copy-start(f32[128,2048]{1,0:T(8,128)} %copy-done.19) | copy-start | bytes 3145732
  1363.5 1813.0 %copy-start.1 = (bf16[2,171,171]{2,0,1:T(2,128)(2,1)S(1)}, bf16[2,171,171]{2,0,1:T(2,128)(2,1)}, u32[]{:S(2)}) copy-start(bf16[2,171,171]{2,0,1:T(2,128)(2,1)} %param.23) | copy-start | bytes 350896
  (71 other events, 477.8 us)
Sparse Core Ops, SparseCore 0:
  9.6 75.8 all-gather.6
  87.1 74.3 all-gather.8
  163.0 74.2 all-gather.10
  238.7 154.7 all-gather.12
  395.0 154.7 all-gather.14
  551.3 154.8 all-gather.16
  1067.9 32.8 all-reduce.110
  1103.8 251.1 reduce-scatter.8
  1357.8 254.5 reduce-scatter.12
  1615.2 249.6 reduce-scatter.10
  1871.8 429.5 reduce-scatter.14
  2308.3 430.5 reduce-scatter.16
  2745.9 430.5 reduce-scatter.18
where the time goes:
time: 3200 us; the launch traced here: 3180 us
  waiting for transfers between devices  2200 us (69%)
  local copies, waits for them, and re-layouts  458 us (14%)
  matrix products  241 us (8%)
  other arithmetic  139 us (4%)
  blocking collectives  114 us (4%)
    unnamed x14, waiting for transfers between devices  441 us
    reduce_scatter x1, waiting for transfers between devices, body(): lax.psum_scatter(ffn_terms[1], ('seq', 'shard'), scatter_dimension=0, til...  437 us
    reduce_scatter x1, waiting for transfers between devices, body(): lax.psum_scatter(ffn_terms[0], ('seq', 'shard'), scatter_dimension=0, til...  437 us
    reduce_scatter x1, waiting for transfers between devices, body(): lax.psum_scatter(block_terms[1], ('seq', 'shard'), scatter_dimension=0, t...  252 us
    reduce_scatter x1, waiting for transfers between devices, body(): lax.psum_scatter(block_terms[2], ('seq', 'shard'), scatter_dimension=0, t...  246 us
    pad x79, local copies, waits for them, and re-layouts, recurrence(): lax.associative_scan(combine_pairs, (decay_step, pushed), axis=0)  187 us
    slice x78, local copies, waits for them, and re-layouts, recurrence(): lax.associative_scan(combine_pairs, (decay_step, pushed), axis=0)  144 us
    all_gather x1, waiting for transfers between devices, body(): lax.all_gather(hidden_down, 'shard', axis=0, tiled=True)  142 us
  transfers between devices with their start and end apart: 15, of which 10 were waited for; matrix products, arithmetic and copies ran while one was open for 15% of the time, Pallas kernels for 0%

commit v1 on v0

v1 whole, which is shorter than its diff:
```python
import functools

import jax
import jax.numpy as jnp
from jax import lax
from jax.experimental import pallas as pl
from jax.experimental.pallas import tpu as pltpu
from jax.sharding import PartitionSpec as P

EPSILON = 1e-06
DECAY_SCALE = 8.0
MULT_FLOOR = 0.01
LANES = 128
SEGMENTS = 8
GELU_C = 0.7978845608028654
GELU_A = 0.044715
F32 = jnp.float32
BF16 = jnp.bfloat16


def dot(left, right, dims=((1,), (0,))):
    return lax.dot_general(left, right, (dims, ((), ())), preferred_element_type=F32)


def gelu_and_slope(x):
    inner = GELU_C * (x + GELU_A * x * x * x)
    t = jnp.tanh(inner)
    half = 0.5 * (1.0 + t)
    slope = half + 0.5 * x * (1.0 - t * t) * (GELU_C * (1.0 + 3.0 * GELU_A * x * x))
    return x * half, slope


def gelu_tanh(x):
    return x * (0.5 * (1.0 + jnp.tanh(GELU_C * (x + GELU_A * x * x * x))))


def sigmoid(x):
    return 0.5 * jnp.tanh(0.5 * x) + 0.5


def softplus(x):
    return jnp.maximum(x, 0.0) + jnp.log1p(jnp.exp(-jnp.abs(x)))


def lane_groups(width):
    return [slice(g * LANES, (g + 1) * LANES) for g in range(width // LANES)]


def put(ref, rows, value):
    for g, lanes in enumerate(lane_groups(value.shape[1])):
        ref[g, rows, :] = value[:, lanes]


def take(ref, rows):
    return jnp.concatenate([ref[g, rows, :] for g in range(ref.shape[0])], axis=1)


def strided_scan(steps, groups, load, store):
    def step(k, carry):
        i = steps(k)
        out = []
        for g in range(groups):
            state, total = carry[g]
            factor, term = load(g, i)
            state = factor * state + term
            total = factor * total
            store(g, i, state, total)
            out.append((state, total))
        return tuple(out)

    return step


TAP, CONV_B, RATE_B, ENTRY_B, DECAY = 0, 4, 5, 6, 7


def gate_values(pre, log_scale, width):
    r = sigmoid(pre[:, :width])
    e = sigmoid(pre[:, width:])
    a = jnp.exp(r * log_scale)
    room = 1.0 - a * a
    m = jnp.sqrt(jnp.maximum(room, MULT_FLOOR))
    return r, e, a, room, m


def scan_forward_kernel(
    parts, quarters, chunk, proj_ref, par_ref, gates_ref, z_ref, h_ref, v_ref, u_pad, a_s, b_s
):
    length, width = h_ref.shape
    seg = length // SEGMENTS
    chunks = length // chunk

    def place(c):
        q = c // parts
        s = c - q * parts
        return pl.multiple_of((s * quarters + q) * chunk, chunk)

    def time_of(c):
        return pl.multiple_of(c * chunk, chunk)

    log_scale = -DECAY_SCALE * softplus(-par_ref[DECAY : DECAY + 1, :])
    bias = jnp.concatenate(
        [par_ref[RATE_B : RATE_B + 1, :], par_ref[ENTRY_B : ENTRY_B + 1, :]], axis=1
    )
    u_pad[0:8, :] = jnp.zeros((8, width), F32)

    def first(c, carry):
        u = proj_ref[pl.ds(place(c), chunk), width : 2 * width].astype(BF16).astype(F32)
        u_pad[pl.ds(pl.multiple_of(time_of(c) + 8, 8), chunk), :] = u
        wide = u_pad[pl.ds(time_of(c), chunk + 8), :]
        v = par_ref[CONV_B : CONV_B + 1, :] + par_ref[0:1, :] * wide[8:]
        for k in range(1, 4):
            v = v + par_ref[k : k + 1, :] * wide[8 - k : 8 - k + chunk]
        v = v.astype(BF16)
        v_ref[pl.ds(time_of(c), chunk), :] = v
        pre = dot(v, gates_ref[...]) + bias
        r, e, a, room, m = gate_values(pre, log_scale, width)
        put(a_s, pl.ds(time_of(c), chunk), a)
        put(b_s, pl.ds(time_of(c), chunk), m * e * v.astype(F32))
        return carry

    lax.fori_loop(0, chunks, first, 0)

    def load(g, i):
        at = pl.ds(i, SEGMENTS, stride=seg)
        return a_s[g, at, :], b_s[g, at, :]

    def store(g, i, state, total):
        at = pl.ds(i, SEGMENTS, stride=seg)
        b_s[g, at, :] = state
        a_s[g, at, :] = total

    groups = width // LANES
    start = (jnp.zeros((SEGMENTS, LANES), F32), jnp.ones((SEGMENTS, LANES), F32))
    ends = lax.fori_loop(
        0, seg, strided_scan(lambda k: k, groups, load, store), (start,) * groups, unroll=8
    )
    final = jnp.concatenate([e[0] for e in ends], axis=1)
    totals = jnp.concatenate([e[1] for e in ends], axis=1)
    carries = [jnp.zeros((1, width), F32)]
    for j in range(SEGMENTS - 1):
        carries.append(totals[j : j + 1] * carries[j] + final[j : j + 1])
    for j in range(SEGMENTS):
        per = seg // chunk

        def last(k, carry, j=j, per=per):
            c = j * per + k
            rows = pl.ds(time_of(c), chunk)
            h = take(b_s, rows) + take(a_s, rows) * carries[j]
            h_ref[rows, :] = h
            y = gelu_tanh(proj_ref[pl.ds(place(c), chunk), 0:width])
            z_ref[pl.ds(place(c), chunk), :] = (h.astype(BF16).astype(F32) * y).astype(BF16)
            return carry

        lax.fori_loop(0, per, last, 0)


def scan_forward(parts, quarters, chunk, proj, params, gates):
    length, width = proj.shape[0], proj.shape[1] // 2
    return pl.pallas_call(
        functools.partial(scan_forward_kernel, parts, quarters, chunk),
        out_shape=(
            jax.ShapeDtypeStruct((length, width), BF16),
            jax.ShapeDtypeStruct((length, width), F32),
            jax.ShapeDtypeStruct((length, width), BF16),
        ),
        in_specs=[pl.BlockSpec(memory_space=pltpu.VMEM)] * 3,
        out_specs=[pl.BlockSpec(memory_space=pltpu.VMEM)] * 3,
        scratch_shapes=[
            pltpu.VMEM((length + 8, width), F32),
            pltpu.VMEM((width // LANES, length, LANES), F32),
            pltpu.VMEM((width // LANES, length, LANES), F32),
        ],
        compiler_params=pltpu.CompilerParams(vmem_limit_bytes=48 * 2**20),
        name="scan_forward",
    )(proj, params, gates)


def scan_backward_kernel(
    parts,
    quarters,
    chunk,
    dz_ref,
    proj_ref,
    h_ref,
    v_ref,
    par_ref,
    gates_ref,
    both_ref,
    gate_grad_ref,
    sums_ref,
    a_s,
    g_s,
    t_s,
    h_pad,
    pre_s,
    dpre_s,
    dv_s,
    u_pad,
):
    length, width = h_ref.shape
    seg = length // SEGMENTS
    chunks = length // chunk

    def place(c):
        q = c // parts
        s = c - q * parts
        return pl.multiple_of((s * quarters + q) * chunk, chunk)

    def time_of(c):
        return pl.multiple_of(c * chunk, chunk)

    softplus_decay = softplus(-par_ref[DECAY : DECAY + 1, :])
    log_scale = -DECAY_SCALE * softplus_decay
    bias = jnp.concatenate(
        [par_ref[RATE_B : RATE_B + 1, :], par_ref[ENTRY_B : ENTRY_B + 1, :]], axis=1
    )
    zeros8 = jnp.zeros((8, width), F32)
    put(a_s, pl.ds(length, 8), zeros8)
    h_pad[0:8, :] = zeros8
    u_pad[0:8, :] = zeros8
    dv_s[pl.ds(length, 8), :] = zeros8

    def first(c, carry):
        rows = pl.ds(time_of(c), chunk)
        later = pl.ds(pl.multiple_of(time_of(c) + 8, 8), chunk)
        there = pl.ds(place(c), chunk)
        h = h_ref[rows, :]
        h_pad[later, :] = h
        u_pad[later, :] = proj_ref[there, width : 2 * width].astype(BF16).astype(F32)
        y, slope = gelu_and_slope(proj_ref[there, 0:width])
        dz = dz_ref[there, :]
        put(g_s, rows, (dz * y).astype(BF16).astype(F32))
        both_ref[there, 0:width] = (dz * h.astype(BF16).astype(F32) * slope).astype(BF16)
        pre = dot(v_ref[rows, :], gates_ref[...]) + bias
        pre_s[rows, :] = pre
        put(a_s, rows, jnp.exp(sigmoid(pre[:, :width]) * log_scale))
        return carry

    lax.fori_loop(0, chunks, first, 0)

    def load(g, i):
        return (
            a_s[g, pl.ds(i + 1, SEGMENTS, stride=seg), :],
            g_s[g, pl.ds(i, SEGMENTS, stride=seg), :],
        )

    def store(g, i, state, total):
        g_s[g, pl.ds(i, SEGMENTS, stride=seg), :] = state
        t_s[g, pl.ds(i, SEGMENTS, stride=seg), :] = total

    groups = width // LANES
    start = (jnp.zeros((SEGMENTS, LANES), F32), jnp.ones((SEGMENTS, LANES), F32))
    ends = lax.fori_loop(
        0,
        seg,
        strided_scan(lambda k: seg - 1 - k, groups, load, store),
        (start,) * groups,
        unroll=8,
    )
    firsts = jnp.concatenate([e[0] for e in ends], axis=1)
    totals = jnp.concatenate([e[1] for e in ends], axis=1)
    carries = [None] * SEGMENTS
    carries[SEGMENTS - 1] = jnp.zeros((1, width), F32)
    for j in range(SEGMENTS - 2, -1, -1):
        carries[j] = totals[j + 1 : j + 2] * carries[j + 1] + firsts[j + 1 : j + 2]

    def fold(values):
        return jnp.sum(values.reshape(chunk // 8, 8, values.shape[1]), axis=0)

    sums_ref[...] = jnp.zeros(sums_ref.shape, F32)

    for j in range(SEGMENTS):
        per = seg // chunk

        def middle(k, carry, j=j, per=per):
            c = j * per + k
            rows = pl.ds(time_of(c), chunk)
            g = take(g_s, rows) + take(t_s, rows) * carries[j]
            before = h_pad[pl.ds(time_of(c), chunk + 8), :][7 : 7 + chunk]
            v = v_ref[rows, :].astype(F32)
            r, e, a, room, m = gate_values(pre_s[rows, :], log_scale, width)
            gv = g * v
            held = jnp.where(room > MULT_FLOOR, gv * e * a / m, 0.0)
            ta = (g * before - held) * a * r
            drpre = (ta * (log_scale * (1.0 - r))).astype(BF16)
            depre = (gv * m * e * (1.0 - e)).astype(BF16)
            dpre_s[rows, 0:width] = drpre
            dpre_s[rows, width : 2 * width] = depre
            sums_ref[0:8, :] += fold(ta)
            sums_ref[8:16, :] += fold(drpre.astype(F32))
            sums_ref[16:24, :] += fold(depre.astype(F32))
            dv = g * m * e + dot(dpre_s[rows, :], gates_ref[...], ((1,), (1,)))
            dv_s[rows, :] = dv
            sums_ref[24:32, :] += fold(dv)
            wide = u_pad[pl.ds(time_of(c), chunk + 8), :]
            for tap in range(4):
                at = 32 + 8 * tap
                sums_ref[at : at + 8, :] += fold(dv * wide[8 - tap : 8 - tap + chunk])
            return carry

        lax.fori_loop(0, per, middle, 0)
    sums_ref[0:8, :] = sums_ref[0:8, :] * (
        DECAY_SCALE * sigmoid(-par_ref[DECAY : DECAY + 1, :])
    )

    def last(c, carry):
        wide = dv_s[pl.ds(time_of(c), chunk + 8), :]
        du = par_ref[0:1, :] * wide[0:chunk]
        for tap in range(1, 4):
            du = du + par_ref[tap : tap + 1, :] * wide[tap : tap + chunk]
        both_ref[pl.ds(place(c), chunk), width : 2 * width] = du.astype(BF16)
        return carry

    lax.fori_loop(0, chunks, last, 0)
    gate_grad_ref[...] = dot(v_ref[...], dpre_s[...], ((0,), (0,)))


def scan_backward(parts, quarters, chunk, dz, proj, h, v, params, gates):
    length, width = h.shape
    return pl.pallas_call(
        functools.partial(scan_backward_kernel, parts, quarters, chunk),
        out_shape=(
            jax.ShapeDtypeStruct((length, 2 * width), BF16),
            jax.ShapeDtypeStruct((width, 2 * width), F32),
            jax.ShapeDtypeStruct((64, width), F32),
        ),
        in_specs=[pl.BlockSpec(memory_space=pltpu.VMEM)] * 6,
        out_specs=[pl.BlockSpec(memory_space=pltpu.VMEM)] * 3,
        scratch_shapes=[
            pltpu.VMEM((width // LANES, length + 8, LANES), F32),
            pltpu.VMEM((width // LANES, length, LANES), F32),
            pltpu.VMEM((width // LANES, length, LANES), F32),
            pltpu.VMEM((length + 8, width), F32),
            pltpu.VMEM((length, 2 * width), F32),
            pltpu.VMEM((length, 2 * width), BF16),
            pltpu.VMEM((length + 8, width), F32),
            pltpu.VMEM((length + 8, width), F32),
        ],
        compiler_params=pltpu.CompilerParams(vmem_limit_bytes=52 * 2**20),
        name="scan_backward",
    )(dz, proj, h, v, params, gates)


def rms_parts(values):
    return lax.rsqrt(jnp.mean(values * values, axis=-1, keepdims=True) + EPSILON)


def rms_back(values, scale, gain, grad):
    k = grad * gain
    return scale * k - scale * scale * scale * values * jnp.mean(
        k * values, axis=-1, keepdims=True
    )


def body(
    tokens,
    first_gain,
    branch_weight,
    input_weight,
    conv_weight,
    conv_bias,
    rate_weight,
    rate_bias,
    entry_weight,
    entry_bias,
    decay_param,
    output_weight,
    second_gain,
    hidden_gate,
    hidden_up,
    hidden_down,
    cotangent,
):
    quarters, _, chunk, model = tokens.shape
    rows = quarters * chunk
    parts = lax.axis_size("seq")
    shards = lax.axis_size("shard")
    inner = 2
    outer = parts // inner
    seq_at = lax.axis_index("seq")
    inner_at = lax.rem(seq_at, inner)
    lru = branch_weight.shape[1]
    channels = lru // parts
    width = (channels + LANES) // LANES * LANES
    spare = width - channels
    blocks, block_width = rate_weight.shape[0], rate_weight.shape[1]
    piece = model // (parts * shards)
    pairs = [[o * inner + i for i in range(inner)] for o in range(outer)]
    columns = [[o * inner + i for o in range(outer)] for i in range(inner)]

    def gather_seq(x):
        return lax.all_gather(x, "seq", axis=0, tiled=True)

    def scatter_seq(x):
        return lax.psum_scatter(x, "seq", scatter_dimension=0, tiled=True)

    def gather_plane(x):
        x = lax.all_gather(x, "shard", axis=0, tiled=True)
        return lax.all_gather(x, "seq", axis=0, tiled=True, axis_index_groups=pairs)

    def scatter_plane(x):
        x = lax.psum_scatter(x, "seq", scatter_dimension=0, tiled=True, axis_index_groups=pairs)
        return lax.psum_scatter(x, "shard", scatter_dimension=0, tiled=True)

    def own(weight, axis):
        part = lax.dynamic_slice_in_dim(weight, seq_at * channels, channels, axis)
        pads = [(0, 0), (0, 0)]
        pads[axis] = (0, spare)
        return jnp.pad(part, pads)

    w_in = lax.all_gather(
        jnp.concatenate([own(branch_weight, 1), own(input_weight, 1)], axis=1),
        "shard",
        axis=0,
        tiled=True,
    )
    w_out = lax.all_gather(own(output_weight, 0), "shard", axis=1, tiled=True)
    params = jnp.pad(
        jnp.concatenate(
            [
                conv_weight.astype(F32),
                conv_bias[None],
                rate_bias[None],
                entry_bias[None],
                decay_param[None],
            ],
            axis=0,
        ),
        ((0, 0), (0, spare)),
    )

    def spread(weight):
        out = jnp.zeros((width, width), BF16)
        for j in range(blocks):
            at = j * block_width
            out = out.at[at : at + block_width, at : at + block_width].set(weight[j])
        return out

    gates = jnp.concatenate([spread(rate_weight), spread(entry_weight)], axis=1)

    xs = tokens.reshape(rows, model).astype(F32)
    scale1 = rms_parts(xs)
    n1 = gather_seq((xs * scale1 * first_gain).astype(BF16))
    proj = dot(n1, w_in)
    z, h, v = scan_forward(parts, quarters, chunk, proj, params, gates)
    mid = xs + scatter_seq(dot(z, w_out).astype(BF16)).astype(F32)
    scale2 = rms_parts(mid)
    n2 = gather_plane((mid * scale2 * second_gain).astype(BF16))
    cot = cotangent.reshape(rows, model)
    cot_all = gather_plane(cot)
    hidden = hidden_gate.shape[1] // inner
    wg = lax.dynamic_slice_in_dim(hidden_gate, inner_at * hidden, hidden, 1)
    wu = lax.dynamic_slice_in_dim(hidden_up, inner_at * hidden, hidden, 1)
    wd = lax.dynamic_slice_in_dim(hidden_down, inner_at * hidden, hidden, 0)
    gm = dot(n2, wg)
    um = dot(n2, wu)
    act, slope = gelu_and_slope(gm)
    mm = (act * um).astype(BF16)
    result = (mid + scatter_plane(dot(mm, wd).astype(BF16)).astype(F32)).astype(BF16)
    dmm = dot(cot_all, wd, ((1,), (1,)))
    dgm = (dmm * um * slope).astype(BF16)
    dum = (dmm * act).astype(BF16)
    ffn_grads = jnp.concatenate(
        [
            dot(n2, dgm, ((0,), (0,))).astype(BF16),
            dot(n2, dum, ((0,), (0,))).astype(BF16),
            dot(cot_all, mm, ((0,), (0,))).astype(BF16),
        ],
        axis=1,
    )
    ffn_sum = lax.psum_scatter(
        ffn_grads, "seq", scatter_dimension=0, tiled=True, axis_index_groups=columns
    )
    dn2 = scatter_plane(
        (dot(dgm, wg, ((1,), (1,))) + dot(dum, wu, ((1,), (1,)))).astype(BF16)
    ).astype(F32)
    dmid = cot.astype(F32) + rms_back(mid, scale2, second_gain, dn2)
    second_gain_grad = jnp.sum(dn2 * mid * scale2, axis=0)
    dout = gather_seq(dmid.astype(BF16))
    dz = dot(dout, w_out, ((1,), (1,)))
    both, gate_grad, sums = scan_backward(
        parts, quarters, chunk, dz, proj, h, v, params, gates
    )
    dn1 = scatter_seq(dot(both, w_in, ((1,), (1,))).astype(BF16)).astype(F32)
    tokens_grad = (dmid + rms_back(xs, scale1, first_gain, dn1)).reshape(tokens.shape)
    first_gain_grad = jnp.sum(dn1 * xs * scale1, axis=0)
    mix_grads = jnp.concatenate(
        [dot(n1, both, ((0,), (0,))).astype(BF16), dot(dout, z, ((0,), (0,))).astype(BF16)],
        axis=1,
    )
    mix_cols = 3 * width
    mix_sum = lax.psum_scatter(
        mix_grads.reshape(parts, shards, piece, mix_cols).transpose(1, 0, 2, 3),
        "shard",
        scatter_dimension=0,
        tiled=True,
    )
    mix = lax.all_to_all(
        mix_sum.reshape(parts, piece, mix_cols), "seq", split_axis=0, concat_axis=0, tiled=True
    )
    mix = mix.reshape(parts, piece, 3, width)[..., :channels].astype(F32)
    mix = mix.transpose(2, 1, 0, 3).reshape(3, piece, lru)
    ffn = lax.all_to_all(
        ffn_sum.reshape(inner, shards, piece, 3 * hidden),
        "shard",
        split_axis=1,
        concat_axis=1,
        tiled=True,
    )
    ffn = lax.all_to_all(
        ffn, "seq", split_axis=0, concat_axis=0, tiled=True, axis_index_groups=pairs
    )
    ffn = ffn.reshape(inner, shards, piece, 3, hidden).transpose(3, 2, 1, 0, 4)
    ffn = ffn.reshape(3, piece, inner * shards * hidden).astype(F32)
    first_gain_sum, second_gain_sum = (
        lax.psum_scatter(x, ("seq", "shard"), scatter_dimension=0, tiled=True)
        for x in (first_gain_grad, second_gain_grad)
    )
    sums = sums.reshape(8, 8, width).sum(axis=1)[:, :channels]

    def blocks_of(at):
        return jnp.stack(
            [
                gate_grad[
                    j * block_width : (j + 1) * block_width,
                    at + j * block_width : at + (j + 1) * block_width,
                ]
                for j in range(blocks)
            ]
        )

    sums, rate_grad, entry_grad = lax.psum((sums, blocks_of(0), blocks_of(width)), "shard")
    return (
        result.reshape(tokens.shape),
        tokens_grad,
        first_gain_sum,
        mix[0],
        mix[1],
        sums[4:8],
        sums[3],
        rate_grad,
        sums[1],
        entry_grad,
        sums[2],
        sums[0],
        mix[2].T,
        second_gain_sum,
        ffn[0],
        ffn[1],
        ffn[2].T,
    )


def solution(mesh):
    placed = (
        P(None, "shard", "seq", None),
        P(),
        P("shard", None),
        P("shard", None),
        P(None, "seq"),
        P("seq"),
        P("seq", None, None),
        P("seq"),
        P("seq", None, None),
        P("seq"),
        P("seq"),
        P(None, "shard"),
        P(),
        P(None, "shard"),
        P(None, "shard"),
        P("shard", None),
        P(None, "shard", "seq", None),
    )
    return jax.shard_map(
        body,
        mesh=mesh,
        in_specs=placed,
        out_specs=(
            P(None, "shard", "seq", None),
            P(None, "shard", "seq", None),
            P(("seq", "shard")),
            P(("seq", "shard"), None),
            P(("seq", "shard"), None),
            P(None, "seq"),
            P("seq"),
            P("seq", None, None),
            P("seq"),
            P("seq", None, None),
            P("seq"),
            P("seq"),
            P(None, ("seq", "shard")),
            P(("seq", "shard")),
            P(("seq", "shard"), None),
            P(("seq", "shard"), None),
            P(None, ("seq", "shard")),
        ),
        check_vma=False,
    )
```

time: 3200 us -> 1110 us (0.35)
  waiting for transfers between devices: 2200 us -> 751 us
  local copies, waits for them, and re-layouts: 458 us -> 85.5 us
  matrix products: 241 us -> 96.4 us
  other arithmetic: 139 us -> 23.4 us
  blocking collectives: 114 us -> 80.2 us
  Pallas kernels: 0 us -> 33 us
    reduce_scatter x5 -> x7, waiting for transfers between devices: 1370 us -> 347 us  [the longest x2 126 us: scatter_seq(): return lax.psum_scatter(x, 'seq', scatter_dimension=0, tiled=True)]
    unnamed x14 -> x18, waiting for transfers between devices: 441 us -> 98 us
    pad x79 -> x2, local copies, waits for them, and re-layouts: 187 us -> 0.78 us  [the longest x1 0.77 us: own(): return jnp.pad(part, pads)]
    dot_general x24 -> x15, matrix products: 241 us -> 96.4 us  [dot(): lax.dot_general(left, right, (dims, ((), ())), preferred_element_type=F32)]
    slice x79 -> x12, local copies, waits for them, and re-layouts: 144 us -> 26.9 us  [the longest x2 13 us: body(): ffn[2]]
    unnamed x159 -> x55, local copies, waits for them, and re-layouts: 71.2 us -> 8.96 us
    all_gather x6 -> x8, waiting for transfers between devices: 348 us -> 289 us  [the longest x2 119 us: gather_seq(): return lax.all_gather(x, 'seq', axis=0, tiled=True)]
    all_to_all x2, waiting for transfers between devices: 41.7 us -> 0.01 us  [the longest x1 0.01 us: body(): lax.all_to_all(ffn, 'seq', split_axis=0, concat_axis=0, tiled=True, axis_...]
  transfers between devices with their start and end apart: 15 -> 19, of which waited for: 10 -> 16; matrix products, arithmetic and copies ran while one was open for 15% -> 14% of each run, Pallas kernels for 0% -> 3%
where the time goes in v1:
time: 1110 us; the launch traced here: 1100 us
  waiting for transfers between devices  751 us (68%)
  matrix products  96.4 us (9%)
  local copies, waits for them, and re-layouts  85.5 us (8%)
  blocking collectives  80.2 us (7%)
  Pallas kernels  33 us (3%)
  other arithmetic  23.4 us (2%)
  between operations  14.9 us (1%)
  starting transfers between devices  11.6 us (1%)
    reduce_scatter x2, waiting for transfers between devices, scatter_seq(): return lax.psum_scatter(x, 'seq', scatter_dimension=0, tiled=True)  126 us
    all_gather x2, waiting for transfers between devices, gather_seq(): return lax.all_gather(x, 'seq', axis=0, tiled=True)  119 us
    reduce_scatter x1, waiting for transfers between devices, body(): lax.psum_scatter(ffn_grads, 'seq', scatter_dimension=0, tiled=True, axis_...  110 us
    all_gather x2, waiting for transfers between devices, gather_plane(): return lax.all_gather(x, 'seq', axis=0, tiled=True, axis_index_groups=pairs)  100 us
    unnamed x18, waiting for transfers between devices  98 us
    dot_general x15, matrix products, dot(): lax.dot_general(left, right, (dims, ((), ())), preferred_element_type=F32)  96.4 us
    reduce_scatter x2, waiting for transfers between devices, scatter_plane(): lax.psum_scatter(x, 'seq', scatter_dimension=0, tiled=True, axis_index_gr...  77.6 us
    all_gather x2, waiting for transfers between devices, gather_plane(): x = lax.all_gather(x, 'shard', axis=0, tiled=True)  46.3 us
  transfers between devices with their start and end apart: 19, of which 16 were waited for; matrix products, arithmetic and copies ran while one was open for 14% of the time, Pallas kernels for 3%

profile of v1, /device:TPU:9, one launch (start us, length us, event | category | flops | bytes accessed | tf_op | source)
XLA Modules:
  0.0 1096.0 jit_solution(5050323319112214256)
XLA Ops:
  17.7 22.7 %all-gather.11.cloned.1.call-done = bf16[2048,768]{0,1:T(8,128)(2,1)} async-done(((bf16[512,768]{0,1:T(8,128)(2,1)}), bf16[2048,768]{0,1:T(8,128)(2,1)}) %all-gather.11.cloned.1.call-update) | async-done | bytes 3145744 | tf_op jit(solution)/shard_map/all_gather | solution.py:412
  40.3 74.1 %all-gather.9.cloned.1.call-done = bf16[1024,2048]{1,0:T(8,128)(2,1)} async-done(((bf16[128,2048]{1,0:T(8,128)(2,1)}), bf16[1024,2048]{1,0:T(8,128)(2,1)}) %all-gather.9.cloned.1.call-update) | async-done | bytes 4194320 | tf_op jit(solution)/shard_map/all_gather | solution.py:393
  114.4 8.3 fusion.53.proj_ref
  122.7 12.0 %scan_forward.1 = (bf16[1024,384]{1,0:T(8,128)(2,1)S(1)}, f32[1024,384]{1,0:T(8,128)S(1)}, bf16[1024,384]{1,0:T(8,128)(2,1)S(1)}) custom-call(f32[1024,768]{1,0:T(8,128)} %fusion.53.proj_ref, f32[8,384]{1,0:T(8,128)S(1)} %pad.37.par_ref, bf16[384,768]{1,0:T(8,128)(2,1)S(1)} %pad_maximum_fusion.2.gates_ref), custom_call_target="tpu_custom_call" | custom-call | tf_op jit(solution)/shard_map/scan_forward/pallas_call | solution.py:160
  142.4 87.8 %reduce-scatter.11.cloned.1.call-done = bf16[128,2048]{1,0:T(8,128)(2,1)} async-done(((bf16[1024,2048]{1,0:T(8,128)(2,1)}), bf16[128,2048]{1,0:T(8,128)(2,1)}) %reduce-scatter.11.cloned.1.call-update) | async-done | bytes 524304 | tf_op jit(solution)/shard_map/reduce_scatter | solution.py:396
  234.2 22.3 %all-gather.15.cloned.1.call-done = bf16[512,2048]{1,0:T(8,128)(2,1)} async-done(((bf16[128,2048]{1,0:T(8,128)(2,1)}), bf16[512,2048]{1,0:T(8,128)(2,1)}) %all-gather.15.cloned.1.call-update) | async-done | bytes 2097168 | tf_op jit(solution)/shard_map/all_gather | solution.py:399
  256.5 24.0 %all-gather.19.cloned.1.call-done = bf16[512,2048]{1,0:T(8,128)(2,1)} async-done(((bf16[128,2048]{1,0:T(8,128)(2,1)}), bf16[512,2048]{1,0:T(8,128)(2,1)}) %all-gather.19.cloned.1.call-update) | async-done | bytes 2097168 | tf_op jit(solution)/shard_map/all_gather | solution.py:399
  280.9 57.7 %all-gather.17.cloned.1.call-done = bf16[1024,2048]{1,0:T(8,128)(2,1)} async-done(((bf16[512,2048]{1,0:T(8,128)(2,1)}), bf16[1024,2048]{1,0:T(8,128)(2,1)}) %all-gather.17.cloned.1.call-update) | async-done | bytes 4194320 | tf_op jit(solution)/shard_map/all_gather | solution.py:400
  338.6 8.4 fusion.15
  354.3 42.7 %all-gather.21.cloned.1.call-done = bf16[1024,2048]{1,0:T(8,128)(2,1)} async-done(((bf16[512,2048]{1,0:T(8,128)(2,1)}), bf16[1024,2048]{1,0:T(8,128)(2,1)}) %all-gather.21.cloned.1.call-update) | async-done | bytes 4194320 | tf_op jit(solution)/shard_map/all_gather | solution.py:400
  397.0 11.4 %fusion.8 = (bf16[1024,768]{1,0:T(8,128)(2,1)S(1)}, bf16[1024,768]{1,0:T(8,128)(2,1)S(1)}, bf16[1024,768]{1,0:T(8,128)(2,1)}) fusion(f32[1024,768]{1,0:T(8,128)} %fusion.19, f32[1024,768]{1,0:T(8,128)} %fusion.15, bf16[1024,2048]{1,0:T(8,128)(2,1)} %all-gather.21.cloned.1.call-done, bf16[1536,2048]{1,0:T(8,128)(2,1)} %param.40, s32[]{:T(128)S(6)} %select_n.5), kind=kOutput, calls=%fused_computation.22 | convolution fusion | flops 3240886272 | bytes 18350084 | tf_op jit(solution)/shard_map/dot_general | solution.py:22
  422.3 54.4 %reduce-scatter.17.cloned.1.call-done = bf16[512,2048]{1,0:T(8,128)(2,1)} async-done(((bf16[1024,2048]{1,0:T(8,128)(2,1)}), bf16[512,2048]{1,0:T(8,128)(2,1)}) %reduce-scatter.17.cloned.1.call-update) | async-done | bytes 2097168 | tf_op jit(solution)/shard_map/reduce_scatter | solution.py:403
  476.8 33.8 %reduce-scatter.19.cloned.1.call-done = bf16[128,2048]{1,0:T(8,128)(2,1)} async-done(((bf16[512,2048]{1,0:T(8,128)(2,1)}), bf16[128,2048]{1,0:T(8,128)(2,1)}) %reduce-scatter.19.cloned.1.call-update) | async-done | bytes 524304 | tf_op jit(solution)/shard_map/reduce_scatter | solution.py:404
  541.0 45.3 %all-gather.23.cloned.1.call-done = bf16[1024,2048]{1,0:T(8,128)(2,1)} async-done(((bf16[128,2048]{1,0:T(8,128)(2,1)}), bf16[1024,2048]{1,0:T(8,128)(2,1)}) %all-gather.23.cloned.1.call-update) | async-done | bytes 4194320 | tf_op jit(solution)/shard_map/all_gather | solution.py:393
  592.5 20.9 %scan_backward.1 = (bf16[1024,768]{1,0:T(8,128)(2,1)}, f32[384,768]{1,0:T(8,128)}, f32[64,384]{1,0:T(8,128)S(1)}) custom-call(f32[1024,384]{1,0:T(8,128)} %fusion.54.dz_ref, f32[1024,768]{1,0:T(8,128)} %fusion.53.proj_ref, f32[1024,384]{1,0:T(8,128)} %copy-done.2, bf16[1024,384]{1,0:T(8,128)(2,1)S(1)} %get-tuple-element.73.v_ref, f32[8,384]{1,0:T(8,128)S(1)} %pad.37.par_ref, ...), custom_call_target="tpu_custom_call" | custom-call | tf_op jit(solution)/shard_map/scan_backward/pallas_call | solution.py:321
  640.2 109.5 %reduce-scatter.23.cloned.1.call-done = bf16[512,2304]{0,1:T(8,128)(2,1)} async-done(((bf16[2048,2304]{0,1:T(8,128)(2,1)}), bf16[512,2304]{0,1:T(8,128)(2,1)}) %reduce-scatter.23.cloned.1.call-update) | async-done | bytes 2359312 | tf_op jit(solution)/shard_map/reduce_scatter | solution.py:472
  755.9 31.0 %all_to_all.15 = bf16[2,4,64,2304]{3,2,0,1:T(8,128)(2,1)S(1)} all-to-all(bf16[2,4,64,2304]{3,2,0,1:T(8,128)(2,1)S(1)} %copy.119), channel_id=1, replica_groups=mesh['seq'=8,'shard'=4] {'shard'}, dimensions={1} | all-to-all | bytes 4718592 | tf_op jit(solution)/shard_map/all_to_all | solution.py:504
  793.6 23.2 %reduce-scatter.13.cloned.1.call-done = bf16[512,2048]{1,0:T(8,128)(2,1)} async-done(((bf16[1024,2048]{1,0:T(8,128)(2,1)}), bf16[512,2048]{1,0:T(8,128)(2,1)}) %reduce-scatter.13.cloned.1.call-update) | async-done | bytes 2097168 | tf_op jit(solution)/shard_map/reduce_scatter | solution.py:403
  817.4 97.3 %all-reduce.14.cloned.1.call-done = bf16[4,8,64,1152]{3,2,0,1:T(8,128)(2,1)} async-done(((bf16[4,8,64,1152]{3,2,0,1:T(8,128)(2,1)}), bf16[4,8,64,1152]{3,2,0,1:T(8,128)(2,1)}) %all-reduce.14.cloned.1.call-update) | async-done | bytes 4718608
  923.2 10.7 psum.21
  935.1 16.7 %all-reduce.16.cloned.1.call-done = (f32[2,171,171]{2,1,0:T(8,128)}, f32[2,171,171]{2,1,0:T(8,128)}) async-done(((f32[2,171,171]{2,1,0:T(8,128)}, f32[2,171,171]{2,1,0:T(8,128)}), (f32[2,171,171]{2,1,0:T(8,128)}, f32[2,171,171]{2,1,0:T(8,128)})) %all-reduce.16.cloned.1.call-update) | async-done | bytes 467872 | tf_op jit(solution)/shard_map/psum | solution.py:533
  963.2 10.6 fusion.49
  1006.0 38.3 %reduce-scatter.21.cloned.1.call-done = bf16[128,2048]{1,0:T(8,128)(2,1)} async-done(((bf16[1024,2048]{1,0:T(8,128)(2,1)}), bf16[128,2048]{1,0:T(8,128)(2,1)}) %reduce-scatter.21.cloned.1.call-update) | async-done | bytes 524304 | tf_op jit(solution)/shard_map/reduce_scatter | solution.py:396
  1045.7 38.5 %all-reduce.9 = (f32[2048]{0:T(1024)S(1)}, f32[2048]{0:T(1024)S(1)}) all-reduce(f32[2048]{0:T(1024)S(1)} %get-tuple-element.181, f32[2048]{0:T(1024)S(1)} %get-tuple-element.179), channel_id=8, replica_groups=mesh['seq'=8,'shard'=4] {'seq','shard'}, use_global_device_ids=true, to_apply=%region_11.12.clone | all-reduce | flops 4096 | bytes 32768
  (169 shorter events, 179.8 us)
Async XLA Ops:
  7.2 33.1 %all-gather.11.cloned.1.call-start = ((), (), s32[]{:S(2)}) async-start(), calls=%async_computation.11 | async-start | bytes 3932160 | tf_op jit(solution)/shard_map/all_gather | solution.py:412
  9.7 104.7 %all-gather.9.cloned.1.call-start = ((), (), s32[]{:S(2)}) async-start(), calls=%async_computation.10 | async-start | bytes 4718592 | tf_op jit(solution)/shard_map/all_gather | solution.py:393
  11.1 125.5 %all-gather.13.cloned.1.call-start = ((), (), s32[]{:S(2)}) async-start(), calls=%async_computation.12 | async-start | bytes 1966080 | tf_op jit(solution)/shard_map/all_gather | solution.py:418
  12.0 218.2 %reduce-scatter.11.cloned.1.call-start = ((), (), s32[]{:S(2)}) async-start(), calls=%async_computation.13 | async-start | bytes 4718592 | tf_op jit(solution)/shard_map/reduce_scatter | solution.py:396
  142.3 89.2 %copy-start.7 = (f32[2048]{0:T(1024)S(1)}, f32[2048]{0:T(1024)}, u32[]{:S(2)}) copy-start(f32[2048]{0:T(1024)} %param.37) | copy-start | bytes 24580
  142.3 114.1 %all-gather.15.cloned.1.call-start = ((), (), s32[]{:S(2)}) async-start(), calls=%async_computation.14 | async-start | bytes 2621440 | tf_op jit(solution)/shard_map/all_gather | solution.py:399
  233.6 47.0 %all-gather.19.cloned.1.call-start = ((), (), s32[]{:S(2)}) async-start(), calls=%async_computation.18 | async-start | bytes 2621440 | tf_op jit(solution)/shard_map/all_gather | solution.py:399
  234.2 104.4 %all-gather.17.cloned.1.call-start = ((), (), s32[]{:S(2)}) async-start(), calls=%async_computation.15 | async-start | bytes 6291456 | tf_op jit(solution)/shard_map/all_gather | solution.py:400
  256.5 140.5 %all-gather.21.cloned.1.call-start = ((), (), s32[]{:S(2)}) async-start(), calls=%async_computation.19 | async-start | bytes 6291456 | tf_op jit(solution)/shard_map/all_gather | solution.py:400
  280.6 196.1 %reduce-scatter.17.cloned.1.call-start = ((), (), s32[]{:S(2)}) async-start(), calls=%async_computation.20 | async-start | bytes 6291456 | tf_op jit(solution)/shard_map/reduce_scatter | solution.py:403
  422.2 88.4 %copy-start.4 = (bf16[128,2048]{1,0:T(8,128)(2,1)S(1)}, bf16[128,2048]{1,0:T(8,128)(2,1)}, u32[]{:S(2)}) copy-start(bf16[128,2048]{1,0:T(8,128)(2,1)} %reduce-scatter.11.cloned.1.call-done) | copy-start | bytes 1572868
  422.2 88.3 %reduce-scatter.19.cloned.1.call-start = ((), (), s32[]{:S(2)}) async-start(), calls=%async_computation.21 | async-start | bytes 2621440 | tf_op jit(solution)/shard_map/reduce_scatter | solution.py:404
  476.7 109.6 %all-gather.23.cloned.1.call-start = ((), (), s32[]{:S(2)}) async-start(), calls=%async_computation.22 | async-start | bytes 4718592 | tf_op jit(solution)/shard_map/all_gather | solution.py:393
  514.5 235.3 %reduce-scatter.23.cloned.1.call-start = ((), (), s32[]{:S(2)}) async-start(), calls=%async_computation.24 | async-start | bytes 11796480 | tf_op jit(solution)/shard_map/reduce_scatter | solution.py:472
  532.8 283.9 %reduce-scatter.13.cloned.1.call-start = ((), (), s32[]{:S(2)}) async-start(), calls=%async_computation.16 | async-start | bytes 6291456 | tf_op jit(solution)/shard_map/reduce_scatter | solution.py:403
  540.8 373.9 %all-reduce.14.cloned.1.call-start = ((), (), s32[]{:S(2)}) async-start(), calls=%async_computation.25 | async-start | bytes 9437184
  592.5 20.9 %copy-start.18 = (bf16[1024,2048]{1,0:T(8,128)(2,1)S(1)}, bf16[1024,2048]{1,0:T(8,128)(2,1)}, u32[]{:S(2)}) copy-start(bf16[1024,2048]{1,0:T(8,128)(2,1)} %all-gather.23.cloned.1.call-done) | copy-start | bytes 12582916
  629.3 322.4 %all-reduce.16.cloned.1.call-start = ((), (), s32[]{:S(2)}) async-start(), calls=%async_computation.26 | async-start | bytes 1441792 | tf_op jit(solution)/shard_map/psum | solution.py:533
  632.3 412.0 %reduce-scatter.21.cloned.1.call-start = ((), (), s32[]{:S(2)}) async-start(), calls=%async_computation.23 | async-start | bytes 4718592 | tf_op jit(solution)/shard_map/reduce_scatter | solution.py:396
  788.5 28.3 %copy-start.20 = (u32[32]{0:T(128)S(1)}, u32[32]{0:T(128)}, u32[]{:S(2)}) copy-start(u32[32]{0:T(128)} %constant.158) | copy-start | bytes 388
  788.5 129.2 %all-to-all-start.2 = ((bf16[2,4,64,2304]{3,2,1,0:T(8,128)(2,1)}), bf16[2,4,64,2304]{3,2,1,0:T(8,128)(2,1)}, u32[]{:S(2)}, u32[]{:S(2)}) async-start(bf16[2,4,64,2304]{3,2,1,0:T(8,128)(2,1)} %copy.120), calls=%async_computation.9 | async-start | bytes 4718592 | tf_op jit(solution)/shard_map/all_to_all | solution.py:511
  793.6 291.8 %reduce-scatter.15.cloned.1.call-start = ((), (), s32[]{:S(2)}) async-start(), calls=%async_computation.17 | async-start | bytes 2621440 | tf_op jit(solution)/shard_map/reduce_scatter | solution.py:404
  917.7 74.8 %all-to-all-start = ((bf16[8,64,1152]{2,1,0:T(8,128)(2,1)}), bf16[8,64,1152]{2,1,0:T(8,128)(2,1)}, u32[]{:S(2)}, u32[]{:S(2)}) async-start(bf16[8,64,1152]{2,1,0:T(8,128)(2,1)} %dynamic-slice_bitcast_fusion), calls=%async_computation.6 | async-start | bytes 2359296 | tf_op jit(solution)/shard_map/all_to_all | solution.py:499
  1003.6 85.4 %copy-start.1 = (bf16[2736,512]{1,0:T(8,128)(2,1)S(1)}, bf16[2736,512]{1,0:T(8,128)(2,1)}, u32[]{:S(2)}) copy-start(bf16[2736,512]{1,0:T(8,128)(2,1)} %param.36) | copy-start | bytes 8404996
  (20 other events, 83.4 us)
Sparse Core Ops, SparseCore 0:
  10.2 30.0 all-gather.10
  43.0 71.3 all-gather.8
  116.5 20.0 all-gather.12
  142.5 87.6 reduce-scatter.10
  233.7 22.7 all-gather.14
  257.9 22.5 all-gather.18
  282.2 56.3 all-gather.16
  340.2 56.7 all-gather.20
  422.3 54.3 reduce-scatter.16
  479.1 31.4 reduce-scatter.18
  514.6 71.6 all-gather.22
  588.6 161.0 reduce-scatter.22
  752.1 64.5 reduce-scatter.12
  819.0 95.6 all-reduce.13
  918.0 33.6 all-reduce.15
  955.2 89.0 reduce-scatter.20
  1046.8 31.1 reduce-scatter.14

commit v2 on v1

--- a/solution.py
+++ b/solution.py
@@ -16,6 +16,16 @@
 GELU_A = 0.044715
 F32 = jnp.float32
 BF16 = jnp.bfloat16
+
+
+MESH = pl.DeviceIdType.MESH
+ANY = pl.BlockSpec(memory_space=pl.ANY)
+IN_VMEM = pl.BlockSpec(memory_space=pltpu.VMEM)
+DMA = pltpu.SemaphoreType.DMA
+
+
+def cost(us):
+    return pl.CostEstimate(flops=0, bytes_accessed=int(us * 3.3e6), transcendentals=0)
 
 
 def dot(left, right, dims=((1,), (0,))):
@@ -172,6 +182,7 @@
             pltpu.VMEM((width // LANES, length, LANES), F32),
         ],
         compiler_params=pltpu.CompilerParams(vmem_limit_bytes=48 * 2**20),
+        cost_estimate=cost(12),
         name="scan_forward",
     )(proj, params, gates)
 
@@ -180,6 +191,8 @@
     parts,
     quarters,
     chunk,
+    blocks,
+    block_width,
     dz_ref,
     proj_ref,
     h_ref,
@@ -187,8 +200,10 @@
     par_ref,
     gates_ref,
     both_ref,
+    blocks_ref,
+    totals_ref,
+    sums_ref,
     gate_grad_ref,
-    sums_ref,
     a_s,
     g_s,
     t_s,
@@ -314,20 +329,34 @@
 
     lax.fori_loop(0, chunks, last, 0)
     gate_grad_ref[...] = dot(v_ref[...], dpre_s[...], ((0,), (0,)))
-
-
-def scan_backward(parts, quarters, chunk, dz, proj, h, v, params, gates):
+    blocks_ref[...] = jnp.zeros(blocks_ref.shape, F32)
+    tall = blocks_ref.shape[0] // (2 * blocks)
+    for gate in range(2):
+        for j in range(blocks):
+            at, lanes = (gate * blocks + j) * tall, gate * width + j * block_width
+            rows = slice(j * block_width, (j + 1) * block_width)
+            blocks_ref[at : at + block_width, :block_width] = gate_grad_ref[
+                rows, lanes : lanes + block_width
+            ]
+    for k in range(8):
+        totals_ref[k : k + 1, :] = jnp.sum(sums_ref[8 * k : 8 * k + 8, :], axis=0, keepdims=True)
+
+
+def scan_backward(parts, quarters, chunk, blocks, block_width, dz, proj, h, v, params, gates):
     length, width = h.shape
+    tall, wide = -(-block_width // 8) * 8, -(-block_width // LANES) * LANES
     return pl.pallas_call(
-        functools.partial(scan_backward_kernel, parts, quarters, chunk),
+        functools.partial(scan_backward_kernel, parts, quarters, chunk, blocks, block_width),
         out_shape=(
             jax.ShapeDtypeStruct((length, 2 * width), BF16),
-            jax.ShapeDtypeStruct((width, 2 * width), F32),
-            jax.ShapeDtypeStruct((64, width), F32),
+            jax.ShapeDtypeStruct((2 * blocks * tall, wide), F32),
+            jax.ShapeDtypeStruct((8, width), F32),
         ),
         in_specs=[pl.BlockSpec(memory_space=pltpu.VMEM)] * 6,
         out_specs=[pl.BlockSpec(memory_space=pltpu.VMEM)] * 3,
         scratch_shapes=[
+            pltpu.VMEM((64, width), F32),
+            pltpu.VMEM((width, 2 * width), F32),
             pltpu.VMEM((width // LANES, length + 8, LANES), F32),
             pltpu.VMEM((width // LANES, length, LANES), F32),
             pltpu.VMEM((width // LANES, length, LANES), F32),
@@ -338,8 +367,782 @@
             pltpu.VMEM((length + 8, width), F32),
         ],
         compiler_params=pltpu.CompilerParams(vmem_limit_bytes=52 * 2**20),
+        cost_estimate=cost(21),
         name="scan_backward",
     )(dz, proj, h, v, params, gates)
+
+
+def remote(src, dst, send, recv, to):
+    return pltpu.make_async_remote_copy(
+        src_ref=src, dst_ref=dst, send_sem=send, recv_sem=recv, device_id=to, device_id_type=MESH
+    )
+
+
+def greet(others):
+    barrier = pltpu.get_barrier_semaphore()
+    for to in others:
+        pl.semaphore_signal(barrier, inc=1, device_id=to, device_id_type=MESH)
+    pl.semaphore_wait(barrier, len(others))
+
+
+def add_rows(rows, fn):
+    def one(k, carry):
+        fn(pl.ds(pl.multiple_of(k * 16, 16), 16))
+        return carry
+
+    lax.fori_loop(0, rows // 16, one, 0)
+
+
+def line_gather_kernel(outer, inner, x_ref, out_ref, local_sem, across, up, down):
+    s, h = lax.axis_index("seq"), lax.axis_index("shard")
+    o, i = s // inner, lax.rem(s, inner)
+    beside = (o * inner + 1 - i, h)
+    above, below = (s + inner, h), (s - inner, h)
+
+    def at(row):
+        return out_ref.at[row * inner + i]
+
+    def branch(o0):
+        others = [beside] + ([above] if o0 < outer - 1 else []) + ([below] if o0 > 0 else [])
+        greet(others)
+        mine = pltpu.make_async_copy(x_ref, out_ref.at[s], local_sem)
+        mine.start()
+        sent = []
+
+        def send(row, sems, to):
+            src = x_ref if row == o0 else at(row)
+            copy = remote(src, at(row), sems.at[0, row], sems.at[1, row], to)
+            copy.start()
+            sent.append(copy)
+
+        def came(row, sems, to):
+            remote(x_ref, at(row), sems.at[0, row], sems.at[1, row], to).wait_recv()
+
+        for k in range(outer):
+            lower, upper = o0 - k, o0 + k
+            if k > 0 and lower >= 0:
+                came(lower, up, below)
+            if lower >= 0 and o0 < outer - 1:
+                send(lower, up, above)
+            if lower >= 0:
+                send(lower, across, beside)
+            if k > 0 and upper < outer:
+                came(upper, down, above)
+            if upper < outer and o0 > 0:
+                send(upper, down, below)
+            if k > 0 and upper < outer:
+                send(upper, across, beside)
+        for row in range(outer):
+            there = out_ref.at[row * inner + 1 - i]
+            remote(x_ref, there, across.at[0, row], across.at[1, row], beside).wait_recv()
+        for copy in sent:
+            copy.wait_send()
+        mine.wait()
+
+    for o0 in range(outer):
+        pl.when(o == o0)(functools.partial(branch, o0))
+
+
+def line_gather(x, outer, inner, collective):
+    rows, cols = x.shape
+    return pl.pallas_call(
+        functools.partial(line_gather_kernel, outer, inner),
+        out_shape=jax.ShapeDtypeStruct((outer * inner, rows, cols), x.dtype),
+        in_specs=[ANY],
+        out_specs=ANY,
+        scratch_shapes=[DMA] + [DMA((2, outer))] * 3,
+        compiler_params=pltpu.CompilerParams(collective_id=collective, has_side_effects=True),
+        cost_estimate=cost(52),
+        name="line_gather",
+    )(x)
+
+
+def line_scatter_kernel(
+    outer, inner, p_ref, out_ref, x_in, up_in, down_in, up_out, down_out, across, up, down
+):
+    s, h = lax.axis_index("seq"), lax.axis_index("shard")
+    o, i = s // inner, lax.rem(s, inner)
+    beside = (o * inner + 1 - i, h)
+    above, below = (s + inner, h), (s - inner, h)
+    rows = p_ref.shape[1]
+
+    def branch(o0):
+        first, last = o0 == 0, o0 == outer - 1
+        greet([beside] + ([] if last else [above]) + ([] if first else [below]))
+        order = sorted(range(outer), key=lambda d: (-abs(d - o0), d))
+        sent = []
+        for d in order:
+            copy = remote(
+                p_ref.at[d * inner + 1 - i], x_in.at[d], across.at[0, d], across.at[1, d], beside
+            )
+            copy.start()
+            sent.append(copy)
+        for d in order:
+            mine = p_ref.at[d * inner + i]
+            remote(mine, x_in.at[d], across.at[0, d], across.at[1, d], beside).wait_recv()
+            terms = [mine, x_in.at[d]]
+            if d >= o0 and not first:
+                remote(mine, up_in.at[d], up.at[0, d], up.at[1, d], below).wait_recv()
+                terms.append(up_in.at[d])
+            if d <= o0 and not last:
+                remote(mine, down_in.at[d], down.at[0, d], down.at[1, d], above).wait_recv()
+                terms.append(down_in.at[d])
+            target = out_ref if d == o0 else (up_out.at[d] if d > o0 else down_out.at[d])
+
+            def add(at, terms=terms, target=target):
+                total = terms[0][at, :].astype(F32)
+                for term in terms[1:]:
+                    total = total + term[at, :].astype(F32)
+                target[at, :] = total.astype(target.dtype)
+
+            add_rows(rows, add)
+            if d != o0:
+                sems, to, land = (up, above, up_in) if d > o0 else (down, below, down_in)
+                copy = remote(target, land.at[d], sems.at[0, d], sems.at[1, d], to)
+                copy.start()
+                sent.append(copy)
+        for copy in sent:
+            copy.wait_send()
+
+    for o0 in range(outer):
+        pl.when(o == o0)(functools.partial(branch, o0))
+
+
+def line_scatter(p, outer, inner, collective):
+    parts, rows, cols = p.shape
+    slots = pltpu.VMEM((outer, rows, cols), p.dtype)
+    return pl.pallas_call(
+        functools.partial(line_scatter_kernel, outer, inner),
+        out_shape=jax.ShapeDtypeStruct((rows, cols), F32),
+        in_specs=[IN_VMEM],
+        out_specs=IN_VMEM,
+        scratch_shapes=[slots] * 5 + [DMA((2, outer))] * 3,
+        compiler_params=pltpu.CompilerParams(
+            collective_id=collective, has_side_effects=True, vmem_limit_bytes=48 * 2**20
+        ),
+        cost_estimate=cost(57),
+        name="line_scatter",
+    )(p)
+
+
+def plane_steps(inner, ys):
+    steps = [(di, dy) for di in range(inner) for dy in range(ys) if (di, dy) != (0, 0)]
+    return sorted(steps, key=lambda d: -((d[0] > 0) + (d[1] > 0)))
+
+
+def plane_place(inner, shards):
+    s, h = lax.axis_index("seq"), lax.axis_index("shard")
+    o, i = s // inner, lax.rem(s, inner)
+    y, core = h // 2, lax.rem(h, 2)
+    ys = shards // 2
+
+    def device(di, dy, other=False):
+        to_i = lax.rem(i + di + inner, inner)
+        to_y = lax.rem(y + dy + ys, ys)
+        to_core = 1 - core if other else core
+        to_h = to_y * 2 + to_core
+        return (o * inner + to_i, to_h), to_i * shards + to_h
+
+    return device
+
+
+def plane_gather_kernel(inner, shards, x_ref, out_ref, local_sem, far, near):
+    device = plane_place(inner, shards)
+    steps = plane_steps(inner, shards // 2)
+    sibling, sibling_slot = device(0, 0, True)
+    _, me = device(0, 0)
+    greet([sibling] + [device(*d)[0] for d in steps])
+    mine = pltpu.make_async_copy(x_ref, out_ref.at[me], local_sem)
+    mine.start()
+    sent = []
+    for k, d in enumerate(steps):
+        copy = remote(x_ref, out_ref.at[me], far.at[0, k], far.at[1, k], device(*d)[0])
+        copy.start()
+        sent.append(copy)
+    last = len(steps)
+    copy = remote(x_ref, out_ref.at[me], near.at[0, last], near.at[1, last], sibling)
+    copy.start()
+    sent.append(copy)
+    for k in reversed(range(len(steps))):
+        di, dy = steps[k]
+        source, slot = device(-di, -dy)
+        here = out_ref.at[slot]
+        remote(x_ref, here, far.at[0, k], far.at[1, k], source).wait_recv()
+        copy = remote(here, here, near.at[0, k], near.at[1, k], sibling)
+        copy.start()
+        sent.append(copy)
+    for k, d in enumerate(steps + [(0, 0)]):
+        _, slot = device(-d[0], -d[1], True)
+        remote(x_ref, out_ref.at[slot], near.at[0, k], near.at[1, k], sibling).wait_recv()
+    for copy in sent:
+        copy.wait_send()
+    mine.wait()
+
+
+def plane_gather(x, inner, shards, collective):
+    rows, cols = x.shape
+    chips = inner * shards // 2
+    return pl.pallas_call(
+        functools.partial(plane_gather_kernel, inner, shards),
+        out_shape=jax.ShapeDtypeStruct((inner * shards, rows, cols), x.dtype),
+        in_specs=[ANY],
+        out_specs=ANY,
+        scratch_shapes=[DMA, DMA((2, chips)), DMA((2, chips))],
+        compiler_params=pltpu.CompilerParams(collective_id=collective, has_side_effects=True),
+        cost_estimate=cost(29),
+        name="plane_gather",
+    )(x)
+
+
+class Sent:
+    def __init__(self):
+        self.copies = []
+
+    def __call__(self, *copy):
+        copy = remote(*copy)
+        copy.start()
+        self.copies.append(copy)
+
+    def finish(self):
+        for copy in self.copies:
+            copy.wait_send()
+
+
+def received(like, here, sem, source):
+    remote(like, here, sem, sem, source).wait_recv()
+
+
+def shard_place(shards):
+    s, h = lax.axis_index("seq"), lax.axis_index("shard")
+    y, core, ys = h // 2, lax.rem(h, 2), shards // 2
+
+    def along(dy, other=False):
+        return lax.rem(y + dy + ys, ys) * 2 + (1 - core if other else core)
+
+    return s, h, along, list(range(1, ys))
+
+
+def opening_kernel(
+    outer,
+    inner,
+    shards,
+    x_ref,
+    wi_ref,
+    wo_ref,
+    cot_ref,
+    n_out,
+    wi_out,
+    wo_out,
+    cot_out,
+    local,
+    across,
+    up,
+    down,
+    w_far,
+    w_near,
+    c_side,
+    c_far,
+    c_near,
+):
+    s, h, along, far_steps = shard_place(shards)
+    o, i = s // inner, lax.rem(s, inner)
+    beside = (o * inner + 1 - i, h)
+    above, below = (s + inner, h), (s - inner, h)
+    sibling = (s, along(0, True))
+    weights = ((wi_ref, wi_out), (wo_ref, wo_out))
+    ys = shards // 2
+
+    def at(row):
+        return n_out.at[row * inner + i]
+
+    def slot(side, dy, other=False):
+        return (1 - i if side else i) * shards + along(dy, other)
+
+    def branch(o0):
+        greet(
+            [beside, sibling]
+            + ([above] if o0 < outer - 1 else [])
+            + ([below] if o0 > 0 else [])
+            + [(s, along(dy)) for dy in far_steps]
+        )
+        keep = [
+            pltpu.make_async_copy(x_ref, n_out.at[s], local.at[0]),
+            pltpu.make_async_copy(wi_ref, wi_out.at[h], local.at[1]),
+            pltpu.make_async_copy(wo_ref, wo_out.at[h], local.at[2]),
+            pltpu.make_async_copy(cot_ref, cot_out.at[slot(0, 0)], local.at[3]),
+        ]
+        send = Sent()
+
+        def pass_on(row, sems, to):
+            src = x_ref if row == o0 else at(row)
+            send(src, at(row), sems.at[0, row], sems.at[1, row], to)
+
+        def came(row, sems, source):
+            received(x_ref, at(row), sems.at[1, row], source)
+
+        def steps(k):
+            lower, upper = o0 - k, o0 + k
+            if k > 0 and lower >= 0:
+                came(lower, up, below)
+            if lower >= 0 and o0 < outer - 1:
+                pass_on(lower, up, above)
+            if lower >= 0:
+                pass_on(lower, across, beside)
+            if k > 0 and upper < outer:
+                came(upper, down, above)
+            if upper < outer and o0 > 0:
+                pass_on(upper, down, below)
+            if k > 0 and upper < outer:
+                pass_on(upper, across, beside)
+
+        steps(0)
+        for n, (src, dst) in enumerate(weights):
+            for dy in far_steps:
+                send(src, dst.at[h], w_far.at[0, n, dy], w_far.at[1, n, dy], (s, along(dy)))
+            send(src, dst.at[h], w_near.at[0, n, 0], w_near.at[1, n, 0], sibling)
+        me = cot_out.at[slot(0, 0)]
+        send(cot_ref, me, c_side.at[0], c_side.at[1], beside)
+        for dy in far_steps:
+            send(cot_ref, me, c_far.at[0, 0, dy], c_far.at[1, 0, dy], (s, along(dy)))
+        send(cot_ref, me, c_near.at[0, 0, 0], c_near.at[1, 0, 0], sibling)
+        for copy in keep:
+            copy.start()
+        for k in range(1, outer):
+            steps(k)
+            if k == 1:
+                for n, (src, dst) in enumerate(weights):
+                    for dy in far_steps:
+                        source = along(-dy)
+                        here = dst.at[source]
+                        received(src, here, w_far.at[1, n, dy], (s, source))
+                        send(here, here, w_near.at[0, n, dy], w_near.at[1, n, dy], sibling)
+                here = cot_out.at[slot(1, 0)]
+                received(cot_ref, here, c_side.at[1], beside)
+                for dy in far_steps:
+                    send(here, here, c_far.at[0, 1, dy], c_far.at[1, 1, dy], (s, along(dy)))
+                send(here, here, c_near.at[0, 1, 0], c_near.at[1, 1, 0], sibling)
+        for side in range(2):
+            for dy in far_steps:
+                here = cot_out.at[slot(side, -dy)]
+                received(cot_ref, here, c_far.at[1, side, dy], (s, along(-dy)))
+                send(here, here, c_near.at[0, side, dy], c_near.at[1, side, dy], sibling)
+        for row in range(outer):
+            received(x_ref, n_out.at[row * inner + 1 - i], across.at[1, row], beside)
+        for dy in range(ys):
+            for n, (src, dst) in enumerate(weights):
+                received(src, dst.at[along(-dy, True)], w_near.at[1, n, dy], sibling)
+            for side in range(2):
+                received(cot_ref, cot_out.at[slot(side, -dy, True)], c_near.at[1, side, dy], sibling)
+        send.finish()
+        for copy in keep:
+            copy.wait()
+
+    for o0 in range(outer):
+        pl.when(o == o0)(functools.partial(branch, o0))
+
+
+def opening(x, w_in, w_out, cot, outer, inner, shards, collective):
+    ys = shards // 2
+    return pl.pallas_call(
+        functools.partial(opening_kernel, outer, inner, shards),
+        out_shape=(
+            jax.ShapeDtypeStruct((outer * inner,) + x.shape, x.dtype),
+            jax.ShapeDtypeStruct((shards,) + w_in.shape, w_in.dtype),
+            jax.ShapeDtypeStruct((shards,) + w_out.shape, w_out.dtype),
+            jax.ShapeDtypeStruct((inner * shards,) + cot.shape, cot.dtype),
+        ),
+        in_specs=[ANY] * 4,
+        out_specs=[ANY] * 4,
+        scratch_shapes=[DMA((4,))]
+        + [DMA((2, outer))] * 3
+        + [DMA((2, 2, ys))] * 2
+        + [DMA((2,)), DMA((2, 2, ys)), DMA((2, 2, ys))],
+        compiler_params=pltpu.CompilerParams(collective_id=collective, has_side_effects=True),
+        cost_estimate=cost(62),
+        name="opening",
+    )(x, w_in, w_out, cot)
+
+
+def closing_kernel(
+    outer,
+    inner,
+    shards,
+    p_ref,
+    g_ref,
+    blocks_ref,
+    sums_ref,
+    dn_ref,
+    mix_ref,
+    blocks_out,
+    sums_out,
+    x_in,
+    up_in,
+    down_in,
+    up_out,
+    down_out,
+    near_in,
+    far_in,
+    far_out,
+    done,
+    block_slots,
+    sum_slots,
+    across,
+    up,
+    down,
+    near,
+    far,
+    final,
+    s_far,
+    s_near,
+    local,
+):
+    s, h, along, far_steps = shard_place(shards)
+    parts = outer * inner
+    o, i = s // inner, lax.rem(s, inner)
+    beside = (o * inner + 1 - i, h)
+    above, below = (s + inner, h), (s - inner, h)
+    sibling = (s, along(0, True))
+    rows, piece, ys = p_ref.shape[1], g_ref.shape[2], shards // 2
+    order = [lax.rem(s + k, parts) for k in range(1, parts + 1)]
+    small = ((blocks_ref, block_slots, blocks_out), (sums_ref, sum_slots, sums_out))
+
+    def branch(o0):
+        first, last = o0 == 0, o0 == outer - 1
+        greet(
+            [sibling]
+            + [(s, along(dy)) for dy in far_steps]
+            + [(lax.rem(s + k, parts), h) for k in range(1, parts)]
+        )
+        send = Sent()
+        line = sorted(range(outer), key=lambda d: (-abs(d - o0), d))
+        for d in line:
+            send(p_ref.at[d * inner + 1 - i], x_in.at[d], across.at[0, d], across.at[1, d], beside)
+        for k, p in enumerate(order):
+            for dy in far_steps + [0]:
+                src = g_ref.at[p, along(dy, True)]
+                send(src, near_in.at[dy, p], near.at[0, dy, k], near.at[1, dy, k], sibling)
+        for k, p in enumerate(order):
+            for dy in far_steps:
+                mine = g_ref.at[p, along(dy)]
+                received(mine, near_in.at[dy, p], near.at[1, dy, k], sibling)
+
+                def add(at, p=p, dy=dy, mine=mine):
+                    total = mine[at, :].astype(F32) + near_in[dy, p, at, :].astype(F32)
+                    far_out[dy - 1, p, at, :] = total.astype(BF16)
+
+                add_rows(piece, add)
+                send(
+                    far_out.at[dy - 1, p],
+                    far_in.at[dy - 1, p],
+                    far.at[0, dy, k],
+                    far.at[1, dy, k],
+                    (s, along(dy)),
+                )
+        for n, (src, slots, _) in enumerate(small):
+            for dy in far_steps:
+                send(src, slots.at[h], s_far.at[0, n, dy], s_far.at[1, n, dy], (s, along(dy)))
+            send(src, slots.at[h], s_near.at[0, n, 0], s_near.at[1, n, 0], sibling)
+            slots[h] = src[...]
+
+        def line_step(d):
+            mine = p_ref.at[d * inner + i]
+            received(mine, x_in.at[d], across.at[1, d], beside)
+            terms = [mine, x_in.at[d]]
+            if d >= o0 and not first:
+                received(mine, up_in.at[d], up.at[1, d], below)
+                terms.append(up_in.at[d])
+            if d <= o0 and not last:
+                received(mine, down_in.at[d], down.at[1, d], above)
+                terms.append(down_in.at[d])
+            target = dn_ref if d == o0 else (up_out.at[d] if d > o0 else down_out.at[d])
+
+            def add(at):
+                total = terms[0][at, :].astype(F32)
+                for term in terms[1:]:
+                    total = total + term[at, :].astype(F32)
+                target[at, :] = total.astype(target.dtype)
+
+            add_rows(rows, add)
+            if d != o0:
+                sems, to, land = (up, above, up_in) if d > o0 else (down, below, down_in)
+                send(target, land.at[d], sems.at[0, d], sems.at[1, d], to)
+
+        def mix_step(k):
+            p = order[k]
+            mine = g_ref.at[p, h]
+            received(mine, near_in.at[0, p], near.at[1, 0, k], sibling)
+            for dy in far_steps:
+                received(mine, far_in.at[dy - 1, p], far.at[1, dy, k], (s, along(-dy)))
+
+            def add(at):
+                total = mine[at, :].astype(F32) + near_in[0, p, at, :].astype(F32)
+                for dy in far_steps:
+                    total = total + far_in[dy - 1, p, at, :].astype(F32)
+                done[p, at, :] = total.astype(BF16)
+
+            add_rows(piece, add)
+            if k < parts - 1:
+                send(done.at[p], mix_ref.at[s], final.at[0, k], final.at[1, k], (p, h))
+
+        for n, d in enumerate(line):
+            line_step(d)
+            for k in range(n * inner, (n + 1) * inner):
+                mix_step(k)
+        mine = pltpu.make_async_copy(done.at[s], mix_ref.at[s], local)
+        mine.start()
+        for n, (src, slots, out) in enumerate(small):
+            for dy in far_steps:
+                here = slots.at[along(-dy)]
+                received(src, here, s_far.at[1, n, dy], (s, along(-dy)))
+                send(here, here, s_near.at[0, n, dy], s_near.at[1, n, dy], sibling)
+        for n, (src, slots, out) in enumerate(small):
+            for dy in [0] + far_steps:
+                received(src, slots.at[along(-dy, True)], s_near.at[1, n, dy], sibling)
+
+            def add(k, carry, slots=slots, out=out):
+                at = pl.ds(pl.multiple_of(k * 8, 8), 8)
+                total = slots[0, at, :]
+                for j in range(1, shards):
+                    total = total + slots[j, at, :]
+                out[at, :] = total
+                return carry
+
+            lax.fori_loop(0, src.shape[0] // 8, add, 0)
+        for k in range(parts - 1):
+            source = lax.rem(s + parts - (k + 1), parts)
+            received(done.at[s], mix_ref.at[source], final.at[1, k], (source, h))
+        send.finish()
+        mine.wait()
+
+    for o0 in range(outer):
+        pl.when(o == o0)(functools.partial(branch, o0))
+
+
+def closing(p, g, blocks, sums, outer, inner, collective):
+    parts, rows, cols = p.shape
+    _, shards, piece, mix_cols = g.shape
+    ys = shards // 2
+    slots = pltpu.VMEM((outer, rows, cols), BF16)
+    far = pltpu.VMEM((max(ys - 1, 1), parts, piece, mix_cols), BF16)
+    return pl.pallas_call(
+        functools.partial(closing_kernel, outer, inner, shards),
+        out_shape=(
+            jax.ShapeDtypeStruct((rows, cols), F32),
+            jax.ShapeDtypeStruct((parts, piece, mix_cols), BF16),
+            jax.ShapeDtypeStruct(blocks.shape, F32),
+            jax.ShapeDtypeStruct(sums.shape, F32),
+        ),
+        in_specs=[IN_VMEM] * 4,
+        out_specs=[IN_VMEM] * 4,
+        scratch_shapes=[slots] * 5
+        + [
+            pltpu.VMEM((ys, parts, piece, mix_cols), BF16),
+            far,
+            far,
+            pltpu.VMEM((parts, piece, mix_cols), BF16),
+            pltpu.VMEM((shards,) + blocks.shape, F32),
+            pltpu.VMEM((shards,) + sums.shape, F32),
+        ]
+        + [DMA((2, outer))] * 3
+        + [DMA((2, ys, parts))] * 2
+        + [DMA((2, parts))]
+        + [DMA((2, 2, ys))] * 2
+        + [DMA],
+        compiler_params=pltpu.CompilerParams(
+            collective_id=collective, has_side_effects=True, vmem_limit_bytes=56 * 2**20
+        ),
+        cost_estimate=cost(75),
+        name="closing",
+    )(p, g, blocks, sums)
+
+
+def finish_kernel(
+    inner, parts, shards, g_ref, u_ref, d_ref, x_ref, g_out, u_out, d_out, x_out, slots, sems, gs, local
+):
+    device = plane_place(inner, shards)
+    steps = [(di, dy, False) for di, dy in plane_steps(inner, shards // 2)]
+    steps = steps + [(di, dy, True) for di, dy, _ in steps] + [(0, 0, True)]
+    _, slot_me = device(0, 0)
+    s, h = lax.axis_index("seq"), lax.axis_index("shard")
+    count = parts * shards
+    me = s * shards + h
+    barrier = pltpu.get_barrier_semaphore()
+    arrays = ((d_ref, d_out), (g_ref, g_out), (u_ref, u_out))
+
+    def other(k):
+        to = lax.rem(me + k, count)
+        return (to // shards, lax.rem(to, shards)), to
+
+    def hello(k, carry):
+        pl.semaphore_signal(barrier, inc=1, device_id=other(k)[0], device_id_type=MESH)
+        return carry
+
+    lax.fori_loop(1, count, hello, 0)
+    pl.semaphore_wait(barrier, count - 1)
+    send = Sent()
+    for n, (src, dst) in enumerate(arrays):
+        for k, d in enumerate(steps):
+            to, slot = device(*d)
+            send(src.at[slot], dst.at[slot_me], sems.at[0, n, k], sems.at[1, n, k], to)
+
+    def gain(k):
+        to, row = other(k)
+        return remote(x_ref.at[row], slots.at[k], gs.at[0, k], gs.at[1, k], to)
+
+    def start(k, carry):
+        gain(k).start()
+        return carry
+
+    def arrive(k, total):
+        gain(k).wait_recv()
+        return total + slots[k]
+
+    def leave(k, carry):
+        gain(k).wait_send()
+        return carry
+
+    lax.fori_loop(1, count, start, 0)
+    keep = [
+        pltpu.make_async_copy(src.at[slot_me], dst.at[slot_me], local.at[n])
+        for n, (src, dst) in enumerate(arrays)
+    ]
+    for copy in keep:
+        copy.start()
+    x_out[...] = lax.fori_loop(1, count, arrive, x_ref[me])
+    lax.fori_loop(1, count, leave, 0)
+    for n, (src, dst) in enumerate(arrays):
+        for k, (di, dy, far) in enumerate(steps):
+            source, slot = device(-di, -dy, far)
+            received(src.at[slot_me], dst.at[slot], sems.at[1, n, k], source)
+    send.finish()
+    for copy in keep:
+        copy.wait()
+
+
+def finish(gate, up, down, gains, inner, parts, shards, collective):
+    slots = gate.shape[0]
+    count, _, lanes = gains.shape
+    same = jax.ShapeDtypeStruct(gate.shape, gate.dtype)
+    return pl.pallas_call(
+        functools.partial(finish_kernel, inner, parts, shards),
+        out_shape=(same, same, same, jax.ShapeDtypeStruct((1, lanes), F32)),
+        in_specs=[ANY, ANY, ANY, IN_VMEM],
+        out_specs=[ANY, ANY, ANY, IN_VMEM],
+        scratch_shapes=[
+            pltpu.VMEM((count, 1, lanes), F32),
+            DMA((2, 3, slots)),
+            DMA((2, count)),
+            DMA((3,)),
+        ],
+        compiler_params=pltpu.CompilerParams(collective_id=collective, has_side_effects=True),
+        cost_estimate=cost(30),
+        name="finish",
+    )(gate, up, down, gains)
+
+
+def twin_scatter_kernel(inner, shards, *refs):
+    p_refs, out_refs, (near_in, far_in, far_out, near, far) = refs[:2], refs[2:4], refs[4:]
+    device = plane_place(inner, shards)
+    steps = plane_steps(inner, shards // 2) + [(0, 0)]
+    sibling, _ = device(0, 0, True)
+    greet([sibling] + [device(*d)[0] for d in steps[:-1]])
+    rows = p_refs[0].shape[1]
+    send = Sent()
+    for n, p_ref in enumerate(p_refs):
+        for k, d in enumerate(steps):
+            _, slot = device(*d, True)
+            send(p_ref.at[slot], near_in.at[n, k], near.at[0, n, k], near.at[1, n, k], sibling)
+    for n, (p_ref, out_ref) in enumerate(zip(p_refs, out_refs, strict=True)):
+        for k, d in enumerate(steps):
+            to, slot = device(*d)
+            received(p_ref.at[slot], near_in.at[n, k], near.at[1, n, k], sibling)
+            home = k == len(steps) - 1
+            target = out_ref if home else far_out.at[n, k]
+
+            def add(at, n=n, k=k, slot=slot, target=target, p_ref=p_ref):
+                total = p_ref[slot, at, :].astype(F32) + near_in[n, k, at, :].astype(F32)
+                target[at, :] = total.astype(target.dtype)
+
+            add_rows(rows, add)
+            if not home:
+                send(far_out.at[n, k], far_in.at[n, k], far.at[0, n, k], far.at[1, n, k], to)
+    for n, out_ref in enumerate(out_refs):
+        for k, d in enumerate(steps[:-1]):
+            source, _ = device(-d[0], -d[1])
+            received(far_out.at[n, k], far_in.at[n, k], far.at[1, n, k], source)
+
+        def total_of(at, n=n, out_ref=out_ref):
+            total = out_ref[at, :]
+            for k in range(len(steps) - 1):
+                total = total + far_in[n, k, at, :].astype(F32)
+            out_ref[at, :] = total
+
+        add_rows(rows, total_of)
+    send.finish()
+
+
+def twin_scatter(p, q, inner, shards, collective):
+    slots, rows, cols = p.shape
+    chips = slots // 2
+    buffers = pltpu.VMEM((2, chips, rows, cols), p.dtype)
+    return pl.pallas_call(
+        functools.partial(twin_scatter_kernel, inner, shards),
+        out_shape=(jax.ShapeDtypeStruct((rows, cols), F32),) * 2,
+        in_specs=[IN_VMEM] * 2,
+        out_specs=[IN_VMEM] * 2,
+        scratch_shapes=[buffers] * 3 + [DMA((2, 2, chips))] * 2,
+        compiler_params=pltpu.CompilerParams(
+            collective_id=collective, has_side_effects=True, vmem_limit_bytes=48 * 2**20
+        ),
+        cost_estimate=cost(52),
+        name="twin_scatter",
+    )(p, q)
+
+
+def unpack_kernel(
+    inner, channels, gate_ref, up_ref, down_ref, mix_ref, gate, up, down, branch, enter, leave
+):
+    slots, piece, hidden = gate_ref.shape
+    shards = slots // inner
+    parts, width = mix_ref.shape[0], mix_ref.shape[2] // 3
+    for i in range(inner):
+        for h in range(shards):
+            at = (h * inner + i) * hidden
+            slot = i * shards + h
+            gate[:, at : at + hidden] = gate_ref[slot].astype(F32)
+            up[:, at : at + hidden] = up_ref[slot].astype(F32)
+            down[at : at + hidden, :] = down_ref[slot].astype(F32).T
+
+    def row(k):
+        lanes = slice(k * width, k * width + width)
+        return jnp.concatenate(
+            [mix_ref[p][:, lanes].astype(F32)[:, :channels] for p in range(parts)], axis=1
+        )
+
+    branch[...] = row(0)
+    enter[...] = row(1)
+    total = parts * channels
+    padded = (total + LANES - 1) // LANES * LANES
+    wide = jnp.concatenate([row(2), jnp.zeros((piece, padded - total), F32)], axis=1)
+    leave[...] = wide.T[:total, :]
+
+
+def unpack(ffn_gate, ffn_up, ffn_down, mix, inner, channels):
+    slots, piece, hidden = ffn_gate.shape
+    lru = mix.shape[0] * channels
+    across = jax.ShapeDtypeStruct((piece, slots * hidden), F32)
+    along = jax.ShapeDtypeStruct((slots * hidden, piece), F32)
+    wide = jax.ShapeDtypeStruct((piece, lru), F32)
+    tall = jax.ShapeDtypeStruct((lru, piece), F32)
+    return pl.pallas_call(
+        functools.partial(unpack_kernel, inner, channels),
+        out_shape=(across, across, along, wide, wide, tall),
+        in_specs=[IN_VMEM] * 4,
+        out_specs=[IN_VMEM] * 6,
+        compiler_params=pltpu.CompilerParams(vmem_limit_bytes=48 * 2**20),
+        cost_estimate=cost(5),
+        name="unpack",
+    )(ffn_gate, ffn_up, ffn_down, mix)
 
 
 def rms_parts(values):
@@ -386,22 +1189,7 @@
     spare = width - channels
     blocks, block_width = rate_weight.shape[0], rate_weight.shape[1]
     piece = model // (parts * shards)
-    pairs = [[o * inner + i for i in range(inner)] for o in range(outer)]
     columns = [[o * inner + i for o in range(outer)] for i in range(inner)]
-
-    def gather_seq(x):
-        return lax.all_gather(x, "seq", axis=0, tiled=True)
-
-    def scatter_seq(x):
-        return lax.psum_scatter(x, "seq", scatter_dimension=0, tiled=True)
-
-    def gather_plane(x):
-        x = lax.all_gather(x, "shard", axis=0, tiled=True)
-        return lax.all_gather(x, "seq", axis=0, tiled=True, axis_index_groups=pairs)
-
-    def scatter_plane(x):
-        x = lax.psum_scatter(x, "seq", scatter_dimension=0, tiled=True, axis_index_groups=pairs)
-        return lax.psum_scatter(x, "shard", scatter_dimension=0, tiled=True)
 
     def own(weight, axis):
         part = lax.dynamic_slice_in_dim(weight, seq_at * channels, channels, axis)
@@ -409,13 +1197,6 @@
         pads[axis] = (0, spare)
         return jnp.pad(part, pads)
 
-    w_in = lax.all_gather(
-        jnp.concatenate([own(branch_weight, 1), own(input_weight, 1)], axis=1),
-        "shard",
-        axis=0,
-        tiled=True,
-    )
-    w_out = lax.all_gather(own(output_weight, 0), "shard", axis=1, tiled=True)
     params = jnp.pad(
         jnp.concatenate(
             [
@@ -440,103 +1221,104 @@
     gates = jnp.concatenate([spread(rate_weight), spread(entry_weight)], axis=1)
 
     xs = tokens.reshape(rows, model).astype(F32)
+    cot = cotangent.reshape(rows, model)
     scale1 = rms_parts(xs)
-    n1 = gather_seq((xs * scale1 * first_gain).astype(BF16))
+    n1, w_in, w_out, cot_all = opening(
+        (xs * scale1 * first_gain).astype(BF16),
+        jnp.concatenate([own(branch_weight, 1), own(input_weight, 1)], axis=1),
+        own(output_weight, 0),
+        cot,
+        outer,
+        inner,
+        shards,
+        0,
+    )
+    n1 = n1.reshape(parts * rows, model)
+    w_in = w_in.reshape(model, 2 * width)
+    w_out = w_out.transpose(1, 0, 2).reshape(width, model)
+    cot_all = cot_all.reshape(inner * shards * rows, model)
     proj = dot(n1, w_in)
     z, h, v = scan_forward(parts, quarters, chunk, proj, params, gates)
-    mid = xs + scatter_seq(dot(z, w_out).astype(BF16)).astype(F32)
+    mid = xs + line_scatter(
+        dot(z, w_out).astype(BF16).reshape(parts, rows, model), outer, inner, 1
+    )
     scale2 = rms_parts(mid)
-    n2 = gather_plane((mid * scale2 * second_gain).astype(BF16))
-    cot = cotangent.reshape(rows, model)
-    cot_all = gather_plane(cot)
+    n2 = plane_gather((mid * scale2 * second_gain).astype(BF16), inner, shards, 2)
+    n2 = n2.reshape(inner * shards * rows, model)
     hidden = hidden_gate.shape[1] // inner
     wg = lax.dynamic_slice_in_dim(hidden_gate, inner_at * hidden, hidden, 1)
     wu = lax.dynamic_slice_in_dim(hidden_up, inner_at * hidden, hidden, 1)
     wd = lax.dynamic_slice_in_dim(hidden_down, inner_at * hidden, hidden, 0)
+
+    def sum_tokens(x):
+        return lax.psum_scatter(
+            x.astype(BF16), "seq", scatter_dimension=0, tiled=True, axis_index_groups=columns
+        ).reshape(inner * shards, piece, hidden)
+
     gm = dot(n2, wg)
     um = dot(n2, wu)
     act, slope = gelu_and_slope(gm)
     mm = (act * um).astype(BF16)
-    result = (mid + scatter_plane(dot(mm, wd).astype(BF16)).astype(F32)).astype(BF16)
+    down_sum = sum_tokens(dot(cot_all, mm, ((0,), (0,))))
     dmm = dot(cot_all, wd, ((1,), (1,)))
     dgm = (dmm * um * slope).astype(BF16)
     dum = (dmm * act).astype(BF16)
-    ffn_grads = jnp.concatenate(
-        [
-            dot(n2, dgm, ((0,), (0,))).astype(BF16),
-            dot(n2, dum, ((0,), (0,))).astype(BF16),
-            dot(cot_all, mm, ((0,), (0,))).astype(BF16),
-        ],
-        axis=1,
-    )
-    ffn_sum = lax.psum_scatter(
-        ffn_grads, "seq", scatter_dimension=0, tiled=True, axis_index_groups=columns
-    )
-    dn2 = scatter_plane(
-        (dot(dgm, wg, ((1,), (1,))) + dot(dum, wu, ((1,), (1,)))).astype(BF16)
-    ).astype(F32)
+    gate_sum = sum_tokens(dot(n2, dgm, ((0,), (0,))))
+    up_terms = dot(n2, dum, ((0,), (0,)))
+    dn2_terms = dot(dgm, wg, ((1,), (1,))) + dot(dum, wu, ((1,), (1,)))
+    dn2, ffn_out = twin_scatter(
+        dn2_terms.astype(BF16).reshape(inner * shards, rows, model),
+        dot(mm, wd).astype(BF16).reshape(inner * shards, rows, model),
+        inner,
+        shards,
+        3,
+    )
+    result = (mid + ffn_out).astype(BF16)
     dmid = cot.astype(F32) + rms_back(mid, scale2, second_gain, dn2)
     second_gain_grad = jnp.sum(dn2 * mid * scale2, axis=0)
-    dout = gather_seq(dmid.astype(BF16))
+    dout = line_gather(dmid.astype(BF16), outer, inner, 4).reshape(parts * rows, model)
+    dout, up_terms = lax.optimization_barrier((dout, up_terms.astype(BF16)))
+    up_sum = sum_tokens(up_terms)
     dz = dot(dout, w_out, ((1,), (1,)))
-    both, gate_grad, sums = scan_backward(
-        parts, quarters, chunk, dz, proj, h, v, params, gates
-    )
-    dn1 = scatter_seq(dot(both, w_in, ((1,), (1,))).astype(BF16)).astype(F32)
-    tokens_grad = (dmid + rms_back(xs, scale1, first_gain, dn1)).reshape(tokens.shape)
-    first_gain_grad = jnp.sum(dn1 * xs * scale1, axis=0)
+    both, small, sums = scan_backward(
+        parts, quarters, chunk, blocks, block_width, dz, proj, h, v, params, gates
+    )
     mix_grads = jnp.concatenate(
         [dot(n1, both, ((0,), (0,))).astype(BF16), dot(dout, z, ((0,), (0,))).astype(BF16)],
         axis=1,
     )
-    mix_cols = 3 * width
-    mix_sum = lax.psum_scatter(
-        mix_grads.reshape(parts, shards, piece, mix_cols).transpose(1, 0, 2, 3),
-        "shard",
-        scatter_dimension=0,
-        tiled=True,
-    )
-    mix = lax.all_to_all(
-        mix_sum.reshape(parts, piece, mix_cols), "seq", split_axis=0, concat_axis=0, tiled=True
-    )
-    mix = mix.reshape(parts, piece, 3, width)[..., :channels].astype(F32)
-    mix = mix.transpose(2, 1, 0, 3).reshape(3, piece, lru)
-    ffn = lax.all_to_all(
-        ffn_sum.reshape(inner, shards, piece, 3 * hidden),
-        "shard",
-        split_axis=1,
-        concat_axis=1,
-        tiled=True,
-    )
-    ffn = lax.all_to_all(
-        ffn, "seq", split_axis=0, concat_axis=0, tiled=True, axis_index_groups=pairs
-    )
-    ffn = ffn.reshape(inner, shards, piece, 3, hidden).transpose(3, 2, 1, 0, 4)
-    ffn = ffn.reshape(3, piece, inner * shards * hidden).astype(F32)
-    first_gain_sum, second_gain_sum = (
-        lax.psum_scatter(x, ("seq", "shard"), scatter_dimension=0, tiled=True)
-        for x in (first_gain_grad, second_gain_grad)
-    )
-    sums = sums.reshape(8, 8, width).sum(axis=1)[:, :channels]
-
-    def blocks_of(at):
-        return jnp.stack(
-            [
-                gate_grad[
-                    j * block_width : (j + 1) * block_width,
-                    at + j * block_width : at + (j + 1) * block_width,
-                ]
-                for j in range(blocks)
-            ]
-        )
-
-    sums, rate_grad, entry_grad = lax.psum((sums, blocks_of(0), blocks_of(width)), "shard")
+    dn1, mix, small, sums = closing(
+        dot(both, w_in, ((1,), (1,))).astype(BF16).reshape(parts, rows, model),
+        mix_grads.reshape(parts, shards, piece, 3 * width),
+        small,
+        sums,
+        outer,
+        inner,
+        5,
+    )
+    tokens_grad = (dmid + rms_back(xs, scale1, first_gain, dn1)).reshape(tokens.shape)
+    first_gain_grad = jnp.sum(dn1 * xs * scale1, axis=0)
+    gains = jnp.concatenate(
+        [x.reshape(parts * shards, 1, piece) for x in (first_gain_grad, second_gain_grad)], axis=2
+    )
+    gain_lanes = -(-2 * piece // LANES) * LANES
+    gains = jnp.pad(gains, ((0, 0), (0, 0), (0, gain_lanes - 2 * piece)))
+    gate_sum, up_sum, down_sum, gains = finish(
+        gate_sum, up_sum, down_sum, gains, inner, parts, shards, 6
+    )
+    gains = gains[0]
+    gate_sum, up_sum, down_sum, branch_sum, input_sum, output_sum = unpack(
+        gate_sum, up_sum, down_sum, mix, inner, channels
+    )
+    sums = sums[:, :channels]
+    small = small.reshape(2, blocks, -1, small.shape[1])[:, :, :block_width, :block_width]
+    rate_grad, entry_grad = small[0], small[1]
     return (
         result.reshape(tokens.shape),
         tokens_grad,
-        first_gain_sum,
-        mix[0],
-        mix[1],
+        gains[:piece],
+        branch_sum,
+        input_sum,
         sums[4:8],
         sums[3],
         rate_grad,
@@ -544,11 +1326,11 @@
         entry_grad,
         sums[2],
         sums[0],
-        mix[2].T,
-        second_gain_sum,
-        ffn[0],
-        ffn[1],
-        ffn[2].T,
+        output_sum,
+        gains[piece : 2 * piece],
+        gate_sum,
+        up_sum,
+        down_sum,
     )
 
 

time: 1110 us -> 615 us (0.55)
  waiting for transfers between devices: 751 us -> 0.05 us
  Pallas kernels: 33 us -> 444 us
  blocking collectives: 80.2 us -> 0 us
  local copies, waits for them, and re-layouts: 85.5 us -> 45.4 us
  matrix products: 96.4 us -> 85.2 us
    pallas_call x0 -> x8, Pallas kernels: none -> 411 us  [the longest x1 84.4 us: closing(): pl.pallas_call(functools.partial(closing_kernel, outer, inner, shards), o...]
    reduce_scatter x7 -> x3, waiting for transfers between devices: 347 us -> 0.01 us  [sum_tokens(): lax.psum_scatter(x.astype(BF16), 'seq', scatter_dimension=0, tiled=True,...]
    all_gather x8 -> x0, waiting for transfers between devices: 289 us -> none  [the longest x2 119 us: gather_seq(): return lax.all_gather(x, 'seq', axis=0, tiled=True)]
    unnamed x18 -> x3, waiting for transfers between devices: 98 us -> 0.05 us
    unnamed x1 -> x0, blocking collectives: 38.5 us -> none
    all_to_all x1 -> x0, blocking collectives: 31 us -> none  [body(): lax.all_to_all(ffn_sum.reshape(inner, shards, piece, 3 * hidden), 'shard'...]
    slice x8 -> x2, local copies, waits for them, and re-layouts: 24.2 us -> 2.51 us  [the longest x1 1.28 us: body(): gains[piece:2 * piece]]
    psum x1 -> x0, waiting for transfers between devices: 16.7 us -> none  [body(): lax.psum((sums, blocks_of(0), blocks_of(width)), 'shard')]
  transfers between devices with their start and end apart: 19 -> 3, of which waited for: 16 -> 0; matrix products, arithmetic and copies ran while one was open for 14% -> 12% of each run, Pallas kernels for 3% -> 39%
where the time goes in v2:
time: 615 us; the launch traced here: 604 us
  Pallas kernels  444 us (72%)
  matrix products  85.2 us (14%)
  local copies, waits for them, and re-layouts  45.4 us (7%)
  between operations  14.5 us (2%)
  other arithmetic  14.4 us (2%)
    dot_general x15, matrix products, dot(): lax.dot_general(left, right, (dims, ((), ())), preferred_element_type=F32)  85.2 us
    pallas_call x1, Pallas kernels, closing(): pl.pallas_call(functools.partial(closing_kernel, outer, inner, shards), o...  84.4 us
    pallas_call x1, Pallas kernels, line_gather(): pl.pallas_call(functools.partial(line_gather_kernel, outer, inner), out_s...  74.1 us
    pallas_call x1, Pallas kernels, opening(): pl.pallas_call(functools.partial(opening_kernel, outer, inner, shards), o...  70.5 us
    pallas_call x1, Pallas kernels, twin_scatter(): pl.pallas_call(functools.partial(twin_scatter_kernel, inner, shards), out...  55.4 us
    pallas_call x1, Pallas kernels, line_scatter(): pl.pallas_call(functools.partial(line_scatter_kernel, outer, inner), out_...  48 us
    pallas_call x1, Pallas kernels, finish(): pl.pallas_call(functools.partial(finish_kernel, inner, parts, shards), ou...  44.3 us
    pallas_call x1, Pallas kernels, plane_gather(): pl.pallas_call(functools.partial(plane_gather_kernel, inner, shards), out...  30.3 us
  transfers between devices with their start and end apart: 3, of which 0 were waited for; matrix products, arithmetic and copies ran while one was open for 12% of the time, Pallas kernels for 39%

profile of v2, /device:TPU:9, one launch (start us, length us, event | category | flops | bytes accessed | tf_op | source)
XLA Modules:
  0.0 603.7 jit_solution(2015509241478090885)
XLA Ops:
  20.2 70.5 %opening.1 = (bf16[8,128,2048]{2,1,0:T(8,128)(2,1)}, bf16[4,512,768]{2,1,0:T(8,128)(2,1)}, bf16[4,384,512]{2,1,0:T(8,128)(2,1)}, bf16[8,128,2048]{2,1,0:T(8,128)(2,1)}) custom-call(bf16[128,2048]{1,0:T(8,128)(2,1)} %fusion.23.x_ref, bf16[512,768]{1,0:T(8,128)(2,1)} %fusion.30.wi_ref, bf16[384,512]{1,0:T(8,128)(2,1)} %pad.37.wo_ref, bf16[128,2048]{1,0:T(8,128)(2,1)} %bitcast.101), custom_call_target="tpu_custom_call" | custom-call | bytes 204600000 | tf_op jit(solution)/shard_map/opening/pallas_call | solution.py:746
  97.0 8.3 %fusion.41.proj_ref = f32[1024,768]{1,0:T(8,128)} fusion(bf16[1024,2048]{1,0:T(8,128)(2,1)} %bitcast.117, bf16[2048,768]{1,0:T(8,128)(2,1)} %bitcast.121), kind=kOutput, calls=%fused_computation.93 | convolution fusion | flops 3221225472 | bytes 10485760 | tf_op jit(solution)/shard_map/dot_general | solution.py:32
  105.3 12.0 %scan_forward.1 = (bf16[1024,384]{1,0:T(8,128)(2,1)S(1)}, f32[1024,384]{1,0:T(8,128)S(1)}, bf16[1024,384]{1,0:T(8,128)(2,1)S(1)}) custom-call(f32[1024,768]{1,0:T(8,128)} %fusion.41.proj_ref, f32[8,384]{1,0:T(8,128)S(1)} %pad.38.par_ref, bf16[384,768]{1,0:T(8,128)(2,1)S(1)} %pad_maximum_fusion.1.gates_ref), custom_call_target="tpu_custom_call" | custom-call | bytes 39600000 | tf_op jit(solution)/shard_map/scan_forward/pallas_call | solution.py:170
  121.7 48.0 %line_scatter.1 = f32[128,2048]{1,0:T(8,128)S(1)} custom-call(bf16[8,128,2048]{2,1,0:T(8,128)(2,1)S(1)} %bitcast.90), custom_call_target="tpu_custom_call" | custom-call | bytes 188100000 | tf_op jit(solution)/shard_map/line_scatter/pallas_call | solution.py:514
  171.1 30.3 %plane_gather.1 = bf16[8,128,2048]{2,1,0:T(8,128)(2,1)} custom-call(bf16[128,2048]{1,0:T(8,128)(2,1)} %multiply_convert_fusion.2.x_ref), custom_call_target="tpu_custom_call" | custom-call | bytes 95700000 | tf_op jit(solution)/shard_map/plane_gather/pallas_call | solution.py:585
  201.5 6.4 %fusion.17 = f32[1024,768]{1,0:T(8,128)S(1)} fusion(bf16[1024,2048]{1,0:T(8,128)(2,1)} %bitcast.119, bf16[1536,2048]{1,0:T(8,128)(2,1)} %param.40, s32[]{:T(128)S(6)} %select_n.5), kind=kOutput, calls=%fused_computation.32 | convolution fusion | flops 3221225472 | bytes 10485764 | tf_op jit(solution)/shard_map/dot_general | solution.py:32
  207.9 5.5 fusion.11
  213.4 6.3 %multiply_convert_fusion = (bf16[1024,768]{1,0:T(8,128)(2,1)S(1)}, bf16[1024,768]{1,0:T(8,128)(2,1)S(1)}, bf16[1024,768]{1,0:T(8,128)(2,1)}) fusion(f32[1024,768]{1,0:T(8,128)S(1)} %fusion.11, f32[1024,768]{1,0:T(8,128)S(1)} %fusion.17, bf16[1024,2048]{1,0:T(8,128)(2,1)S(1)} %bitcast.96, bf16[2048,1536]{1,0:T(8,128)(2,1)S(1)} %bitcast.114, s32[]{:T(128)S(6)} %select_n.5), kind=kOutput, calls=%fused_computation.19 | convolution fusion | flops 3240886272 | bytes 18350084 | tf_op jit(solution)/shard_map/dot_general | solution.py:32
  220.9 5.0 convolution_convert_fusion.3
  226.0 7.4 %convolution_convert_fusion.4 = bf16[2048,768]{1,0:T(8,128)(2,1)} fusion(bf16[1024,2048]{1,0:T(8,128)(2,1)} %bitcast.93, bf16[1024,768]{1,0:T(8,128)(2,1)S(1)} %get-tuple-element.168), kind=kOutput, calls=%fused_computation.8 | convolution fusion | flops 3222798336 | bytes 8912896 | tf_op jit(solution)/shard_map/dot_general | solution.py:32
  233.9 7.9 %convolution_convert_fusion.2 = bf16[1024,2048]{1,0:T(8,128)(2,1)} fusion(bf16[1024,768]{1,0:T(8,128)(2,1)} %copy-done.34, bf16[1536,2048]{1,0:T(8,128)(2,1)} %param.40, s32[]{:T(128)S(6)} %select_n.5), kind=kOutput, calls=%fused_computation.6 | convolution fusion | flops 3223322624 | bytes 8912900 | tf_op jit(solution)/shard_map/dot_general | solution.py:32
  241.8 5.5 fusion.9
  247.3 5.1 add_convert_fusion
  252.4 55.4 %twin_scatter.1 = (f32[128,2048]{1,0:T(8,128)S(1)}, f32[128,2048]{1,0:T(8,128)S(1)}) custom-call(bf16[8,128,2048]{2,1,0:T(8,128)(2,1)} %bitcast.100, bf16[8,128,2048]{2,1,0:T(8,128)(2,1)} %bitcast.99), custom_call_target="tpu_custom_call" | custom-call | bytes 171600000 | tf_op jit(solution)/shard_map/twin_scatter/pallas_call | solution.py:1088
  310.0 74.1 %line_gather.1 = bf16[8,128,2048]{2,1,0:T(8,128)(2,1)} custom-call(bf16[128,2048]{1,0:T(8,128)(2,1)} %get-tuple-element.163.x_ref), custom_call_target="tpu_custom_call" | custom-call | bytes 171600000 | tf_op jit(solution)/shard_map/line_gather/pallas_call | solution.py:448
  384.1 7.4 %convolution_convert_fusion.6 = bf16[2048,768]{1,0:T(8,128)(2,1)} fusion(bf16[1024,2048]{1,0:T(8,128)(2,1)} %bitcast.94, bf16[1024,768]{1,0:T(8,128)(2,1)S(1)} %copy-done.33), kind=kOutput, calls=%fused_computation.10 | convolution fusion | flops 3222798336 | bytes 8912896 | tf_op jit(solution)/shard_map/dot_general | solution.py:32
  392.9 5.7 fusion.42.dz_ref
  398.5 20.4 %scan_backward.1 = (bf16[1024,768]{1,0:T(8,128)(2,1)}, f32[704,256]{1,0:T(8,128)S(1)}, f32[8,384]{1,0:T(8,128)S(1)}) custom-call(f32[1024,384]{1,0:T(8,128)} %fusion.42.dz_ref, f32[1024,768]{1,0:T(8,128)} %fusion.41.proj_ref, f32[1024,384]{1,0:T(8,128)} %copy-done.2, bf16[1024,384]{1,0:T(8,128)(2,1)} %copy-done.5, f32[8,384]{1,0:T(8,128)S(1)} %pad.38.par_ref, ...), custom_call_target="tpu_custom_call" | custom-call | bytes 69300000 | tf_op jit(solution)/shard_map/scan_backward/pallas_call | solution.py:348
  422.0 3.7 convolution_convert_fusion.5
  428.3 6.9 %copy.54 = bf16[2048,1152]{1,0:T(8,128)(2,1)} copy(bf16[2048,1152]{0,1:T(8,128)(2,1)} %pad_maximum_fusion) | data formatting | bytes 9437184 | tf_op jit(solution)/shard_map/concatenate | solution.py:1286
  435.2 6.9 %convolution_convert_fusion.1 = bf16[1024,2048]{1,0:T(8,128)(2,1)} fusion(bf16[1024,768]{1,0:T(8,128)(2,1)S(1)} %copy-done.31, bf16[2048,768]{1,0:T(8,128)(2,1)} %bitcast.122), kind=kOutput, calls=%fused_computation.5 | convolution fusion | flops 3223322624 | bytes 8912896 | tf_op jit(solution)/shard_map/dot_general | solution.py:32
  442.1 84.4 %closing.1 = (f32[128,2048]{1,0:T(8,128)}, bf16[8,64,1152]{2,1,0:T(8,128)(2,1)}, f32[704,256]{1,0:T(8,128)}, f32[8,384]{1,0:T(8,128)}) custom-call(bf16[8,128,2048]{2,1,0:T(8,128)(2,1)} %bitcast.92, bf16[8,4,64,1152]{3,2,1,0:T(8,128)(2,1)} %bitcast.91, f32[704,256]{1,0:T(8,128)} %copy-done.9, f32[8,384]{1,0:T(8,128)} %copy-done.10), custom_call_target="tpu_custom_call" | custom-call | bytes 247500000 | tf_op jit(solution)/shard_map/closing/pallas_call | solution.py:927
  536.7 44.3 %finish.1 = (bf16[8,64,768]{2,1,0:T(8,128)(2,1)}, bf16[8,64,768]{2,1,0:T(8,128)(2,1)}, bf16[8,64,768]{2,1,0:T(8,128)(2,1)}, f32[1,128]{1,0:T(1,128)}) custom-call(bf16[8,64,768]{2,1,0:T(8,128)(2,1)} %bitcast.107, bf16[8,64,768]{2,1,0:T(8,128)(2,1)} %bitcast.108, bf16[8,64,768]{2,1,0:T(8,128)(2,1)} %bitcast.106, f32[32,1,128]{2,1,0:T(1,128)} %pad_maximum_fusion.2.x_ref), custom_call_target="tpu_custom_call" | custom-call | bytes 99000000 | tf_op jit(solution)/shard_map/finish/pallas_call | solution.py:1026
  585.8 4.1 unpack.1
  (139 shorter events, 57.7 us)
Async XLA Ops:
  7.2 8.5 %copy-start = (bf16[2736,512]{1,0:T(8,128)(2,1)S(1)}, bf16[2736,512]{1,0:T(8,128)(2,1)}, u32[]{:S(2)}) copy-start(bf16[2736,512]{1,0:T(8,128)(2,1)} %param.36) | copy-start | bytes 8404996
  7.2 529.5 %reduce-scatter.8.cloned.1.call-start = ((), (), s32[]{:S(2)}) async-start(), calls=%async_computation.5 | async-start | bytes 3932160 | tf_op jit(solution)/shard_map/reduce_scatter | solution.py:1254
  19.2 74.0 %copy-start.27 = (bf16[4,342]{1,0:T(4,128)(2,1)S(1)}, bf16[4,342]{1,0:T(4,128)(2,1)}, u32[]{:S(2)}) copy-start(bf16[4,342]{1,0:T(4,128)(2,1)} %param.29) | copy-start | bytes 8212
  19.2 74.1 %copy-start.22 = (bf16[384,384]{1,0:T(8,128)(2,1)S(1)}, bf16[384,384]{1,0:T(8,128)(2,1)}, u32[]{:S(2)}) copy-start(bf16[384,384]{1,0:T(8,128)(2,1)} %scatter.14) | copy-start | bytes 884740
  20.2 74.9 %copy-start.23 = (bf16[384,384]{1,0:T(8,128)(2,1)S(1)}, bf16[384,384]{1,0:T(8,128)(2,1)}, u32[]{:S(2)}) copy-start(bf16[384,384]{1,0:T(8,128)(2,1)} %scatter.16) | copy-start | bytes 884740
  105.3 14.0 %copy-start.20 = (bf16[384,4,512]{0,2,1:T(8,128)(2,1)S(1)}, bf16[384,4,512]{0,2,1:T(8,128)(2,1)}, u32[]{:S(2)}) copy-start(bf16[384,4,512]{0,2,1:T(8,128)(2,1)} %copy.53) | copy-start | bytes 4718596
  121.7 48.2 %copy-start.24 = (f32[2048]{0:T(1024)S(1)}, f32[2048]{0:T(1024)}, u32[]{:S(2)}) copy-start(f32[2048]{0:T(1024)} %param.37) | copy-start | bytes 24580
  169.9 31.5 %copy-start.13 = (f32[128,2048]{1,0:T(8,128)}, f32[128,2048]{1,0:T(8,128)S(1)}, u32[]{:S(2)}) copy-start(f32[128,2048]{1,0:T(8,128)S(1)} %get-tuple-element.166) | copy-start | bytes 3145732
  201.5 6.4 %copy-start.17 = (bf16[8,128,2048]{2,1,0:T(8,128)(2,1)S(1)}, bf16[8,128,2048]{2,1,0:T(8,128)(2,1)}, u32[]{:S(2)}) copy-start(bf16[8,128,2048]{2,1,0:T(8,128)(2,1)} %plane_gather.1) | copy-start | bytes 12582916
  201.5 11.9 %slice-start = ((s8[6291456]{0:T(1024)(128)(4,1)}), s8[4194304]{0:T(1024)(128)(4,1)S(1)}, s32[]{:S(2)}) async-start(s8[6291456]{0:T(1024)(128)(4,1)} %bitcast.113), calls=%async_computation.6 | async-start | bytes 8388608
  213.4 7.5 %copy-start.29 = (bf16[8,128,2048]{2,1,0:T(8,128)(2,1)S(1)}, bf16[8,128,2048]{2,1,0:T(8,128)(2,1)}, u32[]{:S(2)}) copy-start(bf16[8,128,2048]{2,1,0:T(8,128)(2,1)} %get-tuple-element.97) | copy-start | bytes 12582916
  225.9 310.8 %reduce-scatter.4.cloned.1.call-start = ((), (), s32[]{:S(2)}) async-start(), calls=%async_computation.3 | async-start | bytes 3932160 | tf_op jit(solution)/shard_map/reduce_scatter | solution.py:1254
  233.4 303.3 %reduce-scatter.6.cloned.1.call-start = ((), (), s32[]{:S(2)}) async-start(), calls=%async_computation.4 | async-start | bytes 3932160 | tf_op jit(solution)/shard_map/reduce_scatter | solution.py:1254
  233.9 13.4 %slice-start.2 = ((s8[6291456]{0:T(1024)(128)(4,1)}), s8[4194304]{0:T(1024)(128)(4,1)S(1)}, s32[]{:S(2)}) async-start(s8[6291456]{0:T(1024)(128)(4,1)} %bitcast.115), calls=%async_computation.8 | async-start | bytes 8388608
  252.4 55.5 %copy-start.14 = (f32[128,2048]{1,0:T(8,128)S(1)}, f32[128,2048]{1,0:T(8,128)}, u32[]{:S(2)}) copy-start(f32[128,2048]{1,0:T(8,128)} %copy-done.13) | copy-start | bytes 3145732
  252.4 55.8 %copy-start.19 = (bf16[2,1,64,2048]{3,2,1,0:T(8,128)(2,1)S(1)}, bf16[2,1,64,2048]{3,2,1,0:T(8,128)(2,1)}, u32[]{:S(2)}) copy-start(bf16[2,1,64,2048]{3,2,1,0:T(8,128)(2,1)} %param.41) | copy-start | bytes 1572868
  310.0 74.1 %copy-start.33 = (bf16[1024,768]{1,0:T(8,128)(2,1)S(1)}, bf16[1024,768]{1,0:T(8,128)(2,1)}, u32[]{:S(2)}) copy-start(bf16[1024,768]{1,0:T(8,128)(2,1)} %get-tuple-element.169) | copy-start | bytes 4718596
  398.5 20.4 %copy-start.12 = (bf16[1024,384]{1,0:T(8,128)(2,1)S(1)}, bf16[1024,384]{1,0:T(8,128)(2,1)}, u32[]{:S(2)}) copy-start(bf16[1024,384]{1,0:T(8,128)(2,1)} %copy-done.11) | copy-start | bytes 2359300
  398.5 20.4 %copy-start.18 = (bf16[8,128,2048]{2,1,0:T(8,128)(2,1)S(1)}, bf16[8,128,2048]{2,1,0:T(8,128)(2,1)}, u32[]{:S(2)}) copy-start(bf16[8,128,2048]{2,1,0:T(8,128)(2,1)} %line_gather.1) | copy-start | bytes 12582916
  428.3 6.9 %copy-start.31 = (bf16[1024,768]{1,0:T(8,128)(2,1)S(1)}, bf16[1024,768]{1,0:T(8,128)(2,1)}, u32[]{:S(2)}) copy-start(bf16[1024,768]{1,0:T(8,128)(2,1)} %get-tuple-element.103) | copy-start | bytes 4718596
  526.6 6.9 %copy-start.26 = (f32[8,384]{1,0:T(8,128)S(1)}, f32[8,384]{1,0:T(8,128)}, u32[]{:S(2)}) copy-start(f32[8,384]{1,0:T(8,128)} %get-tuple-element.115) | copy-start | bytes 36868
  526.6 7.5 %copy-start.16 = (f32[128,2048]{1,0:T(8,128)S(1)}, f32[128,2048]{1,0:T(8,128)}, u32[]{:S(2)}) copy-start(f32[128,2048]{1,0:T(8,128)} %get-tuple-element.164) | copy-start | bytes 3145732
  532.7 49.6 %copy-start.4 = (bf16[8,64,1152]{2,1,0:T(8,128)(2,1)S(1)}, bf16[8,64,1152]{2,1,0:T(8,128)(2,1)}, u32[]{:S(2)}) copy-start(bf16[8,64,1152]{2,1,0:T(8,128)(2,1)} %get-tuple-element.112.mix_ref) | copy-start | bytes 3538948
  591.0 6.0 copy-start.1
  (18 other events, 45.5 us)
Sparse Core Ops, SparseCore 0:
  226.0 60.0 reduce-scatter.7
  288.4 76.0 reduce-scatter.3
  391.6 71.4 reduce-scatter.5

commit v3 on v1

--- a/solution.py
+++ b/solution.py
@@ -16,6 +16,16 @@
 GELU_A = 0.044715
 F32 = jnp.float32
 BF16 = jnp.bfloat16
+
+
+MESH = pl.DeviceIdType.MESH
+ANY = pl.BlockSpec(memory_space=pl.ANY)
+IN_VMEM = pl.BlockSpec(memory_space=pltpu.VMEM)
+DMA = pltpu.SemaphoreType.DMA
+
+
+def cost(us):
+    return pl.CostEstimate(flops=0, bytes_accessed=int(us * 3.3e6), transcendentals=0)
 
 
 def dot(left, right, dims=((1,), (0,))):
@@ -84,9 +94,56 @@
 
 
 def scan_forward_kernel(
-    parts, quarters, chunk, proj_ref, par_ref, gates_ref, z_ref, h_ref, v_ref, u_pad, a_s, b_s
+    parts,
+    quarters,
+    chunk,
+    n1_ref,
+    wi_ref,
+    par_ref,
+    rate_ref,
+    entry_ref,
+    z_ref,
+    h_ref,
+    v_ref,
+    proj_ref,
+    gates_ref,
+    n1_s,
+    wi_s,
+    gates_s,
+    u_pad,
+    a_s,
+    b_s,
+    sems,
 ):
     length, width = h_ref.shape
+    rows = quarters * chunk
+
+    def load(p):
+        return pltpu.make_async_copy(
+            n1_ref.at[p], n1_s.at[pl.ds(pl.multiple_of(p * rows, rows), rows)], sems.at[p]
+        )
+
+    weights = pltpu.make_async_copy(wi_ref, wi_s, sems.at[parts])
+    weights.start()
+    for p in range(parts):
+        load(p).start()
+    gates_s[...] = jnp.zeros(gates_s.shape, F32)
+    blocks, block_width = rate_ref.shape[0], rate_ref.shape[1]
+    for gate, src in enumerate((rate_ref, entry_ref)):
+        for j in range(blocks):
+            at, lane = j * block_width, gate * width + j * block_width
+            gates_s[at : at + block_width, lane : lane + block_width] = src[j].astype(F32)
+    gates_ref[...] = gates_s[...].astype(BF16)
+    weights.wait()
+
+    def project(k, carry):
+        load(2 * k).wait()
+        load(2 * k + 1).wait()
+        at = pl.ds(pl.multiple_of(k * 2 * rows, 2 * rows), 2 * rows)
+        proj_ref[at, :] = dot(n1_s[at, :], wi_s[...])
+        return carry
+
+    lax.fori_loop(0, parts // 2, project, 0)
     seg = length // SEGMENTS
     chunks = length // chunk
 
@@ -155,40 +212,56 @@
         lax.fori_loop(0, per, last, 0)
 
 
-def scan_forward(parts, quarters, chunk, proj, params, gates):
-    length, width = proj.shape[0], proj.shape[1] // 2
+def scan_forward(quarters, chunk, n1, w_in, params, rate, entry):
+    parts, rows, model = n1.shape
+    length, width = parts * rows, w_in.shape[1] // 2
     return pl.pallas_call(
         functools.partial(scan_forward_kernel, parts, quarters, chunk),
         out_shape=(
             jax.ShapeDtypeStruct((length, width), BF16),
             jax.ShapeDtypeStruct((length, width), F32),
             jax.ShapeDtypeStruct((length, width), BF16),
+            jax.ShapeDtypeStruct((length, 2 * width), F32),
+            jax.ShapeDtypeStruct((width, 2 * width), BF16),
         ),
-        in_specs=[pl.BlockSpec(memory_space=pltpu.VMEM)] * 3,
-        out_specs=[pl.BlockSpec(memory_space=pltpu.VMEM)] * 3,
+        in_specs=[ANY] * 2 + [IN_VMEM] * 3,
+        out_specs=[IN_VMEM] * 5,
         scratch_shapes=[
+            pltpu.VMEM((length, model), BF16),
+            pltpu.VMEM(w_in.shape, BF16),
+            pltpu.VMEM((width, 2 * width), F32),
             pltpu.VMEM((length + 8, width), F32),
             pltpu.VMEM((width // LANES, length, LANES), F32),
             pltpu.VMEM((width // LANES, length, LANES), F32),
+            DMA((parts + 1,)),
         ],
         compiler_params=pltpu.CompilerParams(vmem_limit_bytes=48 * 2**20),
+        cost_estimate=cost(18),
         name="scan_forward",
-    )(proj, params, gates)
+    )(n1, w_in, params, rate, entry)
 
 
 def scan_backward_kernel(
     parts,
     quarters,
     chunk,
-    dz_ref,
+    blocks,
+    block_width,
+    dout_ref,
+    wo_ref,
     proj_ref,
     h_ref,
     v_ref,
     par_ref,
     gates_ref,
     both_ref,
+    blocks_ref,
+    totals_ref,
+    dout_s,
+    dz_s,
+    sems,
+    sums_ref,
     gate_grad_ref,
-    sums_ref,
     a_s,
     g_s,
     t_s,
@@ -210,8 +283,30 @@
     def time_of(c):
         return pl.multiple_of(c * chunk, chunk)
 
-    softplus_decay = softplus(-par_ref[DECAY : DECAY + 1, :])
-    log_scale = -DECAY_SCALE * softplus_decay
+    span = quarters * chunk
+
+    def load(p):
+        return pltpu.make_async_copy(
+            dout_ref.at[p], dout_s.at[pl.ds(pl.multiple_of(p * span, span), span)], sems.at[p]
+        )
+
+    for p in range(parts):
+        load(p).start()
+
+    def back_project(k, carry):
+        load(2 * k).wait()
+        load(2 * k + 1).wait()
+        at = pl.ds(pl.multiple_of(k * 2 * span, 2 * span), 2 * span)
+        depth = wo_ref.shape[2]
+        total = dot(dout_s[at, 0:depth], wo_ref[0], ((1,), (1,)))
+        for p in range(1, wo_ref.shape[0]):
+            lanes = slice(p * depth, (p + 1) * depth)
+            total = total + dot(dout_s[at, lanes], wo_ref[p], ((1,), (1,)))
+        dz_s[at, :] = total
+        return carry
+
+    lax.fori_loop(0, parts // 2, back_project, 0)
+    log_scale = -DECAY_SCALE * softplus(-par_ref[DECAY : DECAY + 1, :])
     bias = jnp.concatenate(
         [par_ref[RATE_B : RATE_B + 1, :], par_ref[ENTRY_B : ENTRY_B + 1, :]], axis=1
     )
@@ -229,7 +324,7 @@
         h_pad[later, :] = h
         u_pad[later, :] = proj_ref[there, width : 2 * width].astype(BF16).astype(F32)
         y, slope = gelu_and_slope(proj_ref[there, 0:width])
-        dz = dz_ref[there, :]
+        dz = dz_s[there, :]
         put(g_s, rows, (dz * y).astype(BF16).astype(F32))
         both_ref[there, 0:width] = (dz * h.astype(BF16).astype(F32) * slope).astype(BF16)
         pre = dot(v_ref[rows, :], gates_ref[...]) + bias
@@ -314,20 +409,40 @@
 
     lax.fori_loop(0, chunks, last, 0)
     gate_grad_ref[...] = dot(v_ref[...], dpre_s[...], ((0,), (0,)))
-
-
-def scan_backward(parts, quarters, chunk, dz, proj, h, v, params, gates):
+    blocks_ref[...] = jnp.zeros(blocks_ref.shape, F32)
+    tall = blocks_ref.shape[0] // (2 * blocks)
+    for gate in range(2):
+        for j in range(blocks):
+            at, lanes = (gate * blocks + j) * tall, gate * width + j * block_width
+            rows = slice(j * block_width, (j + 1) * block_width)
+            blocks_ref[at : at + block_width, :block_width] = gate_grad_ref[
+                rows, lanes : lanes + block_width
+            ]
+    for k in range(8):
+        totals_ref[k : k + 1, :] = jnp.sum(sums_ref[8 * k : 8 * k + 8, :], axis=0, keepdims=True)
+
+
+def scan_backward(
+    quarters, chunk, blocks, block_width, dout, w_out, proj, h, v, params, gates
+):
+    parts = dout.shape[0]
     length, width = h.shape
+    tall, wide = -(-block_width // 8) * 8, -(-block_width // LANES) * LANES
     return pl.pallas_call(
-        functools.partial(scan_backward_kernel, parts, quarters, chunk),
+        functools.partial(scan_backward_kernel, parts, quarters, chunk, blocks, block_width),
         out_shape=(
             jax.ShapeDtypeStruct((length, 2 * width), BF16),
-            jax.ShapeDtypeStruct((width, 2 * width), F32),
-            jax.ShapeDtypeStruct((64, width), F32),
+            jax.ShapeDtypeStruct((2 * blocks * tall, wide), F32),
+            jax.ShapeDtypeStruct((8, width), F32),
         ),
-        in_specs=[pl.BlockSpec(memory_space=pltpu.VMEM)] * 6,
-        out_specs=[pl.BlockSpec(memory_space=pltpu.VMEM)] * 3,
+        in_specs=[ANY] + [IN_VMEM] * 6,
+        out_specs=[IN_VMEM] * 3,
         scratch_shapes=[
+            pltpu.VMEM((length, dout.shape[2]), BF16),
+            pltpu.VMEM((length, width), F32),
+            DMA((parts,)),
+            pltpu.VMEM((64, width), F32),
+            pltpu.VMEM((width, 2 * width), F32),
             pltpu.VMEM((width // LANES, length + 8, LANES), F32),
             pltpu.VMEM((width // LANES, length, LANES), F32),
             pltpu.VMEM((width // LANES, length, LANES), F32),
@@ -337,20 +452,1026 @@
             pltpu.VMEM((length + 8, width), F32),
             pltpu.VMEM((length + 8, width), F32),
         ],
-        compiler_params=pltpu.CompilerParams(vmem_limit_bytes=52 * 2**20),
+        compiler_params=pltpu.CompilerParams(vmem_limit_bytes=56 * 2**20),
+        cost_estimate=cost(21),
         name="scan_backward",
-    )(dz, proj, h, v, params, gates)
-
-
-def rms_parts(values):
+    )(dout, w_out, proj, h, v, params, gates)
+
+
+def remote(src, dst, send, recv, to):
+    return pltpu.make_async_remote_copy(
+        src_ref=src, dst_ref=dst, send_sem=send, recv_sem=recv, device_id=to, device_id_type=MESH
+    )
+
+
+def add_rows(rows, fn):
+    def one(k, carry):
+        fn(pl.ds(pl.multiple_of(k * 16, 16), 16))
+        return carry
+
+    lax.fori_loop(0, rows // 16, one, 0)
+
+
+class Place:
+    def __init__(self, outer, inner, shards):
+        self.outer, self.inner, self.shards = outer, inner, shards
+        self.parts, self.ys, self.count = outer * inner, shards // 2, outer * inner * shards
+        self.chips = inner * self.ys
+        self.s, self.h = lax.axis_index("seq"), lax.axis_index("shard")
+        self.o, self.i = self.s // inner, lax.rem(self.s, inner)
+        self.y, self.core = self.h // 2, lax.rem(self.h, 2)
+        self.beside = (self.o * inner + 1 - self.i, self.h)
+        self.above, self.below = (self.s + inner, self.h), (self.s - inner, self.h)
+        self.sibling = (self.s, self.along(0, 1))
+
+    def along(self, dy, other=0):
+        y = lax.rem(self.y + dy + self.ys, self.ys)
+        return y * 2 + lax.rem(self.core + other, 2)
+
+    def chip(self, q, back=False):
+        di, dy = q // self.ys, q - q // self.ys * self.ys
+        if back:
+            di, dy = self.inner - di, self.ys - dy
+        return lax.rem(self.i + di, self.inner), lax.rem(self.y + dy, self.ys)
+
+    def near(self, q, other=0, back=False):
+        i, y = self.chip(q, back)
+        h = y * 2 + lax.rem(self.core + other, 2)
+        return (self.o * self.inner + i, h), i * self.shards + h
+
+    def far_first(self, n):
+        sign = 2 * ((2 * self.o) // self.outer) - 1
+        return lax.rem(self.o + sign * (n + 1) + 2 * self.outer, self.outer)
+
+    def branches(self, fn):
+        for o0 in range(self.outer):
+            pl.when(self.o == o0)(functools.partial(fn, o0))
+
+
+def hello(to):
+    barrier = pltpu.get_barrier_semaphore()
+    pl.semaphore_signal(barrier, inc=1, device_id=to, device_id_type=MESH)
+
+
+def welcome(n):
+    pl.semaphore_wait(pltpu.get_barrier_semaphore(), n)
+
+
+def greet(others):
+    for to in others:
+        hello(to)
+    welcome(len(others))
+
+
+def greet_with_line(at, others):
+    up, down = at.o < at.outer - 1, at.o > 0
+    for to in others:
+        hello(to)
+    pl.when(up)(lambda: hello(at.above))
+    pl.when(down)(lambda: hello(at.below))
+    ends = lax.rem(at.o, at.outer - 1) == 0
+    pl.when(ends)(lambda: welcome(len(others) + 1))
+    pl.when(jnp.logical_not(ends))(lambda: welcome(len(others) + 2))
+
+
+class Sent:
+    def __init__(self):
+        self.copies = []
+
+    def __call__(self, src, dst, sems, at, to):
+        copy = remote(src, dst, sems.at[(0,) + at], sems.at[(1,) + at], to)
+        copy.start()
+        self.copies.append(copy)
+
+    def finish(self):
+        for copy in self.copies:
+            copy.wait_send()
+
+
+def received(like, here, sems, at, source):
+    remote(like, here, sems.at[(0,) + at], sems.at[(1,) + at], source).wait_recv()
+
+
+def line_gather(at, o0, x_ref, out, across, up, down, between=lambda k: None):
+    send = Sent()
+
+    def slot(row):
+        return out.at[row * at.inner + at.i]
+
+    def pass_on(row, sems, to):
+        send(x_ref if row == o0 else slot(row), slot(row), sems, (row,), to)
+
+    for k in range(at.outer):
+        lower, upper = o0 - k, o0 + k
+        if k > 0 and lower >= 0:
+            received(x_ref, slot(lower), up, (lower,), at.below)
+        if lower >= 0 and o0 < at.outer - 1:
+            pass_on(lower, up, at.above)
+        if lower >= 0:
+            pass_on(lower, across, at.beside)
+        if k > 0 and upper < at.outer:
+            received(x_ref, slot(upper), down, (upper,), at.above)
+        if upper < at.outer and o0 > 0:
+            pass_on(upper, down, at.below)
+        if k > 0 and upper < at.outer:
+            pass_on(upper, across, at.beside)
+        between(k)
+    for row in range(at.outer):
+        received(x_ref, out.at[row * at.inner + 1 - at.i], across, (row,), at.beside)
+    send.finish()
+
+
+class LineSum:
+    def __init__(self, at, p, bufs, sems):
+        self.at, self.p = at, p
+        self.x_in, self.up_in, self.down_in, self.sums = bufs
+        self.across, self.up, self.down = sems
+        self.rows = self.x_in.shape[1]
+
+    def block(self, d, i):
+        return self.p.at[d, pl.ds(pl.multiple_of(i * self.rows, self.rows), self.rows)]
+
+    def cross(self, d):
+        return remote(
+            self.block(d, 1 - self.at.i),
+            self.x_in.at[d],
+            self.across.at[0, d],
+            self.across.at[1, d],
+            self.at.beside,
+        )
+
+    def steps(self, o0, last_add, between=lambda n: None):
+        at = self.at
+        send = Sent()
+        order = sorted(range(at.outer), key=lambda d: (-abs(d - o0), d))
+        for n, d in enumerate(order):
+            mine = self.block(d, at.i)
+            self.cross(d).wait_recv()
+            terms = [mine, self.x_in.at[d]]
+            if d >= o0 > 0:
+                received(mine, self.up_in.at[d], self.up, (d,), at.below)
+                terms.append(self.up_in.at[d])
+            if d <= o0 < at.outer - 1:
+                received(mine, self.down_in.at[d], self.down, (d,), at.above)
+                terms.append(self.down_in.at[d])
+            target = self.sums.at[d]
+
+            def add(rows, terms=terms, target=target, d=d):
+                total = terms[0][rows, :].astype(F32)
+                for term in terms[1:]:
+                    total = total + term[rows, :].astype(F32)
+                if d == o0:
+                    last_add(rows, total)
+                else:
+                    target[rows, :] = total.astype(target.dtype)
+
+            add_rows(self.rows, add)
+            if d > o0:
+                send(target, self.up_in.at[d], self.up, (d,), at.above)
+            if d < o0:
+                send(target, self.down_in.at[d], self.down, (d,), at.below)
+            between(n)
+        for d in range(at.outer):
+            self.cross(d).wait_send()
+        send.finish()
+
+
+def line_sum_scratch(outer, rows, cols):
+    return [pltpu.VMEM((outer, rows, cols), BF16)] * 4, [DMA((2, outer))] * 3
+
+
+def opening_kernel(
+    outer, inner, shards, x_ref, wi_ref, wo_ref, n_out, wi_out, wo_out, local, across, up, down, far, near
+):
+    at = Place(outer, inner, shards)
+    steps = list(range(1, at.ys))
+    weights = ((wi_ref, wi_out), (wo_ref, wo_out))
+    greet_with_line(at, [at.beside, at.sibling] + [(at.s, at.along(dy)) for dy in steps])
+    keep = [
+        pltpu.make_async_copy(x_ref, n_out.at[at.s], local.at[0]),
+        pltpu.make_async_copy(wi_ref, wi_out.at[at.h], local.at[1]),
+        pltpu.make_async_copy(wo_ref, wo_out.at[at.h], local.at[2]),
+    ]
+    for copy in keep:
+        copy.start()
+    send = Sent()
+    for n, (src, dst) in enumerate(weights):
+        for dy in steps:
+            send(src, dst.at[at.h], far, (n, dy), (at.s, at.along(dy)))
+        send(src, dst.at[at.h], near, (n, 0), at.sibling)
+
+    def branch(o0):
+        forward = Sent()
+
+        def between(k):
+            if k != 1:
+                return
+            for n, (src, dst) in enumerate(weights):
+                for dy in steps:
+                    source = at.along(-dy)
+                    received(src, dst.at[source], far, (n, dy), (at.s, source))
+                    forward(dst.at[source], dst.at[source], near, (n, dy), at.sibling)
+
+        line_gather(at, o0, x_ref, n_out, across, up, down, between)
+        forward.finish()
+
+    at.branches(branch)
+    for n, (src, dst) in enumerate(weights):
+        for dy in range(at.ys):
+            received(src, dst.at[at.along(-dy, 1)], near, (n, dy), at.sibling)
+    send.finish()
+    for copy in keep:
+        copy.wait()
+
+
+def opening(x, w_in, w_out, outer, inner, shards, collective):
+    ys = shards // 2
+    return pl.pallas_call(
+        functools.partial(opening_kernel, outer, inner, shards),
+        out_shape=(
+            jax.ShapeDtypeStruct((outer * inner,) + x.shape, x.dtype),
+            jax.ShapeDtypeStruct((shards,) + w_in.shape, w_in.dtype),
+            jax.ShapeDtypeStruct((shards,) + w_out.shape, w_out.dtype),
+        ),
+        in_specs=[ANY] * 3,
+        out_specs=[ANY] * 3,
+        scratch_shapes=[DMA((3,))] + [DMA((2, outer))] * 3 + [DMA((2, 2, ys))] * 2,
+        compiler_params=pltpu.CompilerParams(collective_id=collective, has_side_effects=True),
+        cost_estimate=cost(55),
+        name="opening",
+    )(x, w_in, w_out)
+
+
+def row_rms(values):
     return lax.rsqrt(jnp.mean(values * values, axis=-1, keepdims=True) + EPSILON)
 
 
 def rms_back(values, scale, gain, grad):
     k = grad * gain
-    return scale * k - scale * scale * scale * values * jnp.mean(
-        k * values, axis=-1, keepdims=True
-    )
+    mean = jnp.mean(k * values, axis=-1, keepdims=True)
+    return scale * k - scale * scale * scale * values * mean
+
+
+def middle_kernel(
+    outer,
+    inner,
+    shards,
+    z_ref,
+    wo_ref,
+    x_ref,
+    gain_ref,
+    cot_ref,
+    cot_beside_ref,
+    mid_ref,
+    n2_out,
+    cot_out,
+    p_s,
+    n2_s,
+    x_in,
+    up_in,
+    down_in,
+    line_out,
+    across,
+    up,
+    down,
+    far,
+    near,
+    c_far,
+    c_near,
+    local,
+):
+    at = Place(outer, inner, shards)
+    line = LineSum(at, p_s, (x_in, up_in, down_in, line_out), (across, up, down))
+    steps = list(range(1, at.ys))
+    cols = wo_ref.shape[2]
+    greet_with_line(at, [at.sibling] + [at.near(q)[0] for q in range(1, at.chips)])
+    send = Sent()
+
+    def project(n, carry):
+        d = at.far_first(n)
+        for k in range(shards):
+            block = dot(z_ref[d], wo_ref[k]).astype(BF16)
+            p_s[d, :, k * cols : (k + 1) * cols] = block
+        line.cross(d).start()
+        return carry
+
+    lax.fori_loop(0, outer, project, 0)
+
+    def slot(side, dy, other=0):
+        i = 1 - at.i if side else at.i
+        return cot_out.at[i * shards + at.along(dy, other)]
+
+    mine = (cot_ref, cot_beside_ref)
+    keep = []
+    for side in range(2):
+        keep.append(pltpu.make_async_copy(mine[side], slot(side, 0), local.at[side]))
+        keep[-1].start()
+        for dy in steps:
+            send(mine[side], slot(side, 0), c_far, (side, dy), (at.s, at.along(dy)))
+        send(mine[side], slot(side, 0), c_near, (side, 0), at.sibling)
+
+    def last_add(rows, total):
+        mid = x_ref[rows, :].astype(F32) + total
+        mid_ref[rows, :] = mid
+        n2_s[rows, :] = (mid * row_rms(mid) * gain_ref[...]).astype(BF16)
+
+    def branch(o0):
+        forward = Sent()
+
+        def between(n):
+            if n != outer - 2:
+                return
+            for side in range(2):
+                for dy in steps:
+                    here = slot(side, -dy)
+                    received(cot_ref, here, c_far, (side, dy), (at.s, at.along(-dy)))
+                    forward(here, here, c_near, (side, dy), at.sibling)
+
+        line.steps(o0, last_add, between)
+        forward.finish()
+
+    at.branches(branch)
+    _, me = at.near(0)
+    keep.append(pltpu.make_async_copy(n2_s, n2_out.at[me], local.at[2]))
+    keep[-1].start()
+    for q in reversed(range(1, at.chips)):
+        send(n2_s, n2_out.at[me], far, (q,), at.near(q)[0])
+    send(n2_s, n2_out.at[me], near, (0,), at.sibling)
+    for q in range(1, at.chips):
+        source, there = at.near(q, back=True)
+        here = n2_out.at[there]
+        received(n2_s, here, far, (q,), source)
+        send(here, here, near, (q,), at.sibling)
+    for q in range(at.chips):
+        received(n2_s, n2_out.at[at.near(q, 1, True)[1]], near, (q,), at.sibling)
+    for side in range(2):
+        for dy in range(at.ys):
+            received(cot_ref, slot(side, -dy, 1), c_near, (side, dy), at.sibling)
+    send.finish()
+    for copy in keep:
+        copy.wait()
+
+
+def middle(z, w_out, x, gain, cot, cot_beside, outer, inner, shards, collective):
+    rows, cols = x.shape
+    ys, chips = shards // 2, inner * shards // 2
+    bufs, sems = line_sum_scratch(outer, rows, cols)
+    plane = jax.ShapeDtypeStruct((inner * shards, rows, cols), BF16)
+    return pl.pallas_call(
+        functools.partial(middle_kernel, outer, inner, shards),
+        out_shape=(jax.ShapeDtypeStruct((rows, cols), F32), plane, plane),
+        in_specs=[IN_VMEM] * 4 + [ANY] * 2,
+        out_specs=[IN_VMEM, ANY, ANY],
+        scratch_shapes=[
+            pltpu.VMEM((outer, inner * rows, cols), BF16),
+            pltpu.VMEM((rows, cols), BF16),
+        ]
+        + bufs
+        + sems
+        + [DMA((2, chips))] * 2
+        + [DMA((2, 2, ys))] * 2
+        + [DMA((3,))],
+        compiler_params=pltpu.CompilerParams(
+            collective_id=collective, has_side_effects=True, vmem_limit_bytes=48 * 2**20
+        ),
+        cost_estimate=cost(80),
+        name="middle",
+    )(z.reshape(outer, inner * rows, z.shape[1]), w_out, x, gain, cot, cot_beside)
+
+
+class PlaneSum:
+    def __init__(self, at, n, p, near_in, far_in, far_out, near, far):
+        self.at, self.n, self.p = at, n, p
+        self.near_in, self.far_in, self.far_out = near_in, far_in, far_out
+        self.near, self.far = near, far
+        self.rows = near_in.shape[2]
+
+    def block(self, q, other):
+        i, y = self.at.chip(q)
+        core = lax.rem(self.at.core + other, 2)
+        rows = pl.ds(pl.multiple_of(core * self.rows, self.rows), self.rows)
+        return self.p.at[i * self.at.ys + y, rows]
+
+    def to_sibling(self, q):
+        n = self.n
+        return remote(
+            self.block(q, 1),
+            self.near_in.at[n, q],
+            self.near.at[0, n, q],
+            self.near.at[1, n, q],
+            self.at.sibling,
+        )
+
+    def onward(self, q, back=False):
+        n = self.n
+        return remote(
+            self.far_out.at[n, q],
+            self.far_in.at[n, q],
+            self.far.at[0, n, q],
+            self.far.at[1, n, q],
+            self.at.near(q, 0, back)[0],
+        )
+
+    def combine(self):
+        def one(k, carry):
+            q = self.at.chips - 1 - k
+            self.to_sibling(q).wait_recv()
+            mine = self.block(q, 0)
+
+            def add(rows):
+                total = mine[rows, :].astype(F32) + self.near_in[self.n, q, rows, :].astype(F32)
+                self.far_out[self.n, q, rows, :] = total.astype(BF16)
+
+            add_rows(self.rows, add)
+            self.onward(q).start()
+            return carry
+
+        lax.fori_loop(0, self.at.chips - 1, one, 0)
+        self.to_sibling(0).wait_recv()
+
+    def total(self, rows):
+        n = self.n
+        value = self.block(0, 0)[rows, :].astype(F32) + self.near_in[n, 0, rows, :].astype(F32)
+        for q in range(1, self.at.chips):
+            value = value + self.far_in[n, q, rows, :].astype(F32)
+        return value
+
+    def arrive(self):
+        for q in range(1, self.at.chips):
+            self.onward(q, True).wait_recv()
+
+    def finish(self):
+        for q in range(self.at.chips):
+            self.to_sibling(q).wait_send()
+        for q in range(1, self.at.chips):
+            self.onward(q).wait_send()
+
+
+def turn_kernel(
+    outer,
+    inner,
+    shards,
+    dgm_ref,
+    dum_ref,
+    mm_ref,
+    wg_ref,
+    wu_ref,
+    wd_ref,
+    mid_ref,
+    cot_ref,
+    gain_ref,
+    dmid_ref,
+    dout_ref,
+    result_ref,
+    gain_grad_ref,
+    p_s,
+    q_s,
+    dout_s,
+    gain_s,
+    wg_s,
+    wu_s,
+    wd_s,
+    near_in,
+    far_in,
+    far_out,
+    near,
+    far,
+    across,
+    up,
+    down,
+    local,
+):
+    at = Place(outer, inner, shards)
+    model, hidden = wg_s.shape
+    own = pl.ds(pl.multiple_of(at.i * hidden, hidden), hidden)
+    load = [
+        pltpu.make_async_copy(wg_ref.at[:, own], wg_s, local.at[1]),
+        pltpu.make_async_copy(wu_ref.at[:, own], wu_s, local.at[2]),
+        pltpu.make_async_copy(wd_ref.at[own, :], wd_s, local.at[3]),
+    ]
+    for copy in load:
+        copy.start()
+    tile = min(512, model)
+    greet_with_line(at, [at.sibling] + [at.near(q)[0] for q in range(1, at.chips)])
+    grad = PlaneSum(at, 0, p_s, near_in, far_in, far_out, near, far)
+    value = PlaneSum(at, 1, q_s, near_in, far_in, far_out, near, far)
+
+    load[0].wait()
+    load[1].wait()
+
+    def back(k, carry):
+        q = at.chips - 1 - k
+        i, y = at.chip(q)
+        c = i * at.ys + y
+        for lane in range(0, model, tile):
+            lanes = slice(lane, lane + tile)
+            block = dot(dgm_ref[c], wg_s[lanes, :], ((1,), (1,)))
+            block = block + dot(dum_ref[c], wu_s[lanes, :], ((1,), (1,)))
+            p_s[c, :, lanes] = block.astype(BF16)
+        grad.to_sibling(q).start()
+        return carry
+
+    lax.fori_loop(0, at.chips, back, 0)
+    grad.combine()
+
+    load[2].wait()
+
+    def ahead(k, carry):
+        q = at.chips - 1 - k
+        i, y = at.chip(q)
+        c = i * at.ys + y
+        for lane in range(0, model, tile):
+            lanes = slice(lane, lane + tile)
+            q_s[c, :, lanes] = dot(mm_ref[c], wd_s[:, lanes]).astype(BF16)
+        value.to_sibling(q).start()
+        return carry
+
+    lax.fori_loop(0, at.chips, ahead, 0)
+    gain_s[...] = jnp.zeros(gain_s.shape, F32)
+    grad.arrive()
+
+    def norm_back(rows):
+        dn2 = grad.total(rows)
+        mid = mid_ref[rows, :]
+        scale = row_rms(mid)
+        gain_s[...] += dn2 * mid * scale
+        dmid = cot_ref[rows, :].astype(F32) + rms_back(mid, scale, gain_ref[...], dn2)
+        dmid_ref[rows, :] = dmid
+        dout_s[rows, :] = dmid.astype(BF16)
+
+    add_rows(dout_s.shape[0], norm_back)
+    gain_grad_ref[...] = jnp.sum(gain_s[...], axis=0, keepdims=True)
+    keep = pltpu.make_async_copy(dout_s, dout_ref.at[at.s], local.at[0])
+    keep.start()
+
+    def branch(o0):
+        def between(k):
+            if k == 0:
+                value.combine()
+
+        line_gather(at, o0, dout_s, dout_ref, across, up, down, between)
+
+    at.branches(branch)
+    value.arrive()
+
+    def output(rows):
+        result_ref[rows, :] = (mid_ref[rows, :] + value.total(rows)).astype(BF16)
+
+    add_rows(result_ref.shape[0], output)
+    grad.finish()
+    value.finish()
+    keep.wait()
+
+
+def turn(dgm, dum, mm, wg, wu, wd, mid, cot, gain, outer, inner, shards, collective):
+    rows, cols = mid.shape
+    hidden = dgm.shape[1]
+    chips = inner * shards // 2
+    buffers = pltpu.VMEM((2, chips, rows, cols), BF16)
+    partial = pltpu.VMEM((chips, 2 * rows, cols), BF16)
+    dgm, dum, mm = (x.reshape(chips, 2 * rows, hidden) for x in (dgm, dum, mm))
+    return pl.pallas_call(
+        functools.partial(turn_kernel, outer, inner, shards),
+        out_shape=(
+            jax.ShapeDtypeStruct((rows, cols), F32),
+            jax.ShapeDtypeStruct((outer * inner, rows, cols), BF16),
+            jax.ShapeDtypeStruct((rows, cols), BF16),
+            jax.ShapeDtypeStruct((1, cols), F32),
+        ),
+        in_specs=[IN_VMEM] * 3 + [ANY] * 3 + [IN_VMEM] * 3,
+        out_specs=[IN_VMEM, ANY, IN_VMEM, IN_VMEM],
+        scratch_shapes=[
+            partial,
+            partial,
+            pltpu.VMEM((rows, cols), BF16),
+            pltpu.VMEM((16, cols), F32),
+            pltpu.VMEM((cols, hidden), BF16),
+            pltpu.VMEM((cols, hidden), BF16),
+            pltpu.VMEM((hidden, cols), BF16),
+        ]
+        + [buffers] * 3
+        + [DMA((2, 2, chips))] * 2
+        + [DMA((2, outer))] * 3
+        + [DMA((4,))],
+        compiler_params=pltpu.CompilerParams(
+            collective_id=collective, has_side_effects=True, vmem_limit_bytes=56 * 2**20
+        ),
+        cost_estimate=cost(120),
+        name="turn",
+    )(dgm, dum, mm, wg, wu, wd, mid, cot, gain)
+
+
+class PlaneExchange:
+    def __init__(self, at, n, x, out, sems, local):
+        self.at, self.n, self.x, self.out, self.sems = at, n, x, out, sems
+        _, self.me = at.near(0)
+        self.keep = pltpu.make_async_copy(x.at[self.me], out.at[self.me], local)
+        self.hops = [(q, other) for q in reversed(range(at.chips)) for other in range(2)][:-2] + [(0, 1)]
+
+    def others(self):
+        return [self.at.near(q, other)[0] for q, other in self.hops]
+
+    def start(self):
+        self.send = Sent()
+        for k, (q, other) in enumerate(self.hops):
+            to, slot = self.at.near(q, other)
+            self.send(self.x.at[slot], self.out.at[self.me], self.sems, (self.n, k), to)
+        self.keep.start()
+
+    def finish(self):
+        for k, (q, other) in enumerate(self.hops):
+            source, slot = self.at.near(q, other, True)
+            received(self.x.at[self.me], self.out.at[slot], self.sems, (self.n, k), source)
+        self.send.finish()
+        self.keep.wait()
+
+
+def closing_kernel(
+    outer,
+    inner,
+    shards,
+    both_ref,
+    wi_ref,
+    z_ref,
+    x_ref,
+    dmid_ref,
+    gain_ref,
+    gain2_ref,
+    blocks_ref,
+    sums_ref,
+    n1_ref,
+    dout_ref,
+    down_ref,
+    gate_ref,
+    grad_ref,
+    mix_ref,
+    blocks_out,
+    sums_out,
+    gains_out,
+    down_out,
+    gate_out,
+    p_s,
+    n1_s,
+    dout_s,
+    g_s,
+    gain_s,
+    gain_rows,
+    gain_slots,
+    near_in,
+    far_in,
+    far_out,
+    done,
+    block_slots,
+    sum_slots,
+    x_in,
+    up_in,
+    down_in,
+    line_out,
+    across,
+    up,
+    low,
+    near,
+    far,
+    final,
+    s_far,
+    s_near,
+    swap,
+    g_sem,
+    local,
+):
+    at = Place(outer, inner, shards)
+    s, h, parts, ys = at.s, at.h, at.parts, at.ys
+    steps = list(range(1, ys))
+    line = LineSum(at, p_s, (x_in, up_in, down_in, line_out), (across, up, low))
+    model = x_ref.shape[1]
+    tile = min(512, model)
+    piece = done.shape[1]
+    span = shards * piece
+    width2 = both_ref.shape[1]
+    me = s * shards + h
+    small = ((blocks_ref, block_slots, blocks_out), (sums_ref, sum_slots, sums_out))
+    load = [
+        pltpu.make_async_copy(n1_ref, n1_s, local.at[0]),
+        pltpu.make_async_copy(dout_ref, dout_s, local.at[1]),
+    ]
+    for copy in load:
+        copy.start()
+
+    def anyone(k):
+        to = lax.rem(me + k, at.count)
+        return (to // shards, lax.rem(to, shards)), to
+
+    def greet_one(k, carry):
+        hello(anyone(k)[0])
+        return carry
+
+    lax.fori_loop(1, at.count, greet_one, 0)
+    welcome(at.count - 1)
+
+    def back(n, carry):
+        d = at.far_first(n)
+        rows = pl.ds(pl.multiple_of(d * p_s.shape[1], p_s.shape[1]), p_s.shape[1])
+        for lane in range(0, model, tile):
+            lanes = slice(lane, lane + tile)
+            p_s[d, :, lanes] = dot(both_ref[rows, :], wi_ref[lanes, :], ((1,), (1,))).astype(BF16)
+        line.cross(d).start()
+        return carry
+
+    lax.fori_loop(0, outer, back, 0)
+    send = Sent()
+    for n, (src, slots, _) in enumerate(small):
+        for dy in steps:
+            send(src, slots.at[h], s_far, (n, dy), (s, at.along(dy)))
+        send(src, slots.at[h], s_near, (n, 0), at.sibling)
+        slots[h] = src[...]
+    for copy in load:
+        copy.wait()
+
+    def owner(k):
+        return lax.rem(s + k + 1, parts)
+
+    def mix_rows(p, shard):
+        return g_s.at[p, pl.ds(pl.multiple_of(shard * piece, piece), piece)]
+
+    def to_sibling(k, dy):
+        p = owner(k)
+        return remote(
+            mix_rows(p, at.along(dy, 1)),
+            near_in.at[dy, p],
+            near.at[0, dy, k],
+            near.at[1, dy, k],
+            at.sibling,
+        )
+
+    def to_shard(k, dy, source=False):
+        p = owner(k)
+        return remote(
+            far_out.at[dy - 1, p],
+            far_in.at[dy - 1, p],
+            far.at[0, dy, k],
+            far.at[1, dy, k],
+            (s, at.along(-dy if source else dy)),
+        )
+
+    def to_owner(k, source=False):
+        p = lax.rem(s + parts - k - 1, parts) if source else owner(k)
+        return remote(
+            done.at[owner(k)],
+            mix_ref.at[p if source else s],
+            final.at[0, k],
+            final.at[1, k],
+            (p, h),
+        )
+
+    def weight_grads(k, carry):
+        p = owner(k)
+        lanes = pl.ds(pl.multiple_of(p * span, span), span)
+        g_s[p, :, 0:width2] = dot(n1_s[:, lanes], both_ref[...], ((0,), (0,))).astype(BF16)
+        g_s[p, :, width2:] = dot(dout_s[:, lanes], z_ref[...], ((0,), (0,))).astype(BF16)
+        for dy in steps + [0]:
+            to_sibling(k, dy).start()
+        return carry
+
+    lax.fori_loop(0, parts, weight_grads, 0)
+    exchanges = [
+        PlaneExchange(at, 0, down_ref, down_out, swap, local.at[2]),
+        PlaneExchange(at, 1, gate_ref, gate_out, swap, local.at[3]),
+    ]
+
+    def sibling_sums(k, carry):
+        p = owner(k)
+        for dy in steps:
+            to_sibling(k, dy).wait_recv()
+            mine = mix_rows(p, at.along(dy))
+
+            def add(rows, dy=dy, mine=mine):
+                total = mine[rows, :].astype(F32) + near_in[dy, p, rows, :].astype(F32)
+                far_out[dy - 1, p, rows, :] = total.astype(BF16)
+
+            add_rows(piece, add)
+            to_shard(k, dy).start()
+        return carry
+
+    lax.fori_loop(0, parts, sibling_sums, 0)
+    for exchange in exchanges:
+        exchange.start()
+    gain_s[...] = jnp.zeros(gain_s.shape, F32)
+
+    def mix_step(k):
+        p = owner(k)
+        mine = mix_rows(p, h)
+        to_sibling(k, 0).wait_recv()
+        for dy in steps:
+            to_shard(k, dy, True).wait_recv()
+
+        def add(rows):
+            total = mine[rows, :].astype(F32) + near_in[0, p, rows, :].astype(F32)
+            for dy in steps:
+                total = total + far_in[dy - 1, p, rows, :].astype(F32)
+            done[p, rows, :] = total.astype(BF16)
+
+        add_rows(piece, add)
+        if k < parts - 1:
+            to_owner(k).start()
+
+    def last_add(rows, dn1):
+        x = x_ref[rows, :].astype(F32)
+        scale = row_rms(x)
+        gain_s[...] += dn1 * x * scale
+        grad_ref[rows, :] = dmid_ref[rows, :] + rms_back(x, scale, gain_ref[...], dn1)
+
+    def branch(o0):
+        def between(n):
+            for k in range(n * inner, (n + 1) * inner):
+                mix_step(k)
+
+        line.steps(o0, last_add, between)
+
+    at.branches(branch)
+    keep = pltpu.make_async_copy(done.at[s], mix_ref.at[s], local.at[4])
+    keep.start()
+    gain1, gain2 = jnp.sum(gain_s[...], axis=0, keepdims=True), gain2_ref[...]
+    spare = gain_rows.shape[2] - 2 * piece
+    for k in range(at.count):
+        lanes = slice(k * piece, (k + 1) * piece)
+        parts_of = [gain1[:, lanes], gain2[:, lanes]]
+        if spare:
+            parts_of.append(jnp.zeros((1, spare), F32))
+        gain_rows[k] = jnp.concatenate(parts_of, axis=1)
+
+    def gain(k):
+        to, row = anyone(k)
+        return remote(gain_rows.at[row], gain_slots.at[k], g_sem.at[0, k], g_sem.at[1, k], to)
+
+    def gain_start(k, carry):
+        gain(k).start()
+        return carry
+
+    def gain_arrive(k, total):
+        gain(k).wait_recv()
+        return total + gain_slots[k]
+
+    def gain_leave(k, carry):
+        gain(k).wait_send()
+        return carry
+
+    lax.fori_loop(1, at.count, gain_start, 0)
+    for n, (src, slots, out) in enumerate(small):
+        for dy in steps:
+            here = slots.at[at.along(-dy)]
+            received(src, here, s_far, (n, dy), (s, at.along(-dy)))
+            send(here, here, s_near, (n, dy), at.sibling)
+    for n, (src, slots, out) in enumerate(small):
+        for dy in range(ys):
+            received(src, slots.at[at.along(-dy, 1)], s_near, (n, dy), at.sibling)
+
+        def add(k, carry, slots=slots, out=out):
+            rows = pl.ds(pl.multiple_of(k * 8, 8), 8)
+            total = slots[0, rows, :]
+            for j in range(1, shards):
+                total = total + slots[j, rows, :]
+            out[rows, :] = total
+            return carry
+
+        lax.fori_loop(0, src.shape[0] // 8, add, 0)
+    gains_out[...] = lax.fori_loop(1, at.count, gain_arrive, gain_rows[me])
+    for k in range(parts - 1):
+        to_owner(k, True).wait_recv()
+    for exchange in exchanges:
+        exchange.finish()
+    for k in range(parts):
+        for dy in range(ys):
+            to_sibling(k, dy).wait_send()
+        for dy in steps:
+            to_shard(k, dy).wait_send()
+        if k < parts - 1:
+            to_owner(k).wait_send()
+    lax.fori_loop(1, at.count, gain_leave, 0)
+    send.finish()
+    keep.wait()
+
+
+def closing(
+    both, w_in, z, x, dmid, gain, gain2, small, sums, n1, dout, down, gate, outer, inner, shards, collective
+):
+    rows, cols = x.shape
+    parts, ys, count = outer * inner, shards // 2, outer * inner * shards
+    piece = cols // count
+    width = z.shape[1]
+    lanes = -(-2 * piece // LANES) * LANES
+    bufs, sems = line_sum_scratch(outer, rows, cols)
+    pieces = pltpu.VMEM((max(ys - 1, 1), parts, piece, 3 * width), BF16)
+    whole = pltpu.VMEM((parts * rows, cols), BF16)
+    same = jax.ShapeDtypeStruct(down.shape, down.dtype)
+    return pl.pallas_call(
+        functools.partial(closing_kernel, outer, inner, shards),
+        out_shape=(
+            jax.ShapeDtypeStruct((rows, cols), F32),
+            jax.ShapeDtypeStruct((parts, piece, 3 * width), BF16),
+            jax.ShapeDtypeStruct(small.shape, F32),
+            jax.ShapeDtypeStruct(sums.shape, F32),
+            jax.ShapeDtypeStruct((1, lanes), F32),
+            same,
+            same,
+        ),
+        in_specs=[IN_VMEM] * 9 + [ANY] * 4,
+        out_specs=[IN_VMEM] * 5 + [ANY] * 2,
+        scratch_shapes=[
+            pltpu.VMEM((outer, inner * rows, cols), BF16),
+            whole,
+            whole,
+            pltpu.VMEM((parts, shards * piece, 3 * width), BF16),
+            pltpu.VMEM((16, cols), F32),
+            pltpu.VMEM((count, 1, lanes), F32),
+            pltpu.VMEM((count, 1, lanes), F32),
+            pltpu.VMEM((ys, parts, piece, 3 * width), BF16),
+            pieces,
+            pieces,
+            pltpu.VMEM((parts, piece, 3 * width), BF16),
+            pltpu.VMEM((shards,) + small.shape, F32),
+            pltpu.VMEM((shards,) + sums.shape, F32),
+        ]
+        + bufs
+        + sems
+        + [DMA((2, ys, parts))] * 2
+        + [DMA((2, parts))]
+        + [DMA((2, 2, ys))] * 2
+        + [DMA((2, 2, inner * shards)), DMA((2, count)), DMA((5,))],
+        compiler_params=pltpu.CompilerParams(
+            collective_id=collective, has_side_effects=True, vmem_limit_bytes=60 * 2**20
+        ),
+        cost_estimate=cost(80),
+        name="closing",
+    )(
+        both,
+        w_in,
+        z,
+        x,
+        dmid,
+        gain,
+        gain2,
+        small,
+        sums,
+        n1,
+        dout,
+        down,
+        gate,
+    )
+
+
+def finish_kernel(outer, inner, shards, x_ref, out_ref, sems, local):
+    at = Place(outer, inner, shards)
+    exchange = PlaneExchange(at, 0, x_ref, out_ref, sems, local)
+    greet(exchange.others())
+    exchange.start()
+    exchange.finish()
+
+
+def finish(x, outer, inner, shards, collective):
+    return pl.pallas_call(
+        functools.partial(finish_kernel, outer, inner, shards),
+        out_shape=jax.ShapeDtypeStruct(x.shape, x.dtype),
+        in_specs=[ANY],
+        out_specs=ANY,
+        scratch_shapes=[DMA((2, 1, inner * shards)), DMA],
+        compiler_params=pltpu.CompilerParams(collective_id=collective, has_side_effects=True),
+        cost_estimate=cost(12),
+        name="finish",
+    )(x)
+
+
+def unpack_kernel(
+    inner, channels, gate_ref, up_ref, down_ref, mix_ref, gate, up, down, branch, enter, leave
+):
+    slots, piece, hidden = gate_ref.shape
+    shards = slots // inner
+    parts, width = mix_ref.shape[0], mix_ref.shape[2] // 3
+    for i in range(inner):
+        for h in range(shards):
+            lanes = slice((h * inner + i) * hidden, (h * inner + i + 1) * hidden)
+            slot = i * shards + h
+            for src, dst in ((gate_ref, gate), (up_ref, up), (down_ref, down)):
+                dst[:, lanes] = src[slot].astype(F32)
+    for k, dst in enumerate((branch, enter, leave)):
+        lanes = slice(k * width, k * width + width)
+        dst[...] = jnp.concatenate(
+            [mix_ref[p][:, lanes].astype(F32)[:, :channels] for p in range(parts)], axis=1
+        )
+
+
+def unpack(ffn_gate, ffn_up, ffn_down, mix, inner, channels):
+    slots, piece, hidden = ffn_gate.shape
+    across = jax.ShapeDtypeStruct((piece, slots * hidden), F32)
+    wide = jax.ShapeDtypeStruct((piece, mix.shape[0] * channels), F32)
+    return pl.pallas_call(
+        functools.partial(unpack_kernel, inner, channels),
+        out_shape=(across,) * 3 + (wide,) * 3,
+        in_specs=[IN_VMEM] * 4,
+        out_specs=[IN_VMEM] * 6,
+        compiler_params=pltpu.CompilerParams(vmem_limit_bytes=48 * 2**20),
+        cost_estimate=cost(4),
+        name="unpack",
+    )(ffn_gate, ffn_up, ffn_down, mix)
 
 
 def body(
@@ -386,22 +1507,7 @@
     spare = width - channels
     blocks, block_width = rate_weight.shape[0], rate_weight.shape[1]
     piece = model // (parts * shards)
-    pairs = [[o * inner + i for i in range(inner)] for o in range(outer)]
     columns = [[o * inner + i for o in range(outer)] for i in range(inner)]
-
-    def gather_seq(x):
-        return lax.all_gather(x, "seq", axis=0, tiled=True)
-
-    def scatter_seq(x):
-        return lax.psum_scatter(x, "seq", scatter_dimension=0, tiled=True)
-
-    def gather_plane(x):
-        x = lax.all_gather(x, "shard", axis=0, tiled=True)
-        return lax.all_gather(x, "seq", axis=0, tiled=True, axis_index_groups=pairs)
-
-    def scatter_plane(x):
-        x = lax.psum_scatter(x, "seq", scatter_dimension=0, tiled=True, axis_index_groups=pairs)
-        return lax.psum_scatter(x, "shard", scatter_dimension=0, tiled=True)
 
     def own(weight, axis):
         part = lax.dynamic_slice_in_dim(weight, seq_at * channels, channels, axis)
@@ -409,13 +1515,6 @@
         pads[axis] = (0, spare)
         return jnp.pad(part, pads)
 
-    w_in = lax.all_gather(
-        jnp.concatenate([own(branch_weight, 1), own(input_weight, 1)], axis=1),
-        "shard",
-        axis=0,
-        tiled=True,
-    )
-    w_out = lax.all_gather(own(output_weight, 0), "shard", axis=1, tiled=True)
     params = jnp.pad(
         jnp.concatenate(
             [
@@ -430,113 +1529,92 @@
         ((0, 0), (0, spare)),
     )
 
-    def spread(weight):
-        out = jnp.zeros((width, width), BF16)
-        for j in range(blocks):
-            at = j * block_width
-            out = out.at[at : at + block_width, at : at + block_width].set(weight[j])
-        return out
-
-    gates = jnp.concatenate([spread(rate_weight), spread(entry_weight)], axis=1)
-
-    xs = tokens.reshape(rows, model).astype(F32)
-    scale1 = rms_parts(xs)
-    n1 = gather_seq((xs * scale1 * first_gain).astype(BF16))
-    proj = dot(n1, w_in)
-    z, h, v = scan_forward(parts, quarters, chunk, proj, params, gates)
-    mid = xs + scatter_seq(dot(z, w_out).astype(BF16)).astype(F32)
-    scale2 = rms_parts(mid)
-    n2 = gather_plane((mid * scale2 * second_gain).astype(BF16))
+    x = tokens.reshape(rows, model)
     cot = cotangent.reshape(rows, model)
-    cot_all = gather_plane(cot)
+    gain1, gain2 = first_gain[None], second_gain[None]
+    xs = x.astype(F32)
+    n1, w_in, w_out = opening(
+        (xs * row_rms(xs) * gain1).astype(BF16),
+        jnp.concatenate([own(branch_weight, 1), own(input_weight, 1)], axis=1),
+        own(output_weight, 0),
+        outer,
+        inner,
+        shards,
+        0,
+    )
+    n1, cot = lax.optimization_barrier((n1, cot))
+    beside = [(o * inner + i, o * inner + 1 - i) for o in range(outer) for i in range(inner)]
+    cot_beside = lax.ppermute(cot, "seq", beside)
+    w_in = w_in.reshape(model, 2 * width)
+    z, h, v, proj, gates = scan_forward(
+        quarters, chunk, n1, w_in, params, rate_weight, entry_weight
+    )
+    mid, n2, cot_all = middle(
+        z, w_out, x, gain2, cot, cot_beside, outer, inner, shards, 1
+    )
+    n2 = n2.reshape(inner * shards * rows, model)
+    cot_all = cot_all.reshape(inner * shards * rows, model)
     hidden = hidden_gate.shape[1] // inner
     wg = lax.dynamic_slice_in_dim(hidden_gate, inner_at * hidden, hidden, 1)
     wu = lax.dynamic_slice_in_dim(hidden_up, inner_at * hidden, hidden, 1)
     wd = lax.dynamic_slice_in_dim(hidden_down, inner_at * hidden, hidden, 0)
+
+    def sum_tokens(x):
+        return lax.psum_scatter(
+            x.astype(BF16), "seq", scatter_dimension=0, tiled=True, axis_index_groups=columns
+        ).reshape(inner * shards, piece, hidden)
+
     gm = dot(n2, wg)
     um = dot(n2, wu)
     act, slope = gelu_and_slope(gm)
     mm = (act * um).astype(BF16)
-    result = (mid + scatter_plane(dot(mm, wd).astype(BF16)).astype(F32)).astype(BF16)
+    down_sum = sum_tokens(dot(cot_all, mm, ((0,), (0,))))
     dmm = dot(cot_all, wd, ((1,), (1,)))
     dgm = (dmm * um * slope).astype(BF16)
     dum = (dmm * act).astype(BF16)
-    ffn_grads = jnp.concatenate(
-        [
-            dot(n2, dgm, ((0,), (0,))).astype(BF16),
-            dot(n2, dum, ((0,), (0,))).astype(BF16),
-            dot(cot_all, mm, ((0,), (0,))).astype(BF16),
-        ],
-        axis=1,
-    )
-    ffn_sum = lax.psum_scatter(
-        ffn_grads, "seq", scatter_dimension=0, tiled=True, axis_index_groups=columns
-    )
-    dn2 = scatter_plane(
-        (dot(dgm, wg, ((1,), (1,))) + dot(dum, wu, ((1,), (1,)))).astype(BF16)
-    ).astype(F32)
-    dmid = cot.astype(F32) + rms_back(mid, scale2, second_gain, dn2)
-    second_gain_grad = jnp.sum(dn2 * mid * scale2, axis=0)
-    dout = gather_seq(dmid.astype(BF16))
-    dz = dot(dout, w_out, ((1,), (1,)))
-    both, gate_grad, sums = scan_backward(
-        parts, quarters, chunk, dz, proj, h, v, params, gates
-    )
-    dn1 = scatter_seq(dot(both, w_in, ((1,), (1,))).astype(BF16)).astype(F32)
-    tokens_grad = (dmid + rms_back(xs, scale1, first_gain, dn1)).reshape(tokens.shape)
-    first_gain_grad = jnp.sum(dn1 * xs * scale1, axis=0)
-    mix_grads = jnp.concatenate(
-        [dot(n1, both, ((0,), (0,))).astype(BF16), dot(dout, z, ((0,), (0,))).astype(BF16)],
-        axis=1,
-    )
-    mix_cols = 3 * width
-    mix_sum = lax.psum_scatter(
-        mix_grads.reshape(parts, shards, piece, mix_cols).transpose(1, 0, 2, 3),
-        "shard",
-        scatter_dimension=0,
-        tiled=True,
-    )
-    mix = lax.all_to_all(
-        mix_sum.reshape(parts, piece, mix_cols), "seq", split_axis=0, concat_axis=0, tiled=True
-    )
-    mix = mix.reshape(parts, piece, 3, width)[..., :channels].astype(F32)
-    mix = mix.transpose(2, 1, 0, 3).reshape(3, piece, lru)
-    ffn = lax.all_to_all(
-        ffn_sum.reshape(inner, shards, piece, 3 * hidden),
-        "shard",
-        split_axis=1,
-        concat_axis=1,
-        tiled=True,
-    )
-    ffn = lax.all_to_all(
-        ffn, "seq", split_axis=0, concat_axis=0, tiled=True, axis_index_groups=pairs
-    )
-    ffn = ffn.reshape(inner, shards, piece, 3, hidden).transpose(3, 2, 1, 0, 4)
-    ffn = ffn.reshape(3, piece, inner * shards * hidden).astype(F32)
-    first_gain_sum, second_gain_sum = (
-        lax.psum_scatter(x, ("seq", "shard"), scatter_dimension=0, tiled=True)
-        for x in (first_gain_grad, second_gain_grad)
-    )
-    sums = sums.reshape(8, 8, width).sum(axis=1)[:, :channels]
-
-    def blocks_of(at):
-        return jnp.stack(
-            [
-                gate_grad[
-                    j * block_width : (j + 1) * block_width,
-                    at + j * block_width : at + (j + 1) * block_width,
-                ]
-                for j in range(blocks)
-            ]
-        )
-
-    sums, rate_grad, entry_grad = lax.psum((sums, blocks_of(0), blocks_of(width)), "shard")
+    gate_sum = sum_tokens(dot(n2, dgm, ((0,), (0,))))
+    up_terms = dot(n2, dum, ((0,), (0,)))
+    dmid, dout, result, gain2_grad = turn(
+        dgm, dum, mm, hidden_gate, hidden_up, hidden_down, mid, cot, gain2, outer, inner, shards, 2
+    )
+    dout, up_terms = lax.optimization_barrier((dout, up_terms.astype(BF16)))
+    up_sum = sum_tokens(up_terms)
+    both, small, sums = scan_backward(
+        quarters, chunk, blocks, block_width, dout, w_out, proj, h, v, params, gates
+    )
+    tokens_grad, mix, small, sums, gains, down_sum, gate_sum = closing(
+        both,
+        w_in,
+        z,
+        x,
+        dmid,
+        gain1,
+        gain2_grad,
+        small,
+        sums,
+        n1.reshape(parts * rows, model),
+        dout.reshape(parts * rows, model),
+        down_sum,
+        gate_sum,
+        outer,
+        inner,
+        shards,
+        3,
+    )
+    gains = gains[0]
+    up_sum = finish(up_sum, outer, inner, shards, 4)
+    gate_sum, up_sum, down_sum, branch_sum, input_sum, output_sum = unpack(
+        gate_sum, up_sum, down_sum, mix, inner, channels
+    )
+    sums = sums[:, :channels]
+    small = small.reshape(2, blocks, -1, small.shape[1])[:, :, :block_width, :block_width]
+    rate_grad, entry_grad = small[0], small[1]
     return (
         result.reshape(tokens.shape),
-        tokens_grad,
-        first_gain_sum,
-        mix[0],
-        mix[1],
+        tokens_grad.reshape(tokens.shape),
+        gains[:piece],
+        branch_sum,
+        input_sum,
         sums[4:8],
         sums[3],
         rate_grad,
@@ -544,11 +1622,11 @@
         entry_grad,
         sums[2],
         sums[0],
-        mix[2].T,
-        second_gain_sum,
-        ffn[0],
-        ffn[1],
-        ffn[2].T,
+        output_sum.T,
+        gains[piece : 2 * piece],
+        gate_sum,
+        up_sum,
+        down_sum.T,
     )
 
 

time: 1110 us -> 510 us (0.46); the launches traced: 1100 us -> 507 us
  waiting for transfers between devices: 751 us -> 0.09 us
  Pallas kernels: 33 us -> 434 us
  blocking collectives: 80.2 us -> 0 us
  local copies, waits for them, and re-layouts: 85.5 us -> 16.6 us
  matrix products: 96.4 us -> 37.1 us
  other arithmetic: 23.4 us -> 3.34 us
    pallas_call x0 -> x6, Pallas kernels: none -> 392 us  [the longest x1 128 us: turn(): pl.pallas_call(functools.partial(turn_kernel, outer, inner, shards), out_...]
    reduce_scatter x7 -> x3, waiting for transfers between devices: 347 us -> 0.04 us  [sum_tokens(): lax.psum_scatter(x.astype(BF16), 'seq', scatter_dimension=0, tiled=True,...]
    all_gather x8 -> x0, waiting for transfers between devices: 289 us -> none  [the longest x2 119 us: gather_seq(): return lax.all_gather(x, 'seq', axis=0, tiled=True)]
    unnamed x18 -> x3, waiting for transfers between devices: 98 us -> 0.05 us
    dot_general x15 -> x6, matrix products: 96.4 us -> 37.1 us  [dot(): lax.dot_general(left, right, (dims, ((), ())), preferred_element_type=F32)]
    unnamed x1 -> x0, blocking collectives: 38.5 us -> none
    all_to_all x1 -> x0, blocking collectives: 31 us -> none  [body(): lax.all_to_all(ffn_sum.reshape(inner, shards, piece, 3 * hidden), 'shard'...]
    slice x10 -> x2, local copies, waits for them, and re-layouts: 25.7 us -> 2.55 us  [the longest x1 1.41 us: body(): gains[piece:2 * piece]]
  transfers between devices with their start and end apart: 19 -> 4, of which waited for: 16 -> 0; matrix products, arithmetic and copies ran while one was open for 14% -> 3% of each run, Pallas kernels for 3% -> 57%
where the time goes in v3:
time: 510 us; the launch traced here: 507 us
  Pallas kernels  434 us (85%)
  matrix products  37.1 us (7%)
  local copies, waits for them, and re-layouts  16.6 us (3%)
  between operations  14.3 us (3%)
    pallas_call x1, Pallas kernels, turn(): pl.pallas_call(functools.partial(turn_kernel, outer, inner, shards), out_...  128 us
    pallas_call x1, Pallas kernels, closing(): pl.pallas_call(functools.partial(closing_kernel, outer, inner, shards), o...  117 us
    pallas_call x1, Pallas kernels, middle(): pl.pallas_call(functools.partial(middle_kernel, outer, inner, shards), ou...  77.4 us
    pallas_call x1, Pallas kernels, opening(): pl.pallas_call(functools.partial(opening_kernel, outer, inner, shards), o...  54.4 us
    dot_general x6, matrix products, dot(): lax.dot_general(left, right, (dims, ((), ())), preferred_element_type=F32)  37.1 us
    pallas_call x1, Pallas kernels, scan_backward(): pl.pallas_call(functools.partial(scan_backward_kernel, parts, quarters, c...  24.9 us
    pallas_call x1, Pallas kernels, scan_forward(): pl.pallas_call(functools.partial(scan_forward_kernel, parts, quarters, ch...  17.8 us
    pallas_call x1, Pallas kernels, finish(): pl.pallas_call(functools.partial(finish_kernel, outer, inner, shards), ou...  12.4 us
  transfers between devices with their start and end apart: 4, of which 0 were waited for; matrix products, arithmetic and copies ran while one was open for 3% of the time, Pallas kernels for 57%

profile of v3, /device:TPU:9, one launch (start us, length us, event | category | flops | bytes accessed | tf_op | source)
XLA Modules:
  0.0 507.5 jit_solution(9143206631401641156)
XLA Ops:
  7.3 1.4 multiply_reduce_fusion
  10.0 1.3 constant_dynamic-slice_fusion.1
  14.5 54.4 %opening.1 = (bf16[8,128,2048]{2,1,0:T(8,128)(2,1)}, bf16[4,512,768]{2,1,0:T(8,128)(2,1)}, bf16[4,384,512]{2,1,0:T(8,128)(2,1)}) custom-call(bf16[128,2048]{1,0:T(8,128)(2,1)} %multiply_convert_fusion.2.x_ref, bf16[512,768]{1,0:T(8,128)(2,1)} %fusion.17.wi_ref, bf16[384,512]{1,0:T(8,128)(2,1)} %pad.17.wo_ref), custom_call_target="tpu_custom_call" | custom-call | bytes 181500000 | tf_op jit(solution)/shard_map/opening/pallas_call | solution.py:689
  68.9 1.3 collective-permute-start
  70.5 17.8 %scan_forward.1 = (bf16[1024,384]{1,0:T(8,128)(2,1)S(1)}, f32[1024,384]{1,0:T(8,128)S(1)}, bf16[1024,384]{1,0:T(8,128)(2,1)S(1)}, f32[1024,768]{1,0:T(8,128)}, bf16[384,768]{1,0:T(8,128)(2,1)S(1)}) custom-call(bf16[8,128,2048]{2,1,0:T(8,128)(2,1)} %get-tuple-element.53.n1_ref, bf16[2048,768]{1,0:T(8,128)(2,1)} %bitcast.52, f32[8,384]{1,0:T(8,128)S(1)} %pad.18.par_ref, ...), custom_call_target="tpu_custom_call" | custom-call | bytes 59400000 | tf_op jit(solution)/shard_map/scan_forward/pallas_call | solution.py:218
  89.2 77.4 %middle.1 = (f32[128,2048]{1,0:T(8,128)S(1)}, bf16[8,128,2048]{2,1,0:T(8,128)(2,1)}, bf16[8,128,2048]{2,1,0:T(8,128)(2,1)}) custom-call(bf16[4,256,384]{2,1,0:T(8,128)(2,1)S(1)} %bitcast.47, bf16[4,384,512]{2,1,0:T(8,128)(2,1)S(1)} %copy-done.3, bf16[128,2048]{1,0:T(8,128)(2,1)S(1)} %bitcast.46, f32[1,2048]{1,0:T(1,128)S(1)} %bitcast.49, ...), custom_call_target="tpu_custom_call" | custom-call | bytes 264000000 | tf_op jit(solution)/shard_map/middle/pallas_call | solution.py:820
  166.7 6.6 %fusion.13 = f32[1024,768]{1,0:T(8,128)S(1)} fusion(bf16[1024,2048]{1,0:T(8,128)(2,1)} %bitcast.74, bf16[1536,2048]{1,0:T(8,128)(2,1)} %wd_ref.1, s32[]{:T(128)S(6)} %select_n.5), kind=kOutput, calls=%fused_computation.21 | convolution fusion | flops 3221225472 | bytes 10485764 | tf_op jit(solution)/shard_map/dot_general | solution.py:32
  173.4 5.1 %fusion.9 = f32[1024,768]{1,0:T(8,128)} fusion(bf16[1024,2048]{1,0:T(8,128)(2,1)S(1)} %bitcast.71, bf16[2048,1536]{1,0:T(8,128)(2,1)S(1)} %bitcast.55, s32[]{:T(128)S(6)} %select_n.5), kind=kOutput, calls=%fused_computation.17 | convolution fusion | flops 3221225472 | bytes 10485764 | tf_op jit(solution)/shard_map/dot_general | solution.py:32
  178.5 8.0 %multiply_convert_fusion = (bf16[1024,768]{1,0:T(8,128)(2,1)S(1)}, bf16[1024,768]{1,0:T(8,128)(2,1)}, bf16[1024,768]{1,0:T(8,128)(2,1)}) fusion(f32[1024,768]{1,0:T(8,128)} %fusion.9, f32[1024,768]{1,0:T(8,128)S(1)} %fusion.13, bf16[1024,2048]{1,0:T(8,128)(2,1)S(1)} %bitcast.72, bf16[2048,1536]{1,0:T(8,128)(2,1)S(1)} %bitcast.57, s32[]{:T(128)S(6)} %select_n.5), kind=kOutput, calls=%fused_computation.13 | convolution fusion | flops 3240886272 | bytes 18350084 | tf_op jit(solution)/shard_map/dot_general | solution.py:32
  186.6 5.0 convolution_convert_fusion.1
  191.6 1.3 copy-done.17
  193.0 7.4 %convolution_convert_fusion = bf16[2048,768]{1,0:T(8,128)(2,1)} fusion(bf16[1024,2048]{1,0:T(8,128)(2,1)} %bitcast.70, bf16[1024,768]{1,0:T(8,128)(2,1)S(1)} %copy-done.17), kind=kOutput, calls=%fused_computation.2 | convolution fusion | flops 3222798336 | bytes 8912896 | tf_op jit(solution)/shard_map/dot_general | solution.py:32
  200.7 127.6 %turn.1 = (f32[128,2048]{1,0:T(8,128)}, bf16[8,128,2048]{2,1,0:T(8,128)(2,1)}, bf16[128,2048]{1,0:T(8,128)(2,1)}, f32[1,2048]{1,0:T(1,128)}) custom-call(bf16[4,256,768]{2,1,0:T(8,128)(2,1)} %bitcast.60, bf16[4,256,768]{2,1,0:T(8,128)(2,1)} %bitcast.58, bf16[4,256,768]{2,1,0:T(8,128)(2,1)} %bitcast.59, bf16[2048,1536]{1,0:T(8,128)(2,1)} %wg_ref.1, ...), custom_call_target="tpu_custom_call" | custom-call | bytes 396000000 | tf_op jit(solution)/shard_map/turn/pallas_call | solution.py:1033
  328.3 4.9 convolution_convert_fusion.2
  333.3 24.9 %scan_backward.1 = (bf16[1024,768]{1,0:T(8,128)(2,1)}, f32[704,256]{1,0:T(8,128)}, f32[8,384]{1,0:T(8,128)}) custom-call(bf16[8,128,2048]{2,1,0:T(8,128)(2,1)} %get-tuple-element.63.dout_ref, bf16[4,384,512]{2,1,0:T(8,128)(2,1)} %get-tuple-element.56.wo_ref, f32[1024,768]{1,0:T(8,128)} %get-tuple-element.64.proj_ref, f32[1024,384]{1,0:T(8,128)} %copy-done.6, ...), custom_call_target="tpu_custom_call" | custom-call | bytes 69300000 | tf_op jit(solution)/shard_map/scan_backward/pallas_call | solution.py:431
  358.2 116.6 %closing.1 = (f32[128,2048]{1,0:T(8,128)}, bf16[8,64,1152]{2,1,0:T(8,128)(2,1)}, f32[704,256]{1,0:T(8,128)}, f32[8,384]{1,0:T(8,128)}, f32[1,128]{1,0:T(1,128)},...) custom-call(bf16[1024,768]{1,0:T(8,128)(2,1)} %get-tuple-element.68.both_ref, bf16[2048,768]{1,0:T(8,128)(2,1)} %bitcast.53, ...), custom_call_target="tpu_custom_call" | custom-call | bytes 264000000 | tf_op jit(solution)/shard_map/closing/pallas_call | solution.py:1366
  474.8 1.3 slice.44
  476.1 1.5 slice_reduce_fusion
  477.6 12.4 %finish.1.up_ref = bf16[8,64,768]{2,1,0:T(8,128)(2,1)} custom-call(bf16[8,64,768]{2,1,0:T(8,128)(2,1)} %bitcast.62), custom_call_target="tpu_custom_call" | custom-call | bytes 39600000 | tf_op jit(solution)/shard_map/finish/pallas_call | solution.py:1431
  490.1 1.4 slice_bitcast_fusion
  491.5 1.1 fusion.21
  492.6 1.0 copy.48
  494.6 1.3 copy-done.11
  495.9 3.2 unpack.1
  (101 shorter events, 8.7 us)
Async XLA Ops:
  7.2 351.0 %reduce-scatter.4.cloned.1.call-start = ((), (), s32[]{:S(2)}) async-start(), calls=%async_computation.3 | async-start | bytes 3932160 | tf_op jit(solution)/shard_map/reduce_scatter | solution.py:1563
  11.3 59.0 %copy-start.25 = (f32[342]{0:T(512)S(1)}, f32[342]{0:T(512)}, u32[]{:S(2)}) copy-start(f32[342]{0:T(512)} %param.22) | copy-start | bytes 4108
  11.3 58.9 %copy-start.26 = (f32[342]{0:T(512)S(1)}, f32[342]{0:T(512)}, u32[]{:S(2)}) copy-start(f32[342]{0:T(512)} %param.24) | copy-start | bytes 4108
  11.3 58.9 %copy-start.27 = (f32[342]{0:T(512)S(1)}, f32[342]{0:T(512)}, u32[]{:S(2)}) copy-start(f32[342]{0:T(512)} %param.26) | copy-start | bytes 4108
  11.3 59.0 %copy-start.28 = (f32[342]{0:T(512)S(1)}, f32[342]{0:T(512)}, u32[]{:S(2)}) copy-start(f32[342]{0:T(512)} %param.27) | copy-start | bytes 4108
  11.3 59.0 %copy-start.21 = (bf16[2,171,171]{2,0,1:T(2,128)(2,1)S(1)}, bf16[2,171,171]{2,0,1:T(2,128)(2,1)}, u32[]{:S(2)}) copy-start(bf16[2,171,171]{2,0,1:T(2,128)(2,1)} %param.23) | copy-start | bytes 350896
  11.6 58.8 %copy-start.22 = (bf16[2,171,171]{2,0,1:T(2,128)(2,1)S(1)}, bf16[2,171,171]{2,0,1:T(2,128)(2,1)}, u32[]{:S(2)}) copy-start(bf16[2,171,171]{2,0,1:T(2,128)(2,1)} %param.25) | copy-start | bytes 350896
  11.6 58.8 %copy-start.24 = (bf16[4,342]{1,0:T(4,128)(2,1)S(1)}, bf16[4,342]{1,0:T(4,128)(2,1)}, u32[]{:S(2)}) copy-start(bf16[4,342]{1,0:T(4,128)(2,1)} %param.21) | copy-start | bytes 8212
  68.9 20.2 %collective-permute-start = (bf16[128,2048]{1,0:T(8,128)(2,1)}, bf16[128,2048]{1,0:T(8,128)(2,1)}, u32[]{:S(2)}, u32[]{:S(2)}) collective-permute-start(bf16[128,2048]{1,0:T(8,128)(2,1)} %bitcast.1.cot_ref), channel_id=1, source_target_pairs={{0,4},{4,0},{8,12},{12,8},{16,20},{20,16},{24,28},{28,24},{1,5},{5... | collective-permute-start | bytes 1572872 | tf_op jit(solution)/shard_map/ppermute | solution.py:1547
  70.4 17.9 %copy-start.13 = (f32[8,384]{1,0:T(8,128)}, f32[8,384]{1,0:T(8,128)S(1)}, u32[]{:S(2)}) copy-start(f32[8,384]{1,0:T(8,128)S(1)} %pad.18.par_ref) | copy-start | bytes 36868
  70.4 18.7 %copy-start.3 = (bf16[4,384,512]{2,1,0:T(8,128)(2,1)S(1)}, bf16[4,384,512]{2,1,0:T(8,128)(2,1)}, u32[]{:S(2)}) copy-start(bf16[4,384,512]{2,1,0:T(8,128)(2,1)} %get-tuple-element.56.wo_ref) | copy-start | bytes 4718596
  70.4 18.7 %copy-start.14 = (f32[2048]{0:T(1024)S(1)}, f32[2048]{0:T(1024)}, u32[]{:S(2)}) copy-start(f32[2048]{0:T(1024)} %param.29) | copy-start | bytes 24580
  89.1 84.2 %copy-start.5 = (bf16[1024,384]{1,0:T(8,128)(2,1)}, bf16[1024,384]{1,0:T(8,128)(2,1)S(1)}, u32[]{:S(2)}) copy-start(bf16[1024,384]{1,0:T(8,128)(2,1)S(1)} %get-tuple-element.55.z_ref) | copy-start | bytes 2359300
  89.1 84.2 %copy-start.6 = (f32[1024,384]{1,0:T(8,128)}, f32[1024,384]{1,0:T(8,128)S(1)}, u32[]{:S(2)}) copy-start(f32[1024,384]{1,0:T(8,128)S(1)} %get-tuple-element.65.h_ref) | copy-start | bytes 4718596
  89.1 84.2 %copy-start.9 = (bf16[1024,384]{1,0:T(8,128)(2,1)}, bf16[1024,384]{1,0:T(8,128)(2,1)S(1)}, u32[]{:S(2)}) copy-start(bf16[1024,384]{1,0:T(8,128)(2,1)S(1)} %get-tuple-element.66.v_ref) | copy-start | bytes 2359300
  89.2 84.2 %slice-start = ((s8[6291456]{0:T(1024)(128)(4,1)}), s8[4194304]{0:T(1024)(128)(4,1)S(1)}, s32[]{:S(2)}) async-start(s8[6291456]{0:T(1024)(128)(4,1)} %bitcast.54), calls=%async_computation.6 | async-start | bytes 8388608
  166.6 6.7 %slice-start.1 = ((s8[6291456]{0:T(1024)(128)(4,1)}), s8[2097152]{0:T(1024)(128)(4,1)S(1)}, s32[]{:S(2)}) async-start(s8[6291456]{0:T(1024)(128)(4,1)} %bitcast.54), calls=%async_computation.7 | async-start | bytes 4194304
  166.7 11.9 %slice-start.2 = ((s8[6291456]{0:T(1024)(128)(4,1)}), s8[4194304]{0:T(1024)(128)(4,1)S(1)}, s32[]{:S(2)}) async-start(s8[6291456]{0:T(1024)(128)(4,1)} %bitcast.56), calls=%async_computation.8 | async-start | bytes 8388608
  178.5 8.0 %copy-start.31 = (bf16[8,128,2048]{2,1,0:T(8,128)(2,1)S(1)}, bf16[8,128,2048]{2,1,0:T(8,128)(2,1)}, u32[]{:S(2)}) copy-start(bf16[8,128,2048]{2,1,0:T(8,128)(2,1)} %get-tuple-element.58) | copy-start | bytes 12582916
  191.6 166.6 %reduce-scatter.6.cloned.1.call-start = ((), (), s32[]{:S(2)}) async-start(), calls=%async_computation.4 | async-start | bytes 3932160 | tf_op jit(solution)/shard_map/reduce_scatter | solution.py:1563
  200.4 277.2 %reduce-scatter.8.cloned.1.call-start = ((), (), s32[]{:S(2)}) async-start(), calls=%async_computation.5 | async-start | bytes 3932160 | tf_op jit(solution)/shard_map/reduce_scatter | solution.py:1563
  200.7 127.6 %copy-start.15 = (bf16[1024,768]{1,0:T(8,128)(2,1)S(1)}, bf16[1024,768]{1,0:T(8,128)(2,1)}, u32[]{:S(2)}) copy-start(bf16[1024,768]{1,0:T(8,128)(2,1)} %get-tuple-element.110) | copy-start | bytes 4718596
  200.7 127.6 %copy-start.30 = (bf16[8,128,2048]{2,1,0:T(8,128)(2,1)S(1)}, bf16[8,128,2048]{2,1,0:T(8,128)(2,1)}, u32[]{:S(2)}) copy-start(bf16[8,128,2048]{2,1,0:T(8,128)(2,1)} %get-tuple-element.59) | copy-start | bytes 12582916
  477.6 21.6 %copy-start.20 = (bf16[128,2048]{1,0:T(8,128)(2,1)S(1)}, bf16[128,2048]{1,0:T(8,128)(2,1)}, u32[]{:S(2)}) copy-start(bf16[128,2048]{1,0:T(8,128)(2,1)} %get-tuple-element.61) | copy-start | bytes 1572868
  (16 other events, 65.8 us)
Sparse Core Ops, SparseCore 0:
  191.7 61.4 reduce-scatter.3
  255.5 81.0 reduce-scatter.5
  338.9 70.9 reduce-scatter.7

commit v4 on v3

--- a/solution.py
+++ b/solution.py
@@ -241,237 +241,6 @@
     )(n1, w_in, params, rate, entry)
 
 
-def scan_backward_kernel(
-    parts,
-    quarters,
-    chunk,
-    blocks,
-    block_width,
-    dout_ref,
-    wo_ref,
-    proj_ref,
-    h_ref,
-    v_ref,
-    par_ref,
-    gates_ref,
-    both_ref,
-    blocks_ref,
-    totals_ref,
-    dout_s,
-    dz_s,
-    sems,
-    sums_ref,
-    gate_grad_ref,
-    a_s,
-    g_s,
-    t_s,
-    h_pad,
-    pre_s,
-    dpre_s,
-    dv_s,
-    u_pad,
-):
-    length, width = h_ref.shape
-    seg = length // SEGMENTS
-    chunks = length // chunk
-
-    def place(c):
-        q = c // parts
-        s = c - q * parts
-        return pl.multiple_of((s * quarters + q) * chunk, chunk)
-
-    def time_of(c):
-        return pl.multiple_of(c * chunk, chunk)
-
-    span = quarters * chunk
-
-    def load(p):
-        return pltpu.make_async_copy(
-            dout_ref.at[p], dout_s.at[pl.ds(pl.multiple_of(p * span, span), span)], sems.at[p]
-        )
-
-    for p in range(parts):
-        load(p).start()
-
-    def back_project(k, carry):
-        load(2 * k).wait()
-        load(2 * k + 1).wait()
-        at = pl.ds(pl.multiple_of(k * 2 * span, 2 * span), 2 * span)
-        depth = wo_ref.shape[2]
-        total = dot(dout_s[at, 0:depth], wo_ref[0], ((1,), (1,)))
-        for p in range(1, wo_ref.shape[0]):
-            lanes = slice(p * depth, (p + 1) * depth)
-            total = total + dot(dout_s[at, lanes], wo_ref[p], ((1,), (1,)))
-        dz_s[at, :] = total
-        return carry
-
-    lax.fori_loop(0, parts // 2, back_project, 0)
-    log_scale = -DECAY_SCALE * softplus(-par_ref[DECAY : DECAY + 1, :])
-    bias = jnp.concatenate(
-        [par_ref[RATE_B : RATE_B + 1, :], par_ref[ENTRY_B : ENTRY_B + 1, :]], axis=1
-    )
-    zeros8 = jnp.zeros((8, width), F32)
-    put(a_s, pl.ds(length, 8), zeros8)
-    h_pad[0:8, :] = zeros8
-    u_pad[0:8, :] = zeros8
-    dv_s[pl.ds(length, 8), :] = zeros8
-
-    def first(c, carry):
-        rows = pl.ds(time_of(c), chunk)
-        later = pl.ds(pl.multiple_of(time_of(c) + 8, 8), chunk)
-        there = pl.ds(place(c), chunk)
-        h = h_ref[rows, :]
-        h_pad[later, :] = h
-        u_pad[later, :] = proj_ref[there, width : 2 * width].astype(BF16).astype(F32)
-        y, slope = gelu_and_slope(proj_ref[there, 0:width])
-        dz = dz_s[there, :]
-        put(g_s, rows, (dz * y).astype(BF16).astype(F32))
-        both_ref[there, 0:width] = (dz * h.astype(BF16).astype(F32) * slope).astype(BF16)
-        pre = dot(v_ref[rows, :], gates_ref[...]) + bias
-        pre_s[rows, :] = pre
-        put(a_s, rows, jnp.exp(sigmoid(pre[:, :width]) * log_scale))
-        return carry
-
-    lax.fori_loop(0, chunks, first, 0)
-
-    def load(g, i):
-        return (
-            a_s[g, pl.ds(i + 1, SEGMENTS, stride=seg), :],
-            g_s[g, pl.ds(i, SEGMENTS, stride=seg), :],
-        )
-
-    def store(g, i, state, total):
-        g_s[g, pl.ds(i, SEGMENTS, stride=seg), :] = state
-        t_s[g, pl.ds(i, SEGMENTS, stride=seg), :] = total
-
-    groups = width // LANES
-    start = (jnp.zeros((SEGMENTS, LANES), F32), jnp.ones((SEGMENTS, LANES), F32))
-    ends = lax.fori_loop(
-        0,
-        seg,
-        strided_scan(lambda k: seg - 1 - k, groups, load, store),
-        (start,) * groups,
-        unroll=8,
-    )
-    firsts = jnp.concatenate([e[0] for e in ends], axis=1)
-    totals = jnp.concatenate([e[1] for e in ends], axis=1)
-    carries = [None] * SEGMENTS
-    carries[SEGMENTS - 1] = jnp.zeros((1, width), F32)
-    for j in range(SEGMENTS - 2, -1, -1):
-        carries[j] = totals[j + 1 : j + 2] * carries[j + 1] + firsts[j + 1 : j + 2]
-
-    def fold(values):
-        return jnp.sum(values.reshape(chunk // 8, 8, values.shape[1]), axis=0)
-
-    sums_ref[...] = jnp.zeros(sums_ref.shape, F32)
-
-    for j in range(SEGMENTS):
-        per = seg // chunk
-
-        def middle(k, carry, j=j, per=per):
-            c = j * per + k
-            rows = pl.ds(time_of(c), chunk)
-            g = take(g_s, rows) + take(t_s, rows) * carries[j]
-            before = h_pad[pl.ds(time_of(c), chunk + 8), :][7 : 7 + chunk]
-            v = v_ref[rows, :].astype(F32)
-            r, e, a, room, m = gate_values(pre_s[rows, :], log_scale, width)
-            gv = g * v
-            held = jnp.where(room > MULT_FLOOR, gv * e * a / m, 0.0)
-            ta = (g * before - held) * a * r
-            drpre = (ta * (log_scale * (1.0 - r))).astype(BF16)
-            depre = (gv * m * e * (1.0 - e)).astype(BF16)
-            dpre_s[rows, 0:width] = drpre
-            dpre_s[rows, width : 2 * width] = depre
-            sums_ref[0:8, :] += fold(ta)
-            sums_ref[8:16, :] += fold(drpre.astype(F32))
-            sums_ref[16:24, :] += fold(depre.astype(F32))
-            dv = g * m * e + dot(dpre_s[rows, :], gates_ref[...], ((1,), (1,)))
-            dv_s[rows, :] = dv
-            sums_ref[24:32, :] += fold(dv)
-            wide = u_pad[pl.ds(time_of(c), chunk + 8), :]
-            for tap in range(4):
-                at = 32 + 8 * tap
-                sums_ref[at : at + 8, :] += fold(dv * wide[8 - tap : 8 - tap + chunk])
-            return carry
-
-        lax.fori_loop(0, per, middle, 0)
-    sums_ref[0:8, :] = sums_ref[0:8, :] * (
-        DECAY_SCALE * sigmoid(-par_ref[DECAY : DECAY + 1, :])
-    )
-
-    def last(c, carry):
-        wide = dv_s[pl.ds(time_of(c), chunk + 8), :]
-        du = par_ref[0:1, :] * wide[0:chunk]
-        for tap in range(1, 4):
-            du = du + par_ref[tap : tap + 1, :] * wide[tap : tap + chunk]
-        both_ref[pl.ds(place(c), chunk), width : 2 * width] = du.astype(BF16)
-        return carry
-
-    lax.fori_loop(0, chunks, last, 0)
-    gate_grad_ref[...] = dot(v_ref[...], dpre_s[...], ((0,), (0,)))
-    blocks_ref[...] = jnp.zeros(blocks_ref.shape, F32)
-    tall = blocks_ref.shape[0] // (2 * blocks)
-    for gate in range(2):
-        for j in range(blocks):
-            at, lanes = (gate * blocks + j) * tall, gate * width + j * block_width
-            rows = slice(j * block_width, (j + 1) * block_width)
-            blocks_ref[at : at + block_width, :block_width] = gate_grad_ref[
-                rows, lanes : lanes + block_width
-            ]
-    for k in range(8):
-        totals_ref[k : k + 1, :] = jnp.sum(sums_ref[8 * k : 8 * k + 8, :], axis=0, keepdims=True)
-
-
-def scan_backward(
-    quarters, chunk, blocks, block_width, dout, w_out, proj, h, v, params, gates
-):
-    parts = dout.shape[0]
-    length, width = h.shape
-    tall, wide = -(-block_width // 8) * 8, -(-block_width // LANES) * LANES
-    return pl.pallas_call(
-        functools.partial(scan_backward_kernel, parts, quarters, chunk, blocks, block_width),
-        out_shape=(
-            jax.ShapeDtypeStruct((length, 2 * width), BF16),
-            jax.ShapeDtypeStruct((2 * blocks * tall, wide), F32),
-            jax.ShapeDtypeStruct((8, width), F32),
-        ),
-        in_specs=[ANY] + [IN_VMEM] * 6,
-        out_specs=[IN_VMEM] * 3,
-        scratch_shapes=[
-            pltpu.VMEM((length, dout.shape[2]), BF16),
-            pltpu.VMEM((length, width), F32),
-            DMA((parts,)),
-            pltpu.VMEM((64, width), F32),
-            pltpu.VMEM((width, 2 * width), F32),
-            pltpu.VMEM((width // LANES, length + 8, LANES), F32),
-            pltpu.VMEM((width // LANES, length, LANES), F32),
-            pltpu.VMEM((width // LANES, length, LANES), F32),
-            pltpu.VMEM((length + 8, width), F32),
-            pltpu.VMEM((length, 2 * width), F32),
-            pltpu.VMEM((length, 2 * width), BF16),
-            pltpu.VMEM((length + 8, width), F32),
-            pltpu.VMEM((length + 8, width), F32),
-        ],
-        compiler_params=pltpu.CompilerParams(vmem_limit_bytes=56 * 2**20),
-        cost_estimate=cost(21),
-        name="scan_backward",
-    )(dout, w_out, proj, h, v, params, gates)
-
-
-def remote(src, dst, send, recv, to):
-    return pltpu.make_async_remote_copy(
-        src_ref=src, dst_ref=dst, send_sem=send, recv_sem=recv, device_id=to, device_id_type=MESH
-    )
-
-
-def add_rows(rows, fn):
-    def one(k, carry):
-        fn(pl.ds(pl.multiple_of(k * 16, 16), 16))
-        return carry
-
-    lax.fori_loop(0, rows // 16, one, 0)
-
-
 class Place:
     def __init__(self, outer, inner, shards):
         self.outer, self.inner, self.shards = outer, inner, shards
@@ -634,6 +403,83 @@
         for d in range(at.outer):
             self.cross(d).wait_send()
         send.finish()
+
+
+class LineReduce:
+    def __init__(self, at, own, land, up, down):
+        self.at, self.own, self.land, self.up, self.down = at, own, land, up, down
+
+    def order(self, o0):
+        return sorted(range(self.at.outer), key=lambda d: (-abs(d - o0), d))
+
+    def ascent(self, d):
+        at = self.at
+        return remote(
+            self.own.at[d], self.land.at[d], self.up.at[0, d], self.up.at[1, d], at.above
+        )
+
+    def descent(self, o0, d):
+        slot = d if d != o0 - 1 else self.at.outer
+        return remote(
+            self.own.at[d], self.land.at[slot], self.down.at[0, d], self.down.at[1, d], self.at.below
+        )
+
+    def early(self, n, d, limit):
+        at = self.at
+        inside = n < limit
+        last = at.outer - 1
+        pl.when(jnp.logical_and(at.o == 0, inside))(lambda: self.ascent(d).start())
+        far = remote(
+            self.own.at[d], self.land.at[d], self.down.at[0, d], self.down.at[1, d], at.below
+        )
+        pl.when(jnp.logical_and(at.o == last, inside))(lambda: far.start())
+
+    def push(self, o0, d):
+        if d > o0:
+            self.ascent(d).start()
+        if d < o0:
+            self.descent(o0, d).start()
+
+    def absorb(self, o0, d):
+        terms = []
+        if d >= o0 > 0:
+            self.ascent(d).wait_recv()
+            terms.append(self.land.at[d])
+        if d <= o0 < self.at.outer - 1:
+            slot = d if d < o0 else self.at.outer
+            self.descent(o0 + 1, d).wait_recv()
+            terms.append(self.land.at[slot])
+        mine = self.own.at[d]
+
+        def add(rows):
+            total = mine[rows, :].astype(F32)
+            for term in terms:
+                total = total + term[rows, :].astype(F32)
+            mine[rows, :] = total.astype(BF16)
+
+        if terms:
+            add_rows(mine.shape[0], add)
+
+    def step(self, o0, n):
+        d = self.order(o0)[n]
+        self.absorb(o0, d)
+        self.push(o0, d)
+
+    def finish(self, o0):
+        for d in range(self.at.outer):
+            if d > o0:
+                self.ascent(d).wait_send()
+            if d < o0:
+                self.descent(o0, d).wait_send()
+
+
+def first_half(hidden):
+    return -(-(hidden // 2) // LANES) * LANES
+
+
+def line_reduce_scratch(outer, rows, cols):
+    blocks = [pltpu.VMEM((outer, rows, cols), BF16), pltpu.VMEM((outer + 1, rows, cols), BF16)]
+    return blocks, [DMA((2, outer))] * 2
 
 
 def line_sum_scratch(outer, rows, cols):
@@ -872,11 +718,11 @@
             self.at.near(q, 0, back)[0],
         )
 
-    def combine(self):
+    def combine(self, own=None):
         def one(k, carry):
             q = self.at.chips - 1 - k
             self.to_sibling(q).wait_recv()
-            mine = self.block(q, 0)
+            mine = self.block(q, 0) if own is None else own.at[q]
 
             def add(rows):
                 total = mine[rows, :].astype(F32) + self.near_in[self.n, q, rows, :].astype(F32)
@@ -889,9 +735,10 @@
         lax.fori_loop(0, self.at.chips - 1, one, 0)
         self.to_sibling(0).wait_recv()
 
-    def total(self, rows):
+    def total(self, rows, own=None):
         n = self.n
-        value = self.block(0, 0)[rows, :].astype(F32) + self.near_in[n, 0, rows, :].astype(F32)
+        mine = self.block(0, 0) if own is None else own.at[0]
+        value = mine[rows, :].astype(F32) + self.near_in[n, 0, rows, :].astype(F32)
         for q in range(1, self.at.chips):
             value = value + self.far_in[n, q, rows, :].astype(F32)
         return value
@@ -914,16 +761,22 @@
     dgm_ref,
     dum_ref,
     mm_ref,
+    mid_ref,
+    cot_ref,
+    gain_ref,
     wg_ref,
     wu_ref,
     wd_ref,
-    mid_ref,
-    cot_ref,
-    gain_ref,
+    n2_ref,
+    cots_ref,
     dmid_ref,
+    gain_grad_ref,
     dout_ref,
-    result_ref,
-    gain_grad_ref,
+    q_ref,
+    down_ref,
+    gate_ref,
+    rest_ref,
+    up_ref,
     p_s,
     q_s,
     dout_s,
@@ -931,62 +784,125 @@
     wg_s,
     wu_s,
     wd_s,
+    n2_s,
+    cots_s,
+    u_s,
+    r_s,
     near_in,
     far_in,
     far_out,
+    down_own,
+    down_land,
+    gate_own,
+    gate_land,
     near,
     far,
     across,
     up,
-    down,
+    low,
+    down_up,
+    down_low,
+    gate_up,
+    gate_low,
     local,
+    q_sem,
+    u_sem,
+    r_sem,
 ):
     at = Place(outer, inner, shards)
     model, hidden = wg_s.shape
+    tile = min(512, model)
+    pair = p_s.shape[1]
+    span = model // outer
     own = pl.ds(pl.multiple_of(at.i * hidden, hidden), hidden)
     load = [
-        pltpu.make_async_copy(wg_ref.at[:, own], wg_s, local.at[1]),
-        pltpu.make_async_copy(wu_ref.at[:, own], wu_s, local.at[2]),
-        pltpu.make_async_copy(wd_ref.at[own, :], wd_s, local.at[3]),
+        pltpu.make_async_copy(cots_ref, cots_s, local.at[1]),
+        pltpu.make_async_copy(wg_ref.at[:, own], wg_s, local.at[2]),
+        pltpu.make_async_copy(wu_ref.at[:, own], wu_s, local.at[3]),
+        pltpu.make_async_copy(n2_ref, n2_s, local.at[4]),
+        pltpu.make_async_copy(wd_ref.at[own, :], wd_s, local.at[5]),
     ]
     for copy in load:
         copy.start()
-    tile = min(512, model)
     greet_with_line(at, [at.sibling] + [at.near(q)[0] for q in range(1, at.chips)])
     grad = PlaneSum(at, 0, p_s, near_in, far_in, far_out, near, far)
-    value = PlaneSum(at, 1, q_s, near_in, far_in, far_out, near, far)
+    down = LineReduce(at, down_own, down_land, down_up, down_low)
+    gate = LineReduce(at, gate_own, gate_land, gate_up, gate_low)
+
+    def columns(d):
+        return pl.ds(pl.multiple_of(d * span, span), span)
 
     load[0].wait()
+
+    def down_grad(n, carry):
+        d = at.far_first(n)
+        down_own[d] = dot(cots_s[:, columns(d)], mm_ref[...], ((0,), (0,))).astype(BF16)
+        down.early(n, d, outer - 2)
+        return carry
+
+    lax.fori_loop(0, outer, down_grad, 0)
     load[1].wait()
+    load[2].wait()
 
     def back(k, carry):
         q = at.chips - 1 - k
         i, y = at.chip(q)
         c = i * at.ys + y
+        rows = pl.ds(pl.multiple_of(c * pair, pair), pair)
         for lane in range(0, model, tile):
             lanes = slice(lane, lane + tile)
-            block = dot(dgm_ref[c], wg_s[lanes, :], ((1,), (1,)))
-            block = block + dot(dum_ref[c], wu_s[lanes, :], ((1,), (1,)))
+            block = dot(dgm_ref[rows, :], wg_s[lanes, :], ((1,), (1,)))
+            block = block + dot(dum_ref[rows, :], wu_s[lanes, :], ((1,), (1,)))
             p_s[c, :, lanes] = block.astype(BF16)
         grad.to_sibling(q).start()
         return carry
 
     lax.fori_loop(0, at.chips, back, 0)
     grad.combine()
-
-    load[2].wait()
-
-    def ahead(k, carry):
-        q = at.chips - 1 - k
-        i, y = at.chip(q)
-        c = i * at.ys + y
+    load[3].wait()
+
+    cut = gate_own.shape[2]
+
+    def keep_r(n):
+        slot = lax.rem(n, 2)
+        return pltpu.make_async_copy(r_s.at[slot], rest_ref.at[at.far_first(n)], r_sem.at[slot])
+
+    def gate_grad(n, carry):
+        d = at.far_first(n)
+        pl.when(n >= 2)(lambda: keep_r(n - 2).wait())
+        block = dot(n2_s[:, columns(d)], dgm_ref[...], ((0,), (0,))).astype(BF16)
+        gate_own[d] = block[:, :cut]
+        r_s[lax.rem(n, 2)] = block[:, cut:]
+        keep_r(n).start()
+        return carry
+
+    lax.fori_loop(0, outer, gate_grad, 0)
+    for n in range(max(outer - 2, 0), outer):
+        keep_r(n).wait()
+
+    def first_down(o0):
+        if 0 < o0 < outer - 1:
+            down.step(o0, 0)
+
+    at.branches(first_down)
+    load[4].wait()
+
+    def keep_q(c):
+        slot = lax.rem(c, 2)
+        return pltpu.make_async_copy(q_s.at[slot], q_ref.at[c], q_sem.at[slot])
+
+    def ahead(c, carry):
+        rows = pl.ds(pl.multiple_of(c * pair, pair), pair)
+        pl.when(c >= 2)(lambda: keep_q(c - 2).wait())
         for lane in range(0, model, tile):
             lanes = slice(lane, lane + tile)
-            q_s[c, :, lanes] = dot(mm_ref[c], wd_s[:, lanes]).astype(BF16)
-        value.to_sibling(q).start()
+            q_s[lax.rem(c, 2), :, lanes] = dot(mm_ref[rows, :], wd_s[:, lanes]).astype(BF16)
+        keep_q(c).start()
         return carry
 
     lax.fori_loop(0, at.chips, ahead, 0)
+    for c in range(max(at.chips - 2, 0), at.chips):
+        keep_q(c).wait()
     gain_s[...] = jnp.zeros(gain_s.shape, F32)
     grad.arrive()
 
@@ -1004,86 +920,470 @@
     keep = pltpu.make_async_copy(dout_s, dout_ref.at[at.s], local.at[0])
     keep.start()
 
+    def keep_u(n):
+        slot = lax.rem(n, 2)
+        return pltpu.make_async_copy(u_s.at[slot], up_ref.at[at.far_first(n)], u_sem.at[slot])
+
+    def up_grad(n, carry):
+        pl.when(n >= 2)(lambda: keep_u(n - 2).wait())
+        u_s[lax.rem(n, 2)] = dot(
+            n2_s[:, columns(at.far_first(n))], dum_ref[...], ((0,), (0,))
+        ).astype(BF16)
+        keep_u(n).start()
+        return carry
+
     def branch(o0):
+        ends = o0 in (0, outer - 1)
+
         def between(k):
             if k == 0:
-                value.combine()
-
-        line_gather(at, o0, dout_s, dout_ref, across, up, down, between)
+                if ends:
+                    down.push(o0, down.order(o0)[outer - 2])
+                    for d in gate.order(o0)[:-1]:
+                        gate.push(o0, d)
+                else:
+                    for n in range(1, outer - 1):
+                        down.step(o0, n)
+                lax.fori_loop(0, outer, up_grad, 0)
+            if k == outer - 1:
+                down.absorb(o0, o0)
+
+        line_gather(at, o0, dout_s, dout_ref, across, up, low, between)
+        if not ends:
+            for n in range(outer - 1):
+                gate.step(o0, n)
+        gate.absorb(o0, o0)
+        down.finish(o0)
+        gate.finish(o0)
 
     at.branches(branch)
-    value.arrive()
-
-    def output(rows):
-        result_ref[rows, :] = (mid_ref[rows, :] + value.total(rows)).astype(BF16)
-
-    add_rows(result_ref.shape[0], output)
+    last = [
+        pltpu.make_async_copy(down_own.at[at.o], down_ref, local.at[1]),
+        pltpu.make_async_copy(gate_own.at[at.o], gate_ref, local.at[2]),
+    ]
+    for copy in last:
+        copy.start()
+    for n in range(max(outer - 2, 0), outer):
+        keep_u(n).wait()
     grad.finish()
-    value.finish()
     keep.wait()
-
-
-def turn(dgm, dum, mm, wg, wu, wd, mid, cot, gain, outer, inner, shards, collective):
+    for copy in last:
+        copy.wait()
+
+
+def turn(
+    dgm, dum, mm, mid, cot, gain, wg, wu, wd, n2, cots, outer, inner, shards, collective
+):
     rows, cols = mid.shape
-    hidden = dgm.shape[1]
-    chips = inner * shards // 2
-    buffers = pltpu.VMEM((2, chips, rows, cols), BF16)
-    partial = pltpu.VMEM((chips, 2 * rows, cols), BF16)
-    dgm, dum, mm = (x.reshape(chips, 2 * rows, hidden) for x in (dgm, dum, mm))
+    tokens, hidden = dgm.shape
+    chips, span = inner * shards // 2, cols // outer
+    buffers = pltpu.VMEM((1, chips, rows, cols), BF16)
+    cut = first_half(hidden)
+    down_vmem, reduce_sems = line_reduce_scratch(outer, span, hidden)
+    gate_vmem, _ = line_reduce_scratch(outer, span, cut)
     return pl.pallas_call(
         functools.partial(turn_kernel, outer, inner, shards),
         out_shape=(
             jax.ShapeDtypeStruct((rows, cols), F32),
+            jax.ShapeDtypeStruct((1, cols), F32),
             jax.ShapeDtypeStruct((outer * inner, rows, cols), BF16),
-            jax.ShapeDtypeStruct((rows, cols), BF16),
-            jax.ShapeDtypeStruct((1, cols), F32),
+            jax.ShapeDtypeStruct((chips, 2 * rows, cols), BF16),
+            jax.ShapeDtypeStruct((span, hidden), BF16),
+            jax.ShapeDtypeStruct((span, cut), BF16),
+            jax.ShapeDtypeStruct((outer, span, hidden - cut), BF16),
+            jax.ShapeDtypeStruct((outer, span, hidden), BF16),
         ),
-        in_specs=[IN_VMEM] * 3 + [ANY] * 3 + [IN_VMEM] * 3,
-        out_specs=[IN_VMEM, ANY, IN_VMEM, IN_VMEM],
+        in_specs=[IN_VMEM] * 6 + [ANY] * 5,
+        out_specs=[IN_VMEM] * 2 + [ANY] * 6,
         scratch_shapes=[
-            partial,
-            partial,
+            pltpu.VMEM((chips, 2 * rows, cols), BF16),
+            pltpu.VMEM((2, 2 * rows, cols), BF16),
             pltpu.VMEM((rows, cols), BF16),
             pltpu.VMEM((16, cols), F32),
             pltpu.VMEM((cols, hidden), BF16),
             pltpu.VMEM((cols, hidden), BF16),
             pltpu.VMEM((hidden, cols), BF16),
+            pltpu.VMEM((tokens, cols), BF16),
+            pltpu.VMEM((tokens, cols), BF16),
+            pltpu.VMEM((2, span, hidden), BF16),
+            pltpu.VMEM((2, span, hidden - cut), BF16),
         ]
         + [buffers] * 3
-        + [DMA((2, 2, chips))] * 2
+        + down_vmem
+        + gate_vmem
+        + [DMA((2, 1, chips))] * 2
         + [DMA((2, outer))] * 3
-        + [DMA((4,))],
+        + reduce_sems * 2
+        + [DMA((6,)), DMA((2,)), DMA((2,)), DMA((2,))],
         compiler_params=pltpu.CompilerParams(
-            collective_id=collective, has_side_effects=True, vmem_limit_bytes=56 * 2**20
+            collective_id=collective, has_side_effects=True, vmem_limit_bytes=60 * 2**20
         ),
-        cost_estimate=cost(120),
+        cost_estimate=cost(110),
         name="turn",
-    )(dgm, dum, mm, wg, wu, wd, mid, cot, gain)
+    )(dgm, dum, mm, mid, cot, gain, wg, wu, wd, n2, cots)
+
+
+def scan_backward_kernel(
+    outer,
+    inner,
+    shards,
+    quarters,
+    chunk,
+    blocks,
+    block_width,
+    dout_ref,
+    wo_ref,
+    proj_ref,
+    h_ref,
+    v_ref,
+    par_ref,
+    gates_ref,
+    mid_ref,
+    q_ref,
+    rest_ref,
+    both_ref,
+    blocks_ref,
+    totals_ref,
+    result_ref,
+    rest_out,
+    q_s,
+    near_in,
+    far_in,
+    far_out,
+    rest_own,
+    rest_land,
+    near,
+    far,
+    q_sem,
+    r_up,
+    r_low,
+    r_sem,
+    dout_s,
+    dz_s,
+    sems,
+    sums_ref,
+    gate_grad_ref,
+    a_s,
+    g_s,
+    t_s,
+    h_pad,
+    pre_s,
+    dpre_s,
+    dv_s,
+    u_pad,
+):
+    length, width = h_ref.shape
+    seg = length // SEGMENTS
+    chunks = length // chunk
+
+    def place(c):
+        q = c // parts
+        s = c - q * parts
+        return pl.multiple_of((s * quarters + q) * chunk, chunk)
+
+    def time_of(c):
+        return pl.multiple_of(c * chunk, chunk)
+
+    at = Place(outer, inner, shards)
+    parts = at.parts
+    rest = LineReduce(at, rest_own, rest_land, r_up, r_low)
+    fetch = pltpu.make_async_copy(rest_ref, rest_own, r_sem)
+    fetch.start()
+    greet_with_line(at, [at.sibling] + [at.near(q)[0] for q in range(1, at.chips)])
+    fetch.wait()
+
+    def rest_early(o0):
+        if o0 in (0, outer - 1):
+            for d in rest.order(o0)[:-1]:
+                rest.push(o0, d)
+
+    def rest_step(n, o0):
+        if 0 < o0 < outer - 1:
+            rest.step(o0, n)
+
+    def rest_last(o0):
+        rest.absorb(o0, o0)
+        rest.finish(o0)
+
+    at.branches(rest_early)
+    value = PlaneSum(at, 0, q_ref, near_in, far_in, far_out, near, far)
+
+    def keep(q):
+        return pltpu.make_async_copy(value.block(q, 0), q_s.at[q], q_sem.at[q])
+
+    for q in reversed(range(at.chips)):
+        value.to_sibling(q).start()
+        keep(q).start()
+    span = quarters * chunk
+
+    def load(p):
+        return pltpu.make_async_copy(
+            dout_ref.at[p], dout_s.at[pl.ds(pl.multiple_of(p * span, span), span)], sems.at[p]
+        )
+
+    for p in range(parts):
+        load(p).start()
+
+    def back_project(k, carry):
+        load(2 * k).wait()
+        load(2 * k + 1).wait()
+        some = pl.ds(pl.multiple_of(k * 2 * span, 2 * span), 2 * span)
+        depth = wo_ref.shape[2]
+        total = dot(dout_s[some, 0:depth], wo_ref[0], ((1,), (1,)))
+        for p in range(1, wo_ref.shape[0]):
+            lanes = slice(p * depth, (p + 1) * depth)
+            total = total + dot(dout_s[some, lanes], wo_ref[p], ((1,), (1,)))
+        dz_s[some, :] = total
+        return carry
+
+    lax.fori_loop(0, parts // 2, back_project, 0)
+    for q in range(at.chips):
+        keep(q).wait()
+    value.combine(q_s)
+    at.branches(functools.partial(rest_step, 0))
+    log_scale = -DECAY_SCALE * softplus(-par_ref[DECAY : DECAY + 1, :])
+    bias = jnp.concatenate(
+        [par_ref[RATE_B : RATE_B + 1, :], par_ref[ENTRY_B : ENTRY_B + 1, :]], axis=1
+    )
+    zeros8 = jnp.zeros((8, width), F32)
+    put(a_s, pl.ds(length, 8), zeros8)
+    h_pad[0:8, :] = zeros8
+    u_pad[0:8, :] = zeros8
+    dv_s[pl.ds(length, 8), :] = zeros8
+
+    def first(c, carry):
+        rows = pl.ds(time_of(c), chunk)
+        later = pl.ds(pl.multiple_of(time_of(c) + 8, 8), chunk)
+        there = pl.ds(place(c), chunk)
+        h = h_ref[rows, :]
+        h_pad[later, :] = h
+        u_pad[later, :] = proj_ref[there, width : 2 * width].astype(BF16).astype(F32)
+        y, slope = gelu_and_slope(proj_ref[there, 0:width])
+        dz = dz_s[there, :]
+        put(g_s, rows, (dz * y).astype(BF16).astype(F32))
+        both_ref[there, 0:width] = (dz * h.astype(BF16).astype(F32) * slope).astype(BF16)
+        pre = dot(v_ref[rows, :], gates_ref[...]) + bias
+        pre_s[rows, :] = pre
+        put(a_s, rows, jnp.exp(sigmoid(pre[:, :width]) * log_scale))
+        return carry
+
+    lax.fori_loop(0, chunks, first, 0)
+
+    def load(g, i):
+        return (
+            a_s[g, pl.ds(i + 1, SEGMENTS, stride=seg), :],
+            g_s[g, pl.ds(i, SEGMENTS, stride=seg), :],
+        )
+
+    def store(g, i, state, total):
+        g_s[g, pl.ds(i, SEGMENTS, stride=seg), :] = state
+        t_s[g, pl.ds(i, SEGMENTS, stride=seg), :] = total
+
+    groups = width // LANES
+    start = (jnp.zeros((SEGMENTS, LANES), F32), jnp.ones((SEGMENTS, LANES), F32))
+    ends = lax.fori_loop(
+        0,
+        seg,
+        strided_scan(lambda k: seg - 1 - k, groups, load, store),
+        (start,) * groups,
+        unroll=8,
+    )
+    firsts = jnp.concatenate([e[0] for e in ends], axis=1)
+    totals = jnp.concatenate([e[1] for e in ends], axis=1)
+    carries = [None] * SEGMENTS
+    carries[SEGMENTS - 1] = jnp.zeros((1, width), F32)
+    for j in range(SEGMENTS - 2, -1, -1):
+        carries[j] = totals[j + 1 : j + 2] * carries[j + 1] + firsts[j + 1 : j + 2]
+
+    def fold(values):
+        return jnp.sum(values.reshape(chunk // 8, 8, values.shape[1]), axis=0)
+
+    sums_ref[...] = jnp.zeros(sums_ref.shape, F32)
+
+    for j in range(SEGMENTS):
+        per = seg // chunk
+
+        def middle(k, carry, j=j, per=per):
+            c = j * per + k
+            rows = pl.ds(time_of(c), chunk)
+            g = take(g_s, rows) + take(t_s, rows) * carries[j]
+            before = h_pad[pl.ds(time_of(c), chunk + 8), :][7 : 7 + chunk]
+            v = v_ref[rows, :].astype(F32)
+            r, e, a, room, m = gate_values(pre_s[rows, :], log_scale, width)
+            gv = g * v
+            held = jnp.where(room > MULT_FLOOR, gv * e * a / m, 0.0)
+            ta = (g * before - held) * a * r
+            drpre = (ta * (log_scale * (1.0 - r))).astype(BF16)
+            depre = (gv * m * e * (1.0 - e)).astype(BF16)
+            dpre_s[rows, 0:width] = drpre
+            dpre_s[rows, width : 2 * width] = depre
+            sums_ref[0:8, :] += fold(ta)
+            sums_ref[8:16, :] += fold(drpre.astype(F32))
+            sums_ref[16:24, :] += fold(depre.astype(F32))
+            dv = g * m * e + dot(dpre_s[rows, :], gates_ref[...], ((1,), (1,)))
+            dv_s[rows, :] = dv
+            sums_ref[24:32, :] += fold(dv)
+            wide = u_pad[pl.ds(time_of(c), chunk + 8), :]
+            for tap in range(4):
+                top = 32 + 8 * tap
+                sums_ref[top : top + 8, :] += fold(dv * wide[8 - tap : 8 - tap + chunk])
+            return carry
+
+        lax.fori_loop(0, per, middle, 0)
+        if j == 3:
+            for n in range(1, outer - 1):
+                at.branches(functools.partial(rest_step, n))
+    at.branches(rest_last)
+    out = pltpu.make_async_copy(rest_own.at[at.o], rest_out, r_sem)
+    out.start()
+    sums_ref[0:8, :] = sums_ref[0:8, :] * (
+        DECAY_SCALE * sigmoid(-par_ref[DECAY : DECAY + 1, :])
+    )
+
+    def last(c, carry):
+        wide = dv_s[pl.ds(time_of(c), chunk + 8), :]
+        du = par_ref[0:1, :] * wide[0:chunk]
+        for tap in range(1, 4):
+            du = du + par_ref[tap : tap + 1, :] * wide[tap : tap + chunk]
+        both_ref[pl.ds(place(c), chunk), width : 2 * width] = du.astype(BF16)
+        return carry
+
+    lax.fori_loop(0, chunks, last, 0)
+    gate_grad_ref[...] = dot(v_ref[...], dpre_s[...], ((0,), (0,)))
+    blocks_ref[...] = jnp.zeros(blocks_ref.shape, F32)
+    tall = blocks_ref.shape[0] // (2 * blocks)
+    for gate in range(2):
+        for j in range(blocks):
+            top, lanes = (gate * blocks + j) * tall, gate * width + j * block_width
+            rows = slice(j * block_width, (j + 1) * block_width)
+            blocks_ref[top : top + block_width, :block_width] = gate_grad_ref[
+                rows, lanes : lanes + block_width
+            ]
+    for k in range(8):
+        totals_ref[k : k + 1, :] = jnp.sum(sums_ref[8 * k : 8 * k + 8, :], axis=0, keepdims=True)
+    value.arrive()
+
+    def output(rows):
+        result_ref[rows, :] = (mid_ref[rows, :] + value.total(rows, q_s)).astype(BF16)
+
+    add_rows(span, output)
+    value.finish()
+    out.wait()
+
+
+def scan_backward(
+    quarters,
+    chunk,
+    blocks,
+    block_width,
+    dout,
+    w_out,
+    proj,
+    h,
+    v,
+    params,
+    gates,
+    mid,
+    q,
+    rest,
+    outer,
+    inner,
+    shards,
+    collective,
+):
+    parts = dout.shape[0]
+    rows, cols = mid.shape
+    chips = q.shape[0]
+    rest_vmem, rest_sems = line_reduce_scratch(*rest.shape)
+    buffers = pltpu.VMEM((1, chips, rows, cols), BF16)
+    length, width = h.shape
+    tall, wide = -(-block_width // 8) * 8, -(-block_width // LANES) * LANES
+    return pl.pallas_call(
+        functools.partial(
+            scan_backward_kernel, outer, inner, shards, quarters, chunk, blocks, block_width
+        ),
+        out_shape=(
+            jax.ShapeDtypeStruct((length, 2 * width), BF16),
+            jax.ShapeDtypeStruct((2 * blocks * tall, wide), F32),
+            jax.ShapeDtypeStruct((8, width), F32),
+            jax.ShapeDtypeStruct((rows, cols), BF16),
+            jax.ShapeDtypeStruct(rest.shape[1:], BF16),
+        ),
+        in_specs=[ANY] + [IN_VMEM] * 7 + [ANY] * 2,
+        out_specs=[IN_VMEM] * 4 + [ANY],
+        scratch_shapes=[
+            pltpu.VMEM((chips, rows, cols), BF16),
+            buffers,
+            buffers,
+            buffers,
+            *rest_vmem,
+            DMA((2, 1, chips)),
+            DMA((2, 1, chips)),
+            DMA((chips,)),
+            *rest_sems,
+            DMA,
+            pltpu.VMEM((length, dout.shape[2]), BF16),
+            pltpu.VMEM((length, width), F32),
+            DMA((parts,)),
+            pltpu.VMEM((64, width), F32),
+            pltpu.VMEM((width, 2 * width), F32),
+            pltpu.VMEM((width // LANES, length + 8, LANES), F32),
+            pltpu.VMEM((width // LANES, length, LANES), F32),
+            pltpu.VMEM((width // LANES, length, LANES), F32),
+            pltpu.VMEM((length + 8, width), F32),
+            pltpu.VMEM((length, 2 * width), F32),
+            pltpu.VMEM((length, 2 * width), BF16),
+            pltpu.VMEM((length + 8, width), F32),
+            pltpu.VMEM((length + 8, width), F32),
+        ],
+        compiler_params=pltpu.CompilerParams(
+            collective_id=collective, has_side_effects=True, vmem_limit_bytes=60 * 2**20
+        ),
+        cost_estimate=cost(21),
+        name="scan_backward",
+    )(dout, w_out, proj, h, v, params, gates, mid, q, rest)
+
+
+def remote(src, dst, send, recv, to):
+    return pltpu.make_async_remote_copy(
+        src_ref=src, dst_ref=dst, send_sem=send, recv_sem=recv, device_id=to, device_id_type=MESH
+    )
+
+
+def add_rows(rows, fn):
+    def one(k, carry):
+        fn(pl.ds(pl.multiple_of(k * 16, 16), 16))
+        return carry
+
+    lax.fori_loop(0, rows // 16, one, 0)
 
 
 class PlaneExchange:
     def __init__(self, at, n, x, out, sems, local):
-        self.at, self.n, self.x, self.out, self.sems = at, n, x, out, sems
+        self.at, self.n, self.x, self.out, self.sems, self.local = at, n, x, out, sems, local
         _, self.me = at.near(0)
-        self.keep = pltpu.make_async_copy(x.at[self.me], out.at[self.me], local)
-        self.hops = [(q, other) for q in reversed(range(at.chips)) for other in range(2)][:-2] + [(0, 1)]
-
-    def others(self):
-        return [self.at.near(q, other)[0] for q, other in self.hops]
+        self.hops = [(q, c) for q in reversed(range(1, at.chips)) for c in range(2)] + [(0, 1)]
+
+    def rows(self, slot):
+        piece = self.out.shape[1]
+        return self.x.at[pl.ds(pl.multiple_of(slot * piece, piece), piece)]
+
+    def mine(self):
+        return pltpu.make_async_copy(self.rows(self.me), self.out.at[self.me], self.local)
 
     def start(self):
         self.send = Sent()
         for k, (q, other) in enumerate(self.hops):
             to, slot = self.at.near(q, other)
-            self.send(self.x.at[slot], self.out.at[self.me], self.sems, (self.n, k), to)
-        self.keep.start()
+            self.send(self.rows(slot), self.out.at[self.me], self.sems, (self.n, k), to)
+        self.mine().start()
 
     def finish(self):
         for k, (q, other) in enumerate(self.hops):
             source, slot = self.at.near(q, other, True)
-            received(self.x.at[self.me], self.out.at[slot], self.sems, (self.n, k), source)
+            received(self.rows(self.me), self.out.at[slot], self.sems, (self.n, k), source)
         self.send.finish()
-        self.keep.wait()
+        self.mine().wait()
 
 
 def closing_kernel(
@@ -1103,6 +1403,8 @@
     dout_ref,
     down_ref,
     gate_ref,
+    rest_ref,
+    up_ref,
     grad_ref,
     mix_ref,
     blocks_out,
@@ -1110,7 +1412,12 @@
     gains_out,
     down_out,
     gate_out,
+    rest_out,
+    up_out,
     p_s,
+    up_own,
+    up_land,
+    up_sum,
     n1_s,
     dout_s,
     g_s,
@@ -1137,6 +1444,9 @@
     s_near,
     swap,
     g_sem,
+    stripe,
+    u_up,
+    u_low,
     local,
 ):
     at = Place(outer, inner, shards)
@@ -1150,11 +1460,21 @@
     width2 = both_ref.shape[1]
     me = s * shards + h
     small = ((blocks_ref, block_slots, blocks_out), (sums_ref, sum_slots, sums_out))
-    load = [
-        pltpu.make_async_copy(n1_ref, n1_s, local.at[0]),
-        pltpu.make_async_copy(dout_ref, dout_s, local.at[1]),
-    ]
-    for copy in load:
+    fetch = pltpu.make_async_copy(up_ref, up_own, local.at[0])
+    fetch.start()
+
+    def stripes(k):
+        lanes = pl.ds(pl.multiple_of(owner(k) * span, span), span)
+        slot = lax.rem(k, 2)
+        return (
+            pltpu.make_async_copy(n1_ref.at[:, lanes], n1_s.at[slot], stripe.at[0, slot]),
+            pltpu.make_async_copy(dout_ref.at[:, lanes], dout_s.at[slot], stripe.at[1, slot]),
+        )
+
+    def owner(k):
+        return lax.rem(s + k + 1, parts)
+
+    for copy in stripes(0):
         copy.start()
 
     def anyone(k):
@@ -1167,6 +1487,10 @@
 
     lax.fori_loop(1, at.count, greet_one, 0)
     welcome(at.count - 1)
+    ups = LineReduce(at, up_own, up_land, u_up, u_low)
+    fetch.wait()
+
+    ups.early(0, at.far_first(0), min(1, outer - 2))
 
     def back(n, carry):
         d = at.far_first(n)
@@ -1184,11 +1508,6 @@
             send(src, slots.at[h], s_far, (n, dy), (s, at.along(dy)))
         send(src, slots.at[h], s_near, (n, 0), at.sibling)
         slots[h] = src[...]
-    for copy in load:
-        copy.wait()
-
-    def owner(k):
-        return lax.rem(s + k + 1, parts)
 
     def mix_rows(p, shard):
         return g_s.at[p, pl.ds(pl.multiple_of(shard * piece, piece), piece)]
@@ -1224,10 +1543,17 @@
         )
 
     def weight_grads(k, carry):
-        p = owner(k)
-        lanes = pl.ds(pl.multiple_of(p * span, span), span)
-        g_s[p, :, 0:width2] = dot(n1_s[:, lanes], both_ref[...], ((0,), (0,))).astype(BF16)
-        g_s[p, :, width2:] = dot(dout_s[:, lanes], z_ref[...], ((0,), (0,))).astype(BF16)
+        p, slot = owner(k), lax.rem(k, 2)
+        for copy in stripes(k):
+            copy.wait()
+
+        @pl.when(k < parts - 1)
+        def _():
+            for copy in stripes(k + 1):
+                copy.start()
+
+        g_s[p, :, 0:width2] = dot(n1_s[slot], both_ref[...], ((0,), (0,))).astype(BF16)
+        g_s[p, :, width2:] = dot(dout_s[slot], z_ref[...], ((0,), (0,))).astype(BF16)
         for dy in steps + [0]:
             to_sibling(k, dy).start()
         return carry
@@ -1236,7 +1562,9 @@
     exchanges = [
         PlaneExchange(at, 0, down_ref, down_out, swap, local.at[2]),
         PlaneExchange(at, 1, gate_ref, gate_out, swap, local.at[3]),
+        PlaneExchange(at, 3, rest_ref, rest_out, swap, local.at[5]),
     ]
+    up_exchange = PlaneExchange(at, 2, up_sum, up_out, swap, local.at[1])
 
     def sibling_sums(k, carry):
         p = owner(k)
@@ -1281,10 +1609,20 @@
         grad_ref[rows, :] = dmid_ref[rows, :] + rms_back(x, scale, gain_ref[...], dn1)
 
     def branch(o0):
+        ends = o0 in (0, outer - 1)
+
+        sooner = min(1, outer - 2) if ends else 0
+
         def between(n):
+            if n + sooner < outer - 1 and ends:
+                ups.push(o0, ups.order(o0)[n + sooner])
             for k in range(n * inner, (n + 1) * inner):
                 mix_step(k)
-
+            if n + 1 < outer - 1 and not ends:
+                ups.step(o0, n + 1)
+
+        if not ends:
+            ups.step(o0, 0)
         line.steps(o0, last_add, between)
 
     at.branches(branch)
@@ -1316,6 +1654,18 @@
         return carry
 
     lax.fori_loop(1, at.count, gain_start, 0)
+
+    def last_up(o0):
+        ups.absorb(o0, o0)
+        ups.finish(o0)
+
+    at.branches(last_up)
+
+    def keep_up(rows):
+        up_sum[rows, :] = up_own[at.o, rows, :]
+
+    add_rows(up_sum.shape[0], keep_up)
+    up_exchange.start()
     for n, (src, slots, out) in enumerate(small):
         for dy in steps:
             here = slots.at[at.along(-dy)]
@@ -1337,7 +1687,7 @@
     gains_out[...] = lax.fori_loop(1, at.count, gain_arrive, gain_rows[me])
     for k in range(parts - 1):
         to_owner(k, True).wait_recv()
-    for exchange in exchanges:
+    for exchange in exchanges + [up_exchange]:
         exchange.finish()
     for k in range(parts):
         for dy in range(ys):
@@ -1352,7 +1702,25 @@
 
 
 def closing(
-    both, w_in, z, x, dmid, gain, gain2, small, sums, n1, dout, down, gate, outer, inner, shards, collective
+    both,
+    w_in,
+    z,
+    x,
+    dmid,
+    gain,
+    gain2,
+    small,
+    sums,
+    n1,
+    dout,
+    down,
+    gate,
+    rest,
+    ups,
+    outer,
+    inner,
+    shards,
+    collective,
 ):
     rows, cols = x.shape
     parts, ys, count = outer * inner, shards // 2, outer * inner * shards
@@ -1361,8 +1729,14 @@
     lanes = -(-2 * piece // LANES) * LANES
     bufs, sems = line_sum_scratch(outer, rows, cols)
     pieces = pltpu.VMEM((max(ys - 1, 1), parts, piece, 3 * width), BF16)
-    whole = pltpu.VMEM((parts * rows, cols), BF16)
-    same = jax.ShapeDtypeStruct(down.shape, down.dtype)
+    stripes = pltpu.VMEM((2, parts * rows, cols // parts), BF16)
+    span, hidden = down.shape
+
+    def swapped(array):
+        shape = (inner * shards, span // (inner * shards), array.shape[-1])
+        return jax.ShapeDtypeStruct(shape, BF16)
+
+    reduce_vmem, reduce_sems = line_reduce_scratch(outer, span, hidden)
     return pl.pallas_call(
         functools.partial(closing_kernel, outer, inner, shards),
         out_shape=(
@@ -1371,15 +1745,16 @@
             jax.ShapeDtypeStruct(small.shape, F32),
             jax.ShapeDtypeStruct(sums.shape, F32),
             jax.ShapeDtypeStruct((1, lanes), F32),
-            same,
-            same,
+            *[swapped(array) for array in (down, gate, rest, ups)],
         ),
-        in_specs=[IN_VMEM] * 9 + [ANY] * 4,
-        out_specs=[IN_VMEM] * 5 + [ANY] * 2,
+        in_specs=[IN_VMEM] * 9 + [ANY] * 6,
+        out_specs=[IN_VMEM] * 5 + [ANY] * 4,
         scratch_shapes=[
             pltpu.VMEM((outer, inner * rows, cols), BF16),
-            whole,
-            whole,
+            *reduce_vmem,
+            pltpu.VMEM((span, hidden), BF16),
+            stripes,
+            stripes,
             pltpu.VMEM((parts, shards * piece, 3 * width), BF16),
             pltpu.VMEM((16, cols), F32),
             pltpu.VMEM((count, 1, lanes), F32),
@@ -1396,7 +1771,9 @@
         + [DMA((2, ys, parts))] * 2
         + [DMA((2, parts))]
         + [DMA((2, 2, ys))] * 2
-        + [DMA((2, 2, inner * shards)), DMA((2, count)), DMA((5,))],
+        + [DMA((2, 4, inner * shards)), DMA((2, count)), DMA((2, 2))]
+        + reduce_sems
+        + [DMA((6,))],
         compiler_params=pltpu.CompilerParams(
             collective_id=collective, has_side_effects=True, vmem_limit_bytes=60 * 2**20
         ),
@@ -1416,42 +1793,38 @@
         dout,
         down,
         gate,
+        rest,
+        ups,
     )
 
 
-def finish_kernel(outer, inner, shards, x_ref, out_ref, sems, local):
-    at = Place(outer, inner, shards)
-    exchange = PlaneExchange(at, 0, x_ref, out_ref, sems, local)
-    greet(exchange.others())
-    exchange.start()
-    exchange.finish()
-
-
-def finish(x, outer, inner, shards, collective):
-    return pl.pallas_call(
-        functools.partial(finish_kernel, outer, inner, shards),
-        out_shape=jax.ShapeDtypeStruct(x.shape, x.dtype),
-        in_specs=[ANY],
-        out_specs=ANY,
-        scratch_shapes=[DMA((2, 1, inner * shards)), DMA],
-        compiler_params=pltpu.CompilerParams(collective_id=collective, has_side_effects=True),
-        cost_estimate=cost(12),
-        name="finish",
-    )(x)
-
-
 def unpack_kernel(
-    inner, channels, gate_ref, up_ref, down_ref, mix_ref, gate, up, down, branch, enter, leave
+    inner,
+    channels,
+    gate_ref,
+    rest_ref,
+    up_ref,
+    down_ref,
+    mix_ref,
+    gate,
+    up,
+    down,
+    branch,
+    enter,
+    leave,
 ):
-    slots, piece, hidden = gate_ref.shape
+    slots, piece, hidden = up_ref.shape
+    cut = gate_ref.shape[2]
     shards = slots // inner
     parts, width = mix_ref.shape[0], mix_ref.shape[2] // 3
     for i in range(inner):
         for h in range(shards):
-            lanes = slice((h * inner + i) * hidden, (h * inner + i + 1) * hidden)
+            first = (h * inner + i) * hidden
             slot = i * shards + h
-            for src, dst in ((gate_ref, gate), (up_ref, up), (down_ref, down)):
-                dst[:, lanes] = src[slot].astype(F32)
+            gate[:, first : first + cut] = gate_ref[slot].astype(F32)
+            gate[:, first + cut : first + hidden] = rest_ref[slot].astype(F32)
+            up[:, first : first + hidden] = up_ref[slot].astype(F32)
+            down[:, first : first + hidden] = down_ref[slot].astype(F32)
     for k, dst in enumerate((branch, enter, leave)):
         lanes = slice(k * width, k * width + width)
         dst[...] = jnp.concatenate(
@@ -1459,19 +1832,19 @@
         )
 
 
-def unpack(ffn_gate, ffn_up, ffn_down, mix, inner, channels):
-    slots, piece, hidden = ffn_gate.shape
+def unpack(ffn_gate, ffn_rest, ffn_up, ffn_down, mix, inner, channels):
+    slots, piece, hidden = ffn_up.shape
     across = jax.ShapeDtypeStruct((piece, slots * hidden), F32)
     wide = jax.ShapeDtypeStruct((piece, mix.shape[0] * channels), F32)
     return pl.pallas_call(
         functools.partial(unpack_kernel, inner, channels),
         out_shape=(across,) * 3 + (wide,) * 3,
-        in_specs=[IN_VMEM] * 4,
+        in_specs=[IN_VMEM] * 5,
         out_specs=[IN_VMEM] * 6,
         compiler_params=pltpu.CompilerParams(vmem_limit_bytes=48 * 2**20),
         cost_estimate=cost(4),
         name="unpack",
-    )(ffn_gate, ffn_up, ffn_down, mix)
+    )(ffn_gate, ffn_rest, ffn_up, ffn_down, mix)
 
 
 def body(
@@ -1507,7 +1880,6 @@
     spare = width - channels
     blocks, block_width = rate_weight.shape[0], rate_weight.shape[1]
     piece = model // (parts * shards)
-    columns = [[o * inner + i for o in range(outer)] for i in range(inner)]
 
     def own(weight, axis):
         part = lax.dynamic_slice_in_dim(weight, seq_at * channels, channels, axis)
@@ -1559,30 +1931,51 @@
     wu = lax.dynamic_slice_in_dim(hidden_up, inner_at * hidden, hidden, 1)
     wd = lax.dynamic_slice_in_dim(hidden_down, inner_at * hidden, hidden, 0)
 
-    def sum_tokens(x):
-        return lax.psum_scatter(
-            x.astype(BF16), "seq", scatter_dimension=0, tiled=True, axis_index_groups=columns
-        ).reshape(inner * shards, piece, hidden)
-
     gm = dot(n2, wg)
     um = dot(n2, wu)
     act, slope = gelu_and_slope(gm)
     mm = (act * um).astype(BF16)
-    down_sum = sum_tokens(dot(cot_all, mm, ((0,), (0,))))
     dmm = dot(cot_all, wd, ((1,), (1,)))
     dgm = (dmm * um * slope).astype(BF16)
     dum = (dmm * act).astype(BF16)
-    gate_sum = sum_tokens(dot(n2, dgm, ((0,), (0,))))
-    up_terms = dot(n2, dum, ((0,), (0,)))
-    dmid, dout, result, gain2_grad = turn(
-        dgm, dum, mm, hidden_gate, hidden_up, hidden_down, mid, cot, gain2, outer, inner, shards, 2
+    dmid, gain2_grad, dout, partial, down_sum, gate_sum, rest_terms, up_terms = turn(
+        dgm,
+        dum,
+        mm,
+        mid,
+        cot,
+        gain2,
+        hidden_gate,
+        hidden_up,
+        hidden_down,
+        n2,
+        cot_all,
+        outer,
+        inner,
+        shards,
+        2,
     )
-    dout, up_terms = lax.optimization_barrier((dout, up_terms.astype(BF16)))
-    up_sum = sum_tokens(up_terms)
-    both, small, sums = scan_backward(
-        quarters, chunk, blocks, block_width, dout, w_out, proj, h, v, params, gates
+    both, small, sums, result, rest_sum = scan_backward(
+        quarters,
+        chunk,
+        blocks,
+        block_width,
+        dout,
+        w_out,
+        proj,
+        h,
+        v,
+        params,
+        gates,
+        mid,
+        partial,
+        rest_terms,
+        outer,
+        inner,
+        shards,
+        3,
     )
-    tokens_grad, mix, small, sums, gains, down_sum, gate_sum = closing(
+    tokens_grad, mix, small, sums, gains, down_sum, gate_sum, rest_sum, up_sum = closing(
         both,
         w_in,
         z,
@@ -1596,15 +1989,16 @@
         dout.reshape(parts * rows, model),
         down_sum,
         gate_sum,
+        rest_sum,
+        up_terms,
         outer,
         inner,
         shards,
-        3,
+        4,
     )
     gains = gains[0]
-    up_sum = finish(up_sum, outer, inner, shards, 4)
     gate_sum, up_sum, down_sum, branch_sum, input_sum, output_sum = unpack(
-        gate_sum, up_sum, down_sum, mix, inner, channels
+        gate_sum, rest_sum, up_sum, down_sum, mix, inner, channels
     )
     sums = sums[:, :channels]
     small = small.reshape(2, blocks, -1, small.shape[1])[:, :, :block_width, :block_width]

time: 510 us -> 477 us (0.935)
  matrix products: 37.1 us -> 16.8 us
  between operations: 14.3 us -> 1.16 us
    dot_general x6 -> x3, matrix products: 37.1 us -> 16.8 us  [dot(): lax.dot_general(left, right, (dims, ((), ())), preferred_element_type=F32)]
    pallas_call x1, Pallas kernels: 128 us -> 115 us  [turn(): pl.pallas_call(functools.partial(turn_kernel, outer, inner, shards), out_...]
    pallas_call x1, Pallas kernels: 117 us -> 129 us  [closing(): pl.pallas_call(functools.partial(closing_kernel, outer, inner, shards), o...]
    pallas_call x2 -> x1, Pallas kernels: 37.4 us -> 39.2 us  [scan_backward(): pl.pallas_call(functools.partial(scan_backward_kernel, outer, inner, shar...]
  transfers between devices with their start and end apart: 4 -> 1, of which waited for: 0 -> 0; matrix products, arithmetic and copies ran while one was open for 3% -> 0% of each run, Pallas kernels for 57% -> 4%
where the time goes in v4:
time: 477 us; the launch traced here: 476 us
  Pallas kernels  436 us (91%)
  local copies, waits for them, and re-layouts  17.3 us (4%)
  matrix products  16.8 us (4%)
    pallas_call x1, Pallas kernels, closing(): pl.pallas_call(functools.partial(closing_kernel, outer, inner, shards), o...  129 us
    pallas_call x1, Pallas kernels, turn(): pl.pallas_call(functools.partial(turn_kernel, outer, inner, shards), out_...  115 us
    pallas_call x1, Pallas kernels, middle(): pl.pallas_call(functools.partial(middle_kernel, outer, inner, shards), ou...  77.3 us
    pallas_call x1, Pallas kernels, opening(): pl.pallas_call(functools.partial(opening_kernel, outer, inner, shards), o...  54.4 us
    pallas_call x1, Pallas kernels, scan_backward(): pl.pallas_call(functools.partial(scan_backward_kernel, outer, inner, shar...  39.2 us
    pallas_call x1, Pallas kernels, scan_forward(): pl.pallas_call(functools.partial(scan_forward_kernel, parts, quarters, ch...  17.9 us
    dot_general x3, matrix products, dot(): lax.dot_general(left, right, (dims, ((), ())), preferred_element_type=F32)  16.8 us
  transfers between devices with their start and end apart: 1, of which 0 were waited for; matrix products, arithmetic and copies ran while one was open for 0% of the time, Pallas kernels for 4%

profile of v4, /device:TPU:9, one launch (start us, length us, event | category | flops | bytes accessed | tf_op | source)
XLA Modules:
  0.0 475.8 jit_solution(17552252608052387768)
XLA Ops:
  0.7 1.4 multiply_reduce_fusion
  3.4 1.3 constant_dynamic-slice_fusion.1
  6.1 1.0 multiply_convert_fusion.2.x_ref
  8.0 54.4 %opening.1 = (bf16[8,128,2048]{2,1,0:T(8,128)(2,1)}, bf16[4,512,768]{2,1,0:T(8,128)(2,1)}, bf16[4,384,512]{2,1,0:T(8,128)(2,1)}) custom-call(bf16[128,2048]{1,0:T(8,128)(2,1)} %multiply_convert_fusion.2.x_ref, bf16[512,768]{1,0:T(8,128)(2,1)} %fusion.17.wi_ref, bf16[384,512]{1,0:T(8,128)(2,1)} %pad.17.wo_ref), custom_call_target="tpu_custom_call" | custom-call | bytes 181500000 | tf_op jit(solution)/shard_map/opening/pallas_call | solution.py:535
  62.4 1.3 collective-permute-start
  63.9 17.9 %scan_forward.1 = (bf16[1024,384]{1,0:T(8,128)(2,1)S(1)}, f32[1024,384]{1,0:T(8,128)S(1)}, bf16[1024,384]{1,0:T(8,128)(2,1)S(1)}, f32[1024,768]{1,0:T(8,128)}, bf16[384,768]{1,0:T(8,128)(2,1)S(1)}) custom-call(bf16[8,128,2048]{2,1,0:T(8,128)(2,1)} %get-tuple-element.59.n1_ref, bf16[2048,768]{1,0:T(8,128)(2,1)} %bitcast.43, f32[8,384]{1,0:T(8,128)S(1)} %pad.18.par_ref, ...), custom_call_target="tpu_custom_call" | custom-call | bytes 59400000 | tf_op jit(solution)/shard_map/scan_forward/pallas_call | solution.py:218
  81.9 1.1 copy-done.7
  83.9 77.3 %middle.1 = (f32[128,2048]{1,0:T(8,128)S(1)}, bf16[8,128,2048]{2,1,0:T(8,128)(2,1)}, bf16[8,128,2048]{2,1,0:T(8,128)(2,1)}) custom-call(bf16[4,256,384]{2,1,0:T(8,128)(2,1)S(1)} %bitcast.35, bf16[4,384,512]{2,1,0:T(8,128)(2,1)S(1)} %copy-done.3, bf16[128,2048]{1,0:T(8,128)(2,1)S(1)} %bitcast.34, f32[1,2048]{1,0:T(1,128)S(1)} %bitcast.40, ...), custom_call_target="tpu_custom_call" | custom-call | bytes 264000000 | tf_op jit(solution)/shard_map/middle/pallas_call | solution.py:666
  161.2 6.6 %fusion.13 = f32[1024,768]{1,0:T(8,128)S(1)} fusion(bf16[1024,2048]{1,0:T(8,128)(2,1)} %bitcast.52, bf16[1536,2048]{1,0:T(8,128)(2,1)} %wd_ref.1, s32[]{:T(128)S(6)} %select_n.5), kind=kOutput, calls=%fused_computation.18 | convolution fusion | flops 3221225472 | bytes 10485764 | tf_op jit(solution)/shard_map/dot_general | solution.py:32
  167.9 3.4 fusion.9
  171.4 6.7 %multiply_convert_fusion = (bf16[1024,768]{1,0:T(8,128)(2,1)}, bf16[1024,768]{1,0:T(8,128)(2,1)}, bf16[1024,768]{1,0:T(8,128)(2,1)}) fusion(f32[1024,768]{1,0:T(8,128)S(1)} %fusion.9, f32[1024,768]{1,0:T(8,128)S(1)} %fusion.13, bf16[1024,2048]{1,0:T(8,128)(2,1)S(1)} %bitcast.51, bf16[2048,1536]{1,0:T(8,128)(2,1)S(1)} %bitcast.48, s32[]{:T(128)S(6)} %select_n.5), kind=kOutput, calls=%fused_computation.10 | convolution fusion | flops 3240886272 | bytes 18350084 | tf_op jit(solution)/shard_map/dot_general | solution.py:32
  178.1 114.8 %turn.1 = (f32[128,2048]{1,0:T(8,128)}, f32[1,2048]{1,0:T(1,128)}, bf16[8,128,2048]{2,1,0:T(8,128)(2,1)}, bf16[4,256,2048]{2,1,0:T(8,128)(2,1)}, bf16[512,768]{1...) custom-call(bf16[1024,768]{1,0:T(8,128)(2,1)} %get-tuple-element.121.dgm_ref,, ...), custom_call_target="tpu_custom_call" | custom-call | bytes 363000000 | tf_op jit(solution)/shard_map/turn/pallas_call | solution.py:984
  292.9 39.2 %scan_backward.1 = (bf16[1024,768]{1,0:T(8,128)(2,1)}, f32[704,256]{1,0:T(8,128)}, f32[8,384]{1,0:T(8,128)}, bf16[128,2048]{1,0:T(8,128)(2,1)}, bf16[512,384]{1,0:T(8,128)(2,1)}) custom-call(bf16[8,128,2048]{2,1,0:T(8,128)(2,1)} %get-tuple-element.67.dout_ref, bf16[4,384,512]{2,1,0:T(8,128)(2,1)} %get-tuple-element.62.wo_ref, ...), custom_call_target="tpu_custom_call" | custom-call | bytes 69300000 | tf_op jit(solution)/shard_map/scan_backward/pallas_call | solution.py:1301
  332.1 129.1 %closing.1 = (f32[128,2048]{1,0:T(8,128)}, bf16[8,64,1152]{2,1,0:T(8,128)(2,1)}, f32[704,256]{1,0:T(8,128)}, f32[8,384]{1,0:T(8,128)}, f32[1,128]{1,0:T(1,128)},...) custom-call(bf16[1024,768]{1,0:T(8,128)(2,1)} %get-tuple-element.75., ...), custom_call_target="tpu_custom_call" | custom-call | bytes 264000000 | tf_op jit(solution)/shard_map/closing/pallas_call | solution.py:1740
  461.3 1.5 slice.44
  462.7 1.5 slice_reduce_fusion
  464.2 1.3 slice_bitcast_fusion
  465.5 1.1 fusion.21
  466.6 1.0 copy.48
  467.6 1.0 copy.49
  468.6 1.1 copy-done.13
  469.8 1.0 copy-done.14
  470.8 3.2 unpack.1
  474.8 1.0 copy.53
  (82 shorter events, 5.4 us)
Async XLA Ops:
  0.7 5.4 %copy-start.2 = (bf16[2,1,64,2048]{3,2,1,0:T(8,128)(2,1)S(1)}, bf16[2,1,64,2048]{3,2,1,0:T(8,128)(2,1)}, u32[]{:S(2)}) copy-start(bf16[2,1,64,2048]{3,2,1,0:T(8,128)(2,1)} %param.17) | copy-start | bytes 1572868
  4.7 57.7 %copy-start.6 = (bf16[2,1,64,2048]{3,2,1,0:T(8,128)(2,1)S(1)}, bf16[2,1,64,2048]{3,2,1,0:T(8,128)(2,1)}, u32[]{:S(2)}) copy-start(bf16[2,1,64,2048]{3,2,1,0:T(8,128)(2,1)} %param.33) | copy-start | bytes 1572868
  4.8 59.0 %copy-start.25 = (f32[342]{0:T(512)S(1)}, f32[342]{0:T(512)}, u32[]{:S(2)}) copy-start(f32[342]{0:T(512)} %param.22) | copy-start | bytes 4108
  4.8 59.0 %copy-start.26 = (f32[342]{0:T(512)S(1)}, f32[342]{0:T(512)}, u32[]{:S(2)}) copy-start(f32[342]{0:T(512)} %param.24) | copy-start | bytes 4108
  4.8 58.9 %copy-start.27 = (f32[342]{0:T(512)S(1)}, f32[342]{0:T(512)}, u32[]{:S(2)}) copy-start(f32[342]{0:T(512)} %param.26) | copy-start | bytes 4108
  4.8 59.0 %copy-start.28 = (f32[342]{0:T(512)S(1)}, f32[342]{0:T(512)}, u32[]{:S(2)}) copy-start(f32[342]{0:T(512)} %param.27) | copy-start | bytes 4108
  4.8 59.0 %copy-start.21 = (bf16[2,171,171]{2,0,1:T(2,128)(2,1)S(1)}, bf16[2,171,171]{2,0,1:T(2,128)(2,1)}, u32[]{:S(2)}) copy-start(bf16[2,171,171]{2,0,1:T(2,128)(2,1)} %param.23) | copy-start | bytes 350896
  5.0 58.8 %copy-start.22 = (bf16[2,171,171]{2,0,1:T(2,128)(2,1)S(1)}, bf16[2,171,171]{2,0,1:T(2,128)(2,1)}, u32[]{:S(2)}) copy-start(bf16[2,171,171]{2,0,1:T(2,128)(2,1)} %param.25) | copy-start | bytes 350896
  5.0 58.8 %copy-start.24 = (bf16[4,342]{1,0:T(4,128)(2,1)S(1)}, bf16[4,342]{1,0:T(4,128)(2,1)}, u32[]{:S(2)}) copy-start(bf16[4,342]{1,0:T(4,128)(2,1)} %param.21) | copy-start | bytes 8212
  62.4 21.4 %collective-permute-start = (bf16[128,2048]{1,0:T(8,128)(2,1)S(1)}, bf16[128,2048]{1,0:T(8,128)(2,1)}, u32[]{:S(2)}, u32[]{:S(2)}) collective-permute-start(bf16[128,2048]{1,0:T(8,128)(2,1)S(1)} %bitcast.37), channel_id=1, source_target_pairs={{0,4},{4,0},{8,12},{12,8},{16,20},{20,16},{24,28},{28,24},{1,5},{5... | collective-permute-start | bytes 1572872 | tf_op jit(solution)/shard_map/ppermute | solution.py:1919
  63.9 18.0 %copy-start.15 = (f32[8,384]{1,0:T(8,128)}, f32[8,384]{1,0:T(8,128)S(1)}, u32[]{:S(2)}) copy-start(f32[8,384]{1,0:T(8,128)S(1)} %pad.18.par_ref) | copy-start | bytes 36868
  63.9 20.0 %copy-start.3 = (bf16[4,384,512]{2,1,0:T(8,128)(2,1)S(1)}, bf16[4,384,512]{2,1,0:T(8,128)(2,1)}, u32[]{:S(2)}) copy-start(bf16[4,384,512]{2,1,0:T(8,128)(2,1)} %get-tuple-element.62.wo_ref) | copy-start | bytes 4718596
  63.9 20.0 %copy-start.16 = (f32[2048]{0:T(1024)S(1)}, f32[2048]{0:T(1024)}, u32[]{:S(2)}) copy-start(f32[2048]{0:T(1024)} %param.29) | copy-start | bytes 24580
  83.9 84.0 %copy-start.5 = (bf16[1024,384]{1,0:T(8,128)(2,1)}, bf16[1024,384]{1,0:T(8,128)(2,1)S(1)}, u32[]{:S(2)}) copy-start(bf16[1024,384]{1,0:T(8,128)(2,1)S(1)} %get-tuple-element.61.z_ref) | copy-start | bytes 2359300
  83.9 84.0 %copy-start.9 = (bf16[1024,384]{1,0:T(8,128)(2,1)}, bf16[1024,384]{1,0:T(8,128)(2,1)S(1)}, u32[]{:S(2)}) copy-start(bf16[1024,384]{1,0:T(8,128)(2,1)S(1)} %get-tuple-element.70.v_ref) | copy-start | bytes 2359300
  83.9 84.0 %slice-start = ((s8[6291456]{0:T(1024)(128)(4,1)}), s8[2097152]{0:T(1024)(128)(4,1)S(1)}, s32[]{:S(2)}) async-start(s8[6291456]{0:T(1024)(128)(4,1)} %bitcast.45), calls=%async_computation | async-start | bytes 4194304
  161.2 6.7 %copy-start.4 = (f32[128,2048]{1,0:T(8,128)}, f32[128,2048]{1,0:T(8,128)S(1)}, u32[]{:S(2)}) copy-start(f32[128,2048]{1,0:T(8,128)S(1)} %get-tuple-element.66.mid_ref) | copy-start | bytes 3145732
  161.2 6.7 %slice-start.1 = ((s8[6291456]{0:T(1024)(128)(4,1)}), s8[4194304]{0:T(1024)(128)(4,1)S(1)}, s32[]{:S(2)}) async-start(s8[6291456]{0:T(1024)(128)(4,1)} %bitcast.45), calls=%async_computation.1 | async-start | bytes 8388608
  161.2 6.7 %copy-start.17 = (bf16[8,128,2048]{2,1,0:T(8,128)(2,1)S(1)}, bf16[8,128,2048]{2,1,0:T(8,128)(2,1)}, u32[]{:S(2)}) copy-start(bf16[8,128,2048]{2,1,0:T(8,128)(2,1)} %get-tuple-element.65) | copy-start | bytes 12582916
  161.2 10.2 %slice-start.2 = ((s8[6291456]{0:T(1024)(128)(4,1)}), s8[4194304]{0:T(1024)(128)(4,1)S(1)}, s32[]{:S(2)}) async-start(s8[6291456]{0:T(1024)(128)(4,1)} %bitcast.47), calls=%async_computation.2 | async-start | bytes 8388608
  461.2 7.4 %copy-start.8 = (bf16[8,64,1152]{2,1,0:T(8,128)(2,1)S(1)}, bf16[8,64,1152]{2,1,0:T(8,128)(2,1)}, u32[]{:S(2)}) copy-start(bf16[8,64,1152]{2,1,0:T(8,128)(2,1)} %get-tuple-element.90.mix_ref) | copy-start | bytes 3538948
  461.2 7.4 %copy-start.10 = (bf16[8,64,768]{2,1,0:T(8,128)(2,1)S(1)}, bf16[8,64,768]{2,1,0:T(8,128)(2,1)}, u32[]{:S(2)}) copy-start(bf16[8,64,768]{2,1,0:T(8,128)(2,1)} %get-tuple-element.89.down_ref) | copy-start | bytes 2359300
  461.3 7.4 %copy-start.11 = (bf16[8,64,768]{2,1,0:T(8,128)(2,1)S(1)}, bf16[8,64,768]{2,1,0:T(8,128)(2,1)}, u32[]{:S(2)}) copy-start(bf16[8,64,768]{2,1,0:T(8,128)(2,1)} %get-tuple-element.88.up_ref) | copy-start | bytes 2359300
  468.6 7.2 %copy-start.1 = (bf16[2736,512]{1,0:T(8,128)(2,1)S(1)}, bf16[2736,512]{1,0:T(8,128)(2,1)}, u32[]{:S(2)}) copy-start(bf16[2736,512]{1,0:T(8,128)(2,1)} %param.28) | copy-start | bytes 8404996
  (10 other events, 24.0 us)

commit v5 on v4

--- a/solution.py
+++ b/solution.py
@@ -19,7 +19,7 @@
 
 
 MESH = pl.DeviceIdType.MESH
-ANY = pl.BlockSpec(memory_space=pl.ANY)
+IN_HBM = pl.BlockSpec(memory_space=pltpu.HBM)
 IN_VMEM = pl.BlockSpec(memory_space=pltpu.VMEM)
 DMA = pltpu.SemaphoreType.DMA
 
@@ -93,154 +93,6 @@
     return r, e, a, room, m
 
 
-def scan_forward_kernel(
-    parts,
-    quarters,
-    chunk,
-    n1_ref,
-    wi_ref,
-    par_ref,
-    rate_ref,
-    entry_ref,
-    z_ref,
-    h_ref,
-    v_ref,
-    proj_ref,
-    gates_ref,
-    n1_s,
-    wi_s,
-    gates_s,
-    u_pad,
-    a_s,
-    b_s,
-    sems,
-):
-    length, width = h_ref.shape
-    rows = quarters * chunk
-
-    def load(p):
-        return pltpu.make_async_copy(
-            n1_ref.at[p], n1_s.at[pl.ds(pl.multiple_of(p * rows, rows), rows)], sems.at[p]
-        )
-
-    weights = pltpu.make_async_copy(wi_ref, wi_s, sems.at[parts])
-    weights.start()
-    for p in range(parts):
-        load(p).start()
-    gates_s[...] = jnp.zeros(gates_s.shape, F32)
-    blocks, block_width = rate_ref.shape[0], rate_ref.shape[1]
-    for gate, src in enumerate((rate_ref, entry_ref)):
-        for j in range(blocks):
-            at, lane = j * block_width, gate * width + j * block_width
-            gates_s[at : at + block_width, lane : lane + block_width] = src[j].astype(F32)
-    gates_ref[...] = gates_s[...].astype(BF16)
-    weights.wait()
-
-    def project(k, carry):
-        load(2 * k).wait()
-        load(2 * k + 1).wait()
-        at = pl.ds(pl.multiple_of(k * 2 * rows, 2 * rows), 2 * rows)
-        proj_ref[at, :] = dot(n1_s[at, :], wi_s[...])
-        return carry
-
-    lax.fori_loop(0, parts // 2, project, 0)
-    seg = length // SEGMENTS
-    chunks = length // chunk
-
-    def place(c):
-        q = c // parts
-        s = c - q * parts
-        return pl.multiple_of((s * quarters + q) * chunk, chunk)
-
-    def time_of(c):
-        return pl.multiple_of(c * chunk, chunk)
-
-    log_scale = -DECAY_SCALE * softplus(-par_ref[DECAY : DECAY + 1, :])
-    bias = jnp.concatenate(
-        [par_ref[RATE_B : RATE_B + 1, :], par_ref[ENTRY_B : ENTRY_B + 1, :]], axis=1
-    )
-    u_pad[0:8, :] = jnp.zeros((8, width), F32)
-
-    def first(c, carry):
-        u = proj_ref[pl.ds(place(c), chunk), width : 2 * width].astype(BF16).astype(F32)
-        u_pad[pl.ds(pl.multiple_of(time_of(c) + 8, 8), chunk), :] = u
-        wide = u_pad[pl.ds(time_of(c), chunk + 8), :]
-        v = par_ref[CONV_B : CONV_B + 1, :] + par_ref[0:1, :] * wide[8:]
-        for k in range(1, 4):
-            v = v + par_ref[k : k + 1, :] * wide[8 - k : 8 - k + chunk]
-        v = v.astype(BF16)
-        v_ref[pl.ds(time_of(c), chunk), :] = v
-        pre = dot(v, gates_ref[...]) + bias
-        r, e, a, room, m = gate_values(pre, log_scale, width)
-        put(a_s, pl.ds(time_of(c), chunk), a)
-        put(b_s, pl.ds(time_of(c), chunk), m * e * v.astype(F32))
-        return carry
-
-    lax.fori_loop(0, chunks, first, 0)
-
-    def load(g, i):
-        at = pl.ds(i, SEGMENTS, stride=seg)
-        return a_s[g, at, :], b_s[g, at, :]
-
-    def store(g, i, state, total):
-        at = pl.ds(i, SEGMENTS, stride=seg)
-        b_s[g, at, :] = state
-        a_s[g, at, :] = total
-
-    groups = width // LANES
-    start = (jnp.zeros((SEGMENTS, LANES), F32), jnp.ones((SEGMENTS, LANES), F32))
-    ends = lax.fori_loop(
-        0, seg, strided_scan(lambda k: k, groups, load, store), (start,) * groups, unroll=8
-    )
-    final = jnp.concatenate([e[0] for e in ends], axis=1)
-    totals = jnp.concatenate([e[1] for e in ends], axis=1)
-    carries = [jnp.zeros((1, width), F32)]
-    for j in range(SEGMENTS - 1):
-        carries.append(totals[j : j + 1] * carries[j] + final[j : j + 1])
-    for j in range(SEGMENTS):
-        per = seg // chunk
-
-        def last(k, carry, j=j, per=per):
-            c = j * per + k
-            rows = pl.ds(time_of(c), chunk)
-            h = take(b_s, rows) + take(a_s, rows) * carries[j]
-            h_ref[rows, :] = h
-            y = gelu_tanh(proj_ref[pl.ds(place(c), chunk), 0:width])
-            z_ref[pl.ds(place(c), chunk), :] = (h.astype(BF16).astype(F32) * y).astype(BF16)
-            return carry
-
-        lax.fori_loop(0, per, last, 0)
-
-
-def scan_forward(quarters, chunk, n1, w_in, params, rate, entry):
-    parts, rows, model = n1.shape
-    length, width = parts * rows, w_in.shape[1] // 2
-    return pl.pallas_call(
-        functools.partial(scan_forward_kernel, parts, quarters, chunk),
-        out_shape=(
-            jax.ShapeDtypeStruct((length, width), BF16),
-            jax.ShapeDtypeStruct((length, width), F32),
-            jax.ShapeDtypeStruct((length, width), BF16),
-            jax.ShapeDtypeStruct((length, 2 * width), F32),
-            jax.ShapeDtypeStruct((width, 2 * width), BF16),
-        ),
-        in_specs=[ANY] * 2 + [IN_VMEM] * 3,
-        out_specs=[IN_VMEM] * 5,
-        scratch_shapes=[
-            pltpu.VMEM((length, model), BF16),
-            pltpu.VMEM(w_in.shape, BF16),
-            pltpu.VMEM((width, 2 * width), F32),
-            pltpu.VMEM((length + 8, width), F32),
-            pltpu.VMEM((width // LANES, length, LANES), F32),
-            pltpu.VMEM((width // LANES, length, LANES), F32),
-            DMA((parts + 1,)),
-        ],
-        compiler_params=pltpu.CompilerParams(vmem_limit_bytes=48 * 2**20),
-        cost_estimate=cost(18),
-        name="scan_forward",
-    )(n1, w_in, params, rate, entry)
-
-
 class Place:
     def __init__(self, outer, inner, shards):
         self.outer, self.inner, self.shards = outer, inner, shards
@@ -321,7 +173,9 @@
     remote(like, here, sems.at[(0,) + at], sems.at[(1,) + at], source).wait_recv()
 
 
-def line_gather(at, o0, x_ref, out, across, up, down, between=lambda k: None):
+def line_gather(
+    at, o0, x_ref, out, across, up, down, between=lambda k: None, each=lambda row: None
+):
     send = Sent()
 
     def slot(row):
@@ -345,8 +199,10 @@
         if k > 0 and upper < at.outer:
             pass_on(upper, across, at.beside)
         between(k)
-    for row in range(at.outer):
+    between(at.outer)
+    for row in sorted(range(at.outer), key=lambda row: abs(row - o0)):
         received(x_ref, out.at[row * at.inner + 1 - at.i], across, (row,), at.beside)
+        each(row)
     send.finish()
 
 
@@ -486,27 +342,210 @@
     return [pltpu.VMEM((outer, rows, cols), BF16)] * 4, [DMA((2, outer))] * 3
 
 
-def opening_kernel(
-    outer, inner, shards, x_ref, wi_ref, wo_ref, n_out, wi_out, wo_out, local, across, up, down, far, near
+def row_rms(values):
+    return lax.rsqrt(jnp.mean(values * values, axis=-1, keepdims=True) + EPSILON)
+
+
+def rms_back(values, scale, gain, grad):
+    k = grad * gain
+    mean = jnp.mean(k * values, axis=-1, keepdims=True)
+    return scale * k - scale * scale * scale * values * mean
+
+
+def run_scan(
+    parts, quarters, chunk, proj_ref, par_ref, gates_ref, z_ref, h_ref, v_ref, u_pad, a_s, b_s
+):
+    length, width = h_ref.shape
+    seg = length // SEGMENTS
+    chunks = length // chunk
+
+    def place(c):
+        q = c // parts
+        s = c - q * parts
+        return pl.multiple_of((s * quarters + q) * chunk, chunk)
+
+    def time_of(c):
+        return pl.multiple_of(c * chunk, chunk)
+
+    log_scale = -DECAY_SCALE * softplus(-par_ref[DECAY : DECAY + 1, :])
+    bias = jnp.concatenate(
+        [par_ref[RATE_B : RATE_B + 1, :], par_ref[ENTRY_B : ENTRY_B + 1, :]], axis=1
+    )
+    u_pad[0:8, :] = jnp.zeros((8, width), F32)
+
+    def first(c, carry):
+        u = proj_ref[pl.ds(place(c), chunk), width : 2 * width].astype(BF16).astype(F32)
+        u_pad[pl.ds(pl.multiple_of(time_of(c) + 8, 8), chunk), :] = u
+        wide = u_pad[pl.ds(time_of(c), chunk + 8), :]
+        v = par_ref[CONV_B : CONV_B + 1, :] + par_ref[0:1, :] * wide[8:]
+        for k in range(1, 4):
+            v = v + par_ref[k : k + 1, :] * wide[8 - k : 8 - k + chunk]
+        v = v.astype(BF16)
+        v_ref[pl.ds(time_of(c), chunk), :] = v
+        pre = dot(v, gates_ref[...]) + bias
+        r, e, a, room, m = gate_values(pre, log_scale, width)
+        put(a_s, pl.ds(time_of(c), chunk), a)
+        put(b_s, pl.ds(time_of(c), chunk), m * e * v.astype(F32))
+        return carry
+
+    lax.fori_loop(0, chunks, first, 0)
+
+    def load(g, i):
+        at = pl.ds(i, SEGMENTS, stride=seg)
+        return a_s[g, at, :], b_s[g, at, :]
+
+    def store(g, i, state, total):
+        at = pl.ds(i, SEGMENTS, stride=seg)
+        b_s[g, at, :] = state
+        a_s[g, at, :] = total
+
+    groups = width // LANES
+    start = (jnp.zeros((SEGMENTS, LANES), F32), jnp.ones((SEGMENTS, LANES), F32))
+    ends = lax.fori_loop(
+        0, seg, strided_scan(lambda k: k, groups, load, store), (start,) * groups, unroll=8
+    )
+    final = jnp.concatenate([e[0] for e in ends], axis=1)
+    totals = jnp.concatenate([e[1] for e in ends], axis=1)
+    carries = [jnp.zeros((1, width), F32)]
+    for j in range(SEGMENTS - 1):
+        carries.append(totals[j : j + 1] * carries[j] + final[j : j + 1])
+    for j in range(SEGMENTS):
+        per = seg // chunk
+
+        def last(k, carry, j=j, per=per):
+            c = j * per + k
+            rows = pl.ds(time_of(c), chunk)
+            h = take(b_s, rows) + take(a_s, rows) * carries[j]
+            h_ref[rows, :] = h
+            y = gelu_tanh(proj_ref[pl.ds(place(c), chunk), 0:width])
+            z_ref[pl.ds(place(c), chunk), :] = (h.astype(BF16).astype(F32) * y).astype(BF16)
+            return carry
+
+        lax.fori_loop(0, per, last, 0)
+
+
+def forward_kernel(
+    outer,
+    inner,
+    shards,
+    quarters,
+    chunk,
+    x_ref,
+    gain1_ref,
+    gain2_ref,
+    taps_ref,
+    conv_b_ref,
+    rate_b_ref,
+    entry_b_ref,
+    decay_ref,
+    rate_ref,
+    entry_ref,
+    cot_ref,
+    wi_ref,
+    wo_ref,
+    par_ref,
+    mid_ref,
+    z_out,
+    h_out,
+    v_out,
+    proj_out,
+    gates_out,
+    n1_out,
+    wi_out,
+    wo_out,
+    n2_out,
+    cot_out,
+    own_s,
+    n1_s,
+    wi_s,
+    wo_s,
+    gates_s,
+    u_pad,
+    a_s,
+    b_s,
+    z_ref,
+    h_ref,
+    v_ref,
+    proj_ref,
+    gates_ref,
+    p_s,
+    cot_s,
+    x_in,
+    up_in,
+    down_in,
+    line_out,
+    g_across,
+    g_up,
+    g_down,
+    w_far,
+    w_near,
+    across,
+    up,
+    down,
+    far,
+    near,
+    c_side,
+    c_far,
+    c_near,
+    local,
 ):
     at = Place(outer, inner, shards)
+    parts, rows = at.parts, x_ref.shape[0]
     steps = list(range(1, at.ys))
-    weights = ((wi_ref, wi_out), (wo_ref, wo_out))
-    greet_with_line(at, [at.beside, at.sibling] + [(at.s, at.along(dy)) for dy in steps])
+    width2 = wi_ref.shape[1]
+    width, depth, cols = width2 // 2, wi_ref.shape[0], wo_ref.shape[1]
+
+    def normalize(some):
+        x = x_ref[some, :].astype(F32)
+        own_s[some, :] = (x * row_rms(x) * gain1_ref[...]).astype(BF16)
+
+    add_rows(rows, normalize)
+    greet_with_line(at, [at.sibling] + [at.near(q)[0] for q in range(1, at.chips)])
+    weights = ((wi_ref, wi_s), (wo_ref, wo_s))
     keep = [
-        pltpu.make_async_copy(x_ref, n_out.at[at.s], local.at[0]),
-        pltpu.make_async_copy(wi_ref, wi_out.at[at.h], local.at[1]),
-        pltpu.make_async_copy(wo_ref, wo_out.at[at.h], local.at[2]),
+        pltpu.make_async_copy(own_s, n1_s.at[at.s], local.at[0]),
+        pltpu.make_async_copy(wi_ref, wi_s.at[at.h], local.at[1]),
+        pltpu.make_async_copy(wo_ref, wo_s.at[at.h], local.at[2]),
     ]
     for copy in keep:
         copy.start()
     send = Sent()
-    for n, (src, dst) in enumerate(weights):
-        for dy in steps:
-            send(src, dst.at[at.h], far, (n, dy), (at.s, at.along(dy)))
-        send(src, dst.at[at.h], near, (n, 0), at.sibling)
-
-    def branch(o0):
+
+    def send_weights():
+        for n, (src, dst) in enumerate(weights):
+            for dy in steps:
+                send(src, dst.at[at.h], w_far, (n, dy), (at.s, at.along(dy)))
+            send(src, dst.at[at.h], w_near, (n, 0), at.sibling)
+
+    send_weights()
+    channels = decay_ref.shape[0]
+    par_ref[...] = jnp.zeros(par_ref.shape, F32)
+    par_ref[0:4, :channels] = taps_ref[...].astype(F32)
+    for row, src in (
+        (CONV_B, conv_b_ref),
+        (RATE_B, rate_b_ref),
+        (ENTRY_B, entry_b_ref),
+        (DECAY, decay_ref),
+    ):
+        par_ref[row, :channels] = src[...]
+    gates_s[...] = jnp.zeros(gates_s.shape, F32)
+    block_width, blocks = rate_ref.shape[0], rate_ref.shape[1]
+    for gate, src in enumerate((rate_ref, entry_ref)):
+        for j in range(blocks):
+            top, lane = j * block_width, gate * width + j * block_width
+            gates_s[top : top + block_width, lane : lane + block_width] = src[:, j, :].astype(F32)
+    gates_ref[...] = gates_s[...].astype(BF16)
+
+    def project(d):
+        total = None
+        for k in range(shards):
+            lanes = slice(k * depth, (k + 1) * depth)
+            pair = jnp.concatenate([n1_s[d * inner + i, :, lanes] for i in range(inner)], axis=0)
+            term = dot(pair, wi_s[k])
+            total = term if total is None else total + term
+        proj_ref[d * inner * rows : (d + 1) * inner * rows, :] = total
+
+    def gather(o0):
         forward = Sent()
 
         def between(k):
@@ -515,111 +554,71 @@
             for n, (src, dst) in enumerate(weights):
                 for dy in steps:
                     source = at.along(-dy)
-                    received(src, dst.at[source], far, (n, dy), (at.s, source))
-                    forward(dst.at[source], dst.at[source], near, (n, dy), at.sibling)
-
-        line_gather(at, o0, x_ref, n_out, across, up, down, between)
+                    received(src, dst.at[source], w_far, (n, dy), (at.s, source))
+                    forward(dst.at[source], dst.at[source], w_near, (n, dy), at.sibling)
+            for n, (src, dst) in enumerate(weights):
+                for dy in range(at.ys):
+                    received(src, dst.at[at.along(-dy, 1)], w_near, (n, dy), at.sibling)
+            for copy in keep:
+                copy.wait()
+
+        def each(row):
+            project(row)
+
+        line_gather(at, o0, own_s, n1_s, g_across, g_up, g_down, between, each)
         forward.finish()
 
-    at.branches(branch)
-    for n, (src, dst) in enumerate(weights):
-        for dy in range(at.ys):
-            received(src, dst.at[at.along(-dy, 1)], near, (n, dy), at.sibling)
-    send.finish()
+    at.branches(gather)
+    send(cot_ref, cot_s, c_side, (), at.beside)
+    keep = [
+        pltpu.make_async_copy(n1_s, n1_out, local.at[0]),
+        pltpu.make_async_copy(wi_s, wi_out, local.at[1]),
+        pltpu.make_async_copy(wo_s, wo_out, local.at[2]),
+    ]
     for copy in keep:
-        copy.wait()
-
-
-def opening(x, w_in, w_out, outer, inner, shards, collective):
-    ys = shards // 2
-    return pl.pallas_call(
-        functools.partial(opening_kernel, outer, inner, shards),
-        out_shape=(
-            jax.ShapeDtypeStruct((outer * inner,) + x.shape, x.dtype),
-            jax.ShapeDtypeStruct((shards,) + w_in.shape, w_in.dtype),
-            jax.ShapeDtypeStruct((shards,) + w_out.shape, w_out.dtype),
-        ),
-        in_specs=[ANY] * 3,
-        out_specs=[ANY] * 3,
-        scratch_shapes=[DMA((3,))] + [DMA((2, outer))] * 3 + [DMA((2, 2, ys))] * 2,
-        compiler_params=pltpu.CompilerParams(collective_id=collective, has_side_effects=True),
-        cost_estimate=cost(55),
-        name="opening",
-    )(x, w_in, w_out)
-
-
-def row_rms(values):
-    return lax.rsqrt(jnp.mean(values * values, axis=-1, keepdims=True) + EPSILON)
-
-
-def rms_back(values, scale, gain, grad):
-    k = grad * gain
-    mean = jnp.mean(k * values, axis=-1, keepdims=True)
-    return scale * k - scale * scale * scale * values * mean
-
-
-def middle_kernel(
-    outer,
-    inner,
-    shards,
-    z_ref,
-    wo_ref,
-    x_ref,
-    gain_ref,
-    cot_ref,
-    cot_beside_ref,
-    mid_ref,
-    n2_out,
-    cot_out,
-    p_s,
-    n2_s,
-    x_in,
-    up_in,
-    down_in,
-    line_out,
-    across,
-    up,
-    down,
-    far,
-    near,
-    c_far,
-    c_near,
-    local,
-):
-    at = Place(outer, inner, shards)
+        copy.start()
+    run_scan(
+        parts, quarters, chunk, proj_ref, par_ref, gates_ref, z_ref, h_ref, v_ref, u_pad, a_s, b_s
+    )
+    made = (
+        (z_ref, z_out),
+        (h_ref, h_out),
+        (v_ref, v_out),
+        (proj_ref, proj_out),
+        (gates_ref, gates_out),
+    )
+    for n, (src, dst) in enumerate(made):
+        keep.append(pltpu.make_async_copy(src, dst, local.at[6 + n]))
+        keep[-1].start()
     line = LineSum(at, p_s, (x_in, up_in, down_in, line_out), (across, up, down))
-    steps = list(range(1, at.ys))
-    cols = wo_ref.shape[2]
-    greet_with_line(at, [at.sibling] + [at.near(q)[0] for q in range(1, at.chips)])
-    send = Sent()
-
-    def project(n, carry):
+
+    def back_project(n, carry):
         d = at.far_first(n)
+        some = pl.ds(pl.multiple_of(d * inner * rows, inner * rows), inner * rows)
         for k in range(shards):
-            block = dot(z_ref[d], wo_ref[k]).astype(BF16)
-            p_s[d, :, k * cols : (k + 1) * cols] = block
+            p_s[d, :, k * cols : (k + 1) * cols] = dot(z_ref[some, :], wo_s[k]).astype(BF16)
         line.cross(d).start()
         return carry
 
-    lax.fori_loop(0, outer, project, 0)
+    lax.fori_loop(0, outer, back_project, 0)
+    received(cot_ref, cot_s, c_side, (), at.beside)
 
     def slot(side, dy, other=0):
         i = 1 - at.i if side else at.i
         return cot_out.at[i * shards + at.along(dy, other)]
 
-    mine = (cot_ref, cot_beside_ref)
-    keep = []
+    mine = (cot_ref, cot_s)
     for side in range(2):
-        keep.append(pltpu.make_async_copy(mine[side], slot(side, 0), local.at[side]))
+        keep.append(pltpu.make_async_copy(mine[side], slot(side, 0), local.at[3 + side]))
         keep[-1].start()
         for dy in steps:
             send(mine[side], slot(side, 0), c_far, (side, dy), (at.s, at.along(dy)))
         send(mine[side], slot(side, 0), c_near, (side, 0), at.sibling)
 
-    def last_add(rows, total):
-        mid = x_ref[rows, :].astype(F32) + total
-        mid_ref[rows, :] = mid
-        n2_s[rows, :] = (mid * row_rms(mid) * gain_ref[...]).astype(BF16)
+    def last_add(some, total):
+        mid = x_ref[some, :].astype(F32) + total
+        mid_ref[some, :] = mid
+        own_s[some, :] = (mid * row_rms(mid) * gain2_ref[...]).astype(BF16)
 
     def branch(o0):
         forward = Sent()
@@ -638,18 +637,18 @@
 
     at.branches(branch)
     _, me = at.near(0)
-    keep.append(pltpu.make_async_copy(n2_s, n2_out.at[me], local.at[2]))
+    keep.append(pltpu.make_async_copy(own_s, n2_out.at[me], local.at[5]))
     keep[-1].start()
     for q in reversed(range(1, at.chips)):
-        send(n2_s, n2_out.at[me], far, (q,), at.near(q)[0])
-    send(n2_s, n2_out.at[me], near, (0,), at.sibling)
+        send(own_s, n2_out.at[me], far, (q,), at.near(q)[0])
+    send(own_s, n2_out.at[me], near, (0,), at.sibling)
     for q in range(1, at.chips):
         source, there = at.near(q, back=True)
         here = n2_out.at[there]
-        received(n2_s, here, far, (q,), source)
+        received(own_s, here, far, (q,), source)
         send(here, here, near, (q,), at.sibling)
     for q in range(at.chips):
-        received(n2_s, n2_out.at[at.near(q, 1, True)[1]], near, (q,), at.sibling)
+        received(own_s, n2_out.at[at.near(q, 1, True)[1]], near, (q,), at.sibling)
     for side in range(2):
         for dy in range(at.ys):
             received(cot_ref, slot(side, -dy, 1), c_near, (side, dy), at.sibling)
@@ -658,31 +657,77 @@
         copy.wait()
 
 
-def middle(z, w_out, x, gain, cot, cot_beside, outer, inner, shards, collective):
+def forward(
+    x,
+    gain1,
+    gain2,
+    channel,
+    rate,
+    entry,
+    cot,
+    w_in,
+    w_out,
+    quarters,
+    chunk,
+    outer,
+    inner,
+    shards,
+    collective,
+):
     rows, cols = x.shape
-    ys, chips = shards // 2, inner * shards // 2
+    parts, ys, chips = outer * inner, shards // 2, inner * shards // 2
+    length, width = parts * rows, w_in.shape[1] // 2
     bufs, sems = line_sum_scratch(outer, rows, cols)
     plane = jax.ShapeDtypeStruct((inner * shards, rows, cols), BF16)
+    lanes = pltpu.VMEM((width // LANES, length, LANES), F32)
+    made = (
+        ((length, width), BF16),
+        ((length, width), F32),
+        ((length, width), BF16),
+        ((length, 2 * width), F32),
+        ((width, 2 * width), BF16),
+    )
     return pl.pallas_call(
-        functools.partial(middle_kernel, outer, inner, shards),
-        out_shape=(jax.ShapeDtypeStruct((rows, cols), F32), plane, plane),
-        in_specs=[IN_VMEM] * 4 + [ANY] * 2,
-        out_specs=[IN_VMEM, ANY, ANY],
+        functools.partial(forward_kernel, outer, inner, shards, quarters, chunk),
+        out_shape=(
+            jax.ShapeDtypeStruct((8, width), F32),
+            jax.ShapeDtypeStruct((rows, cols), F32),
+            *[jax.ShapeDtypeStruct(shape, dtype) for shape, dtype in made],
+            jax.ShapeDtypeStruct((parts, rows, cols), BF16),
+            jax.ShapeDtypeStruct((shards,) + w_in.shape, BF16),
+            jax.ShapeDtypeStruct((shards,) + w_out.shape, BF16),
+            plane,
+            plane,
+        ),
+        in_specs=[IN_VMEM] * 11 + [IN_HBM] * 2,
+        out_specs=[IN_VMEM] * 2 + [IN_HBM] * 10,
         scratch_shapes=[
+            pltpu.VMEM((rows, cols), BF16),
+            pltpu.VMEM((parts, rows, cols), BF16),
+            pltpu.VMEM((shards,) + w_in.shape, BF16),
+            pltpu.VMEM((shards,) + w_out.shape, BF16),
+            pltpu.VMEM((width, 2 * width), F32),
+            pltpu.VMEM((length + 8, width), F32),
+            lanes,
+            lanes,
+            *[pltpu.VMEM(shape, dtype) for shape, dtype in made],
             pltpu.VMEM((outer, inner * rows, cols), BF16),
             pltpu.VMEM((rows, cols), BF16),
         ]
         + bufs
+        + [DMA((2, outer))] * 3
+        + [DMA((2, 2, ys))] * 2
         + sems
         + [DMA((2, chips))] * 2
+        + [DMA((2,))]
         + [DMA((2, 2, ys))] * 2
-        + [DMA((3,))],
+        + [DMA((11,))],
         compiler_params=pltpu.CompilerParams(
-            collective_id=collective, has_side_effects=True, vmem_limit_bytes=48 * 2**20
+            collective_id=collective, has_side_effects=True, vmem_limit_bytes=60 * 2**20
         ),
-        cost_estimate=cost(80),
-        name="middle",
-    )(z.reshape(outer, inner * rows, z.shape[1]), w_out, x, gain, cot, cot_beside)
+        cost_estimate=cost(140),
+        name="forward",
+    )(x, gain1, gain2, *channel, rate, entry, cot, w_in, w_out)
 
 
 class PlaneSum:
@@ -718,18 +763,21 @@
             self.at.near(q, 0, back)[0],
         )
 
+    def combine_one(self, k, own=None):
+        q = self.at.chips - 1 - k
+        self.to_sibling(q).wait_recv()
+        mine = self.block(q, 0) if own is None else own.at[q]
+
+        def add(rows):
+            total = mine[rows, :].astype(F32) + self.near_in[self.n, q, rows, :].astype(F32)
+            self.far_out[self.n, q, rows, :] = total.astype(BF16)
+
+        add_rows(self.rows, add)
+        self.onward(q).start()
+
     def combine(self, own=None):
         def one(k, carry):
-            q = self.at.chips - 1 - k
-            self.to_sibling(q).wait_recv()
-            mine = self.block(q, 0) if own is None else own.at[q]
-
-            def add(rows):
-                total = mine[rows, :].astype(F32) + self.near_in[self.n, q, rows, :].astype(F32)
-                self.far_out[self.n, q, rows, :] = total.astype(BF16)
-
-            add_rows(self.rows, add)
-            self.onward(q).start()
+            self.combine_one(k, own)
             return carry
 
         lax.fori_loop(0, self.at.chips - 1, one, 0)
@@ -840,7 +888,7 @@
         down.early(n, d, outer - 2)
         return carry
 
-    lax.fori_loop(0, outer, down_grad, 0)
+    down_grad(0, 0)
     load[1].wait()
     load[2].wait()
 
@@ -855,17 +903,20 @@
             block = block + dot(dum_ref[rows, :], wu_s[lanes, :], ((1,), (1,)))
             p_s[c, :, lanes] = block.astype(BF16)
         grad.to_sibling(q).start()
+        pl.when(k > 0)(lambda: grad.combine_one(k - 1))
         return carry
 
     lax.fori_loop(0, at.chips, back, 0)
-    grad.combine()
+    grad.to_sibling(0).wait_recv()
+    lax.fori_loop(1, outer, down_grad, 0)
     load[3].wait()
 
     cut = gate_own.shape[2]
 
     def keep_r(n):
         slot = lax.rem(n, 2)
-        return pltpu.make_async_copy(r_s.at[slot], rest_ref.at[at.far_first(n)], r_sem.at[slot])
+        there = rest_ref.at[at.far_first(n), :, : hidden - cut]
+        return pltpu.make_async_copy(r_s.at[slot], there, r_sem.at[slot])
 
     def gate_grad(n, carry):
         d = at.far_first(n)
@@ -920,9 +971,26 @@
     keep = pltpu.make_async_copy(dout_s, dout_ref.at[at.s], local.at[0])
     keep.start()
 
-    def keep_u(n):
-        slot = lax.rem(n, 2)
-        return pltpu.make_async_copy(u_s.at[slot], up_ref.at[at.far_first(n)], u_sem.at[slot])
+    head = u_s.shape[2] - up_ref.shape[2]
+
+    class keep_u:
+        def __init__(self, n):
+            slot, d = lax.rem(n, 2), at.far_first(n)
+            block = u_s.at[slot]
+            self.copies = (
+                pltpu.make_async_copy(
+                    block.at[:, :head], rest_ref.at[d, :, hidden - cut :], u_sem.at[0, slot]
+                ),
+                pltpu.make_async_copy(block.at[:, head:], up_ref.at[d], u_sem.at[1, slot]),
+            )
+
+        def start(self):
+            for copy in self.copies:
+                copy.start()
+
+        def wait(self):
+            for copy in self.copies:
+                copy.wait()
 
     def up_grad(n, carry):
         pl.when(n >= 2)(lambda: keep_u(n - 2).wait())
@@ -947,11 +1015,11 @@
                 lax.fori_loop(0, outer, up_grad, 0)
             if k == outer - 1:
                 down.absorb(o0, o0)
+            if k == outer and not ends:
+                for n in range(outer - 1):
+                    gate.step(o0, n)
 
         line_gather(at, o0, dout_s, dout_ref, across, up, low, between)
-        if not ends:
-            for n in range(outer - 1):
-                gate.step(o0, n)
         gate.absorb(o0, o0)
         down.finish(o0)
         gate.finish(o0)
@@ -990,11 +1058,11 @@
             jax.ShapeDtypeStruct((chips, 2 * rows, cols), BF16),
             jax.ShapeDtypeStruct((span, hidden), BF16),
             jax.ShapeDtypeStruct((span, cut), BF16),
-            jax.ShapeDtypeStruct((outer, span, hidden - cut), BF16),
-            jax.ShapeDtypeStruct((outer, span, hidden), BF16),
+            jax.ShapeDtypeStruct((outer, span, hidden - cut + LANES), BF16),
+            jax.ShapeDtypeStruct((outer, span, hidden - LANES), BF16),
         ),
-        in_specs=[IN_VMEM] * 6 + [ANY] * 5,
-        out_specs=[IN_VMEM] * 2 + [ANY] * 6,
+        in_specs=[IN_VMEM] * 6 + [IN_HBM] * 5,
+        out_specs=[IN_VMEM] * 2 + [IN_HBM] * 6,
         scratch_shapes=[
             pltpu.VMEM((chips, 2 * rows, cols), BF16),
             pltpu.VMEM((2, 2 * rows, cols), BF16),
@@ -1014,7 +1082,7 @@
         + [DMA((2, 1, chips))] * 2
         + [DMA((2, outer))] * 3
         + reduce_sems * 2
-        + [DMA((6,)), DMA((2,)), DMA((2,)), DMA((2,))],
+        + [DMA((6,)), DMA((2,)), DMA((2, 2)), DMA((2,))],
         compiler_params=pltpu.CompilerParams(
             collective_id=collective, has_side_effects=True, vmem_limit_bytes=60 * 2**20
         ),
@@ -1140,7 +1208,6 @@
     for q in range(at.chips):
         keep(q).wait()
     value.combine(q_s)
-    at.branches(functools.partial(rest_step, 0))
     log_scale = -DECAY_SCALE * softplus(-par_ref[DECAY : DECAY + 1, :])
     bias = jnp.concatenate(
         [par_ref[RATE_B : RATE_B + 1, :], par_ref[ENTRY_B : ENTRY_B + 1, :]], axis=1
@@ -1230,12 +1297,12 @@
             return carry
 
         lax.fori_loop(0, per, middle, 0)
-        if j == 3:
-            for n in range(1, outer - 1):
-                at.branches(functools.partial(rest_step, n))
-    at.branches(rest_last)
-    out = pltpu.make_async_copy(rest_own.at[at.o], rest_out, r_sem)
-    out.start()
+        if j == 2:
+            at.branches(functools.partial(rest_step, 0))
+        if j == SEGMENTS - 2:
+            at.branches(functools.partial(rest_step, 1))
+    for n in range(2, outer - 1):
+        at.branches(functools.partial(rest_step, n))
     sums_ref[0:8, :] = sums_ref[0:8, :] * (
         DECAY_SCALE * sigmoid(-par_ref[DECAY : DECAY + 1, :])
     )
@@ -1268,6 +1335,9 @@
 
     add_rows(span, output)
     value.finish()
+    at.branches(rest_last)
+    out = pltpu.make_async_copy(rest_own.at[at.o], rest_out, r_sem)
+    out.start()
     out.wait()
 
 
@@ -1309,8 +1379,8 @@
             jax.ShapeDtypeStruct((rows, cols), BF16),
             jax.ShapeDtypeStruct(rest.shape[1:], BF16),
         ),
-        in_specs=[ANY] + [IN_VMEM] * 7 + [ANY] * 2,
-        out_specs=[IN_VMEM] * 4 + [ANY],
+        in_specs=[IN_HBM] + [IN_VMEM] * 7 + [IN_HBM] * 2,
+        out_specs=[IN_VMEM] * 4 + [IN_HBM],
         scratch_shapes=[
             pltpu.VMEM((chips, rows, cols), BF16),
             buffers,
@@ -1730,7 +1800,7 @@
     bufs, sems = line_sum_scratch(outer, rows, cols)
     pieces = pltpu.VMEM((max(ys - 1, 1), parts, piece, 3 * width), BF16)
     stripes = pltpu.VMEM((2, parts * rows, cols // parts), BF16)
-    span, hidden = down.shape
+    span, hidden = ups.shape[1:]
 
     def swapped(array):
         shape = (inner * shards, span // (inner * shards), array.shape[-1])
@@ -1747,8 +1817,8 @@
             jax.ShapeDtypeStruct((1, lanes), F32),
             *[swapped(array) for array in (down, gate, rest, ups)],
         ),
-        in_specs=[IN_VMEM] * 9 + [ANY] * 6,
-        out_specs=[IN_VMEM] * 5 + [ANY] * 4,
+        in_specs=[IN_VMEM] * 9 + [IN_HBM] * 6,
+        out_specs=[IN_VMEM] * 5 + [IN_HBM] * 4,
         scratch_shapes=[
             pltpu.VMEM((outer, inner * rows, cols), BF16),
             *reduce_vmem,
@@ -1798,53 +1868,100 @@
     )
 
 
-def unpack_kernel(
-    inner,
-    channels,
-    gate_ref,
-    rest_ref,
-    up_ref,
-    down_ref,
-    mix_ref,
-    gate,
-    up,
-    down,
-    branch,
-    enter,
-    leave,
-):
-    slots, piece, hidden = up_ref.shape
+def unpack_kernel(inner, channels, block_width, *refs):
+    sources, targets = refs[:10], refs[10:27]
+    held, made, in_sem, out_sem = refs[27:36], refs[36:42], refs[42], refs[43]
+    gate_ref, rest_ref, up_ref, down_ref, mix_ref, blocks_ref, sums_ref = held[:7]
+    fetch = [
+        pltpu.make_async_copy(sources[k], held[k], in_sem.at[k]) for k in range(len(held))
+    ]
+    for copy in fetch:
+        copy.start()
+    store = []
+    gains_ref = sources[9]
+    rate, entry, taps, conv_b, rate_b, entry_b, decay, first_gain, second_gain = targets[8:]
+    for copy in fetch:
+        copy.wait()
+    for k in range(2):
+        copy = pltpu.make_async_copy(held[7 + k], targets[6 + k], out_sem.at[6 + k])
+        copy.start()
+        store.append(copy)
+    gate, up, down = made[:3]
+    slots, piece, hidden = down_ref.shape
     cut = gate_ref.shape[2]
+    tail = hidden - cut
+    head = hidden - up_ref.shape[2]
     shards = slots // inner
     parts, width = mix_ref.shape[0], mix_ref.shape[2] // 3
-    for i in range(inner):
-        for h in range(shards):
-            first = (h * inner + i) * hidden
-            slot = i * shards + h
-            gate[:, first : first + cut] = gate_ref[slot].astype(F32)
-            gate[:, first + cut : first + hidden] = rest_ref[slot].astype(F32)
-            up[:, first : first + hidden] = up_ref[slot].astype(F32)
-            down[:, first : first + hidden] = down_ref[slot].astype(F32)
-    for k, dst in enumerate((branch, enter, leave)):
+    places = [
+        ((h * inner + i) * hidden, i * shards + h) for i in range(inner) for h in range(shards)
+    ]
+
+    def ship(k):
+        copy = pltpu.make_async_copy(made[k], targets[k], out_sem.at[k])
+        copy.start()
+        store.append(copy)
+
+    for first, slot in places:
+        gate[:, first : first + cut] = gate_ref[slot].astype(F32)
+        gate[:, first + cut : first + hidden] = rest_ref[slot][:, :tail].astype(F32)
+    ship(0)
+    for first, slot in places:
+        up[:, first : first + head] = rest_ref[slot][:, tail:].astype(F32)
+        up[:, first + head : first + hidden] = up_ref[slot].astype(F32)
+    ship(1)
+    for first, slot in places:
+        down[:, first : first + hidden] = down_ref[slot].astype(F32)
+    ship(2)
+    for k in range(3):
         lanes = slice(k * width, k * width + width)
-        dst[...] = jnp.concatenate(
+        made[3 + k][...] = jnp.concatenate(
             [mix_ref[p][:, lanes].astype(F32)[:, :channels] for p in range(parts)], axis=1
         )
-
-
-def unpack(ffn_gate, ffn_rest, ffn_up, ffn_down, mix, inner, channels):
-    slots, piece, hidden = ffn_up.shape
+        ship(3 + k)
+    blocks = rate.shape[1]
+    tall = blocks_ref.shape[0] // (2 * blocks)
+    for k, dst in enumerate((rate, entry)):
+        for j in range(blocks):
+            top = (k * blocks + j) * tall
+            dst[:, j, :] = blocks_ref[top : top + block_width, :block_width]
+    taps[...] = sums_ref[4:8, :channels]
+    for row, dst in ((3, conv_b), (1, rate_b), (2, entry_b), (0, decay)):
+        dst[...] = sums_ref[row, :channels]
+    first_gain[...] = gains_ref[0, :piece]
+    second_gain[...] = gains_ref[0, piece : 2 * piece]
+    for copy in store:
+        copy.wait()
+
+
+def unpack(
+    gate, rest, up, down, mix, small, sums, result, grad, gains, inner, channels, blocks, block_width
+):
+    slots, piece, hidden = down.shape
     across = jax.ShapeDtypeStruct((piece, slots * hidden), F32)
     wide = jax.ShapeDtypeStruct((piece, mix.shape[0] * channels), F32)
+    square = jax.ShapeDtypeStruct((block_width, blocks, block_width), F32)
+    vector = jax.ShapeDtypeStruct((channels,), F32)
+    taps = jax.ShapeDtypeStruct((4, channels), F32)
+    gain = jax.ShapeDtypeStruct((piece,), F32)
+    held = (gate, rest, up, down, mix, small, sums, result, grad)
+    made = (across,) * 3 + (wide,) * 3
     return pl.pallas_call(
-        functools.partial(unpack_kernel, inner, channels),
-        out_shape=(across,) * 3 + (wide,) * 3,
-        in_specs=[IN_VMEM] * 5,
-        out_specs=[IN_VMEM] * 6,
-        compiler_params=pltpu.CompilerParams(vmem_limit_bytes=48 * 2**20),
-        cost_estimate=cost(4),
+        functools.partial(unpack_kernel, inner, channels, block_width),
+        out_shape=made
+        + tuple(jax.ShapeDtypeStruct(x.shape, x.dtype) for x in (result, grad))
+        + (square,) * 2
+        + (taps,)
+        + (vector,) * 4
+        + (gain,) * 2,
+        in_specs=[IN_HBM] * 9 + [IN_VMEM],
+        out_specs=[IN_HBM] * 8 + [IN_VMEM] * 9,
+        scratch_shapes=[pltpu.VMEM(x.shape, x.dtype) for x in held + made]
+        + [DMA((len(held),)), DMA((8,))],
+        compiler_params=pltpu.CompilerParams(vmem_limit_bytes=60 * 2**20),
+        cost_estimate=cost(5),
         name="unpack",
-    )(ffn_gate, ffn_rest, ffn_up, ffn_down, mix)
+    )(*held, gains)
 
 
 def body(
@@ -1887,43 +2004,27 @@
         pads[axis] = (0, spare)
         return jnp.pad(part, pads)
 
-    params = jnp.pad(
-        jnp.concatenate(
-            [
-                conv_weight.astype(F32),
-                conv_bias[None],
-                rate_bias[None],
-                entry_bias[None],
-                decay_param[None],
-            ],
-            axis=0,
-        ),
-        ((0, 0), (0, spare)),
-    )
-
     x = tokens.reshape(rows, model)
     cot = cotangent.reshape(rows, model)
     gain1, gain2 = first_gain[None], second_gain[None]
-    xs = x.astype(F32)
-    n1, w_in, w_out = opening(
-        (xs * row_rms(xs) * gain1).astype(BF16),
+    params, mid, z, h, v, proj, gates, n1, w_in, w_out, n2, cot_all = forward(
+        x,
+        gain1,
+        gain2,
+        (conv_weight, conv_bias, rate_bias, entry_bias, decay_param),
+        rate_weight.transpose(1, 0, 2),
+        entry_weight.transpose(1, 0, 2),
+        cot,
         jnp.concatenate([own(branch_weight, 1), own(input_weight, 1)], axis=1),
         own(output_weight, 0),
+        quarters,
+        chunk,
         outer,
         inner,
         shards,
         0,
     )
-    n1, cot = lax.optimization_barrier((n1, cot))
-    beside = [(o * inner + i, o * inner + 1 - i) for o in range(outer) for i in range(inner)]
-    cot_beside = lax.ppermute(cot, "seq", beside)
     w_in = w_in.reshape(model, 2 * width)
-    z, h, v, proj, gates = scan_forward(
-        quarters, chunk, n1, w_in, params, rate_weight, entry_weight
-    )
-    mid, n2, cot_all = middle(
-        z, w_out, x, gain2, cot, cot_beside, outer, inner, shards, 1
-    )
     n2 = n2.reshape(inner * shards * rows, model)
     cot_all = cot_all.reshape(inner * shards * rows, model)
     hidden = hidden_gate.shape[1] // inner
@@ -1953,7 +2054,7 @@
         outer,
         inner,
         shards,
-        2,
+        1,
     )
     both, small, sums, result, rest_sum = scan_backward(
         quarters,
@@ -1973,7 +2074,7 @@
         outer,
         inner,
         shards,
-        3,
+        2,
     )
     tokens_grad, mix, small, sums, gains, down_sum, gate_sum, rest_sum, up_sum = closing(
         both,
@@ -1994,33 +2095,60 @@
         outer,
         inner,
         shards,
-        4,
+        3,
     )
-    gains = gains[0]
-    gate_sum, up_sum, down_sum, branch_sum, input_sum, output_sum = unpack(
-        gate_sum, rest_sum, up_sum, down_sum, mix, inner, channels
+    (
+        gate_grad,
+        up_grad,
+        down_grad,
+        branch_grad,
+        input_grad,
+        output_grad,
+        result,
+        tokens_grad,
+        rate_grad,
+        entry_grad,
+        tap_grad,
+        conv_bias_grad,
+        rate_bias_grad,
+        entry_bias_grad,
+        decay_grad,
+        gain1_grad,
+        gain2_grad,
+    ) = unpack(
+        gate_sum,
+        rest_sum,
+        up_sum,
+        down_sum,
+        mix,
+        small,
+        sums,
+        result,
+        tokens_grad,
+        gains,
+        inner,
+        channels,
+        blocks,
+        block_width,
     )
-    sums = sums[:, :channels]
-    small = small.reshape(2, blocks, -1, small.shape[1])[:, :, :block_width, :block_width]
-    rate_grad, entry_grad = small[0], small[1]
     return (
         result.reshape(tokens.shape),
         tokens_grad.reshape(tokens.shape),
-        gains[:piece],
-        branch_sum,
-        input_sum,
-        sums[4:8],
-        sums[3],
-        rate_grad,
-        sums[1],
-        entry_grad,
-        sums[2],
-        sums[0],
-        output_sum.T,
-        gains[piece : 2 * piece],
-        gate_sum,
-        up_sum,
-        down_sum.T,
+        gain1_grad,
+        branch_grad,
+        input_grad,
+        tap_grad,
+        conv_bias_grad,
+        rate_grad.transpose(1, 0, 2),
+        rate_bias_grad,
+        entry_grad.transpose(1, 0, 2),
+        entry_bias_grad,
+        decay_grad,
+        output_grad.T,
+        gain2_grad,
+        gate_grad,
+        up_grad,
+        down_grad.T,
     )
 
 

time: 477 us -> 465 us (0.975); the launches traced: 476 us -> 458 us
  local copies, waits for them, and re-layouts: 17.3 us -> 4.36 us
    pallas_call x1, Pallas kernels: 39.2 us -> 52.9 us  [scan_backward(): pl.pallas_call(functools.partial(scan_backward_kernel, outer, inner, shar...]
    pallas_call x1, Pallas kernels: 115 us -> 104 us  [turn(): pl.pallas_call(functools.partial(turn_kernel, outer, inner, shards), out_...]
    pallas_call x1, Pallas kernels: 129 us -> 119 us  [closing(): pl.pallas_call(functools.partial(closing_kernel, outer, inner, shards), o...]
    unnamed x74 -> x16, local copies, waits for them, and re-layouts: 8.93 us -> 2.24 us
    pallas_call x4 -> x2, Pallas kernels: 153 us -> 159 us  [the longest x1 151 us: forward(): pl.pallas_call(functools.partial(forward_kernel, outer, inner, shards, qu...]
    slice x4 -> x0, local copies, waits for them, and re-layouts: 5.35 us -> none  [the longest x1 1.47 us: body(): sums[0]]
  transfers between devices with their start and end apart: 1 -> 0, of which waited for: 0 -> 0; matrix products, arithmetic and copies ran while one was open for 0% -> 0% of each run, Pallas kernels for 4% -> 0%
where the time goes in v5:
time: 465 us; the launch traced here: 458 us
  Pallas kernels  435 us (94%)
  matrix products  16.5 us (4%)
    pallas_call x1, Pallas kernels, forward(): pl.pallas_call(functools.partial(forward_kernel, outer, inner, shards, qu...  151 us
    pallas_call x1, Pallas kernels, closing(): pl.pallas_call(functools.partial(closing_kernel, outer, inner, shards), o...  119 us
    pallas_call x1, Pallas kernels, turn(): pl.pallas_call(functools.partial(turn_kernel, outer, inner, shards), out_...  104 us
    pallas_call x1, Pallas kernels, scan_backward(): pl.pallas_call(functools.partial(scan_backward_kernel, outer, inner, shar...  52.9 us
    dot_general x3, matrix products, dot(): lax.dot_general(left, right, (dims, ((), ())), preferred_element_type=F32)  16.5 us

profile of v5, /device:TPU:9, one launch (start us, length us, event | category | flops | bytes accessed | tf_op | source)
XLA Modules:
  0.0 457.8 jit_solution(663358848834879000)
XLA Ops:
  0.7 0.0 copy-start
  0.7 1.8 copy-done
  2.5 0.1 constant_dynamic-slice_fusion
  2.5 0.8 pad.13.wo_ref
  3.3 1.3 constant_dynamic-slice_fusion.1
  4.6 0.2 copy.39
  4.8 0.2 copy.38
  5.0 1.0 fusion.17.wi_ref
  6.0 151.2 %forward.1 = (f32[8,384]{1,0:T(8,128)}, f32[128,2048]{1,0:T(8,128)}, bf16[1024,384]{1,0:T(8,128)(2,1)}, f32[1024,384]{1,0:T(8,128)}, bf16[1024,384]{1,0:T(8,128)...) custom-call(bf16[128,2048]{1,0:T(8,128)(2,1)} %bitcast.38, ...), custom_call_target="tpu_custom_call" | custom-call | bytes 462000000 | tf_op jit(solution)/shard_map/forward/pallas_call | solution.py:690
  157.2 0.0 slice-start.1
  157.2 0.0 copy-start.2
  157.2 0.0 slice-start.2
  157.2 6.4 %fusion.13 = f32[1024,768]{1,0:T(8,128)S(1)} fusion(bf16[1024,2048]{1,0:T(8,128)(2,1)} %bitcast.32, bf16[1536,2048]{1,0:T(8,128)(2,1)} %wd_ref.1, s32[]{:T(128)S(6)} %select_n.5), kind=kOutput, calls=%fused_computation.18 | convolution fusion | flops 3221225472 | bytes 10485764 | tf_op jit(solution)/shard_map/dot_general | solution.py:32
  163.6 0.0 slice-done
  163.6 0.0 slice-start.3
  163.6 3.4 fusion.9
  167.1 0.0 slice-done.2
  167.1 0.0 slice-done.3
  167.1 6.7 %multiply_convert_fusion = (bf16[1024,768]{1,0:T(8,128)(2,1)}, bf16[1024,768]{1,0:T(8,128)(2,1)}, bf16[1024,768]{1,0:T(8,128)(2,1)}) fusion(f32[1024,768]{1,0:T(8,128)S(1)} %fusion.9, f32[1024,768]{1,0:T(8,128)S(1)} %fusion.13, bf16[1024,2048]{1,0:T(8,128)(2,1)S(1)} %bitcast.31, bf16[2048,1536]{1,0:T(8,128)(2,1)S(1)} %bitcast.28, s32[]{:T(128)S(6)} %select_n.5), kind=kOutput, calls=%fused_computation.10 | convolution fusion | flops 3240886272 | bytes 18350084 | tf_op jit(solution)/shard_map/dot_general | solution.py:32
  173.8 103.8 %turn.1 = (f32[128,2048]{1,0:T(8,128)}, f32[1,2048]{1,0:T(1,128)}, bf16[8,128,2048]{2,1,0:T(8,128)(2,1)}, bf16[4,256,2048]{2,1,0:T(8,128)(2,1)}, bf16[512,768]{1...) custom-call(bf16[1024,768]{1,0:T(8,128)(2,1)} %get-tuple-element.137.dgm_ref,, ...), custom_call_target="tpu_custom_call" | custom-call | bytes 363000000 | tf_op jit(solution)/shard_map/turn/pallas_call | solution.py:1052
  277.7 52.9 %scan_backward.1 = (bf16[1024,768]{1,0:T(8,128)(2,1)}, f32[704,256]{1,0:T(8,128)}, f32[8,384]{1,0:T(8,128)}, bf16[128,2048]{1,0:T(8,128)(2,1)}, bf16[512,512]{1,0:T(8,128)(2,1)}) custom-call(bf16[8,128,2048]{2,1,0:T(8,128)(2,1)} %get-tuple-element.71.dout_ref, bf16[4,384,512]{2,1,0:T(8,128)(2,1)} %get-tuple-element.72.wo_ref, ...), custom_call_target="tpu_custom_call" | custom-call | bytes 69300000 | tf_op jit(solution)/shard_map/scan_backward/pallas_call | solution.py:1371
  330.6 0.0 copy-start.1
  330.6 119.0 %closing.1 = (f32[128,2048]{1,0:T(8,128)}, bf16[8,64,1152]{2,1,0:T(8,128)(2,1)}, f32[704,256]{1,0:T(8,128)}, f32[8,384]{1,0:T(8,128)}, f32[1,128]{1,0:T(1,128)},...) custom-call(bf16[1024,768]{1,0:T(8,128)(2,1)} %get-tuple-element.80., ...), custom_call_target="tpu_custom_call" | custom-call | bytes 264000000 | tf_op jit(solution)/shard_map/closing/pallas_call | solution.py:1810
  449.7 7.6 %unpack.1 = (f32[64,6144]{1,0:T(8,128)}, f32[64,6144]{1,0:T(8,128)}, f32[64,6144]{1,0:T(8,128)}, f32[64,2736]{1,0:T(8,128)}, f32[64,2736]{1,0:T(8,128)}, /*index...) custom-call(bf16[8,64,384]{2,1,0:T(8,128)(2,1)} %get-tuple-element.9, ...), custom_call_target="tpu_custom_call" | custom-call | bytes 16500000 | tf_op jit(solution)/shard_map/unpack/pallas_call | solution.py:1949
  (6 shorter events, 0.0 us)
Async XLA Ops:
  0.7 1.8 copy-start
  6.0 157.6 %slice-start = ((s8[6291456]{0:T(1024)(128)(4,1)}), s8[2097152]{0:T(1024)(128)(4,1)S(1)}, s32[]{:S(2)}) async-start(s8[6291456]{0:T(1024)(128)(4,1)} %bitcast.25), calls=%async_computation | async-start | bytes 4194304
  157.2 6.4 %slice-start.1 = ((s8[6291456]{0:T(1024)(128)(4,1)}), s8[4194304]{0:T(1024)(128)(4,1)S(1)}, s32[]{:S(2)}) async-start(s8[6291456]{0:T(1024)(128)(4,1)} %bitcast.25), calls=%async_computation.1 | async-start | bytes 8388608
  157.2 6.4 %copy-start.2 = (bf16[8,128,2048]{2,1,0:T(8,128)(2,1)S(1)}, bf16[8,128,2048]{2,1,0:T(8,128)(2,1)}, u32[]{:S(2)}) copy-start(bf16[8,128,2048]{2,1,0:T(8,128)(2,1)} %get-tuple-element.69) | copy-start | bytes 12582916
  157.2 9.9 %slice-start.2 = ((s8[6291456]{0:T(1024)(128)(4,1)}), s8[4194304]{0:T(1024)(128)(4,1)S(1)}, s32[]{:S(2)}) async-start(s8[6291456]{0:T(1024)(128)(4,1)} %bitcast.27), calls=%async_computation.2 | async-start | bytes 8388608
  163.6 3.4 slice-start.3
  330.6 126.7 %copy-start.1 = (bf16[2736,512]{1,0:T(8,128)(2,1)S(1)}, bf16[2736,512]{1,0:T(8,128)(2,1)}, u32[]{:S(2)}) copy-start(bf16[2736,512]{1,0:T(8,128)(2,1)} %param.28) | copy-start | bytes 8404996

commit v6 on v5

--- a/solution.py
+++ b/solution.py
@@ -174,90 +174,207 @@
 
 
 def line_gather(
-    at, o0, x_ref, out, across, up, down, between=lambda k: None, each=lambda row: None
+    at,
+    o0,
+    x_ref,
+    out,
+    across,
+    up,
+    down,
+    between=lambda k: None,
+    each=lambda row: None,
+    side=None,
+    slim=0,
 ):
     send = Sent()
-
-    def slot(row):
-        return out.at[row * at.inner + at.i]
-
-    def pass_on(row, sems, to):
-        send(x_ref if row == o0 else slot(row), slot(row), sems, (row,), to)
+    rows = x_ref.shape[0]
+    half = rows // HALVES
+    low = pl.ds(rows - slim, slim)
+
+    def slot(row, other=False):
+        return out.at[row * at.inner + (1 - at.i if other else at.i)]
+
+    def some(row, part):
+        less = slim if slim and row != o0 and part == HALVES - 1 else 0
+        return pl.ds(part * half, half - less)
+
+    def pass_on(row, part, sems, to):
+        some_rows = pl.ds(part * half, half)
+        src = x_ref if row == o0 else slot(row)
+        send(src.at[some_rows], slot(row).at[some_rows], sems, (row, part), to)
+
+    def cross(row, part):
+        src = x_ref if row == o0 else slot(row)
+        send(src.at[some(row, part)], slot(row).at[some(row, part)], across, (row, part), at.beside)
+
+    def crossed(row):
+        for part in range(HALVES):
+            here = slot(row, True).at[some(row, part)]
+            received(here, here, across, (row, part), at.beside)
+
+    def slim_on(row):
+        here = slot(row, True).at[low]
+        if row <= o0 < at.outer - 1:
+            send(here, here, side[0], (row,), at.above)
+        if row >= o0 > 0:
+            send(here, here, side[1], (row,), at.below)
+
+    def slim_came(row, sems, source):
+        here = slot(row, True).at[low]
+        received(here, here, sems, (row,), source)
 
     for k in range(at.outer):
         lower, upper = o0 - k, o0 + k
-        if k > 0 and lower >= 0:
-            received(x_ref, slot(lower), up, (lower,), at.below)
-        if lower >= 0 and o0 < at.outer - 1:
-            pass_on(lower, up, at.above)
-        if lower >= 0:
-            pass_on(lower, across, at.beside)
-        if k > 0 and upper < at.outer:
-            received(x_ref, slot(upper), down, (upper,), at.above)
-        if upper < at.outer and o0 > 0:
-            pass_on(upper, down, at.below)
-        if k > 0 and upper < at.outer:
-            pass_on(upper, across, at.beside)
+        for part in range(HALVES):
+            here = x_ref.at[pl.ds(part * half, half)]
+            if lower >= 0:
+                if k > 0:
+                    received(here, here, up, (lower, part), at.below)
+                if o0 < at.outer - 1:
+                    pass_on(lower, part, up, at.above)
+                cross(lower, part)
+            if upper < at.outer:
+                if k > 0:
+                    received(here, here, down, (upper, part), at.above)
+                if o0 > 0:
+                    pass_on(upper, part, down, at.below)
+                if k > 0:
+                    cross(upper, part)
+        if slim and k == 1:
+            crossed(o0)
+            slim_on(o0)
+        if slim and k > 1:
+            for row, sems, source in (
+                (o0 - k + 1, side[0], at.below),
+                (o0 + k - 1, side[1], at.above),
+            ):
+                if 0 <= row < at.outer:
+                    slim_came(row, sems, source)
+                    slim_on(row)
         between(k)
     between(at.outer)
     for row in sorted(range(at.outer), key=lambda row: abs(row - o0)):
-        received(x_ref, out.at[row * at.inner + 1 - at.i], across, (row,), at.beside)
+        if row != o0 or not slim:
+            crossed(row)
+        if slim and row != o0 and abs(row - o0) == at.outer - 1:
+            slim_came(row, side[0] if row < o0 else side[1], at.below if row < o0 else at.above)
         each(row)
     send.finish()
 
 
 class LineSum:
-    def __init__(self, at, p, bufs, sems):
+    def __init__(self, at, p, bufs, sems, side=None):
         self.at, self.p = at, p
         self.x_in, self.up_in, self.down_in, self.sums = bufs
         self.across, self.up, self.down = sems
         self.rows = self.x_in.shape[1]
+        self.slim = 0
+        if side is not None:
+            self.s_up_in, self.s_down_in, self.s_sums, self.s_in = side[:4]
+            self.s_up, self.s_down, self.s_across = side[4:]
+            self.slim = self.s_in.shape[0]
 
     def block(self, d, i):
         return self.p.at[d, pl.ds(pl.multiple_of(i * self.rows, self.rows), self.rows)]
 
-    def cross(self, d):
+    def cross(self, d, part):
+        half = self.rows // HALVES
+        some = pl.ds(part * half, half - (self.slim if part == HALVES - 1 else 0))
         return remote(
-            self.block(d, 1 - self.at.i),
-            self.x_in.at[d],
-            self.across.at[0, d],
-            self.across.at[1, d],
+            self.block(d, 1 - self.at.i).at[some],
+            self.x_in.at[d].at[some],
+            self.across.at[0, d, part],
+            self.across.at[1, d, part],
             self.at.beside,
         )
 
+    def start(self, d):
+        for part in range(HALVES):
+            self.cross(d, part).start()
+
     def steps(self, o0, last_add, between=lambda n: None):
-        at = self.at
+        at, rows, slim = self.at, self.rows, self.slim
         send = Sent()
         order = sorted(range(at.outer), key=lambda d: (-abs(d - o0), d))
+        low, half = rows - slim, rows // HALVES
+
+        def arrivals(d, index, mine, up_in, down_in, up, down):
+            terms = []
+            if d >= o0 > 0:
+                received(mine, mine, up, index, at.below)
+                terms.append(up_in.at[d])
+            if d <= o0 < at.outer - 1:
+                received(mine, mine, down, index, at.above)
+                terms.append(down_in.at[d])
+            return terms
+
+        def total_of(terms, some):
+            total = terms[0][some, :].astype(F32)
+            for term in terms[1:]:
+                total = total + term[some, :].astype(F32)
+            return total
+
         for n, d in enumerate(order):
             mine = self.block(d, at.i)
-            self.cross(d).wait_recv()
-            terms = [mine, self.x_in.at[d]]
-            if d >= o0 > 0:
-                received(mine, self.up_in.at[d], self.up, (d,), at.below)
-                terms.append(self.up_in.at[d])
-            if d <= o0 < at.outer - 1:
-                received(mine, self.down_in.at[d], self.down, (d,), at.above)
-                terms.append(self.down_in.at[d])
             target = self.sums.at[d]
-
-            def add(rows, terms=terms, target=target, d=d):
-                total = terms[0][rows, :].astype(F32)
-                for term in terms[1:]:
-                    total = total + term[rows, :].astype(F32)
+            for part in range(HALVES):
+                part_rows = pl.ds(part * half, half)
+                self.cross(d, part).wait_recv()
+                along = [mine] + arrivals(
+                    d,
+                    (d, part),
+                    mine.at[part_rows],
+                    self.up_in,
+                    self.down_in,
+                    self.up,
+                    self.down,
+                )
+                both = along + [self.x_in.at[d]]
+
+                def add(some, both=both, target=target, d=d):
+                    total = total_of(both, some)
+                    if d == o0:
+                        last_add(some, total)
+                    else:
+                        target[some, :] = total.astype(BF16)
+
+                def add_low(some, along=along, target=target):
+                    target[some, :] = total_of(along, some).astype(BF16)
+
+                add_rows(min((part + 1) * half, low), add, part * half)
+                if slim and d != o0 and part == HALVES - 1:
+                    add_rows(rows, add_low, low)
+                if d > o0:
+                    here, there = target.at[part_rows], self.up_in.at[d].at[part_rows]
+                    send(here, there, self.up, (d, part), at.above)
+                if d < o0:
+                    here, there = target.at[part_rows], self.down_in.at[d].at[part_rows]
+                    send(here, there, self.down, (d, part), at.below)
+            if slim:
+                theirs = self.block(d, 1 - at.i).at[pl.ds(low, slim)]
+                extra = [theirs] + arrivals(
+                    d, (d,), theirs, self.s_up_in, self.s_down_in, self.s_up, self.s_down
+                )
+                aside = self.s_sums.at[d]
+
+                def add_aside(some, extra=extra, aside=aside):
+                    aside[some, :] = total_of(extra, some).astype(BF16)
+
+                add_rows(slim, add_aside)
+                if d > o0:
+                    send(aside, self.s_up_in.at[d], self.s_up, (d,), at.above)
+                if d < o0:
+                    send(aside, self.s_down_in.at[d], self.s_down, (d,), at.below)
                 if d == o0:
-                    last_add(rows, total)
-                else:
-                    target[rows, :] = total.astype(target.dtype)
-
-            add_rows(self.rows, add)
-            if d > o0:
-                send(target, self.up_in.at[d], self.up, (d,), at.above)
-            if d < o0:
-                send(target, self.down_in.at[d], self.down, (d,), at.below)
+                    send(aside, self.s_in, self.s_across, (), at.beside)
+                    received(aside, self.s_in, self.s_across, (), at.beside)
+                    for k in range(slim // 16):
+                        some, here = pl.ds(low + 16 * k, 16), pl.ds(16 * k, 16)
+                        last_add(some, total_of(along, some) + self.s_in[here, :].astype(F32))
             between(n)
         for d in range(at.outer):
-            self.cross(d).wait_send()
+            for part in range(HALVES):
+                self.cross(d, part).wait_send()
         send.finish()
 
 
@@ -338,8 +455,17 @@
     return blocks, [DMA((2, outer))] * 2
 
 
+SLIM = 16
+HALVES = 2
+
+
+def slim_scratch(outer, cols):
+    blocks = [pltpu.VMEM((outer, SLIM, cols), BF16)] * 3 + [pltpu.VMEM((SLIM, cols), BF16)]
+    return blocks, [DMA((2, outer))] * 2 + [DMA((2,))]
+
+
 def line_sum_scratch(outer, rows, cols):
-    return [pltpu.VMEM((outer, rows, cols), BF16)] * 4, [DMA((2, outer))] * 3
+    return [pltpu.VMEM((outer, rows, cols), BF16)] * 4, [DMA((2, outer, HALVES))] * 3
 
 
 def row_rms(values):
@@ -488,6 +614,15 @@
     c_far,
     c_near,
     local,
+    s_up_in,
+    s_down_in,
+    s_sums,
+    s_in,
+    s_up,
+    s_down,
+    s_across,
+    g_side_up,
+    g_side_down,
 ):
     at = Place(outer, inner, shards)
     parts, rows = at.parts, x_ref.shape[0]
@@ -518,23 +653,24 @@
             send(src, dst.at[at.h], w_near, (n, 0), at.sibling)
 
     send_weights()
-    channels = decay_ref.shape[0]
-    par_ref[...] = jnp.zeros(par_ref.shape, F32)
-    par_ref[0:4, :channels] = taps_ref[...].astype(F32)
-    for row, src in (
-        (CONV_B, conv_b_ref),
-        (RATE_B, rate_b_ref),
-        (ENTRY_B, entry_b_ref),
-        (DECAY, decay_ref),
-    ):
-        par_ref[row, :channels] = src[...]
-    gates_s[...] = jnp.zeros(gates_s.shape, F32)
-    block_width, blocks = rate_ref.shape[0], rate_ref.shape[1]
-    for gate, src in enumerate((rate_ref, entry_ref)):
-        for j in range(blocks):
-            top, lane = j * block_width, gate * width + j * block_width
-            gates_s[top : top + block_width, lane : lane + block_width] = src[:, j, :].astype(F32)
-    gates_ref[...] = gates_s[...].astype(BF16)
+    def build_gates():
+        channels = decay_ref.shape[0]
+        par_ref[...] = jnp.zeros(par_ref.shape, F32)
+        par_ref[0:4, :channels] = taps_ref[...].astype(F32)
+        for row, src in (
+            (CONV_B, conv_b_ref),
+            (RATE_B, rate_b_ref),
+            (ENTRY_B, entry_b_ref),
+            (DECAY, decay_ref),
+        ):
+            par_ref[row, :channels] = src[...]
+        gates_s[...] = jnp.zeros(gates_s.shape, F32)
+        block_width, blocks = rate_ref.shape[0], rate_ref.shape[1]
+        for gate, src in enumerate((rate_ref, entry_ref)):
+            for j in range(blocks):
+                top, lane = j * block_width, gate * width + j * block_width
+                gates_s[top : top + block_width, lane : lane + block_width] = src[:, j, :].astype(F32)
+        gates_ref[...] = gates_s[...].astype(BF16)
 
     def project(d):
         total = None
@@ -549,7 +685,9 @@
         forward = Sent()
 
         def between(k):
-            if k != 1:
+            if k == 0:
+                build_gates()
+            if k != outer - 1:
                 return
             for n, (src, dst) in enumerate(weights):
                 for dy in steps:
@@ -565,7 +703,8 @@
         def each(row):
             project(row)
 
-        line_gather(at, o0, own_s, n1_s, g_across, g_up, g_down, between, each)
+        side = (g_side_up, g_side_down)
+        line_gather(at, o0, own_s, n1_s, g_across, g_up, g_down, between, each, side, SLIM)
         forward.finish()
 
     at.branches(gather)
@@ -590,14 +729,15 @@
     for n, (src, dst) in enumerate(made):
         keep.append(pltpu.make_async_copy(src, dst, local.at[6 + n]))
         keep[-1].start()
-    line = LineSum(at, p_s, (x_in, up_in, down_in, line_out), (across, up, down))
+    side = (s_up_in, s_down_in, s_sums, s_in, s_up, s_down, s_across)
+    line = LineSum(at, p_s, (x_in, up_in, down_in, line_out), (across, up, down), side)
 
     def back_project(n, carry):
         d = at.far_first(n)
         some = pl.ds(pl.multiple_of(d * inner * rows, inner * rows), inner * rows)
         for k in range(shards):
             p_s[d, :, k * cols : (k + 1) * cols] = dot(z_ref[some, :], wo_s[k]).astype(BF16)
-        line.cross(d).start()
+        line.start(d)
         return carry
 
     lax.fori_loop(0, outer, back_project, 0)
@@ -639,14 +779,24 @@
     _, me = at.near(0)
     keep.append(pltpu.make_async_copy(own_s, n2_out.at[me], local.at[5]))
     keep[-1].start()
-    for q in reversed(range(1, at.chips)):
+    quad = inner == 2 and at.ys == 2
+    for q in (1, 2) if quad else reversed(range(1, at.chips)):
         send(own_s, n2_out.at[me], far, (q,), at.near(q)[0])
     send(own_s, n2_out.at[me], near, (0,), at.sibling)
-    for q in range(1, at.chips):
+    for q in (1, 2) if quad else range(1, at.chips):
         source, there = at.near(q, back=True)
         here = n2_out.at[there]
         received(own_s, here, far, (q,), source)
+        if quad:
+            half = here.at[pl.ds((2 - q) * (rows // 2), rows // 2)]
+            send(half, half, far, (3 if q == 2 else 0,), at.near(3 - q)[0])
         send(here, here, near, (q,), at.sibling)
+    if quad:
+        here = n2_out.at[at.near(3)[1]]
+        for q in (1, 2):
+            half = here.at[pl.ds((q - 1) * (rows // 2), rows // 2)]
+            received(half, half, far, (3 if q == 1 else 0,), at.near(q)[0])
+        send(here, here, near, (3,), at.sibling)
     for q in range(at.chips):
         received(own_s, n2_out.at[at.near(q, 1, True)[1]], near, (q,), at.sibling)
     for side in range(2):
@@ -678,6 +828,7 @@
     parts, ys, chips = outer * inner, shards // 2, inner * shards // 2
     length, width = parts * rows, w_in.shape[1] // 2
     bufs, sems = line_sum_scratch(outer, rows, cols)
+    side_vmem, side_sems = slim_scratch(outer, cols)
     plane = jax.ShapeDtypeStruct((inner * shards, rows, cols), BF16)
     lanes = pltpu.VMEM((width // LANES, length, LANES), F32)
     made = (
@@ -715,13 +866,16 @@
             pltpu.VMEM((rows, cols), BF16),
         ]
         + bufs
-        + [DMA((2, outer))] * 3
+        + [DMA((2, outer, HALVES))] * 3
         + [DMA((2, 2, ys))] * 2
         + sems
         + [DMA((2, chips))] * 2
         + [DMA((2,))]
         + [DMA((2, 2, ys))] * 2
-        + [DMA((11,))],
+        + [DMA((11,))]
+        + side_vmem
+        + side_sems
+        + [DMA((2, outer))] * 2,
         compiler_params=pltpu.CompilerParams(
             collective_id=collective, has_side_effects=True, vmem_limit_bytes=60 * 2**20
         ),
@@ -1080,7 +1234,7 @@
         + down_vmem
         + gate_vmem
         + [DMA((2, 1, chips))] * 2
-        + [DMA((2, outer))] * 3
+        + [DMA((2, outer, HALVES))] * 3
         + reduce_sems * 2
         + [DMA((6,)), DMA((2,)), DMA((2, 2)), DMA((2,))],
         compiler_params=pltpu.CompilerParams(
@@ -1420,12 +1574,21 @@
     )
 
 
-def add_rows(rows, fn):
+def add_rows(rows, fn, start=0):
     def one(k, carry):
         fn(pl.ds(pl.multiple_of(k * 16, 16), 16))
         return carry
 
-    lax.fori_loop(0, rows // 16, one, 0)
+    lax.fori_loop(start // 16, rows // 16, one, 0)
+
+
+def fetch(pairs, sems):
+    copies = [
+        pltpu.make_async_copy(src, dst, sems.at[k]) for k, (src, dst) in enumerate(pairs)
+    ]
+    for copy in copies:
+        copy.start()
+    return copies
 
 
 class PlaneExchange:
@@ -1568,7 +1731,7 @@
         for lane in range(0, model, tile):
             lanes = slice(lane, lane + tile)
             p_s[d, :, lanes] = dot(both_ref[rows, :], wi_ref[lanes, :], ((1,), (1,))).astype(BF16)
-        line.cross(d).start()
+        line.start(d)
         return carry
 
     lax.fori_loop(0, outer, back, 0)

time: 465 us -> 450 us (0.968)
  Pallas kernels: 435 us -> 419 us
    pallas_call x1, Pallas kernels: 151 us -> 140 us  [forward(): pl.pallas_call(functools.partial(forward_kernel, outer, inner, shards, qu...]
where the time goes in v6:
time: 450 us; the launch traced here: 442 us
  Pallas kernels  419 us (93%)
  matrix products  16.5 us (4%)
    pallas_call x1, Pallas kernels, forward(): pl.pallas_call(functools.partial(forward_kernel, outer, inner, shards, qu...  140 us
    pallas_call x1, Pallas kernels, closing(): pl.pallas_call(functools.partial(closing_kernel, outer, inner, shards), o...  118 us
    pallas_call x1, Pallas kernels, turn(): pl.pallas_call(functools.partial(turn_kernel, outer, inner, shards), out_...  104 us
    pallas_call x1, Pallas kernels, scan_backward(): pl.pallas_call(functools.partial(scan_backward_kernel, outer, inner, shar...  49.5 us
    dot_general x3, matrix products, dot(): lax.dot_general(left, right, (dims, ((), ())), preferred_element_type=F32)  16.5 us

profile of v6, /device:TPU:9, one launch (start us, length us, event | category | flops | bytes accessed | tf_op | source)
XLA Modules:
  0.0 441.9 jit_solution(11533136172984206772)
XLA Ops:
  0.7 0.0 copy-start
  0.7 1.8 copy-done
  2.5 0.1 constant_dynamic-slice_fusion
  2.5 0.8 pad.13.wo_ref
  3.3 1.3 constant_dynamic-slice_fusion.1
  4.6 0.2 copy.39
  4.8 0.2 copy.38
  5.0 1.0 fusion.17.wi_ref
  6.0 139.7 %forward.1 = (f32[8,384]{1,0:T(8,128)}, f32[128,2048]{1,0:T(8,128)}, bf16[1024,384]{1,0:T(8,128)(2,1)}, f32[1024,384]{1,0:T(8,128)}, bf16[1024,384]{1,0:T(8,128)...) custom-call(bf16[128,2048]{1,0:T(8,128)(2,1)} %bitcast.38, ...), custom_call_target="tpu_custom_call" | custom-call | bytes 462000000 | tf_op jit(solution)/shard_map/forward/pallas_call | solution.py:841
  145.7 0.0 slice-start.1
  145.7 0.0 slice-start.2
  145.7 6.4 %fusion.13 = f32[1024,768]{1,0:T(8,128)S(1)} fusion(bf16[1024,2048]{1,0:T(8,128)(2,1)} %bitcast.32, bf16[1536,2048]{1,0:T(8,128)(2,1)} %wd_ref.1, s32[]{:T(128)S(6)} %select_n.5), kind=kOutput, calls=%fused_computation.18 | convolution fusion | flops 3221225472 | bytes 10485764 | tf_op jit(solution)/shard_map/dot_general | solution.py:32
  152.1 0.0 slice-done
  152.1 0.0 slice-done.1
  152.1 0.0 copy-done.2
  152.1 0.0 slice-start.3
  152.1 3.4 fusion.9
  155.6 6.7 %multiply_convert_fusion = (bf16[1024,768]{1,0:T(8,128)(2,1)}, bf16[1024,768]{1,0:T(8,128)(2,1)}, bf16[1024,768]{1,0:T(8,128)(2,1)}) fusion(f32[1024,768]{1,0:T(8,128)S(1)} %fusion.9, f32[1024,768]{1,0:T(8,128)S(1)} %fusion.13, bf16[1024,2048]{1,0:T(8,128)(2,1)S(1)} %bitcast.31, bf16[2048,1536]{1,0:T(8,128)(2,1)S(1)} %bitcast.28, s32[]{:T(128)S(6)} %select_n.5), kind=kOutput, calls=%fused_computation.10 | convolution fusion | flops 3240886272 | bytes 18350084 | tf_op jit(solution)/shard_map/dot_general | solution.py:32
  162.3 104.2 %turn.1 = (f32[128,2048]{1,0:T(8,128)}, f32[1,2048]{1,0:T(1,128)}, bf16[8,128,2048]{2,1,0:T(8,128)(2,1)}, bf16[4,256,2048]{2,1,0:T(8,128)(2,1)}, bf16[512,768]{1...) custom-call(bf16[1024,768]{1,0:T(8,128)(2,1)} %get-tuple-element.137.dgm_ref,, ...), custom_call_target="tpu_custom_call" | custom-call | bytes 363000000 | tf_op jit(solution)/shard_map/turn/pallas_call | solution.py:1206
  266.6 49.5 %scan_backward.1 = (bf16[1024,768]{1,0:T(8,128)(2,1)}, f32[704,256]{1,0:T(8,128)}, f32[8,384]{1,0:T(8,128)}, bf16[128,2048]{1,0:T(8,128)(2,1)}, bf16[512,512]{1,0:T(8,128)(2,1)}) custom-call(bf16[8,128,2048]{2,1,0:T(8,128)(2,1)} %get-tuple-element.71.dout_ref, bf16[4,384,512]{2,1,0:T(8,128)(2,1)} %get-tuple-element.72.wo_ref, ...), custom_call_target="tpu_custom_call" | custom-call | bytes 69300000 | tf_op jit(solution)/shard_map/scan_backward/pallas_call | solution.py:1525
  316.1 0.0 copy-start.1
  316.1 117.7 %closing.1 = (f32[128,2048]{1,0:T(8,128)}, bf16[8,64,1152]{2,1,0:T(8,128)(2,1)}, f32[704,256]{1,0:T(8,128)}, f32[8,384]{1,0:T(8,128)}, f32[1,128]{1,0:T(1,128)},...) custom-call(bf16[1024,768]{1,0:T(8,128)(2,1)} %get-tuple-element.80., ...), custom_call_target="tpu_custom_call" | custom-call | bytes 264000000 | tf_op jit(solution)/shard_map/closing/pallas_call | solution.py:1973
  433.8 7.6 %unpack.1 = (f32[64,6144]{1,0:T(8,128)}, f32[64,6144]{1,0:T(8,128)}, f32[64,6144]{1,0:T(8,128)}, f32[64,2736]{1,0:T(8,128)}, f32[64,2736]{1,0:T(8,128)}, /*index...) custom-call(bf16[8,64,384]{2,1,0:T(8,128)(2,1)} %get-tuple-element.9, ...), custom_call_target="tpu_custom_call" | custom-call | bytes 16500000 | tf_op jit(solution)/shard_map/unpack/pallas_call | solution.py:2112
  441.4 0.0 copy-done.1
  (6 shorter events, 0.0 us)
Async XLA Ops:
  0.7 1.8 copy-start
  6.0 146.1 %slice-start = ((s8[6291456]{0:T(1024)(128)(4,1)}), s8[2097152]{0:T(1024)(128)(4,1)S(1)}, s32[]{:S(2)}) async-start(s8[6291456]{0:T(1024)(128)(4,1)} %bitcast.25), calls=%async_computation | async-start | bytes 4194304
  145.7 6.4 %slice-start.1 = ((s8[6291456]{0:T(1024)(128)(4,1)}), s8[4194304]{0:T(1024)(128)(4,1)S(1)}, s32[]{:S(2)}) async-start(s8[6291456]{0:T(1024)(128)(4,1)} %bitcast.25), calls=%async_computation.1 | async-start | bytes 8388608
  145.7 6.4 %copy-start.2 = (bf16[8,128,2048]{2,1,0:T(8,128)(2,1)S(1)}, bf16[8,128,2048]{2,1,0:T(8,128)(2,1)}, u32[]{:S(2)}) copy-start(bf16[8,128,2048]{2,1,0:T(8,128)(2,1)} %get-tuple-element.69) | copy-start | bytes 12582916
  145.7 9.9 %slice-start.2 = ((s8[6291456]{0:T(1024)(128)(4,1)}), s8[4194304]{0:T(1024)(128)(4,1)S(1)}, s32[]{:S(2)}) async-start(s8[6291456]{0:T(1024)(128)(4,1)} %bitcast.27), calls=%async_computation.2 | async-start | bytes 8388608
  152.1 3.5 slice-start.3
  316.1 125.3 %copy-start.1 = (bf16[2736,512]{1,0:T(8,128)(2,1)S(1)}, bf16[2736,512]{1,0:T(8,128)(2,1)}, u32[]{:S(2)}) copy-start(bf16[2736,512]{1,0:T(8,128)(2,1)} %param.28) | copy-start | bytes 8404996

commit v7 on v6

--- a/solution.py
+++ b/solution.py
@@ -960,11 +960,11 @@
     outer,
     inner,
     shards,
-    dgm_ref,
-    dum_ref,
-    mm_ref,
-    mid_ref,
-    cot_ref,
+    dgm_from,
+    dum_from,
+    mm_from,
+    mid_from,
+    cot_from,
     gain_ref,
     wg_ref,
     wu_ref,
@@ -979,6 +979,12 @@
     gate_ref,
     rest_ref,
     up_ref,
+    mm_ref,
+    dgm_ref,
+    dum_ref,
+    mid_ref,
+    cot_ref,
+    early_sem,
     p_s,
     q_s,
     dout_s,
@@ -1017,6 +1023,7 @@
     pair = p_s.shape[1]
     span = model // outer
     own = pl.ds(pl.multiple_of(at.i * hidden, hidden), hidden)
+    first = load_all([(mm_from, mm_ref)], early_sem)
     load = [
         pltpu.make_async_copy(cots_ref, cots_s, local.at[1]),
         pltpu.make_async_copy(wg_ref.at[:, own], wg_s, local.at[2]),
@@ -1024,8 +1031,12 @@
         pltpu.make_async_copy(n2_ref, n2_s, local.at[4]),
         pltpu.make_async_copy(wd_ref.at[own, :], wd_s, local.at[5]),
     ]
-    for copy in load:
+    for copy in load[:3]:
         copy.start()
+    second = load_all([(dgm_from, dgm_ref), (dum_from, dum_ref)], early_sem.at[pl.ds(1, 2)])
+    for copy in load[3:]:
+        copy.start()
+    third = load_all([(mid_from, mid_ref), (cot_from, cot_ref)], early_sem.at[pl.ds(3, 2)])
     greet_with_line(at, [at.sibling] + [at.near(q)[0] for q in range(1, at.chips)])
     grad = PlaneSum(at, 0, p_s, near_in, far_in, far_out, near, far)
     down = LineReduce(at, down_own, down_land, down_up, down_low)
@@ -1035,6 +1046,7 @@
         return pl.ds(pl.multiple_of(d * span, span), span)
 
     load[0].wait()
+    first[0].wait()
 
     def down_grad(n, carry):
         d = at.far_first(n)
@@ -1043,8 +1055,8 @@
         return carry
 
     down_grad(0, 0)
-    load[1].wait()
-    load[2].wait()
+    for copy in load[1:3] + second:
+        copy.wait()
 
     def back(k, carry):
         q = at.chips - 1 - k
@@ -1109,6 +1121,8 @@
     for c in range(max(at.chips - 2, 0), at.chips):
         keep_q(c).wait()
     gain_s[...] = jnp.zeros(gain_s.shape, F32)
+    for copy in third:
+        copy.wait()
     grad.arrive()
 
     def norm_back(rows):
@@ -1215,9 +1229,15 @@
             jax.ShapeDtypeStruct((outer, span, hidden - cut + LANES), BF16),
             jax.ShapeDtypeStruct((outer, span, hidden - LANES), BF16),
         ),
-        in_specs=[IN_VMEM] * 6 + [IN_HBM] * 5,
+        in_specs=[IN_HBM] * 5 + [IN_VMEM] + [IN_HBM] * 5,
         out_specs=[IN_VMEM] * 2 + [IN_HBM] * 6,
         scratch_shapes=[
+            pltpu.VMEM((tokens, hidden), BF16),
+            pltpu.VMEM((tokens, hidden), BF16),
+            pltpu.VMEM((tokens, hidden), BF16),
+            pltpu.VMEM((rows, cols), F32),
+            pltpu.VMEM((rows, cols), BF16),
+            DMA((5,)),
             pltpu.VMEM((chips, 2 * rows, cols), BF16),
             pltpu.VMEM((2, 2 * rows, cols), BF16),
             pltpu.VMEM((rows, cols), BF16),
@@ -1254,13 +1274,13 @@
     blocks,
     block_width,
     dout_ref,
-    wo_ref,
-    proj_ref,
-    h_ref,
-    v_ref,
+    wo_from,
+    proj_from,
+    h_from,
+    v_from,
+    mid_from,
     par_ref,
     gates_ref,
-    mid_ref,
     q_ref,
     rest_ref,
     both_ref,
@@ -1268,6 +1288,12 @@
     totals_ref,
     result_ref,
     rest_out,
+    wo_ref,
+    proj_ref,
+    h_ref,
+    v_ref,
+    mid_ref,
+    early_sem,
     q_s,
     near_in,
     far_in,
@@ -1336,6 +1362,7 @@
     for q in reversed(range(at.chips)):
         value.to_sibling(q).start()
         keep(q).start()
+    early = load_all([(wo_from, wo_ref)], early_sem)
     span = quarters * chunk
 
     def load(p):
@@ -1345,6 +1372,11 @@
 
     for p in range(parts):
         load(p).start()
+    later = load_all(
+        [(proj_from, proj_ref), (h_from, h_ref), (v_from, v_ref), (mid_from, mid_ref)],
+        early_sem.at[pl.ds(1, 4)],
+    )
+    early[0].wait()
 
     def back_project(k, carry):
         load(2 * k).wait()
@@ -1362,6 +1394,8 @@
     for q in range(at.chips):
         keep(q).wait()
     value.combine(q_s)
+    for copy in later:
+        copy.wait()
     log_scale = -DECAY_SCALE * softplus(-par_ref[DECAY : DECAY + 1, :])
     bias = jnp.concatenate(
         [par_ref[RATE_B : RATE_B + 1, :], par_ref[ENTRY_B : ENTRY_B + 1, :]], axis=1
@@ -1533,9 +1567,11 @@
             jax.ShapeDtypeStruct((rows, cols), BF16),
             jax.ShapeDtypeStruct(rest.shape[1:], BF16),
         ),
-        in_specs=[IN_HBM] + [IN_VMEM] * 7 + [IN_HBM] * 2,
+        in_specs=[IN_HBM] * 6 + [IN_VMEM] * 2 + [IN_HBM] * 2,
         out_specs=[IN_VMEM] * 4 + [IN_HBM],
         scratch_shapes=[
+            *[pltpu.VMEM(x.shape, x.dtype) for x in (w_out, proj, h, v, mid)],
+            DMA((5,)),
             pltpu.VMEM((chips, rows, cols), BF16),
             buffers,
             buffers,
@@ -1565,7 +1601,7 @@
         ),
         cost_estimate=cost(21),
         name="scan_backward",
-    )(dout, w_out, proj, h, v, params, gates, mid, q, rest)
+    )(dout, w_out, proj, h, v, mid, params, gates, q, rest)
 
 
 def remote(src, dst, send, recv, to):
@@ -1582,7 +1618,7 @@
     lax.fori_loop(start // 16, rows // 16, one, 0)
 
 
-def fetch(pairs, sems):
+def load_all(pairs, sems):
     copies = [
         pltpu.make_async_copy(src, dst, sems.at[k]) for k, (src, dst) in enumerate(pairs)
     ]
@@ -1604,18 +1640,24 @@
     def mine(self):
         return pltpu.make_async_copy(self.rows(self.me), self.out.at[self.me], self.local)
 
+    def hop(self, k):
+        to, slot = self.at.near(*self.hops[k])
+        sems, n = self.sems, self.n
+        return remote(
+            self.rows(slot), self.out.at[self.me], sems.at[0, n, k], sems.at[1, n, k], to
+        )
+
     def start(self):
-        self.send = Sent()
-        for k, (q, other) in enumerate(self.hops):
-            to, slot = self.at.near(q, other)
-            self.send(self.rows(slot), self.out.at[self.me], self.sems, (self.n, k), to)
+        for k in range(len(self.hops)):
+            self.hop(k).start()
         self.mine().start()
 
     def finish(self):
         for k, (q, other) in enumerate(self.hops):
             source, slot = self.at.near(q, other, True)
             received(self.rows(self.me), self.out.at[slot], self.sems, (self.n, k), source)
-        self.send.finish()
+        for k in range(len(self.hops)):
+            self.hop(k).wait_send()
         self.mine().wait()
 
 
@@ -1623,11 +1665,11 @@
     outer,
     inner,
     shards,
-    both_ref,
-    wi_ref,
-    z_ref,
-    x_ref,
-    dmid_ref,
+    both_from,
+    wi_from,
+    z_from,
+    x_from,
+    dmid_from,
     gain_ref,
     gain2_ref,
     blocks_ref,
@@ -1647,6 +1689,12 @@
     gate_out,
     rest_out,
     up_out,
+    both_ref,
+    wi_ref,
+    z_ref,
+    x_ref,
+    dmid_ref,
+    early_sem,
     p_s,
     up_own,
     up_land,
@@ -1707,8 +1755,12 @@
     def owner(k):
         return lax.rem(s + k + 1, parts)
 
+    pairs = [(both_from, both_ref), (wi_from, wi_ref)]
+    first = load_all(pairs, early_sem)
     for copy in stripes(0):
         copy.start()
+    pairs = [(z_from, z_ref), (x_from, x_ref), (dmid_from, dmid_ref)]
+    second = load_all(pairs, early_sem.at[pl.ds(2, 3)])
 
     def anyone(k):
         to = lax.rem(me + k, at.count)
@@ -1724,6 +1776,9 @@
     fetch.wait()
 
     ups.early(0, at.far_first(0), min(1, outer - 2))
+
+    for copy in first:
+        copy.wait()
 
     def back(n, carry):
         d = at.far_first(n)
@@ -1775,6 +1830,9 @@
             (p, h),
         )
 
+    for copy in second:
+        copy.wait()
+
     def weight_grads(k, carry):
         p, slot = owner(k), lax.rem(k, 2)
         for copy in stripes(k):
@@ -1814,8 +1872,6 @@
         return carry
 
     lax.fori_loop(0, parts, sibling_sums, 0)
-    for exchange in exchanges:
-        exchange.start()
     gain_s[...] = jnp.zeros(gain_s.shape, F32)
 
     def mix_step(k):
@@ -1841,6 +1897,15 @@
         gain_s[...] += dn1 * x * scale
         grad_ref[rows, :] = dmid_ref[rows, :] + rms_back(x, scale, gain_ref[...], dn1)
 
+    def finish_ups(o0):
+        ups.absorb(o0, o0)
+
+        def keep_up(rows):
+            up_sum[rows, :] = up_own[at.o, rows, :]
+
+        add_rows(up_sum.shape[0], keep_up)
+        up_exchange.start()
+
     def branch(o0):
         ends = o0 in (0, outer - 1)
 
@@ -1849,10 +1914,14 @@
         def between(n):
             if n + sooner < outer - 1 and ends:
                 ups.push(o0, ups.order(o0)[n + sooner])
-            for k in range(n * inner, (n + 1) * inner):
-                mix_step(k)
+            for k in range(n * inner, parts if n == outer - 2 else (n + 1) * inner):
+                if n < outer - 1:
+                    mix_step(k)
             if n + 1 < outer - 1 and not ends:
                 ups.step(o0, n + 1)
+            if n == outer - 2:
+                for exchange in exchanges:
+                    exchange.start()
 
         if not ends:
             ups.step(o0, 0)
@@ -1887,18 +1956,8 @@
         return carry
 
     lax.fori_loop(1, at.count, gain_start, 0)
-
-    def last_up(o0):
-        ups.absorb(o0, o0)
-        ups.finish(o0)
-
-    at.branches(last_up)
-
-    def keep_up(rows):
-        up_sum[rows, :] = up_own[at.o, rows, :]
-
-    add_rows(up_sum.shape[0], keep_up)
-    up_exchange.start()
+    at.branches(finish_ups)
+
     for n, (src, slots, out) in enumerate(small):
         for dy in steps:
             here = slots.at[at.along(-dy)]
@@ -1922,6 +1981,7 @@
         to_owner(k, True).wait_recv()
     for exchange in exchanges + [up_exchange]:
         exchange.finish()
+    at.branches(ups.finish)
     for k in range(parts):
         for dy in range(ys):
             to_sibling(k, dy).wait_send()
@@ -1980,9 +2040,11 @@
             jax.ShapeDtypeStruct((1, lanes), F32),
             *[swapped(array) for array in (down, gate, rest, ups)],
         ),
-        in_specs=[IN_VMEM] * 9 + [IN_HBM] * 6,
+        in_specs=[IN_HBM] * 5 + [IN_VMEM] * 4 + [IN_HBM] * 6,
         out_specs=[IN_VMEM] * 5 + [IN_HBM] * 4,
         scratch_shapes=[
+            *[pltpu.VMEM(value.shape, value.dtype) for value in (both, w_in, z, x, dmid)],
+            DMA((5,)),
             pltpu.VMEM((outer, inner * rows, cols), BF16),
             *reduce_vmem,
             pltpu.VMEM((span, hidden), BF16),

time: 450 us -> 444 us (0.987)
  Pallas kernels: 419 us -> 413 us
where the time goes in v7:
time: 444 us; the launch traced here: 437 us
  Pallas kernels  413 us (93%)
  matrix products  16.5 us (4%)
    pallas_call x1, Pallas kernels, forward(): pl.pallas_call(functools.partial(forward_kernel, outer, inner, shards, qu...  140 us
    pallas_call x1, Pallas kernels, closing(): pl.pallas_call(functools.partial(closing_kernel, outer, inner, shards), o...  114 us
    pallas_call x1, Pallas kernels, turn(): pl.pallas_call(functools.partial(turn_kernel, outer, inner, shards), out_...  105 us
    pallas_call x1, Pallas kernels, scan_backward(): pl.pallas_call(functools.partial(scan_backward_kernel, outer, inner, shar...  47.3 us
    dot_general x3, matrix products, dot(): lax.dot_general(left, right, (dims, ((), ())), preferred_element_type=F32)  16.5 us

profile of v7, /device:TPU:9, one launch (start us, length us, event | category | flops | bytes accessed | tf_op | source)
XLA Modules:
  0.0 436.6 jit_solution(7831981608325487845)
XLA Ops:
  0.7 0.0 copy-start
  0.7 1.8 copy-done
  2.5 0.1 constant_dynamic-slice_fusion
  2.5 0.8 pad.13.wo_ref
  3.3 1.3 constant_dynamic-slice_fusion.1
  4.6 0.2 copy.39
  4.8 0.2 copy.38
  5.0 1.0 fusion.17.wi_ref
  6.0 139.7 %forward.1 = (f32[8,384]{1,0:T(8,128)}, f32[128,2048]{1,0:T(8,128)}, bf16[1024,384]{1,0:T(8,128)(2,1)}, f32[1024,384]{1,0:T(8,128)}, bf16[1024,384]{1,0:T(8,128)...) custom-call(bf16[128,2048]{1,0:T(8,128)(2,1)} %bitcast.38, ...), custom_call_target="tpu_custom_call" | custom-call | bytes 462000000 | tf_op jit(solution)/shard_map/forward/pallas_call | solution.py:841
  145.7 0.0 slice-start.1
  145.7 0.0 copy-start.2
  145.7 0.0 slice-start.2
  145.7 6.4 %fusion.13 = f32[1024,768]{1,0:T(8,128)S(1)} fusion(bf16[1024,2048]{1,0:T(8,128)(2,1)} %bitcast.32, bf16[1536,2048]{1,0:T(8,128)(2,1)} %wd_ref.1, s32[]{:T(128)S(6)} %select_n.5), kind=kOutput, calls=%fused_computation.18 | convolution fusion | flops 3221225472 | bytes 10485764 | tf_op jit(solution)/shard_map/dot_general | solution.py:32
  152.1 0.0 slice-done
  152.1 0.0 slice-done.1
  152.1 0.0 copy-done.2
  152.1 0.0 slice-start.3
  152.1 3.4 fusion.9
  155.6 6.7 %multiply_convert_fusion = (bf16[1024,768]{1,0:T(8,128)(2,1)}, bf16[1024,768]{1,0:T(8,128)(2,1)}, bf16[1024,768]{1,0:T(8,128)(2,1)}) fusion(f32[1024,768]{1,0:T(8,128)S(1)} %fusion.9, f32[1024,768]{1,0:T(8,128)S(1)} %fusion.13, bf16[1024,2048]{1,0:T(8,128)(2,1)S(1)} %bitcast.31, bf16[2048,1536]{1,0:T(8,128)(2,1)S(1)} %bitcast.28, s32[]{:T(128)S(6)} %select_n.5), kind=kOutput, calls=%fused_computation.10 | convolution fusion | flops 3240886272 | bytes 18350084 | tf_op jit(solution)/shard_map/dot_general | solution.py:32
  162.3 104.6 %turn.1 = (f32[128,2048]{1,0:T(8,128)}, f32[1,2048]{1,0:T(1,128)}, bf16[8,128,2048]{2,1,0:T(8,128)(2,1)}, bf16[4,256,2048]{2,1,0:T(8,128)(2,1)}, bf16[512,768]{1...) custom-call(bf16[1024,768]{1,0:T(8,128)(2,1)} %get-tuple-element.137.dgm_from, ...), custom_call_target="tpu_custom_call" | custom-call | bytes 363000000 | tf_op jit(solution)/shard_map/turn/pallas_call | solution.py:1220
  267.0 47.3 %scan_backward.1 = (bf16[1024,768]{1,0:T(8,128)(2,1)}, f32[704,256]{1,0:T(8,128)}, f32[8,384]{1,0:T(8,128)}, bf16[128,2048]{1,0:T(8,128)(2,1)}, bf16[512,512]{1,0:T(8,128)(2,1)}) custom-call(bf16[8,128,2048]{2,1,0:T(8,128)(2,1)} %get-tuple-element.71.dout_ref, bf16[4,384,512]{2,1,0:T(8,128)(2,1)} %get-tuple-element.72.wo_from, ...), custom_call_target="tpu_custom_call" | custom-call | bytes 69300000 | tf_op jit(solution)/shard_map/scan_backward/pallas_call | solution.py:1559
  314.2 0.0 copy-start.1
  314.2 114.2 %closing.1 = (f32[128,2048]{1,0:T(8,128)}, bf16[8,64,1152]{2,1,0:T(8,128)(2,1)}, f32[704,256]{1,0:T(8,128)}, f32[8,384]{1,0:T(8,128)}, f32[1,128]{1,0:T(1,128)},...) custom-call(bf16[1024,768]{1,0:T(8,128)(2,1)} %get-tuple-element.80., ...), custom_call_target="tpu_custom_call" | custom-call | bytes 264000000 | tf_op jit(solution)/shard_map/closing/pallas_call | solution.py:2033
  428.5 7.6 %unpack.1 = (f32[64,6144]{1,0:T(8,128)}, f32[64,6144]{1,0:T(8,128)}, f32[64,6144]{1,0:T(8,128)}, f32[64,2736]{1,0:T(8,128)}, f32[64,2736]{1,0:T(8,128)}, /*index...) custom-call(bf16[8,64,384]{2,1,0:T(8,128)(2,1)} %get-tuple-element.9, ...), custom_call_target="tpu_custom_call" | custom-call | bytes 16500000 | tf_op jit(solution)/shard_map/unpack/pallas_call | solution.py:2174
  (6 shorter events, 0.0 us)
Async XLA Ops:
  0.7 1.8 copy-start
  6.0 146.1 %slice-start = ((s8[6291456]{0:T(1024)(128)(4,1)}), s8[2097152]{0:T(1024)(128)(4,1)S(1)}, s32[]{:S(2)}) async-start(s8[6291456]{0:T(1024)(128)(4,1)} %bitcast.25), calls=%async_computation | async-start | bytes 4194304
  145.7 6.4 %slice-start.1 = ((s8[6291456]{0:T(1024)(128)(4,1)}), s8[4194304]{0:T(1024)(128)(4,1)S(1)}, s32[]{:S(2)}) async-start(s8[6291456]{0:T(1024)(128)(4,1)} %bitcast.25), calls=%async_computation.1 | async-start | bytes 8388608
  145.7 6.4 %copy-start.2 = (bf16[8,128,2048]{2,1,0:T(8,128)(2,1)S(1)}, bf16[8,128,2048]{2,1,0:T(8,128)(2,1)}, u32[]{:S(2)}) copy-start(bf16[8,128,2048]{2,1,0:T(8,128)(2,1)} %get-tuple-element.69) | copy-start | bytes 12582916
  145.7 9.9 %slice-start.2 = ((s8[6291456]{0:T(1024)(128)(4,1)}), s8[4194304]{0:T(1024)(128)(4,1)S(1)}, s32[]{:S(2)}) async-start(s8[6291456]{0:T(1024)(128)(4,1)} %bitcast.27), calls=%async_computation.2 | async-start | bytes 8388608
  152.1 3.5 slice-start.3
  314.2 121.9 %copy-start.1 = (bf16[2736,512]{1,0:T(8,128)(2,1)S(1)}, bf16[2736,512]{1,0:T(8,128)(2,1)}, u32[]{:S(2)}) copy-start(bf16[2736,512]{1,0:T(8,128)(2,1)} %param.28) | copy-start | bytes 8404996

commit v8 on v7

--- a/solution.py
+++ b/solution.py
@@ -1075,8 +1075,12 @@
     lax.fori_loop(0, at.chips, back, 0)
     grad.to_sibling(0).wait_recv()
     lax.fori_loop(1, outer, down_grad, 0)
+    def first_down(o0):
+        if 0 < o0 < outer - 1:
+            down.step(o0, 0)
+
+    at.branches(first_down)
     load[3].wait()
-
     cut = gate_own.shape[2]
 
     def keep_r(n):
@@ -1097,11 +1101,6 @@
     for n in range(max(outer - 2, 0), outer):
         keep_r(n).wait()
 
-    def first_down(o0):
-        if 0 < o0 < outer - 1:
-            down.step(o0, 0)
-
-    at.branches(first_down)
     load[4].wait()
 
     def keep_q(c):
@@ -1117,9 +1116,6 @@
         keep_q(c).start()
         return carry
 
-    lax.fori_loop(0, at.chips, ahead, 0)
-    for c in range(max(at.chips - 2, 0), at.chips):
-        keep_q(c).wait()
     gain_s[...] = jnp.zeros(gain_s.shape, F32)
     for copy in third:
         copy.wait()
@@ -1177,7 +1173,9 @@
                     down.push(o0, down.order(o0)[outer - 2])
                     for d in gate.order(o0)[:-1]:
                         gate.push(o0, d)
-                else:
+                lax.fori_loop(0, at.chips, ahead, 0)
+            if k == 1:
+                if not ends:
                     for n in range(1, outer - 1):
                         down.step(o0, n)
                 lax.fori_loop(0, outer, up_grad, 0)
@@ -1201,6 +1199,8 @@
         copy.start()
     for n in range(max(outer - 2, 0), outer):
         keep_u(n).wait()
+    for c in range(max(at.chips - 2, 0), at.chips):
+        keep_q(c).wait()
     grad.finish()
     keep.wait()
     for copy in last:
@@ -2100,17 +2100,18 @@
     fetch = [
         pltpu.make_async_copy(sources[k], held[k], in_sem.at[k]) for k in range(len(held))
     ]
-    for copy in fetch:
+    for copy in fetch[7:] + fetch[:7]:
         copy.start()
     store = []
     gains_ref = sources[9]
     rate, entry, taps, conv_b, rate_b, entry_b, decay, first_gain, second_gain = targets[8:]
-    for copy in fetch:
-        copy.wait()
     for k in range(2):
+        fetch[7 + k].wait()
         copy = pltpu.make_async_copy(held[7 + k], targets[6 + k], out_sem.at[6 + k])
         copy.start()
         store.append(copy)
+    fetch[0].wait()
+    fetch[1].wait()
     gate, up, down = made[:3]
     slots, piece, hidden = down_ref.shape
     cut = gate_ref.shape[2]
@@ -2131,19 +2132,24 @@
         gate[:, first : first + cut] = gate_ref[slot].astype(F32)
         gate[:, first + cut : first + hidden] = rest_ref[slot][:, :tail].astype(F32)
     ship(0)
+    fetch[2].wait()
     for first, slot in places:
         up[:, first : first + head] = rest_ref[slot][:, tail:].astype(F32)
         up[:, first + head : first + hidden] = up_ref[slot].astype(F32)
     ship(1)
+    fetch[3].wait()
     for first, slot in places:
         down[:, first : first + hidden] = down_ref[slot].astype(F32)
     ship(2)
+    fetch[4].wait()
     for k in range(3):
         lanes = slice(k * width, k * width + width)
         made[3 + k][...] = jnp.concatenate(
             [mix_ref[p][:, lanes].astype(F32)[:, :channels] for p in range(parts)], axis=1
         )
         ship(3 + k)
+    fetch[5].wait()
+    fetch[6].wait()
     blocks = rate.shape[1]
     tall = blocks_ref.shape[0] // (2 * blocks)
     for k, dst in enumerate((rate, entry)):

time: 444 us -> 440 us (level)
  no operation moved by 1% of the time
where the time goes in v8:
time: 440 us; the launch traced here: 433 us
  Pallas kernels  410 us (93%)
  matrix products  16.5 us (4%)
    pallas_call x1, Pallas kernels, forward(): pl.pallas_call(functools.partial(forward_kernel, outer, inner, shards, qu...  140 us
    pallas_call x1, Pallas kernels, closing(): pl.pallas_call(functools.partial(closing_kernel, outer, inner, shards), o...  114 us
    pallas_call x1, Pallas kernels, turn(): pl.pallas_call(functools.partial(turn_kernel, outer, inner, shards), out_...  102 us
    pallas_call x1, Pallas kernels, scan_backward(): pl.pallas_call(functools.partial(scan_backward_kernel, outer, inner, shar...  47.5 us
    dot_general x3, matrix products, dot(): lax.dot_general(left, right, (dims, ((), ())), preferred_element_type=F32)  16.5 us

profile of v8, /device:TPU:9, one launch (start us, length us, event | category | flops | bytes accessed | tf_op | source)
XLA Modules:
  0.0 432.9 jit_solution(16047827567228312803)
XLA Ops:
  0.7 0.0 copy-start
  0.7 1.8 copy-done
  2.5 0.1 constant_dynamic-slice_fusion
  2.5 0.8 pad.13.wo_ref
  3.3 1.3 constant_dynamic-slice_fusion.1
  4.6 0.2 copy.39
  4.8 0.2 copy.38
  5.0 1.0 fusion.17.wi_ref
  6.0 139.7 %forward.1 = (f32[8,384]{1,0:T(8,128)}, f32[128,2048]{1,0:T(8,128)}, bf16[1024,384]{1,0:T(8,128)(2,1)}, f32[1024,384]{1,0:T(8,128)}, bf16[1024,384]{1,0:T(8,128)...) custom-call(bf16[128,2048]{1,0:T(8,128)(2,1)} %bitcast.38, ...), custom_call_target="tpu_custom_call" | custom-call | bytes 462000000 | tf_op jit(solution)/shard_map/forward/pallas_call | solution.py:841
  145.7 0.0 slice-start.1
  145.7 0.0 copy-start.2
  145.7 0.0 slice-start.2
  145.7 6.4 %fusion.13 = f32[1024,768]{1,0:T(8,128)S(1)} fusion(bf16[1024,2048]{1,0:T(8,128)(2,1)} %bitcast.32, bf16[1536,2048]{1,0:T(8,128)(2,1)} %wd_ref.1, s32[]{:T(128)S(6)} %select_n.5), kind=kOutput, calls=%fused_computation.18 | convolution fusion | flops 3221225472 | bytes 10485764 | tf_op jit(solution)/shard_map/dot_general | solution.py:32
  152.1 0.0 slice-done
  152.1 0.0 slice-start.3
  152.1 3.4 fusion.9
  155.6 0.0 slice-done.2
  155.6 0.0 slice-done.3
  155.6 6.7 %multiply_convert_fusion = (bf16[1024,768]{1,0:T(8,128)(2,1)}, bf16[1024,768]{1,0:T(8,128)(2,1)}, bf16[1024,768]{1,0:T(8,128)(2,1)}) fusion(f32[1024,768]{1,0:T(8,128)S(1)} %fusion.9, f32[1024,768]{1,0:T(8,128)S(1)} %fusion.13, bf16[1024,2048]{1,0:T(8,128)(2,1)S(1)} %bitcast.31, bf16[2048,1536]{1,0:T(8,128)(2,1)S(1)} %bitcast.28, s32[]{:T(128)S(6)} %select_n.5), kind=kOutput, calls=%fused_computation.10 | convolution fusion | flops 3240886272 | bytes 18350084 | tf_op jit(solution)/shard_map/dot_general | solution.py:32
  162.3 101.9 %turn.1 = (f32[128,2048]{1,0:T(8,128)}, f32[1,2048]{1,0:T(1,128)}, bf16[8,128,2048]{2,1,0:T(8,128)(2,1)}, bf16[4,256,2048]{2,1,0:T(8,128)(2,1)}, bf16[512,768]{1...) custom-call(bf16[1024,768]{1,0:T(8,128)(2,1)} %get-tuple-element.137.dgm_from, ...), custom_call_target="tpu_custom_call" | custom-call | bytes 363000000 | tf_op jit(solution)/shard_map/turn/pallas_call | solution.py:1220
  264.3 47.5 %scan_backward.1 = (bf16[1024,768]{1,0:T(8,128)(2,1)}, f32[704,256]{1,0:T(8,128)}, f32[8,384]{1,0:T(8,128)}, bf16[128,2048]{1,0:T(8,128)(2,1)}, bf16[512,512]{1,0:T(8,128)(2,1)}) custom-call(bf16[8,128,2048]{2,1,0:T(8,128)(2,1)} %get-tuple-element.71.dout_ref, bf16[4,384,512]{2,1,0:T(8,128)(2,1)} %get-tuple-element.72.wo_from, ...), custom_call_target="tpu_custom_call" | custom-call | bytes 69300000 | tf_op jit(solution)/shard_map/scan_backward/pallas_call | solution.py:1559
  311.8 0.0 copy-start.1
  311.8 114.0 %closing.1 = (f32[128,2048]{1,0:T(8,128)}, bf16[8,64,1152]{2,1,0:T(8,128)(2,1)}, f32[704,256]{1,0:T(8,128)}, f32[8,384]{1,0:T(8,128)}, f32[1,128]{1,0:T(1,128)},...) custom-call(bf16[1024,768]{1,0:T(8,128)(2,1)} %get-tuple-element.80., ...), custom_call_target="tpu_custom_call" | custom-call | bytes 264000000 | tf_op jit(solution)/shard_map/closing/pallas_call | solution.py:2033
  425.8 6.6 %unpack.1 = (f32[64,6144]{1,0:T(8,128)}, f32[64,6144]{1,0:T(8,128)}, f32[64,6144]{1,0:T(8,128)}, f32[64,2736]{1,0:T(8,128)}, f32[64,2736]{1,0:T(8,128)}, /*index...) custom-call(bf16[8,64,384]{2,1,0:T(8,128)(2,1)} %get-tuple-element.9, ...), custom_call_target="tpu_custom_call" | custom-call | bytes 16500000 | tf_op jit(solution)/shard_map/unpack/pallas_call | solution.py:2180
  (6 shorter events, 0.0 us)
Async XLA Ops:
  0.7 1.8 copy-start
  6.0 146.1 %slice-start = ((s8[6291456]{0:T(1024)(128)(4,1)}), s8[2097152]{0:T(1024)(128)(4,1)S(1)}, s32[]{:S(2)}) async-start(s8[6291456]{0:T(1024)(128)(4,1)} %bitcast.25), calls=%async_computation | async-start | bytes 4194304
  145.7 6.4 %slice-start.1 = ((s8[6291456]{0:T(1024)(128)(4,1)}), s8[4194304]{0:T(1024)(128)(4,1)S(1)}, s32[]{:S(2)}) async-start(s8[6291456]{0:T(1024)(128)(4,1)} %bitcast.25), calls=%async_computation.1 | async-start | bytes 8388608
  145.7 6.4 %copy-start.2 = (bf16[8,128,2048]{2,1,0:T(8,128)(2,1)S(1)}, bf16[8,128,2048]{2,1,0:T(8,128)(2,1)}, u32[]{:S(2)}) copy-start(bf16[8,128,2048]{2,1,0:T(8,128)(2,1)} %get-tuple-element.69) | copy-start | bytes 12582916
  145.7 9.9 %slice-start.2 = ((s8[6291456]{0:T(1024)(128)(4,1)}), s8[4194304]{0:T(1024)(128)(4,1)S(1)}, s32[]{:S(2)}) async-start(s8[6291456]{0:T(1024)(128)(4,1)} %bitcast.27), calls=%async_computation.2 | async-start | bytes 8388608
  152.1 3.5 slice-start.3
  311.8 120.6 %copy-start.1 = (bf16[2736,512]{1,0:T(8,128)(2,1)S(1)}, bf16[2736,512]{1,0:T(8,128)(2,1)}, u32[]{:S(2)}) copy-start(bf16[2736,512]{1,0:T(8,128)(2,1)} %param.28) | copy-start | bytes 8404996

commit v9 on v8

--- a/solution.py
+++ b/solution.py
@@ -188,14 +188,15 @@
 ):
     send = Sent()
     rows = x_ref.shape[0]
-    half = rows // HALVES
+    parts = across.shape[2]
+    half = rows // parts
     low = pl.ds(rows - slim, slim)
 
     def slot(row, other=False):
         return out.at[row * at.inner + (1 - at.i if other else at.i)]
 
     def some(row, part):
-        less = slim if slim and row != o0 and part == HALVES - 1 else 0
+        less = slim if slim and row != o0 and part == parts - 1 else 0
         return pl.ds(part * half, half - less)
 
     def pass_on(row, part, sems, to):
@@ -208,7 +209,7 @@
         send(src.at[some(row, part)], slot(row).at[some(row, part)], across, (row, part), at.beside)
 
     def crossed(row):
-        for part in range(HALVES):
+        for part in range(parts):
             here = slot(row, True).at[some(row, part)]
             received(here, here, across, (row, part), at.beside)
 
@@ -225,7 +226,7 @@
 
     for k in range(at.outer):
         lower, upper = o0 - k, o0 + k
-        for part in range(HALVES):
+        for part in range(parts):
             here = x_ref.at[pl.ds(part * half, half)]
             if lower >= 0:
                 if k > 0:
@@ -268,6 +269,7 @@
         self.x_in, self.up_in, self.down_in, self.sums = bufs
         self.across, self.up, self.down = sems
         self.rows = self.x_in.shape[1]
+        self.parts = self.across.shape[2]
         self.slim = 0
         if side is not None:
             self.s_up_in, self.s_down_in, self.s_sums, self.s_in = side[:4]
@@ -278,8 +280,8 @@
         return self.p.at[d, pl.ds(pl.multiple_of(i * self.rows, self.rows), self.rows)]
 
     def cross(self, d, part):
-        half = self.rows // HALVES
-        some = pl.ds(part * half, half - (self.slim if part == HALVES - 1 else 0))
+        half = self.rows // self.parts
+        some = pl.ds(part * half, half - (self.slim if part == self.parts - 1 else 0))
         return remote(
             self.block(d, 1 - self.at.i).at[some],
             self.x_in.at[d].at[some],
@@ -289,14 +291,14 @@
         )
 
     def start(self, d):
-        for part in range(HALVES):
+        for part in range(self.parts):
             self.cross(d, part).start()
 
     def steps(self, o0, last_add, between=lambda n: None):
         at, rows, slim = self.at, self.rows, self.slim
         send = Sent()
         order = sorted(range(at.outer), key=lambda d: (-abs(d - o0), d))
-        low, half = rows - slim, rows // HALVES
+        low, half = rows - slim, rows // self.parts
 
         def arrivals(d, index, mine, up_in, down_in, up, down):
             terms = []
@@ -317,7 +319,7 @@
         for n, d in enumerate(order):
             mine = self.block(d, at.i)
             target = self.sums.at[d]
-            for part in range(HALVES):
+            for part in range(self.parts):
                 part_rows = pl.ds(part * half, half)
                 self.cross(d, part).wait_recv()
                 along = [mine] + arrivals(
@@ -342,7 +344,7 @@
                     target[some, :] = total_of(along, some).astype(BF16)
 
                 add_rows(min((part + 1) * half, low), add, part * half)
-                if slim and d != o0 and part == HALVES - 1:
+                if slim and d != o0 and part == self.parts - 1:
                     add_rows(rows, add_low, low)
                 if d > o0:
                     here, there = target.at[part_rows], self.up_in.at[d].at[part_rows]
@@ -373,7 +375,7 @@
                         last_add(some, total_of(along, some) + self.s_in[here, :].astype(F32))
             between(n)
         for d in range(at.outer):
-            for part in range(HALVES):
+            for part in range(self.parts):
                 self.cross(d, part).wait_send()
         send.finish()
 
@@ -464,8 +466,8 @@
     return blocks, [DMA((2, outer))] * 2 + [DMA((2,))]
 
 
-def line_sum_scratch(outer, rows, cols):
-    return [pltpu.VMEM((outer, rows, cols), BF16)] * 4, [DMA((2, outer, HALVES))] * 3
+def line_sum_scratch(outer, rows, cols, parts=HALVES):
+    return [pltpu.VMEM((outer, rows, cols), BF16)] * 4, [DMA((2, outer, parts))] * 3
 
 
 def row_rms(values):
@@ -827,7 +829,7 @@
     rows, cols = x.shape
     parts, ys, chips = outer * inner, shards // 2, inner * shards // 2
     length, width = parts * rows, w_in.shape[1] // 2
-    bufs, sems = line_sum_scratch(outer, rows, cols)
+    bufs, sems = line_sum_scratch(outer, rows, cols, 2 * HALVES)
     side_vmem, side_sems = slim_scratch(outer, cols)
     plane = jax.ShapeDtypeStruct((inner * shards, rows, cols), BF16)
     lanes = pltpu.VMEM((width // LANES, length, LANES), F32)
@@ -866,7 +868,7 @@
             pltpu.VMEM((rows, cols), BF16),
         ]
         + bufs
-        + [DMA((2, outer, HALVES))] * 3
+        + [DMA((2, outer, 2 * HALVES))] * 3
         + [DMA((2, 2, ys))] * 2
         + sems
         + [DMA((2, chips))] * 2
@@ -1922,6 +1924,7 @@
             if n == outer - 2:
                 for exchange in exchanges:
                     exchange.start()
+                finish_ups(o0)
 
         if not ends:
             ups.step(o0, 0)
@@ -1956,7 +1959,6 @@
         return carry
 
     lax.fori_loop(1, at.count, gain_start, 0)
-    at.branches(finish_ups)
 
     for n, (src, slots, out) in enumerate(small):
         for dy in steps:

time: 440 us -> 437 us (level)
  the two profiles are of different devices: /device:TPU:9 before, /device:TPU:0 now
where the time goes in v9:
time: 437 us; the launch traced here: 430 us
  Pallas kernels  407 us (93%)
  matrix products  16.5 us (4%)
    pallas_call x1, Pallas kernels, forward(): pl.pallas_call(functools.partial(forward_kernel, outer, inner, shards, qu...  137 us
    pallas_call x1, Pallas kernels, closing(): pl.pallas_call(functools.partial(closing_kernel, outer, inner, shards), o...  109 us
    pallas_call x1, Pallas kernels, turn(): pl.pallas_call(functools.partial(turn_kernel, outer, inner, shards), out_...  106 us
    pallas_call x1, Pallas kernels, scan_backward(): pl.pallas_call(functools.partial(scan_backward_kernel, outer, inner, shar...  47.8 us
    dot_general x3, matrix products, dot(): lax.dot_general(left, right, (dims, ((), ())), preferred_element_type=F32)  16.5 us

profile of v9, /device:TPU:0, one launch (start us, length us, event | category | flops | bytes accessed | tf_op | source)
XLA Modules:
  0.0 429.9 jit_solution(3509651877702334910)
XLA Ops:
  0.7 0.0 copy-start
  0.7 1.8 copy-done
  2.5 0.1 constant_dynamic-slice_fusion
  2.5 0.8 pad.13.wo_ref
  3.3 1.3 constant_dynamic-slice_fusion.1
  4.6 0.2 copy.39
  4.8 0.2 copy.38
  5.0 1.0 fusion.17.wi_ref
  6.0 136.7 %forward.1 = (f32[8,384]{1,0:T(8,128)}, f32[128,2048]{1,0:T(8,128)}, bf16[1024,384]{1,0:T(8,128)(2,1)}, f32[1024,384]{1,0:T(8,128)}, bf16[1024,384]{1,0:T(8,128)...) custom-call(bf16[128,2048]{1,0:T(8,128)(2,1)} %bitcast.38, ...), custom_call_target="tpu_custom_call" | custom-call | bytes 462000000 | tf_op jit(solution)/shard_map/forward/pallas_call | solution.py:843
  142.7 0.0 slice-start.1
  142.7 0.0 copy-start.2
  142.7 0.0 slice-start.2
  142.7 6.4 %fusion.13 = f32[1024,768]{1,0:T(8,128)S(1)} fusion(bf16[1024,2048]{1,0:T(8,128)(2,1)} %bitcast.32, bf16[1536,2048]{1,0:T(8,128)(2,1)} %wd_ref.1, s32[]{:T(128)S(6)} %select_n.5), kind=kOutput, calls=%fused_computation.18 | convolution fusion | flops 3221225472 | bytes 10485764 | tf_op jit(solution)/shard_map/dot_general | solution.py:32
  149.1 0.0 slice-done
  149.1 0.0 slice-done.1
  149.1 0.0 slice-start.3
  149.1 3.4 fusion.9
  152.6 6.7 %multiply_convert_fusion = (bf16[1024,768]{1,0:T(8,128)(2,1)}, bf16[1024,768]{1,0:T(8,128)(2,1)}, bf16[1024,768]{1,0:T(8,128)(2,1)}) fusion(f32[1024,768]{1,0:T(8,128)S(1)} %fusion.9, f32[1024,768]{1,0:T(8,128)S(1)} %fusion.13, bf16[1024,2048]{1,0:T(8,128)(2,1)S(1)} %bitcast.31, bf16[2048,1536]{1,0:T(8,128)(2,1)S(1)} %bitcast.28, s32[]{:T(128)S(6)} %select_n.5), kind=kOutput, calls=%fused_computation.10 | convolution fusion | flops 3240886272 | bytes 18350084 | tf_op jit(solution)/shard_map/dot_general | solution.py:32
  159.3 106.4 %turn.1 = (f32[128,2048]{1,0:T(8,128)}, f32[1,2048]{1,0:T(1,128)}, bf16[8,128,2048]{2,1,0:T(8,128)(2,1)}, bf16[4,256,2048]{2,1,0:T(8,128)(2,1)}, bf16[512,768]{1...) custom-call(bf16[1024,768]{1,0:T(8,128)(2,1)} %get-tuple-element.137.dgm_from, ...), custom_call_target="tpu_custom_call" | custom-call | bytes 363000000 | tf_op jit(solution)/shard_map/turn/pallas_call | solution.py:1222
  265.7 47.8 %scan_backward.1 = (bf16[1024,768]{1,0:T(8,128)(2,1)}, f32[704,256]{1,0:T(8,128)}, f32[8,384]{1,0:T(8,128)}, bf16[128,2048]{1,0:T(8,128)(2,1)}, bf16[512,512]{1,0:T(8,128)(2,1)}) custom-call(bf16[8,128,2048]{2,1,0:T(8,128)(2,1)} %get-tuple-element.71.dout_ref, bf16[4,384,512]{2,1,0:T(8,128)(2,1)} %get-tuple-element.72.wo_from, ...), custom_call_target="tpu_custom_call" | custom-call | bytes 69300000 | tf_op jit(solution)/shard_map/scan_backward/pallas_call | solution.py:1561
  313.5 0.0 copy-start.1
  313.5 109.3 %closing.1 = (f32[128,2048]{1,0:T(8,128)}, bf16[8,64,1152]{2,1,0:T(8,128)(2,1)}, f32[704,256]{1,0:T(8,128)}, f32[8,384]{1,0:T(8,128)}, f32[1,128]{1,0:T(1,128)},...) custom-call(bf16[1024,768]{1,0:T(8,128)(2,1)} %get-tuple-element.80., ...), custom_call_target="tpu_custom_call" | custom-call | bytes 264000000 | tf_op jit(solution)/shard_map/closing/pallas_call | solution.py:2035
  422.8 6.6 %unpack.1 = (f32[64,6144]{1,0:T(8,128)}, f32[64,6144]{1,0:T(8,128)}, f32[64,6144]{1,0:T(8,128)}, f32[64,2736]{1,0:T(8,128)}, f32[64,2736]{1,0:T(8,128)}, /*index...) custom-call(bf16[8,64,384]{2,1,0:T(8,128)(2,1)} %get-tuple-element.9, ...), custom_call_target="tpu_custom_call" | custom-call | bytes 16500000 | tf_op jit(solution)/shard_map/unpack/pallas_call | solution.py:2182
  429.5 0.0 copy-done.1
  (6 shorter events, 0.0 us)
Async XLA Ops:
  0.7 1.8 copy-start
  6.0 143.1 %slice-start = ((s8[6291456]{0:T(1024)(128)(4,1)}), s8[2097152]{0:T(1024)(128)(4,1)S(1)}, s32[]{:S(2)}) async-start(s8[6291456]{0:T(1024)(128)(4,1)} %bitcast.25), calls=%async_computation | async-start | bytes 4194304
  142.7 6.4 %slice-start.1 = ((s8[6291456]{0:T(1024)(128)(4,1)}), s8[4194304]{0:T(1024)(128)(4,1)S(1)}, s32[]{:S(2)}) async-start(s8[6291456]{0:T(1024)(128)(4,1)} %bitcast.25), calls=%async_computation.1 | async-start | bytes 8388608
  142.7 6.4 %copy-start.2 = (bf16[8,128,2048]{2,1,0:T(8,128)(2,1)S(1)}, bf16[8,128,2048]{2,1,0:T(8,128)(2,1)}, u32[]{:S(2)}) copy-start(bf16[8,128,2048]{2,1,0:T(8,128)(2,1)} %get-tuple-element.69) | copy-start | bytes 12582916
  142.7 9.9 %slice-start.2 = ((s8[6291456]{0:T(1024)(128)(4,1)}), s8[4194304]{0:T(1024)(128)(4,1)S(1)}, s32[]{:S(2)}) async-start(s8[6291456]{0:T(1024)(128)(4,1)} %bitcast.27), calls=%async_computation.2 | async-start | bytes 8388608
  149.1 3.4 slice-start.3
  313.5 116.0 %copy-start.1 = (bf16[2736,512]{1,0:T(8,128)(2,1)S(1)}, bf16[2736,512]{1,0:T(8,128)(2,1)}, u32[]{:S(2)}) copy-start(bf16[2736,512]{1,0:T(8,128)(2,1)} %param.28) | copy-start | bytes 8404996
